TPU v7x, 32 devices: a whole 2x2x4 slice. The times are simulated.
32 devices in a mesh: dp: 8 (over z, core), seq: 4 (over y, x).
Axes of the slice: x: 2, y: 2, z: 4, core: 2. Of those that a mesh axis runs over, the one named last changes fastest.
Arguments:
- tokens: bfloat16 [1024, 4096], P(('dp', 'seq')), may hold values from -6 to 6
- modality: int32 [1024], P(('dp', 'seq')), may hold values from 0 to 1, as said below
- gate_weight: bfloat16 [4096, 14336], P(None, 'dp'), may hold values from -0.09375 to 0.09375
- up_weight: bfloat16 [4096, 14336], P(None, 'dp'), may hold values from -0.09375 to 0.09375
- down_weight: bfloat16 [14336, 4096], P('dp'), may hold values from -0.046875 to 0.046875
- out_grad: bfloat16 [768, 4096], P(('dp', 'seq')), may hold values from -1.5 to 1.5
Outputs:
- output: bfloat16 [768, 4096], P(('dp', 'seq'))
- in_grad: bfloat16 [768, 4096], P(('dp', 'seq'))
- gate_grad: bfloat16 [4096, 14336], P('seq', 'dp')
- up_grad: bfloat16 [4096, 14336], P('seq', 'dp')
- down_grad: bfloat16 [14336, 4096], P('dp', 'seq')
Inputs may be any that keep to these rules, and one draw needn't show every extreme that they name: In each aligned block of 32 tokens (the tokens of one device) exactly 24 tokens have modality 1 (vision); all others have 0 (text).
All inputs are finite; a program needn't handle non-finite values.
Results may differ from a plain program's by a relative error of at most 0.014.
Values may be sent and summed in bfloat16 or wider, within the bound.
No kernel may reach another device: no remote copies, remote signals or barrier semaphores. Data moves between devices by JAX's collectives and lax.ppermute only.
A program may use at most 192 MiB of HBM per device.

v0:
```python
import jax
import jax.numpy as jnp
from jax import lax
from jax.sharding import PartitionSpec as P


def silu_parts(gate_proj):
    sigmoid_value = jax.nn.sigmoid(gate_proj)
    return (gate_proj * sigmoid_value, sigmoid_value * (1.0 + gate_proj * (1.0 - sigmoid_value)))


def contract_cols(left_matrix, right_matrix):
    return lax.dot_general(
        left_matrix, right_matrix, (((1,), (1,)), ((), ())), preferred_element_type=jnp.float32
    )


def group_sum(left_blocks, right_blocks, form):
    partials = jnp.einsum(
        form, left_blocks, right_blocks, preferred_element_type=jnp.float32
    ).astype(jnp.bfloat16)
    partials = lax.optimization_barrier(partials)
    return jnp.sum(partials.astype(jnp.float32), axis=0)


def on_device(tokens, modality, gate_weight, up_weight, down_weight, out_grad):
    vision_count = out_grad.shape[0]
    flags = (modality == 1).astype(jnp.int32)
    ranks = jnp.cumsum(flags) - 1
    slot_ids = jnp.arange(vision_count, dtype=jnp.int32)[:, None]
    selector = ((ranks[None, :] == slot_ids) & (flags[None, :] == 1)).astype(jnp.bfloat16)
    picked = jnp.dot(selector, tokens, preferred_element_type=jnp.float32).astype(jnp.bfloat16)
    token_rows = lax.all_gather(picked, "dp", axis=0, tiled=True)
    gate_proj = jnp.dot(token_rows, gate_weight, preferred_element_type=jnp.float32)
    up_proj = jnp.dot(token_rows, up_weight, preferred_element_type=jnp.float32)
    active, slope = silu_parts(gate_proj)
    hidden = (active * up_proj).astype(jnp.bfloat16)
    output = lax.psum_scatter(
        jnp.dot(hidden, down_weight, preferred_element_type=jnp.float32).astype(jnp.bfloat16),
        "dp",
        scatter_dimension=0,
        tiled=True,
    )
    cotangent_rows = lax.all_gather(out_grad, "dp", axis=0, tiled=True)
    back_hidden = contract_cols(cotangent_rows, down_weight)
    gate_back = (back_hidden * up_proj * slope).astype(jnp.bfloat16)
    up_back = (back_hidden * active).astype(jnp.bfloat16)
    in_grad = lax.psum_scatter(
        (contract_cols(gate_back, gate_weight) + contract_cols(up_back, up_weight)).astype(
            jnp.bfloat16
        ),
        "dp",
        scatter_dimension=0,
        tiled=True,
    )
    group_count = lax.axis_size("seq")
    row_total = token_rows.shape[0]
    split_tokens, split_cotangent = (
        lax.all_to_all(token_rows, "seq", split_axis=1, concat_axis=0, tiled=True),
        lax.all_to_all(cotangent_rows, "seq", split_axis=1, concat_axis=0, tiled=True),
    )
    all_hidden, all_gate_back, all_up_back = (
        lax.all_gather(hidden, "seq", axis=0, tiled=True),
        lax.all_gather(gate_back, "seq", axis=0, tiled=True),
        lax.all_gather(up_back, "seq", axis=0, tiled=True),
    )

    def per_group(matrix):
        return matrix.reshape(group_count, row_total, matrix.shape[1])

    gate_total = group_sum(per_group(split_tokens), per_group(all_gate_back), "jrd,jrf->jdf")
    up_total = group_sum(per_group(split_tokens), per_group(all_up_back), "jrd,jrf->jdf")
    down_total = group_sum(per_group(all_hidden), per_group(split_cotangent), "jrf,jrd->jfd")
    return (
        output,
        in_grad,
        gate_total.astype(jnp.bfloat16),
        up_total.astype(jnp.bfloat16),
        down_total.astype(jnp.bfloat16),
    )


def solution(mesh):
    placed = (
        P(("dp", "seq"), None),
        P(("dp", "seq")),
        P(None, "dp"),
        P(None, "dp"),
        P("dp", None),
        P(("dp", "seq"), None),
    )
    return jax.shard_map(
        on_device,
        mesh=mesh,
        in_specs=placed,
        out_specs=(
            P(("dp", "seq"), None),
            P(("dp", "seq"), None),
            P("seq", "dp"),
            P("seq", "dp"),
            P("dp", "seq"),
        ),
        check_vma=False,
    )
```

profile of v0, /device:TPU:0, one launch (start us, length us, event | category | flops | bytes accessed | tf_op | source)
XLA Modules:
  0.0 296.2 jit_solution(6966429705825907858)
XLA Ops:
  7.2 0.0 copy-start
  7.2 0.0 all-gather.6.cloned.1.call-start
  7.2 0.7 fusion.9
  7.9 0.1 copy.13
  8.0 0.1 reduce-window.8
  8.1 0.1 add_reduce_fusion
  8.2 0.0 copy-done
  8.2 0.9 convolution_convert_fusion.4
  9.1 0.0 all-gather.6.cloned.1.call-update
  9.1 0.0 all-gather.8.cloned.1.call-start
  9.1 0.7 all-gather.8.cloned.1.call-update
  9.8 0.0 all-gather.14.cloned.1.call-start
  9.9 28.3 %all-gather.6.cloned.1.call-done = bf16[192,4096]{1,0:T(8,128)(2,1)} async-done(((bf16[24,4096]{1,0:T(8,128)(2,1)}), bf16[192,4096]{1,0:T(8,128)(2,1)}) %all-gather.6.cloned.1.call-update) | async-done | bytes 1572880 | tf_op jit(solution)/shard_map/all_gather | solution.py:33
  38.2 0.0 copy-start.2
  38.2 0.0 copy-start.5
  38.2 9.3 %fusion.12 = f32[192,1792]{1,0:T(8,128)S(1)} fusion(bf16[192,4096]{1,0:T(8,128)(2,1)} %all-gather.6.cloned.1.call-done, bf16[4096,1792]{1,0:T(8,128)(2,1)} %param.9), kind=kOutput, calls=%fused_computation.26 | convolution fusion | flops 2818572288 | bytes 17629184 | tf_op jit(solution)/shard_map/dot_general | solution.py:35
  47.5 0.0 copy-done.2
  47.5 1.3 copy-done.5
  48.8 4.2 %fusion.11 = f32[192,1792]{1,0:T(8,128)} fusion(bf16[192,4096]{1,0:T(8,128)(2,1)S(1)} %copy-done.2, bf16[4096,1792]{1,0:T(8,128)(2,1)S(1)} %copy-done.5), kind=kOutput, calls=%fused_computation.25 | convolution fusion | flops 2818572288 | bytes 17629184 | tf_op jit(solution)/shard_map/dot_general | solution.py:34
  53.0 11.3 %all-gather.8.cloned.1.call-done = bf16[192,4096]{1,0:T(8,128)(2,1)} async-done(((bf16[24,4096]{1,0:T(8,128)(2,1)}), bf16[192,4096]{1,0:T(8,128)(2,1)}) %all-gather.8.cloned.1.call-update) | async-done | bytes 1572880 | tf_op jit(solution)/shard_map/all_gather | solution.py:44
  64.3 12.5 %multiply_convert_fusion = (bf16[192,1792]{1,0:T(8,128)(2,1)}, bf16[192,1792]{1,0:T(8,128)(2,1)}, bf16[192,1792]{1,0:T(8,128)(2,1)}) fusion(f32[192,1792]{1,0:T(8,128)} %fusion.11, f32[192,1792]{1,0:T(8,128)S(1)} %fusion.12, bf16[192,4096]{1,0:T(8,128)(2,1)} %all-gather.8.cloned.1.call-done, bf16[1792,4096]{1,0:T(8,128)(2,1)} %param.10), kind=kOutput, calls=%fused_computation.12 | convolution fusion | flops 2823733248 | bytes 21069824 | tf_op jit(solution)/shard_map/dot_general | solution.py:13
  76.8 0.0 all-gather.14.cloned.1.call-update
  76.8 0.0 all-gather.12.cloned.1.call-start
  76.9 0.5 all-gather.12.cloned.1.call-update
  77.4 0.0 all-gather.10.cloned.1.call-start
  77.5 0.5 all-gather.10.cloned.1.call-update
  78.0 0.0 copy-start.3
  78.0 0.0 reduce-scatter.3.cloned.1.call-start
  78.1 9.9 %convolution_convert_fusion.3 = bf16[192,4096]{1,0:T(8,128)(2,1)} fusion(bf16[192,1792]{1,0:T(8,128)(2,1)} %get-tuple-element.7, bf16[1792,4096]{1,0:T(8,128)(2,1)} %param.10), kind=kOutput, calls=%fused_computation.5 | convolution fusion | flops 2819358720 | bytes 16941056 | tf_op jit(solution)/shard_map/dot_general | solution.py:39
  88.0 0.0 reduce-scatter.3.cloned.1.call-update
  88.0 0.0 copy-done.3
  88.0 1.3 copy.20
  89.3 3.7 %all-to-all-start.1 = ((bf16[192,4,1024]{2,0,1:T(8,128)(2,1)}), bf16[192,4,1024]{2,0,1:T(8,128)(2,1)S(1)}, u32[]{:S(2)}, u32[]{:S(2)}) async-start(bf16[192,4,1024]{2,0,1:T(8,128)(2,1)} %bitcast.35), calls=%async_computation.3 | async-start | bytes 3145728 | tf_op jit(solution)/shard_map/all_to_all | solution.py:60
  93.1 0.0 copy-start.4
  93.1 1.3 copy.21
  94.4 0.0 copy-done.4
  94.4 11.7 %fusion.13 = f32[192,4096]{1,0:T(8,128)} fusion(bf16[192,1792]{1,0:T(8,128)(2,1)S(1)} %copy-done.4, bf16[4096,1792]{1,0:T(8,128)(2,1)} %param.8), kind=kOutput, calls=%fused_computation.27 | convolution fusion | flops 2818572288 | bytes 18513920 | tf_op jit(solution)/shard_map/dot_general | solution.py:13
  106.1 18.2 %all-to-all-done.1 = bf16[192,4,1024]{2,0,1:T(8,128)(2,1)S(1)} async-done(((bf16[192,4,1024]{2,0,1:T(8,128)(2,1)}), bf16[192,4,1024]{2,0,1:T(8,128)(2,1)S(1)}, u32[]{:S(2)}, u32[]{:S(2)}) %all-to-all-start.1) | async-done | bytes 1572896 | tf_op jit(solution)/shard_map/all_to_all | solution.py:60
  124.3 3.6 %all-to-all-start = ((bf16[192,4,1024]{2,0,1:T(8,128)(2,1)}), bf16[192,4,1024]{2,0,1:T(8,128)(2,1)S(1)}, u32[]{:S(2)}, u32[]{:S(2)}) async-start(bf16[192,4,1024]{2,0,1:T(8,128)(2,1)} %bitcast.37), calls=%async_computation.2 | async-start | bytes 3145728 | tf_op jit(solution)/shard_map/all_to_all | solution.py:59
  127.8 0.0 reduce-scatter.5.cloned.1.call-start
  127.9 12.3 %fusion = bf16[192,4096]{1,0:T(8,128)(2,1)} fusion(f32[192,4096]{1,0:T(8,128)} %fusion.13, bf16[192,1792]{1,0:T(8,128)(2,1)} %get-tuple-element.5, bf16[4096,1792]{1,0:T(8,128)(2,1)} %param.9), kind=kOutput, calls=%fused_computation.4 | convolution fusion | flops 2820145152 | bytes 20086784 | tf_op jit(solution)/shard_map/dot_general | solution.py:13
  140.2 0.0 reduce-scatter.5.cloned.1.call-update
  140.2 0.0 all-gather.14.cloned.1.call-done
  140.3 9.5 %convolution_convert_fusion = bf16[4,1792,1024]{2,1,0:T(8,128)(2,1)} fusion(bf16[4,192,1792]{2,1,0:T(8,128)(2,1)} %bitcast.40, bf16[192,4,1024]{2,0,1:T(8,128)(2,1)S(1)} %all-to-all-done.1), kind=kOutput, calls=%fused_computation | convolution fusion | flops 2825912320 | bytes 19005440 | tf_op jit(solution)/shard_map/jrf,jrd->jfd/dot_general | solution.py:19
  149.8 0.0 all-to-all-done
  149.8 24.9 %all-gather.12.cloned.1.call-done = bf16[768,1792]{1,0:T(8,128)(2,1)} async-done(((bf16[192,1792]{1,0:T(8,128)(2,1)}), bf16[768,1792]{1,0:T(8,128)(2,1)}) %all-gather.12.cloned.1.call-update) | async-done | bytes 2752528 | tf_op jit(solution)/shard_map/all_gather | solution.py:65
  174.7 9.2 %convolution_convert_fusion.1 = bf16[4,1024,1792]{2,1,0:T(8,128)(2,1)} fusion(bf16[4,192,1792]{2,1,0:T(8,128)(2,1)} %bitcast.38, bf16[192,4,1024]{2,0,1:T(8,128)(2,1)S(1)} %all-to-all-done), kind=kOutput, calls=%fused_computation.1 | convolution fusion | flops 2825912320 | bytes 19005440 | tf_op jit(solution)/shard_map/jrd,jrf->jdf/dot_general | solution.py:19
  183.9 11.1 %reduce_sum.38 = bf16[1792,1024]{1,0:T(8,128)(2,1)} reduce(bf16[4,1792,1024]{2,1,0:T(8,128)(2,1)} %convolution_convert_fusion, bf16[]{:T(256)} %constant.15.clone.1), dimensions={0}, to_apply=%region_5.6 | reduce | flops 5505024 | bytes 18350082 | tf_op jit(solution)/shard_map/reduce_sum | solution.py:23
  195.1 10.9 %reduce_sum.37 = bf16[1024,1792]{1,0:T(8,128)(2,1)} reduce(bf16[4,1024,1792]{2,1,0:T(8,128)(2,1)} %convolution_convert_fusion.1, bf16[]{:T(256)} %constant.15.clone.1), dimensions={0}, to_apply=%region_4.5 | reduce | flops 5505024 | bytes 18350082 | tf_op jit(solution)/shard_map/reduce_sum | solution.py:23
  206.0 11.0 %all-gather.10.cloned.1.call-done = bf16[768,1792]{1,0:T(8,128)(2,1)} async-done(((bf16[192,1792]{1,0:T(8,128)(2,1)}), bf16[768,1792]{1,0:T(8,128)(2,1)}) %all-gather.10.cloned.1.call-update) | async-done | bytes 2752528 | tf_op jit(solution)/shard_map/all_gather | solution.py:64
  217.0 9.2 %convolution_convert_fusion.2 = bf16[4,1024,1792]{2,1,0:T(8,128)(2,1)} fusion(bf16[4,192,1792]{2,1,0:T(8,128)(2,1)} %bitcast.39, bf16[192,4,1024]{2,0,1:T(8,128)(2,1)S(1)} %all-to-all-done), kind=kOutput, calls=%fused_computation.2 | convolution fusion | flops 2825912320 | bytes 19005440 | tf_op jit(solution)/shard_map/jrd,jrf->jdf/dot_general | solution.py:19
  226.2 0.0 copy-start.1
  226.2 10.7 %reduce_sum.36 = bf16[1024,1792]{1,0:T(8,128)(2,1)} reduce(bf16[4,1024,1792]{2,1,0:T(8,128)(2,1)} %convolution_convert_fusion.2, bf16[]{:T(256)} %constant.15.clone.1), dimensions={0}, to_apply=%region_3.4 | reduce | flops 5505024 | bytes 18350082 | tf_op jit(solution)/shard_map/reduce_sum | solution.py:23
  237.0 16.9 %reduce-scatter.3.cloned.1.call-done = bf16[24,4096]{1,0:T(8,128)(2,1)} async-done(((bf16[192,4096]{1,0:T(8,128)(2,1)}), bf16[24,4096]{1,0:T(8,128)(2,1)}) %reduce-scatter.3.cloned.1.call-update) | async-done | bytes 196624 | tf_op jit(solution)/shard_map/reduce_scatter | solution.py:38
  253.9 35.5 %reduce-scatter.5.cloned.1.call-done = bf16[24,4096]{1,0:T(8,128)(2,1)} async-done(((bf16[192,4096]{1,0:T(8,128)(2,1)}), bf16[24,4096]{1,0:T(8,128)(2,1)}) %reduce-scatter.5.cloned.1.call-update) | async-done | bytes 196624 | tf_op jit(solution)/shard_map/reduce_scatter | solution.py:48
  289.3 0.0 copy-done.1
Async XLA Ops:
  7.2 1.0 copy-start
  7.2 31.0 %all-gather.6.cloned.1.call-start = ((), (), s32[]{:S(2)}) async-start(), calls=%async_computation.4 | async-start | bytes 1769472 | tf_op jit(solution)/shard_map/all_gather | solution.py:33
  9.1 55.2 %all-gather.8.cloned.1.call-start = ((), (), s32[]{:S(2)}) async-start(), calls=%async_computation.6 | async-start | bytes 1769472 | tf_op jit(solution)/shard_map/all_gather | solution.py:44
  9.8 130.4 %all-gather.14.cloned.1.call-start = ((), (), s32[]{:S(2)}) async-start(), calls=%async_computation.10 | async-start | bytes 3440640 | tf_op jit(solution)/shard_map/all_gather | solution.py:63
  38.2 9.3 %copy-start.2 = (bf16[192,4096]{1,0:T(8,128)(2,1)S(1)}, bf16[192,4096]{1,0:T(8,128)(2,1)}, u32[]{:S(2)}) copy-start(bf16[192,4096]{1,0:T(8,128)(2,1)} %all-gather.6.cloned.1.call-done) | copy-start | bytes 4718596
  38.2 10.6 %copy-start.5 = (bf16[4096,1792]{1,0:T(8,128)(2,1)S(1)}, bf16[4096,1792]{1,0:T(8,128)(2,1)}, u32[]{:S(2)}) copy-start(bf16[4096,1792]{1,0:T(8,128)(2,1)} %param.8) | copy-start | bytes 44040196
  76.8 97.8 %all-gather.12.cloned.1.call-start = ((), (), s32[]{:S(2)}) async-start(), calls=%async_computation.9 | async-start | bytes 3440640 | tf_op jit(solution)/shard_map/all_gather | solution.py:65
  77.4 139.6 %all-gather.10.cloned.1.call-start = ((), (), s32[]{:S(2)}) async-start(), calls=%async_computation.8 | async-start | bytes 3440640 | tf_op jit(solution)/shard_map/all_gather | solution.py:64
  78.0 10.0 %copy-start.3 = (bf16[192,4096]{1,0:T(8,128)(2,1)S(1)}, bf16[192,4096]{1,0:T(8,128)(2,1)}, u32[]{:S(2)}) copy-start(bf16[192,4096]{1,0:T(8,128)(2,1)} %all-gather.8.cloned.1.call-done) | copy-start | bytes 4718596
  78.0 175.8 %reduce-scatter.3.cloned.1.call-start = ((), (), s32[]{:S(2)}) async-start(), calls=%async_computation.5 | async-start | bytes 1769472 | tf_op jit(solution)/shard_map/reduce_scatter | solution.py:38
  89.3 34.9 %all-to-all-start.1 = ((bf16[192,4,1024]{2,0,1:T(8,128)(2,1)}), bf16[192,4,1024]{2,0,1:T(8,128)(2,1)S(1)}, u32[]{:S(2)}, u32[]{:S(2)}) async-start(bf16[192,4,1024]{2,0,1:T(8,128)(2,1)} %bitcast.35), calls=%async_computation.3 | async-start | bytes 3145728 | tf_op jit(solution)/shard_map/all_to_all | solution.py:60
  93.1 1.3 copy-start.4
  124.3 25.5 %all-to-all-start = ((bf16[192,4,1024]{2,0,1:T(8,128)(2,1)}), bf16[192,4,1024]{2,0,1:T(8,128)(2,1)S(1)}, u32[]{:S(2)}, u32[]{:S(2)}) async-start(bf16[192,4,1024]{2,0,1:T(8,128)(2,1)} %bitcast.37), calls=%async_computation.2 | async-start | bytes 3145728 | tf_op jit(solution)/shard_map/all_to_all | solution.py:59
  127.8 161.5 %reduce-scatter.5.cloned.1.call-start = ((), (), s32[]{:S(2)}) async-start(), calls=%async_computation.7 | async-start | bytes 1769472 | tf_op jit(solution)/shard_map/reduce_scatter | solution.py:48
  226.2 63.1 %copy-start.1 = (bf16[32,4096]{1,0:T(8,128)(2,1)S(1)}, bf16[32,4096]{1,0:T(8,128)(2,1)}, u32[]{:S(2)}) copy-start(bf16[32,4096]{1,0:T(8,128)(2,1)} %param.6) | copy-start | bytes 786436
Sparse Core Ops, SparseCore 0:
  10.2 27.9 all-gather.5
  39.9 24.3 all-gather.7
  77.0 50.7 all-gather.13
  129.4 45.1 all-gather.11
  176.4 40.5 all-gather.9
  219.7 34.0 reduce-scatter.2
  256.7 32.5 reduce-scatter.4
where the time goes:
time: 297 us; the launch traced here: 296 us
  waiting for transfers between devices  148 us (50%)
  matrix products  88.8 us (30%)
  other arithmetic  33.7 us (11%)
  between operations  14.2 us (5%)
  starting transfers between devices  7.58 us (3%)
  local copies, waits for them, and re-layouts  3.98 us (1%)
    dot_general x3, matrix products, contract_cols(): lax.dot_general(left_matrix, right_matrix, (((1,), (1,)), ((), ())), pref...  36.6 us
    reduce_scatter x1, waiting for transfers between devices, on_device(): lax.psum_scatter((contract_cols(gate_back, gate_weight) + contract_cols(u...  35.5 us
    reduce_sum x3, other arithmetic, group_sum(): return jnp.sum(partials.astype(jnp.float32), axis=0)  32.8 us
    all_gather x1, waiting for transfers between devices, on_device(): token_rows = lax.all_gather(picked, 'dp', axis=0, tiled=True)  28.3 us
    dot_general x3, matrix products, group_sum(): jnp.einsum(form, left_blocks, right_blocks, preferred_element_type=jnp.fl...  28 us
    all_gather x1, waiting for transfers between devices, on_device(): lax.all_gather(up_back, 'seq', axis=0, tiled=True)  24.9 us
    all_to_all x1, waiting for transfers between devices, on_device(): lax.all_to_all(cotangent_rows, 'seq', split_axis=1, concat_axis=0, tiled=...  18.2 us
    reduce_scatter x1, waiting for transfers between devices, on_device(): lax.psum_scatter(jnp.dot(hidden, down_weight, preferred_element_type=jnp....  16.9 us
  transfers between devices with their start and end apart: 9, of which 7 were waited for; matrix products, arithmetic and copies ran while one was open for 37% of the time, Pallas kernels for 0%

commit v1 on v0

v1 whole, which is shorter than its diff:
```python
import jax
import jax.numpy as jnp
from jax import lax
from jax.experimental import pallas as pl
from jax.experimental.pallas import tpu as pltpu
from jax.sharding import PartitionSpec as P


BF = jnp.bfloat16
F32 = jnp.float32
CORES = 2
MIB = 1 << 20


ANY = pl.BlockSpec(memory_space=pl.ANY)
VMEM = pl.BlockSpec(memory_space=pltpu.VMEM)


def tile_of(extent, options):
    for option in options:
        if extent % option == 0:
            return option
    return extent


def cost(flops, nbytes):
    return pl.CostEstimate(flops=flops, bytes_accessed=nbytes, transcendentals=0)


def shape(dims, dtype=BF):
    return jax.ShapeDtypeStruct(dims, dtype)


def grant(*arrays):
    total = sum(2 * r * c if d == BF else 4 * r * c for r, c, d in arrays)
    return pltpu.CompilerParams(vmem_limit_bytes=min(total + 6 * MIB, 60 * MIB))


def nt_dot(left, right):
    return lax.dot_general(left, right, (((1,), (1,)), ((), ())), preferred_element_type=F32)


def nn_dot(left, right):
    return jnp.dot(left, right, preferred_element_type=F32)


def pick_kernel(flag_ref, tokens_ref, out_ref):
    rows = out_ref.shape[0]
    count = tokens_ref.shape[0]
    flags = (flag_ref[...] == 1).astype(F32)
    before = lax.broadcasted_iota(jnp.int32, (count, count), 0)
    after = lax.broadcasted_iota(jnp.int32, (count, count), 1)
    ranks = nn_dot(flags, (before <= after).astype(F32))
    slots = lax.broadcasted_iota(jnp.int32, (rows, count), 0).astype(F32) + 1.0
    chosen = (jnp.broadcast_to(ranks, (rows, count)) == slots) & (
        jnp.broadcast_to(flags, (rows, count)) == 1.0
    )
    out_ref[...] = nn_dot(chosen.astype(BF), tokens_ref[...]).astype(BF)


def pick(modality, tokens, rows):
    return pl.pallas_call(
        pick_kernel,
        out_shape=shape((rows, tokens.shape[1])),
        name="pick",
    )(modality.reshape(1, -1), tokens)


def enter_kernel(tile, xa_ref, xb_ref, gate_hbm, up_hbm, hid_ref, active_ref, turn_ref,
                 x_ref, gate_ref, up_ref, sems):
    half = xa_ref.shape[0]
    tiles = gate_ref.shape[0]

    def copies(j):
        column = pl.ds(pl.multiple_of(j * tile, tile), tile)
        return (
            pltpu.make_async_copy(gate_hbm.at[:, column], gate_ref.at[j], sems.at[0, j]),
            pltpu.make_async_copy(up_hbm.at[:, column], up_ref.at[j], sems.at[1, j]),
        )

    for j in range(tiles):
        for copy in copies(j):
            copy.start()
    x_ref[:half] = xa_ref[...]
    x_ref[half:] = xb_ref[...]

    @pl.loop(0, tiles)
    def _(j):
        column = pl.ds(pl.multiple_of(j * tile, tile), tile)
        for copy in copies(j):
            copy.wait()
        gate_proj = nn_dot(x_ref[...], gate_ref[j])
        up_proj = nn_dot(x_ref[...], up_ref[j])
        sig = jax.nn.sigmoid(gate_proj)
        active = gate_proj * sig
        hid_ref[:, column] = (active * up_proj).astype(BF)
        active_ref[:, column] = active
        turn_ref[:, column] = up_proj * (sig * (1.0 + gate_proj * (1.0 - sig)))


def enter(own, other, gate, up):
    half, width = own.shape
    units = gate.shape[1]
    rows = 2 * half
    tile = tile_of(units, (256, 128))
    tiles = units // tile
    return pl.pallas_call(
        lambda *refs: enter_kernel(tile, *refs),
        in_specs=[VMEM, VMEM, ANY, ANY],
        out_specs=[VMEM] * 3,
        out_shape=[shape((rows, units)), shape((rows, units), F32), shape((rows, units), F32)],
        scratch_shapes=[
            pltpu.VMEM((rows, width), BF),
            pltpu.VMEM((tiles, width, tile), BF),
            pltpu.VMEM((tiles, width, tile), BF),
            pltpu.SemaphoreType.DMA((2, tiles)),
        ],
        compiler_params=grant((2 * width, units, BF), (2 * rows, width, BF),
                              (rows, units, BF), (2 * rows, units, F32)),
        cost_estimate=cost(4 * rows * width * units, 4 * width * units),
        name="enter",
    )(own, other, gate, up)


def turn_kernel(tile, step, ca_ref, cb_ref, down_hbm, hid_ref, active_ref, factor_ref,
                gb_ref, ub_ref, own_ref, other_ref, c_ref, down_ref, sems):
    half = ca_ref.shape[0]
    units, width = down_ref.shape
    tiles = units // tile

    def copy(j):
        row = pl.ds(pl.multiple_of(j * tile, tile), tile)
        return pltpu.make_async_copy(down_hbm.at[row, :], down_ref.at[row, :], sems.at[j])

    for j in range(tiles):
        copy(j).start()
    c_ref[:half] = ca_ref[...]
    c_ref[half:] = cb_ref[...]

    @pl.loop(0, tiles)
    def _(j):
        span = pl.ds(pl.multiple_of(j * tile, tile), tile)
        copy(j).wait()
        back = nt_dot(c_ref[...], down_ref[span, :])
        gb_ref[:, span] = (back * factor_ref[:, span]).astype(BF)
        ub_ref[:, span] = (back * active_ref[:, span]).astype(BF)

    @pl.loop(0, width // step)
    def _(j):
        span = pl.ds(pl.multiple_of(j * step, step), step)
        result = nn_dot(hid_ref[...], down_ref[:, span]).astype(BF)
        own_ref[0, :, span] = result[:half]
        other_ref[0, :, span] = result[half:]


def turn(own, other, down, hid, active, factor):
    half, width = own.shape
    units = down.shape[0]
    rows = 2 * half
    tile = tile_of(units, (256, 128))
    step = tile_of(width, (512, 256, 128))
    return pl.pallas_call(
        lambda *refs: turn_kernel(tile, step, *refs),
        grid=(1,),
        in_specs=[VMEM, VMEM, ANY, VMEM, VMEM, VMEM],
        out_specs=[VMEM, VMEM] + [pl.BlockSpec((1, half, width), lambda i: (0, 0, 0))] * 2,
        out_shape=[shape((rows, units))] * 2 + [shape((2, half, width))] * 2,
        scratch_shapes=[
            pltpu.VMEM((rows, width), BF),
            pltpu.VMEM((units, width), BF),
            pltpu.SemaphoreType.DMA((units // tile,)),
        ],
        compiler_params=grant((width, units, BF), (4 * rows, width, BF),
                              (4 * rows, units, BF), (2 * rows, units, F32)),
        cost_estimate=cost(4 * rows * width * units, 2 * width * units),
        name="turn",
    )(own, other, down, hid, active, factor)


def leave_kernel(step, gb_ref, ub_ref, gate_hbm, up_hbm, own_in, other_in, own_ref, other_ref,
                 gate_ref, up_ref, sems):
    half = own_ref.shape[1]
    steps = gate_ref.shape[0] // step

    def copies(j):
        row = pl.ds(pl.multiple_of(j * step, step), step)
        return (
            pltpu.make_async_copy(gate_hbm.at[row, :], gate_ref.at[row, :], sems.at[0, j]),
            pltpu.make_async_copy(up_hbm.at[row, :], up_ref.at[row, :], sems.at[1, j]),
        )

    for j in range(steps):
        for copy in copies(j):
            copy.start()

    @pl.loop(0, steps)
    def _(j):
        span = pl.ds(pl.multiple_of(j * step, step), step)
        for copy in copies(j):
            copy.wait()
        result = nt_dot(gb_ref[...], gate_ref[span, :]) + nt_dot(ub_ref[...], up_ref[span, :])
        result = result.astype(BF)
        own_ref[0, :, span] = result[:half]
        other_ref[0, :, span] = result[half:]


def leave(gb, ub, gate, up, own, other):
    rows, units = gb.shape
    half, width = own.shape[1:]
    step = tile_of(width, (512, 256, 128))
    return pl.pallas_call(
        lambda *refs: leave_kernel(step, *refs),
        grid=(1,),
        in_specs=[VMEM, VMEM, ANY, ANY, ANY, ANY],
        out_specs=[pl.BlockSpec((1, half, width), lambda i: (1, 0, 0))] * 2,
        out_shape=[shape((2, half, width))] * 2,
        scratch_shapes=[
            pltpu.VMEM((width, units), BF),
            pltpu.VMEM((width, units), BF),
            pltpu.SemaphoreType.DMA((2, width // step)),
        ],
        input_output_aliases={4: 0, 5: 1},
        compiler_params=grant((2 * width, units, BF), (2 * rows, width, BF), (2 * rows, units, BF)),
        cost_estimate=cost(4 * rows * width * units, 4 * width * units),
        name="leave",
    )(gb, ub, gate, up, own, other)


def rows_dot(left, right):
    left, right = jnp.concatenate(left, axis=0), jnp.concatenate(right, axis=0)
    return lax.dot_general(
        left, right, (((0,), (0,)), ((), ())), preferred_element_type=F32
    ).astype(BF)


def on_device(tokens, modality, gate, up, down, out_grad):
    count, width = out_grad.shape
    groups = lax.axis_size("seq")
    ring = lax.axis_size("dp") // CORES
    me = lax.axis_index("seq")
    part = width // groups

    def shift(value, k):
        return lax.ppermute(value, "dp", [
            (z * CORES + c, (z + k) % ring * CORES + c) for z in range(ring) for c in range(CORES)])

    def swap(value):
        return lax.ppermute(value, "dp", [
            (z * CORES + c, z * CORES + 1 - c) for z in range(ring) for c in range(CORES)])

    def across(value, mask):
        return lax.ppermute(value, "seq", [(g, g ^ mask) for g in range(groups)])

    def gathered(block):
        return jnp.concatenate([block] + [shift(block, k) for k in range(1, ring)], axis=0)

    def cut(matrix, group):
        return lax.dynamic_slice_in_dim(matrix, group * part, part, axis=1)

    def slices_of(own):
        half = own.shape[0]
        far = [across(cut(own, me ^ m), m) for m in range(1, groups)]
        got = jnp.concatenate(far, axis=0)
        mate = swap(got)
        pairs = []
        for m in range(1, groups):
            pairs += [got[(m - 1) * half:m * half], mate[(m - 1) * half:m * half]]
        return pairs

    def spread(value, low):
        held = [value]
        for m in range(1, groups):
            bit = m & -m if low else 1 << (m.bit_length() - 1)
            held.append(across(held[m ^ bit], bit))
        return held

    block = pick(modality, tokens, count)
    tok = gathered(block)
    tok_mate = swap(tok)
    cot = gathered(out_grad)
    cot_mate = swap(cot)
    tok_far = slices_of(tok)
    hid, active, factor = enter(tok, tok_mate, gate, up)
    all_hid = spread(hid, True)
    cot_far = slices_of(cot)
    gb, ub, own, other = turn(cot, cot_mate, down, hid, active, factor)
    all_gb = spread(gb, True)
    all_ub = spread(ub, False)
    own, other = leave(gb, ub, gate, up, own, other)

    mate = swap(other)
    pieces = (own.astype(F32) + mate.astype(F32)).astype(BF).reshape(2, ring, count, width)
    total = pieces[:, 0].astype(F32)
    for k in range(1, ring):
        total = total + shift(pieces[:, k], -k).astype(F32)
    total = total.astype(BF)

    tok_all = [cut(tok, me), cut(tok_mate, me)] + tok_far
    cot_all = [cut(cot, me), cut(cot_mate, me)] + cot_far
    down_grad = rows_dot(all_hid, cot_all)
    gate_grad = rows_dot(tok_all, all_gb)
    up_grad = rows_dot(tok_all, all_ub)
    return total[0], total[1], gate_grad, up_grad, down_grad


def solution(mesh):
    rows = P(("dp", "seq"), None)
    return jax.shard_map(
        on_device,
        mesh=mesh,
        in_specs=(rows, P(("dp", "seq")), P(None, "dp"), P(None, "dp"), P("dp", None), rows),
        out_specs=(rows, rows, P("seq", "dp"), P("seq", "dp"), P("dp", "seq")),
        check_vma=False,
    )
```

time: 297 us -> 203 us (0.68)
  the two profiles are of different devices: /device:TPU:0 before, /device:TPU:26 now
where the time goes in v1:
time: 203 us
  waiting for transfers between devices  108 us (53%)
  starting transfers between devices  38 us (19%)
  Pallas kernels  37.7 us (19%)
  matrix products  14.4 us (7%)
  local copies, waits for them, and re-layouts  2.19 us (1%)
    ppermute x15, waiting for transfers between devices, across(): return lax.ppermute(value, 'seq', [(g, g ^ mask) for g in range(groups)])  66.4 us
    ppermute x9, waiting for transfers between devices, shift(): lax.ppermute(value, 'dp', [(z * CORES + c, (z + k) % ring * CORES + c) fo...  41.8 us
    ppermute x9, starting transfers between devices, shift(): lax.ppermute(value, 'dp', [(z * CORES + c, (z + k) % ring * CORES + c) fo...  22.4 us
    ppermute x15, starting transfers between devices, across(): return lax.ppermute(value, 'seq', [(g, g ^ mask) for g in range(groups)])  15.4 us
    dot_general x3, matrix products, rows_dot(): lax.dot_general(left, right, (((0,), (0,)), ((), ())), preferred_element_...  14.4 us
    pallas_call x1, Pallas kernels, leave(): pl.pallas_call(lambda *refs: leave_kernel(step, *refs), grid=(1,), in_spe...  12.9 us
    pallas_call x1, Pallas kernels, turn(): pl.pallas_call(lambda *refs: turn_kernel(tile, step, *refs), grid=(1,), i...  12 us
    pallas_call x1, Pallas kernels, enter(): pl.pallas_call(lambda *refs: enter_kernel(tile, *refs), in_specs=[VMEM, V...  10.8 us
  transfers between devices with their start and end apart: 29, of which 15 were waited for; matrix products, arithmetic and copies ran while one was open for 9% of the time, Pallas kernels for 19%

profile of v1, /device:TPU:26, one launch (start us, length us, event | category | flops | bytes accessed | tf_op | source)
XLA Modules:
  0.0 203.2 jit_solution(14438011666916240633)
XLA Ops:
  0.6 0.3 collective-permute-start
  0.9 1.7 collective-permute-start.1
  2.6 2.0 pick.1
  4.6 0.4 collective-permute-start.6
  5.0 2.6 %collective-permute-start.5 = (bf16[24,4096]{1,0:T(8,128)(2,1)}, bf16[24,4096]{1,0:T(8,128)(2,1)S(1)}, u32[]{:S(2)}, u32[]{:S(2)}) collective-permute-start(bf16[24,4096]{1,0:T(8,128)(2,1)} %pick.1), channel_id=1, source_target_pairs={{0,16},{4,20},{8,24},{12,28},{16,0},{20,4},{24,8},{28,12},{1,17},{... | collective-permute-start | bytes 589832 | tf_op jit(solution)/shard_map/ppermute | solution.py:244
  7.6 1.1 collective-permute-start.4
  8.7 0.9 constant_dynamic-update-slice_fusion.3
  9.7 7.3 %collective-permute-done.6 = bf16[24,4096]{1,0:T(8,128)(2,1)S(1)} collective-permute-done((bf16[24,4096]{1,0:T(8,128)(2,1)}, bf16[24,4096]{1,0:T(8,128)(2,1)S(1)}, u32[]{:S(2)}, u32[]{:S(2)}) %collective-permute-start.6) | collective-permute-done | bytes 196640 | tf_op jit(solution)/shard_map/ppermute | solution.py:244
  17.0 11.1 %collective-permute-start.2 = (bf16[24,4096]{1,0:T(8,128)(2,1)}, bf16[24,4096]{1,0:T(8,128)(2,1)S(1)}, u32[]{:S(2)}, u32[]{:S(2)}) collective-permute-start(bf16[24,4096]{1,0:T(8,128)(2,1)} %param.11), channel_id=1, source_target_pairs={{0,24},{4,28},{8,0},{12,4},{16,8},{20,12},{24,16},{28,20},{1,25},{... | collective-permute-start | bytes 589832 | tf_op jit(solution)/shard_map/ppermute | solution.py:244
  28.1 5.8 %collective-permute-done.5 = bf16[24,4096]{1,0:T(8,128)(2,1)S(1)} collective-permute-done((bf16[24,4096]{1,0:T(8,128)(2,1)}, bf16[24,4096]{1,0:T(8,128)(2,1)S(1)}, u32[]{:S(2)}, u32[]{:S(2)}) %collective-permute-start.5) | collective-permute-done | bytes 196640 | tf_op jit(solution)/shard_map/ppermute | solution.py:244
  33.9 0.0 collective-permute-done.4
  33.9 1.0 pad_maximum_fusion.refs_0_
  34.9 0.1 collective-permute-start.7
  34.9 0.1 constant_dynamic-slice_fusion.4
  35.0 0.6 collective-permute-start.12
  35.6 2.4 %collective-permute-start.14 = (bf16[96,1024]{1,0:T(8,128)(2,1)S(1)}, bf16[96,1024]{1,0:T(8,128)(2,1)S(1)}, u32[]{:S(2)}, u32[]{:S(2)}) collective-permute-start(bf16[96,1024]{1,0:T(8,128)(2,1)S(1)} %get-tuple-element.31), channel_id=1, source_target_pairs={{0,3},{1,2},{2,1},{3,0},{4,7},{5,6},{6,5},{7,4},{8,11},{9,10},{10,... | collective-permute-start | bytes 589832 | tf_op jit(solution)/shard_map/ppermute | solution.py:252
  38.1 0.6 collective-permute-start.13
  38.7 0.0 collective-permute-done.2
  38.7 0.1 constant_dynamic-slice_fusion.1
  38.8 0.6 collective-permute-start.25
  39.4 3.5 %collective-permute-done.12 = bf16[96,1024]{1,0:T(8,128)(2,1)S(1)} collective-permute-done((bf16[96,1024]{1,0:T(8,128)(2,1)S(1)}, bf16[96,1024]{1,0:T(8,128)(2,1)S(1)}, u32[]{:S(2)}, u32[]{:S(2)}) %collective-permute-start.12) | collective-permute-done | bytes 196640 | tf_op jit(solution)/shard_map/ppermute | solution.py:252
  42.9 1.5 collective-permute-start.27
  44.4 3.7 %collective-permute-done.14 = bf16[96,1024]{1,0:T(8,128)(2,1)S(1)} collective-permute-done((bf16[96,1024]{1,0:T(8,128)(2,1)S(1)}, bf16[96,1024]{1,0:T(8,128)(2,1)S(1)}, u32[]{:S(2)}, u32[]{:S(2)}) %collective-permute-start.14) | collective-permute-done | bytes 196640 | tf_op jit(solution)/shard_map/ppermute | solution.py:252
  48.1 0.5 collective-permute-start.26
  48.6 0.5 collective-permute-done.13
  49.2 2.2 %collective-permute-done.25 = bf16[96,1024]{1,0:T(8,128)(2,1)S(1)} collective-permute-done((bf16[96,1024]{1,0:T(8,128)(2,1)S(1)}, bf16[96,1024]{1,0:T(8,128)(2,1)S(1)}, u32[]{:S(2)}, u32[]{:S(2)}) %collective-permute-start.25) | collective-permute-done | bytes 196640 | tf_op jit(solution)/shard_map/ppermute | solution.py:252
  51.3 0.0 collective-permute-start.15
  51.3 4.8 %collective-permute-done.27 = bf16[96,1024]{1,0:T(8,128)(2,1)S(1)} collective-permute-done((bf16[96,1024]{1,0:T(8,128)(2,1)S(1)}, bf16[96,1024]{1,0:T(8,128)(2,1)S(1)}, u32[]{:S(2)}, u32[]{:S(2)}) %collective-permute-start.27) | collective-permute-done | bytes 196640 | tf_op jit(solution)/shard_map/ppermute | solution.py:252
  56.1 2.1 %collective-permute-done.26 = bf16[96,1024]{1,0:T(8,128)(2,1)S(1)} collective-permute-done((bf16[96,1024]{1,0:T(8,128)(2,1)S(1)}, bf16[96,1024]{1,0:T(8,128)(2,1)S(1)}, u32[]{:S(2)}, u32[]{:S(2)}) %collective-permute-start.26) | collective-permute-done | bytes 196640 | tf_op jit(solution)/shard_map/ppermute | solution.py:252
  58.3 0.1 collective-permute-start.28
  58.4 0.0 collective-permute-done.7.refs_1_
  58.4 10.8 %enter.1 = (bf16[192,1792]{1,0:T(8,128)(2,1)S(1)}, f32[192,1792]{1,0:T(8,128)S(1)}, f32[192,1792]{1,0:T(8,128)S(1)}) custom-call(bf16[96,4096]{1,0:T(8,128)(2,1)S(1)} %pad_maximum_fusion.refs_0_, bf16[96,4096]{1,0:T(8,128)(2,1)S(1)} %collective-permute-done.7.refs_1_, bf16[4096,1792]{1,0:T(8,128)(2,1)} %refs_2_.5, bf16[4096,1792]{1,0:T(8,128)(2,1)} %refs_3_.3), custom_call_target="tpu_custom_call" | custom-call | flops 5637144576 | bytes 29360128 | tf_op jit(solution)/shard_map/enter/pallas_call | solution.py:107
  69.2 0.0 collective-permute-done.3.refs_1_
  69.2 12.0 %turn.1 = (bf16[192,1792]{1,0:T(8,128)(2,1)S(1)}, bf16[192,1792]{1,0:T(8,128)(2,1)S(1)}, bf16[2,96,4096]{2,1,0:T(8,128)(2,1)S(1)}, bf16[2,96,4096]{2,1,0:T(8,128)(2,1)S(1)}) custom-call(bf16[96,4096]{1,0:T(8,128)(2,1)S(1)} %constant_dynamic-update-slice_fusion.refs_0_, bf16[96,4096]{1,0:T(8,128)(2,1)S(1)} %collective-permute-done.3.refs_1_, ...), custom_call_target="tpu_custom_call" | custom-call | flops 5637144576 | bytes 14680064 | tf_op jit(solution)/shard_map/turn/pallas_call | solution.py:162
  81.2 0.6 collective-permute-start.17
  81.8 0.5 collective-permute-start.16
  82.3 1.5 collective-permute-start.23
  83.9 0.0 collective-permute-done.15
  83.9 1.5 collective-permute-start.22
  85.6 0.6 collective-permute-start.19
  86.3 13.3 %collective-permute-done.17 = bf16[192,1792]{1,0:T(8,128)(2,1)S(1)} collective-permute-done((bf16[192,1792]{1,0:T(8,128)(2,1)S(1)}, bf16[192,1792]{1,0:T(8,128)(2,1)S(1)}, u32[]{:S(2)}, u32[]{:S(2)}) %collective-permute-start.17) | collective-permute-done | bytes 688160 | tf_op jit(solution)/shard_map/ppermute | solution.py:252
  99.6 0.5 collective-permute-start.18
  100.1 12.9 %leave.1 = (bf16[2,96,4096]{2,1,0:T(8,128)(2,1)S(1)}, bf16[2,96,4096]{2,1,0:T(8,128)(2,1)S(1)}) custom-call(bf16[192,1792]{1,0:T(8,128)(2,1)S(1)} %get-tuple-element.17.refs_0_, bf16[192,1792]{1,0:T(8,128)(2,1)S(1)} %get-tuple-element.18.refs_1_, bf16[4096,1792]{1,0:T(8,128)(2,1)} %refs_2_.5, ...), custom_call_target="tpu_custom_call", output_to_operand_aliasing={{0}: (4, {}), {1}: (5, {})} | custom-call | flops 5637144576 | bytes 29360128 | tf_op jit(solution)/shard_map/leave/pallas_call | solution.py:211
  113.1 0.1 collective-permute-start.8
  113.1 0.7 collective-permute-done.23
  113.9 0.8 collective-permute-start.24
  114.7 14.9 %collective-permute-done.19 = bf16[192,1792]{1,0:T(8,128)(2,1)S(1)} collective-permute-done((bf16[192,1792]{1,0:T(8,128)(2,1)S(1)}, bf16[192,1792]{1,0:T(8,128)(2,1)S(1)}, u32[]{:S(2)}, u32[]{:S(2)}) %collective-permute-start.19) | collective-permute-done | bytes 688160 | tf_op jit(solution)/shard_map/ppermute | solution.py:252
  129.6 1.5 collective-permute-start.20
  131.1 13.2 %collective-permute-done.18 = bf16[192,1792]{1,0:T(8,128)(2,1)S(1)} collective-permute-done((bf16[192,1792]{1,0:T(8,128)(2,1)S(1)}, bf16[192,1792]{1,0:T(8,128)(2,1)S(1)}, u32[]{:S(2)}, u32[]{:S(2)}) %collective-permute-start.18) | collective-permute-done | bytes 688160 | tf_op jit(solution)/shard_map/ppermute | solution.py:252
  144.3 1.5 collective-permute-start.21
  145.9 4.9 %convolution_convert_fusion.2 = bf16[1024,1792]{1,0:T(8,128)(2,1)} fusion(bf16[768,1024]{1,0:T(8,128)(2,1)S(1)} %slice_dynamic-update-slice_fusion.3, bf16[192,1792]{1,0:T(8,128)(2,1)S(1)} %collective-permute-done.18, bf16[192,1792]{1,0:T(8,128)(2,1)S(1)} %collective-permute-done.17, bf16[192,1792]{1,0:T(8,128)(2,1)S(1)} %collective-permute-done.16, ...), kind=kOutput, calls=%fused_computation.2 | convolution fusion | flops 2831417344 | bytes 7995392 | tf_op jit(solution)/shard_map/dot_general | solution.py:231
  150.8 0.0 collective-permute-done.22
  150.8 7.6 %collective-permute-done.24 = bf16[192,1792]{1,0:T(8,128)(2,1)S(1)} collective-permute-done((bf16[192,1792]{1,0:T(8,128)(2,1)S(1)}, bf16[192,1792]{1,0:T(8,128)(2,1)S(1)}, u32[]{:S(2)}, u32[]{:S(2)}) %collective-permute-start.24) | collective-permute-done | bytes 688160 | tf_op jit(solution)/shard_map/ppermute | solution.py:252
  158.3 4.5 %convolution_convert_fusion = bf16[1792,1024]{1,0:T(8,128)(2,1)} fusion(bf16[768,1024]{1,0:T(8,128)(2,1)S(1)} %slice_dynamic-update-slice_fusion, bf16[192,1792]{1,0:T(8,128)(2,1)S(1)} %collective-permute-done.24, bf16[192,1792]{1,0:T(8,128)(2,1)S(1)} %collective-permute-done.23, bf16[192,1792]{1,0:T(8,128)(2,1)S(1)} %collective-permute-done.22, ...), kind=kOutput, calls=%fused_computation | convolution fusion | flops 2831417344 | bytes 7995392 | tf_op jit(solution)/shard_map/dot_general | solution.py:231
  162.8 0.0 collective-permute-done.8
  162.8 0.5 add_convert_fusion
  163.4 0.1 slice_bitcast_fusion.2
  163.5 1.2 collective-permute-start.11
  164.7 3.9 %collective-permute-start.10 = (bf16[2,24,4096]{2,1,0:T(8,128)(2,1)S(1)}, bf16[2,24,4096]{2,1,0:T(8,128)(2,1)S(1)}, u32[]{:S(2)}, u32[]{:S(2)}) collective-permute-start(bf16[2,24,4096]{2,1,0:T(8,128)(2,1)S(1)} %get-tuple-element.24), channel_id=1, source_target_pairs={{0,16},{4,20},{8,24},{12,28},{16,0},{20,4},{24,8},{28,12},{1,17},{... | collective-permute-start | bytes 1179656 | tf_op jit(solution)/shard_map/ppermute | solution.py:244
  168.6 4.9 %convolution_convert_fusion.1 = bf16[1024,1792]{1,0:T(8,128)(2,1)} fusion(bf16[768,1024]{1,0:T(8,128)(2,1)S(1)} %slice_dynamic-update-slice_fusion.3, bf16[192,1792]{1,0:T(8,128)(2,1)S(1)} %collective-permute-done.21, bf16[192,1792]{1,0:T(8,128)(2,1)S(1)} %collective-permute-done.20, bf16[192,1792]{1,0:T(8,128)(2,1)S(1)} %collective-permute-done.19, ...), kind=kOutput, calls=%fused_computation.1 | convolution fusion | flops 2831417344 | bytes 7995392 | tf_op jit(solution)/shard_map/dot_general | solution.py:231
  173.6 2.2 %collective-permute-done.11 = bf16[2,24,4096]{2,1,0:T(8,128)(2,1)S(1)} collective-permute-done((bf16[2,24,4096]{2,1,0:T(8,128)(2,1)S(1)}, bf16[2,24,4096]{2,1,0:T(8,128)(2,1)S(1)}, u32[]{:S(2)}, u32[]{:S(2)}) %collective-permute-start.11) | collective-permute-done | bytes 393248 | tf_op jit(solution)/shard_map/ppermute | solution.py:244
  175.8 26.5 %collective-permute-done.10 = bf16[2,24,4096]{2,1,0:T(8,128)(2,1)S(1)} collective-permute-done((bf16[2,24,4096]{2,1,0:T(8,128)(2,1)S(1)}, bf16[2,24,4096]{2,1,0:T(8,128)(2,1)S(1)}, u32[]{:S(2)}, u32[]{:S(2)}) %collective-permute-start.10) | collective-permute-done | bytes 393248 | tf_op jit(solution)/shard_map/ppermute | solution.py:244
  202.3 0.2 fusion.23
  202.5 0.8 slice_bitcast_fusion.4
  (28 shorter events, 0.4 us)
Async XLA Ops:
  0.6 35.0 %collective-permute-start = (bf16[24,4096]{1,0:T(8,128)(2,1)}, bf16[24,4096]{1,0:T(8,128)(2,1)S(1)}, u32[]{:S(2)}, u32[]{:S(2)}) collective-permute-start(bf16[24,4096]{1,0:T(8,128)(2,1)} %param.11), channel_id=1, source_target_pairs={{0,8},{4,12},{8,16},{12,20},{16,24},{20,28},{24,0},{28,4},{1,9},{5... | collective-permute-start | bytes 589832 | tf_op jit(solution)/shard_map/ppermute | solution.py:244
  0.9 37.2 %collective-permute-start.1 = (bf16[24,4096]{1,0:T(8,128)(2,1)}, bf16[24,4096]{1,0:T(8,128)(2,1)S(1)}, u32[]{:S(2)}, u32[]{:S(2)}) collective-permute-start(bf16[24,4096]{1,0:T(8,128)(2,1)} %param.11), channel_id=1, source_target_pairs={{0,16},{4,20},{8,24},{12,28},{16,0},{20,4},{24,8},{28,12},{1,17},{... | collective-permute-start | bytes 589832 | tf_op jit(solution)/shard_map/ppermute | solution.py:244
  4.6 12.5 %collective-permute-start.6 = (bf16[24,4096]{1,0:T(8,128)(2,1)}, bf16[24,4096]{1,0:T(8,128)(2,1)S(1)}, u32[]{:S(2)}, u32[]{:S(2)}) collective-permute-start(bf16[24,4096]{1,0:T(8,128)(2,1)} %pick.1), channel_id=1, source_target_pairs={{0,24},{4,28},{8,0},{12,4},{16,8},{20,12},{24,16},{28,20},{1,25},{... | collective-permute-start | bytes 589832 | tf_op jit(solution)/shard_map/ppermute | solution.py:244
  5.0 28.9 %collective-permute-start.5 = (bf16[24,4096]{1,0:T(8,128)(2,1)}, bf16[24,4096]{1,0:T(8,128)(2,1)S(1)}, u32[]{:S(2)}, u32[]{:S(2)}) collective-permute-start(bf16[24,4096]{1,0:T(8,128)(2,1)} %pick.1), channel_id=1, source_target_pairs={{0,16},{4,20},{8,24},{12,28},{16,0},{20,4},{24,8},{28,12},{1,17},{... | collective-permute-start | bytes 589832 | tf_op jit(solution)/shard_map/ppermute | solution.py:244
  7.6 26.3 %collective-permute-start.4 = (bf16[24,4096]{1,0:T(8,128)(2,1)}, bf16[24,4096]{1,0:T(8,128)(2,1)S(1)}, u32[]{:S(2)}, u32[]{:S(2)}) collective-permute-start(bf16[24,4096]{1,0:T(8,128)(2,1)} %pick.1), channel_id=1, source_target_pairs={{0,8},{4,12},{8,16},{12,20},{16,24},{20,28},{24,0},{28,4},{1,9},{5... | collective-permute-start | bytes 589832 | tf_op jit(solution)/shard_map/ppermute | solution.py:244
  17.0 21.7 %collective-permute-start.2 = (bf16[24,4096]{1,0:T(8,128)(2,1)}, bf16[24,4096]{1,0:T(8,128)(2,1)S(1)}, u32[]{:S(2)}, u32[]{:S(2)}) collective-permute-start(bf16[24,4096]{1,0:T(8,128)(2,1)} %param.11), channel_id=1, source_target_pairs={{0,24},{4,28},{8,0},{12,4},{16,8},{20,12},{24,16},{28,20},{1,25},{... | collective-permute-start | bytes 589832 | tf_op jit(solution)/shard_map/ppermute | solution.py:244
  34.9 23.5 %collective-permute-start.7 = (bf16[96,4096]{1,0:T(8,128)(2,1)S(1)}, bf16[96,4096]{1,0:T(8,128)(2,1)S(1)}, u32[]{:S(2)}, u32[]{:S(2)}) collective-permute-start(bf16[96,4096]{1,0:T(8,128)(2,1)S(1)} %pad_maximum_fusion.refs_0_), channel_id=1, source_target_pairs={{0,4},{4,0},{8,12},{12,8},{16,20},{20,16},{24,28},{28,24},{1,5},{5... | collective-permute-start | bytes 2359304 | tf_op jit(solution)/shard_map/ppermute | solution.py:248
  35.0 7.8 %collective-permute-start.12 = (bf16[96,1024]{1,0:T(8,128)(2,1)S(1)}, bf16[96,1024]{1,0:T(8,128)(2,1)S(1)}, u32[]{:S(2)}, u32[]{:S(2)}) collective-permute-start(bf16[96,1024]{1,0:T(8,128)(2,1)S(1)} %get-tuple-element.32), channel_id=1, source_target_pairs={{0,1},{1,0},{2,3},{3,2},{4,5},{5,4},{6,7},{7,6},{8,9},{9,8},{10,11... | collective-permute-start | bytes 589832 | tf_op jit(solution)/shard_map/ppermute | solution.py:252
  35.6 12.5 %collective-permute-start.14 = (bf16[96,1024]{1,0:T(8,128)(2,1)S(1)}, bf16[96,1024]{1,0:T(8,128)(2,1)S(1)}, u32[]{:S(2)}, u32[]{:S(2)}) collective-permute-start(bf16[96,1024]{1,0:T(8,128)(2,1)S(1)} %get-tuple-element.31), channel_id=1, source_target_pairs={{0,3},{1,2},{2,1},{3,0},{4,7},{5,6},{6,5},{7,4},{8,11},{9,10},{10,... | collective-permute-start | bytes 589832 | tf_op jit(solution)/shard_map/ppermute | solution.py:252
  38.1 11.0 %collective-permute-start.13 = (bf16[96,1024]{1,0:T(8,128)(2,1)S(1)}, bf16[96,1024]{1,0:T(8,128)(2,1)S(1)}, u32[]{:S(2)}, u32[]{:S(2)}) collective-permute-start(bf16[96,1024]{1,0:T(8,128)(2,1)S(1)} %get-tuple-element.30), channel_id=1, source_target_pairs={{0,2},{1,3},{2,0},{3,1},{4,6},{5,7},{6,4},{7,5},{8,10},{9,11},{10,... | collective-permute-start | bytes 589832 | tf_op jit(solution)/shard_map/ppermute | solution.py:252
  38.8 12.5 %collective-permute-start.25 = (bf16[96,1024]{1,0:T(8,128)(2,1)S(1)}, bf16[96,1024]{1,0:T(8,128)(2,1)S(1)}, u32[]{:S(2)}, u32[]{:S(2)}) collective-permute-start(bf16[96,1024]{1,0:T(8,128)(2,1)S(1)} %get-tuple-element.28), channel_id=1, source_target_pairs={{0,1},{1,0},{2,3},{3,2},{4,5},{5,4},{6,7},{7,6},{8,9},{9,8},{10,11... | collective-permute-start | bytes 589832 | tf_op jit(solution)/shard_map/ppermute | solution.py:252
  42.9 13.3 %collective-permute-start.27 = (bf16[96,1024]{1,0:T(8,128)(2,1)S(1)}, bf16[96,1024]{1,0:T(8,128)(2,1)S(1)}, u32[]{:S(2)}, u32[]{:S(2)}) collective-permute-start(bf16[96,1024]{1,0:T(8,128)(2,1)S(1)} %get-tuple-element.27), channel_id=1, source_target_pairs={{0,3},{1,2},{2,1},{3,0},{4,7},{5,6},{6,5},{7,4},{8,11},{9,10},{10,... | collective-permute-start | bytes 589832 | tf_op jit(solution)/shard_map/ppermute | solution.py:252
  48.1 10.2 %collective-permute-start.26 = (bf16[96,1024]{1,0:T(8,128)(2,1)S(1)}, bf16[96,1024]{1,0:T(8,128)(2,1)S(1)}, u32[]{:S(2)}, u32[]{:S(2)}) collective-permute-start(bf16[96,1024]{1,0:T(8,128)(2,1)S(1)} %get-tuple-element.26), channel_id=1, source_target_pairs={{0,2},{1,3},{2,0},{3,1},{4,6},{5,7},{6,4},{7,5},{8,10},{9,11},{10,... | collective-permute-start | bytes 589832 | tf_op jit(solution)/shard_map/ppermute | solution.py:252
  49.1 20.1 %collective-permute-start.3 = (bf16[96,4096]{1,0:T(8,128)(2,1)S(1)}, bf16[96,4096]{1,0:T(8,128)(2,1)S(1)}, u32[]{:S(2)}, u32[]{:S(2)}) collective-permute-start(bf16[96,4096]{1,0:T(8,128)(2,1)S(1)} %constant_dynamic-update-slice_fusion.refs_0_), channel_id=1, source_target_pairs={{0,4},{4,0},{8,12},{12,8},{16,20},{20,16},{24,28},{28,24},{1,5},{5... | collective-permute-start | bytes 2359304 | tf_op jit(solution)/shard_map/ppermute | solution.py:248
  51.3 32.6 %collective-permute-start.15 = (bf16[288,1024]{1,0:T(8,128)(2,1)S(1)}, bf16[288,1024]{1,0:T(8,128)(2,1)S(1)}, u32[]{:S(2)}, u32[]{:S(2)}) collective-permute-start(bf16[288,1024]{1,0:T(8,128)(2,1)S(1)} %pad_maximum_fusion.1), channel_id=1, source_target_pairs={{0,4},{4,0},{8,12},{12,8},{16,20},{20,16},{24,28},{28,24},{1,5},{5... | collective-permute-start | bytes 1769480 | tf_op jit(solution)/shard_map/ppermute | solution.py:248
  58.3 27.3 %collective-permute-start.28 = (bf16[288,1024]{1,0:T(8,128)(2,1)S(1)}, bf16[288,1024]{1,0:T(8,128)(2,1)S(1)}, u32[]{:S(2)}, u32[]{:S(2)}) collective-permute-start(bf16[288,1024]{1,0:T(8,128)(2,1)S(1)} %pad_maximum_fusion.2), channel_id=1, source_target_pairs={{0,4},{4,0},{8,12},{12,8},{16,20},{20,16},{24,28},{28,24},{1,5},{5... | collective-permute-start | bytes 1769480 | tf_op jit(solution)/shard_map/ppermute | solution.py:248
  81.2 18.4 %collective-permute-start.17 = (bf16[192,1792]{1,0:T(8,128)(2,1)S(1)}, bf16[192,1792]{1,0:T(8,128)(2,1)S(1)}, u32[]{:S(2)}, u32[]{:S(2)}) collective-permute-start(bf16[192,1792]{1,0:T(8,128)(2,1)S(1)} %get-tuple-element.17.refs_0_), channel_id=1, source_target_pairs={{0,2},{1,3},{2,0},{3,1},{4,6},{5,7},{6,4},{7,5},{8,10},{9,11},{10,... | collective-permute-start | bytes 2064392 | tf_op jit(solution)/shard_map/ppermute | solution.py:252
  81.8 31.3 %collective-permute-start.16 = (bf16[192,1792]{1,0:T(8,128)(2,1)S(1)}, bf16[192,1792]{1,0:T(8,128)(2,1)S(1)}, u32[]{:S(2)}, u32[]{:S(2)}) collective-permute-start(bf16[192,1792]{1,0:T(8,128)(2,1)S(1)} %get-tuple-element.17.refs_0_), channel_id=1, source_target_pairs={{0,1},{1,0},{2,3},{3,2},{4,5},{5,4},{6,7},{7,6},{8,9},{9,8},{10,11... | collective-permute-start | bytes 2064392 | tf_op jit(solution)/shard_map/ppermute | solution.py:252
  82.3 31.5 %collective-permute-start.23 = (bf16[192,1792]{1,0:T(8,128)(2,1)S(1)}, bf16[192,1792]{1,0:T(8,128)(2,1)S(1)}, u32[]{:S(2)}, u32[]{:S(2)}) collective-permute-start(bf16[192,1792]{1,0:T(8,128)(2,1)S(1)} %get-tuple-element.14.refs_3_), channel_id=1, source_target_pairs={{0,2},{1,3},{2,0},{3,1},{4,6},{5,7},{6,4},{7,5},{8,10},{9,11},{10,... | collective-permute-start | bytes 2064392 | tf_op jit(solution)/shard_map/ppermute | solution.py:252
  83.9 66.9 %collective-permute-start.22 = (bf16[192,1792]{1,0:T(8,128)(2,1)S(1)}, bf16[192,1792]{1,0:T(8,128)(2,1)S(1)}, u32[]{:S(2)}, u32[]{:S(2)}) collective-permute-start(bf16[192,1792]{1,0:T(8,128)(2,1)S(1)} %get-tuple-element.14.refs_3_), channel_id=1, source_target_pairs={{0,1},{1,0},{2,3},{3,2},{4,5},{5,4},{6,7},{7,6},{8,9},{9,8},{10,11... | collective-permute-start | bytes 2064392 | tf_op jit(solution)/shard_map/ppermute | solution.py:252
  85.6 44.0 %collective-permute-start.19 = (bf16[192,1792]{1,0:T(8,128)(2,1)S(1)}, bf16[192,1792]{1,0:T(8,128)(2,1)S(1)}, u32[]{:S(2)}, u32[]{:S(2)}) collective-permute-start(bf16[192,1792]{1,0:T(8,128)(2,1)S(1)} %get-tuple-element.18.refs_1_), channel_id=1, source_target_pairs={{0,1},{1,0},{2,3},{3,2},{4,5},{5,4},{6,7},{7,6},{8,9},{9,8},{10,11... | collective-permute-start | bytes 2064392 | tf_op jit(solution)/shard_map/ppermute | solution.py:252
  99.6 44.7 %collective-permute-start.18 = (bf16[192,1792]{1,0:T(8,128)(2,1)S(1)}, bf16[192,1792]{1,0:T(8,128)(2,1)S(1)}, u32[]{:S(2)}, u32[]{:S(2)}) collective-permute-start(bf16[192,1792]{1,0:T(8,128)(2,1)S(1)} %collective-permute-done.17), channel_id=1, source_target_pairs={{0,1},{1,0},{2,3},{3,2},{4,5},{5,4},{6,7},{7,6},{8,9},{9,8},{10,11... | collective-permute-start | bytes 2064392 | tf_op jit(solution)/shard_map/ppermute | solution.py:252
  113.1 49.8 %collective-permute-start.8 = (bf16[2,96,4096]{2,1,0:T(8,128)(2,1)S(1)}, bf16[2,96,4096]{2,1,0:T(8,128)(2,1)S(1)}, u32[]{:S(2)}, u32[]{:S(2)}) collective-permute-start(bf16[2,96,4096]{2,1,0:T(8,128)(2,1)S(1)} %get-tuple-element.22), channel_id=1, source_target_pairs={{0,4},{4,0},{8,12},{12,8},{16,20},{20,16},{24,28},{28,24},{1,5},{5... | collective-permute-start | bytes 4718600 | tf_op jit(solution)/shard_map/ppermute | solution.py:248
  113.9 44.5 %collective-permute-start.24 = (bf16[192,1792]{1,0:T(8,128)(2,1)S(1)}, bf16[192,1792]{1,0:T(8,128)(2,1)S(1)}, u32[]{:S(2)}, u32[]{:S(2)}) collective-permute-start(bf16[192,1792]{1,0:T(8,128)(2,1)S(1)} %collective-permute-done.23), channel_id=1, source_target_pairs={{0,1},{1,0},{2,3},{3,2},{4,5},{5,4},{6,7},{7,6},{8,9},{9,8},{10,11... | collective-permute-start | bytes 2064392 | tf_op jit(solution)/shard_map/ppermute | solution.py:252
  129.6 39.0 %collective-permute-start.20 = (bf16[192,1792]{1,0:T(8,128)(2,1)S(1)}, bf16[192,1792]{1,0:T(8,128)(2,1)S(1)}, u32[]{:S(2)}, u32[]{:S(2)}) collective-permute-start(bf16[192,1792]{1,0:T(8,128)(2,1)S(1)} %get-tuple-element.18.refs_1_), channel_id=1, source_target_pairs={{0,2},{1,3},{2,0},{3,1},{4,6},{5,7},{6,4},{7,5},{8,10},{9,11},{10,... | collective-permute-start | bytes 2064392 | tf_op jit(solution)/shard_map/ppermute | solution.py:252
  144.3 24.3 %collective-permute-start.21 = (bf16[192,1792]{1,0:T(8,128)(2,1)S(1)}, bf16[192,1792]{1,0:T(8,128)(2,1)S(1)}, u32[]{:S(2)}, u32[]{:S(2)}) collective-permute-start(bf16[192,1792]{1,0:T(8,128)(2,1)S(1)} %collective-permute-done.19), channel_id=1, source_target_pairs={{0,2},{1,3},{2,0},{3,1},{4,6},{5,7},{6,4},{7,5},{8,10},{9,11},{10,... | collective-permute-start | bytes 2064392 | tf_op jit(solution)/shard_map/ppermute | solution.py:252
  163.5 12.3 %collective-permute-start.11 = (bf16[2,24,4096]{2,1,0:T(8,128)(2,1)S(1)}, bf16[2,24,4096]{2,1,0:T(8,128)(2,1)S(1)}, u32[]{:S(2)}, u32[]{:S(2)}) collective-permute-start(bf16[2,24,4096]{2,1,0:T(8,128)(2,1)S(1)} %get-tuple-element.25), channel_id=1, source_target_pairs={{0,8},{4,12},{8,16},{12,20},{16,24},{20,28},{24,0},{28,4},{1,9},{5... | collective-permute-start | bytes 1179656 | tf_op jit(solution)/shard_map/ppermute | solution.py:244
  164.7 37.5 %collective-permute-start.10 = (bf16[2,24,4096]{2,1,0:T(8,128)(2,1)S(1)}, bf16[2,24,4096]{2,1,0:T(8,128)(2,1)S(1)}, u32[]{:S(2)}, u32[]{:S(2)}) collective-permute-start(bf16[2,24,4096]{2,1,0:T(8,128)(2,1)S(1)} %get-tuple-element.24), channel_id=1, source_target_pairs={{0,16},{4,20},{8,24},{12,28},{16,0},{20,4},{24,8},{28,12},{1,17},{... | collective-permute-start | bytes 1179656 | tf_op jit(solution)/shard_map/ppermute | solution.py:244
  168.6 33.6 %collective-permute-start.9 = (bf16[2,24,4096]{2,1,0:T(8,128)(2,1)S(1)}, bf16[2,24,4096]{2,1,0:T(8,128)(2,1)S(1)}, u32[]{:S(2)}, u32[]{:S(2)}) collective-permute-start(bf16[2,24,4096]{2,1,0:T(8,128)(2,1)S(1)} %get-tuple-element.23), channel_id=1, source_target_pairs={{0,24},{4,28},{8,0},{12,4},{16,8},{20,12},{24,16},{28,20},{1,25},{... | collective-permute-start | bytes 1179656 | tf_op jit(solution)/shard_map/ppermute | solution.py:244

commit v2 on v1

--- a/solution.py
+++ b/solution.py
@@ -267,12 +267,21 @@
             pairs += [got[(m - 1) * half:m * half], mate[(m - 1) * half:m * half]]
         return pairs
 
-    def spread(value, low):
-        held = [value]
+    def spread(value, way):
+        held = [[value]]
         for m in range(1, groups):
-            bit = m & -m if low else 1 << (m.bit_length() - 1)
-            held.append(across(held[m ^ bit], bit))
-        return held
+            low, high = m & -m, 1 << (m.bit_length() - 1)
+            if low == high:
+                held.append([across(value, m)])
+            elif way == "both":
+                a = jnp.concatenate(held[m ^ low], axis=0)
+                b = jnp.concatenate(held[m ^ high], axis=0)
+                half = a.shape[0] // 2
+                held.append([across(a[:half], low), across(b[half:], high)])
+            else:
+                bit = low if way == "low" else high
+                held.append([across(held[m ^ bit][0], bit)])
+        return sum(held, [])
 
     block = pick(modality, tokens, count)
     tok = gathered(block)
@@ -281,11 +290,11 @@
     cot_mate = swap(cot)
     tok_far = slices_of(tok)
     hid, active, factor = enter(tok, tok_mate, gate, up)
-    all_hid = spread(hid, True)
+    all_hid = spread(hid, "both")
     cot_far = slices_of(cot)
     gb, ub, own, other = turn(cot, cot_mate, down, hid, active, factor)
-    all_gb = spread(gb, True)
-    all_ub = spread(ub, False)
+    all_gb = spread(gb, "low")
+    all_ub = spread(ub, "high")
     own, other = leave(gb, ub, gate, up, own, other)
 
     mate = swap(other)

time: 203 us -> 201 us (level)
  waiting for transfers between devices: 108 us -> 105 us
    ppermute x9, waiting for transfers between devices: 41.8 us -> 39.1 us  [shift(): lax.ppermute(value, 'dp', [(z * CORES + c, (z + k) % ring * CORES + c) fo...]
    ppermute x15 -> x16, starting transfers between devices: 15.4 us -> 15.8 us  [across(): return lax.ppermute(value, 'seq', [(g, g ^ mask) for g in range(groups)])]
    ppermute x15 -> x16, waiting for transfers between devices: 66.4 us -> 66.1 us  [across(): return lax.ppermute(value, 'seq', [(g, g ^ mask) for g in range(groups)])]
  transfers between devices with their start and end apart: 29 -> 30, of which waited for: 15 -> 14; matrix products, arithmetic and copies ran while one was open for 9% -> 9% of each run, Pallas kernels for 19% -> 19%
where the time goes in v2:
time: 201 us
  waiting for transfers between devices  105 us (52%)
  starting transfers between devices  38.4 us (19%)
  Pallas kernels  37.7 us (19%)
  matrix products  14.4 us (7%)
  local copies, waits for them, and re-layouts  2.44 us (1%)
    ppermute x16, waiting for transfers between devices, across(): return lax.ppermute(value, 'seq', [(g, g ^ mask) for g in range(groups)])  66.1 us
    ppermute x9, waiting for transfers between devices, shift(): lax.ppermute(value, 'dp', [(z * CORES + c, (z + k) % ring * CORES + c) fo...  39.1 us
    ppermute x9, starting transfers between devices, shift(): lax.ppermute(value, 'dp', [(z * CORES + c, (z + k) % ring * CORES + c) fo...  22.4 us
    ppermute x16, starting transfers between devices, across(): return lax.ppermute(value, 'seq', [(g, g ^ mask) for g in range(groups)])  15.8 us
    dot_general x3, matrix products, rows_dot(): lax.dot_general(left, right, (((0,), (0,)), ((), ())), preferred_element_...  14.4 us
    pallas_call x1, Pallas kernels, leave(): pl.pallas_call(lambda *refs: leave_kernel(step, *refs), grid=(1,), in_spe...  12.9 us
    pallas_call x1, Pallas kernels, turn(): pl.pallas_call(lambda *refs: turn_kernel(tile, step, *refs), grid=(1,), i...  12 us
    pallas_call x1, Pallas kernels, enter(): pl.pallas_call(lambda *refs: enter_kernel(tile, *refs), in_specs=[VMEM, V...  10.8 us
  transfers between devices with their start and end apart: 30, of which 14 were waited for; matrix products, arithmetic and copies ran while one was open for 9% of the time, Pallas kernels for 19%

profile of v2, /device:TPU:26, one launch (start us, length us, event | category | flops | bytes accessed | tf_op | source)
XLA Modules:
  0.0 200.8 jit_solution(10593915982863341276)
XLA Ops:
  0.6 0.3 collective-permute-start
  0.9 1.7 collective-permute-start.1
  2.6 2.0 pick.1
  4.6 0.4 collective-permute-start.6
  5.0 2.6 %collective-permute-start.5 = (bf16[24,4096]{1,0:T(8,128)(2,1)}, bf16[24,4096]{1,0:T(8,128)(2,1)S(1)}, u32[]{:S(2)}, u32[]{:S(2)}) collective-permute-start(bf16[24,4096]{1,0:T(8,128)(2,1)} %pick.1), channel_id=1, source_target_pairs={{0,16},{4,20},{8,24},{12,28},{16,0},{20,4},{24,8},{28,12},{1,17},{... | collective-permute-start | bytes 589832 | tf_op jit(solution)/shard_map/ppermute | solution.py:244
  7.6 1.1 collective-permute-start.4
  8.7 0.9 constant_dynamic-update-slice_fusion.3
  9.7 7.3 %collective-permute-done.6 = bf16[24,4096]{1,0:T(8,128)(2,1)S(1)} collective-permute-done((bf16[24,4096]{1,0:T(8,128)(2,1)}, bf16[24,4096]{1,0:T(8,128)(2,1)S(1)}, u32[]{:S(2)}, u32[]{:S(2)}) %collective-permute-start.6) | collective-permute-done | bytes 196640 | tf_op jit(solution)/shard_map/ppermute | solution.py:244
  17.0 11.1 %collective-permute-start.2 = (bf16[24,4096]{1,0:T(8,128)(2,1)}, bf16[24,4096]{1,0:T(8,128)(2,1)S(1)}, u32[]{:S(2)}, u32[]{:S(2)}) collective-permute-start(bf16[24,4096]{1,0:T(8,128)(2,1)} %param.11), channel_id=1, source_target_pairs={{0,24},{4,28},{8,0},{12,4},{16,8},{20,12},{24,16},{28,20},{1,25},{... | collective-permute-start | bytes 589832 | tf_op jit(solution)/shard_map/ppermute | solution.py:244
  28.1 5.8 %collective-permute-done.5 = bf16[24,4096]{1,0:T(8,128)(2,1)S(1)} collective-permute-done((bf16[24,4096]{1,0:T(8,128)(2,1)}, bf16[24,4096]{1,0:T(8,128)(2,1)S(1)}, u32[]{:S(2)}, u32[]{:S(2)}) %collective-permute-start.5) | collective-permute-done | bytes 196640 | tf_op jit(solution)/shard_map/ppermute | solution.py:244
  33.9 1.0 pad_maximum_fusion.refs_0_
  34.9 0.1 collective-permute-start.7
  34.9 0.1 constant_dynamic-slice_fusion.4
  35.0 0.6 collective-permute-start.12
  35.6 2.4 %collective-permute-start.14 = (bf16[96,1024]{1,0:T(8,128)(2,1)S(1)}, bf16[96,1024]{1,0:T(8,128)(2,1)S(1)}, u32[]{:S(2)}, u32[]{:S(2)}) collective-permute-start(bf16[96,1024]{1,0:T(8,128)(2,1)S(1)} %get-tuple-element.31), channel_id=1, source_target_pairs={{0,3},{1,2},{2,1},{3,0},{4,7},{5,6},{6,5},{7,4},{8,11},{9,10},{10,... | collective-permute-start | bytes 589832 | tf_op jit(solution)/shard_map/ppermute | solution.py:252
  38.1 0.6 collective-permute-start.13
  38.7 0.0 collective-permute-done.2
  38.7 0.1 constant_dynamic-slice_fusion.1
  38.8 0.6 collective-permute-start.26
  39.4 3.5 %collective-permute-done.12 = bf16[96,1024]{1,0:T(8,128)(2,1)S(1)} collective-permute-done((bf16[96,1024]{1,0:T(8,128)(2,1)S(1)}, bf16[96,1024]{1,0:T(8,128)(2,1)S(1)}, u32[]{:S(2)}, u32[]{:S(2)}) %collective-permute-start.12) | collective-permute-done | bytes 196640 | tf_op jit(solution)/shard_map/ppermute | solution.py:252
  42.9 1.5 collective-permute-start.28
  44.4 3.7 %collective-permute-done.14 = bf16[96,1024]{1,0:T(8,128)(2,1)S(1)} collective-permute-done((bf16[96,1024]{1,0:T(8,128)(2,1)S(1)}, bf16[96,1024]{1,0:T(8,128)(2,1)S(1)}, u32[]{:S(2)}, u32[]{:S(2)}) %collective-permute-start.14) | collective-permute-done | bytes 196640 | tf_op jit(solution)/shard_map/ppermute | solution.py:252
  48.1 0.5 collective-permute-start.27
  48.6 0.5 collective-permute-done.13
  49.2 2.2 %collective-permute-done.26 = bf16[96,1024]{1,0:T(8,128)(2,1)S(1)} collective-permute-done((bf16[96,1024]{1,0:T(8,128)(2,1)S(1)}, bf16[96,1024]{1,0:T(8,128)(2,1)S(1)}, u32[]{:S(2)}, u32[]{:S(2)}) %collective-permute-start.26) | collective-permute-done | bytes 196640 | tf_op jit(solution)/shard_map/ppermute | solution.py:252
  51.3 0.0 collective-permute-start.15
  51.3 4.8 %collective-permute-done.28 = bf16[96,1024]{1,0:T(8,128)(2,1)S(1)} collective-permute-done((bf16[96,1024]{1,0:T(8,128)(2,1)S(1)}, bf16[96,1024]{1,0:T(8,128)(2,1)S(1)}, u32[]{:S(2)}, u32[]{:S(2)}) %collective-permute-start.28) | collective-permute-done | bytes 196640 | tf_op jit(solution)/shard_map/ppermute | solution.py:252
  56.1 2.1 %collective-permute-done.27 = bf16[96,1024]{1,0:T(8,128)(2,1)S(1)} collective-permute-done((bf16[96,1024]{1,0:T(8,128)(2,1)S(1)}, bf16[96,1024]{1,0:T(8,128)(2,1)S(1)}, u32[]{:S(2)}, u32[]{:S(2)}) %collective-permute-start.27) | collective-permute-done | bytes 196640 | tf_op jit(solution)/shard_map/ppermute | solution.py:252
  58.3 0.1 collective-permute-start.29
  58.4 0.0 collective-permute-done.7.refs_1_
  58.4 10.8 %enter.1 = (bf16[192,1792]{1,0:T(8,128)(2,1)S(1)}, f32[192,1792]{1,0:T(8,128)S(1)}, f32[192,1792]{1,0:T(8,128)S(1)}) custom-call(bf16[96,4096]{1,0:T(8,128)(2,1)S(1)} %pad_maximum_fusion.refs_0_, bf16[96,4096]{1,0:T(8,128)(2,1)S(1)} %collective-permute-done.7.refs_1_, bf16[4096,1792]{1,0:T(8,128)(2,1)} %refs_2_.5, bf16[4096,1792]{1,0:T(8,128)(2,1)} %refs_3_.3), custom_call_target="tpu_custom_call" | custom-call | flops 5637144576 | bytes 29360128 | tf_op jit(solution)/shard_map/enter/pallas_call | solution.py:107
  69.2 0.0 collective-permute-done.3.refs_1_
  69.2 12.0 %turn.1 = (bf16[192,1792]{1,0:T(8,128)(2,1)S(1)}, bf16[192,1792]{1,0:T(8,128)(2,1)S(1)}, bf16[2,96,4096]{2,1,0:T(8,128)(2,1)S(1)}, bf16[2,96,4096]{2,1,0:T(8,128)(2,1)S(1)}) custom-call(bf16[96,4096]{1,0:T(8,128)(2,1)S(1)} %constant_dynamic-update-slice_fusion.refs_0_, bf16[96,4096]{1,0:T(8,128)(2,1)S(1)} %collective-permute-done.3.refs_1_, ...), custom_call_target="tpu_custom_call" | custom-call | flops 5637144576 | bytes 14680064 | tf_op jit(solution)/shard_map/turn/pallas_call | solution.py:162
  81.2 0.6 collective-permute-start.17
  81.8 0.5 collective-permute-start.16
  82.3 1.5 collective-permute-start.22
  83.9 0.0 collective-permute-done.15
  83.9 1.6 collective-permute-start.23
  85.7 0.0 collective-permute-done.29
  85.7 0.6 collective-permute-start.19
  86.4 12.9 %leave.1 = (bf16[2,96,4096]{2,1,0:T(8,128)(2,1)S(1)}, bf16[2,96,4096]{2,1,0:T(8,128)(2,1)S(1)}) custom-call(bf16[192,1792]{1,0:T(8,128)(2,1)S(1)} %get-tuple-element.17.refs_0_, bf16[192,1792]{1,0:T(8,128)(2,1)S(1)} %get-tuple-element.18.refs_1_, bf16[4096,1792]{1,0:T(8,128)(2,1)} %refs_2_.5, ...), custom_call_target="tpu_custom_call", output_to_operand_aliasing={{0}: (4, {}), {1}: (5, {})} | custom-call | flops 5637144576 | bytes 29360128 | tf_op jit(solution)/shard_map/leave/pallas_call | solution.py:211
  99.3 14.5 %collective-permute-done.23 = bf16[192,1792]{1,0:T(8,128)(2,1)S(1)} collective-permute-done((bf16[192,1792]{1,0:T(8,128)(2,1)S(1)}, bf16[192,1792]{1,0:T(8,128)(2,1)S(1)}, u32[]{:S(2)}, u32[]{:S(2)}) %collective-permute-start.23) | collective-permute-done | bytes 688160 | tf_op jit(solution)/shard_map/ppermute | solution.py:252
  113.9 0.6 collective-permute-start.24
  114.5 0.4 collective-permute-done.22
  114.9 1.6 collective-permute-start.25
  116.6 19.7 %collective-permute-done.24 = bf16[96,1792]{1,0:T(8,128)(2,1)S(1)} collective-permute-done((bf16[96,1792]{1,0:T(8,128)(2,1)S(1)}, bf16[96,1792]{1,0:T(8,128)(2,1)S(1)}, u32[]{:S(2)}, u32[]{:S(2)}) %collective-permute-start.24) | collective-permute-done | bytes 344096 | tf_op jit(solution)/shard_map/ppermute | solution.py:252
  136.3 1.6 collective-permute-start.20
  137.8 0.0 collective-permute-done.19
  137.8 0.5 collective-permute-start.18
  138.4 0.0 collective-permute-done.25
  138.4 0.5 collective-permute-start.21
  138.9 4.5 %convolution_convert_fusion = bf16[1792,1024]{1,0:T(8,128)(2,1)} fusion(bf16[768,1792]{1,0:T(8,128)(2,1)S(1)} %constant_dynamic-update-slice_fusion.7, bf16[768,1024]{1,0:T(8,128)(2,1)S(1)} %slice_dynamic-update-slice_fusion), kind=kOutput, calls=%fused_computation | convolution fusion | flops 2820407296 | bytes 7995392 | tf_op jit(solution)/shard_map/dot_general | solution.py:231
  143.4 12.0 %collective-permute-done.18 = bf16[192,1792]{1,0:T(8,128)(2,1)S(1)} collective-permute-done((bf16[192,1792]{1,0:T(8,128)(2,1)S(1)}, bf16[192,1792]{1,0:T(8,128)(2,1)S(1)}, u32[]{:S(2)}, u32[]{:S(2)}) %collective-permute-start.18) | collective-permute-done | bytes 688160 | tf_op jit(solution)/shard_map/ppermute | solution.py:252
  155.4 4.9 %convolution_convert_fusion.2 = bf16[1024,1792]{1,0:T(8,128)(2,1)} fusion(bf16[768,1024]{1,0:T(8,128)(2,1)S(1)} %slice_dynamic-update-slice_fusion.3, bf16[192,1792]{1,0:T(8,128)(2,1)S(1)} %collective-permute-done.18, bf16[192,1792]{1,0:T(8,128)(2,1)S(1)} %collective-permute-done.17, bf16[192,1792]{1,0:T(8,128)(2,1)S(1)} %collective-permute-done.16, ...), kind=kOutput, calls=%fused_computation.2 | convolution fusion | flops 2831417344 | bytes 7995392 | tf_op jit(solution)/shard_map/dot_general | solution.py:231
  160.3 0.5 add_convert_fusion
  160.9 0.1 slice_bitcast_fusion.2
  161.0 1.3 collective-permute-start.11
  162.2 3.9 %collective-permute-start.10 = (bf16[2,24,4096]{2,1,0:T(8,128)(2,1)S(1)}, bf16[2,24,4096]{2,1,0:T(8,128)(2,1)S(1)}, u32[]{:S(2)}, u32[]{:S(2)}) collective-permute-start(bf16[2,24,4096]{2,1,0:T(8,128)(2,1)S(1)} %get-tuple-element.24), channel_id=1, source_target_pairs={{0,16},{4,20},{8,24},{12,28},{16,0},{20,4},{24,8},{28,12},{1,17},{... | collective-permute-start | bytes 1179656 | tf_op jit(solution)/shard_map/ppermute | solution.py:244
  166.2 0.0 collective-permute-start.9
  166.2 2.8 %collective-permute-done.21 = bf16[192,1792]{1,0:T(8,128)(2,1)S(1)} collective-permute-done((bf16[192,1792]{1,0:T(8,128)(2,1)S(1)}, bf16[192,1792]{1,0:T(8,128)(2,1)S(1)}, u32[]{:S(2)}, u32[]{:S(2)}) %collective-permute-start.21) | collective-permute-done | bytes 688160 | tf_op jit(solution)/shard_map/ppermute | solution.py:252
  168.9 4.9 %convolution_convert_fusion.1 = bf16[1024,1792]{1,0:T(8,128)(2,1)} fusion(bf16[768,1024]{1,0:T(8,128)(2,1)S(1)} %slice_dynamic-update-slice_fusion.3, bf16[192,1792]{1,0:T(8,128)(2,1)S(1)} %collective-permute-done.21, bf16[192,1792]{1,0:T(8,128)(2,1)S(1)} %collective-permute-done.20, bf16[192,1792]{1,0:T(8,128)(2,1)S(1)} %collective-permute-done.19, ...), kind=kOutput, calls=%fused_computation.1 | convolution fusion | flops 2831417344 | bytes 7995392 | tf_op jit(solution)/shard_map/dot_general | solution.py:231
  173.9 25.9 %collective-permute-done.10 = bf16[2,24,4096]{2,1,0:T(8,128)(2,1)S(1)} collective-permute-done((bf16[2,24,4096]{2,1,0:T(8,128)(2,1)S(1)}, bf16[2,24,4096]{2,1,0:T(8,128)(2,1)S(1)}, u32[]{:S(2)}, u32[]{:S(2)}) %collective-permute-start.10) | collective-permute-done | bytes 393248 | tf_op jit(solution)/shard_map/ppermute | solution.py:244
  199.8 0.2 fusion.16
  200.0 0.8 slice_bitcast_fusion.4
  (37 shorter events, 0.6 us)
Async XLA Ops:
  0.6 35.0 %collective-permute-start = (bf16[24,4096]{1,0:T(8,128)(2,1)}, bf16[24,4096]{1,0:T(8,128)(2,1)S(1)}, u32[]{:S(2)}, u32[]{:S(2)}) collective-permute-start(bf16[24,4096]{1,0:T(8,128)(2,1)} %param.11), channel_id=1, source_target_pairs={{0,8},{4,12},{8,16},{12,20},{16,24},{20,28},{24,0},{28,4},{1,9},{5... | collective-permute-start | bytes 589832 | tf_op jit(solution)/shard_map/ppermute | solution.py:244
  0.9 37.2 %collective-permute-start.1 = (bf16[24,4096]{1,0:T(8,128)(2,1)}, bf16[24,4096]{1,0:T(8,128)(2,1)S(1)}, u32[]{:S(2)}, u32[]{:S(2)}) collective-permute-start(bf16[24,4096]{1,0:T(8,128)(2,1)} %param.11), channel_id=1, source_target_pairs={{0,16},{4,20},{8,24},{12,28},{16,0},{20,4},{24,8},{28,12},{1,17},{... | collective-permute-start | bytes 589832 | tf_op jit(solution)/shard_map/ppermute | solution.py:244
  4.6 12.5 %collective-permute-start.6 = (bf16[24,4096]{1,0:T(8,128)(2,1)}, bf16[24,4096]{1,0:T(8,128)(2,1)S(1)}, u32[]{:S(2)}, u32[]{:S(2)}) collective-permute-start(bf16[24,4096]{1,0:T(8,128)(2,1)} %pick.1), channel_id=1, source_target_pairs={{0,24},{4,28},{8,0},{12,4},{16,8},{20,12},{24,16},{28,20},{1,25},{... | collective-permute-start | bytes 589832 | tf_op jit(solution)/shard_map/ppermute | solution.py:244
  5.0 28.9 %collective-permute-start.5 = (bf16[24,4096]{1,0:T(8,128)(2,1)}, bf16[24,4096]{1,0:T(8,128)(2,1)S(1)}, u32[]{:S(2)}, u32[]{:S(2)}) collective-permute-start(bf16[24,4096]{1,0:T(8,128)(2,1)} %pick.1), channel_id=1, source_target_pairs={{0,16},{4,20},{8,24},{12,28},{16,0},{20,4},{24,8},{28,12},{1,17},{... | collective-permute-start | bytes 589832 | tf_op jit(solution)/shard_map/ppermute | solution.py:244
  7.6 26.3 %collective-permute-start.4 = (bf16[24,4096]{1,0:T(8,128)(2,1)}, bf16[24,4096]{1,0:T(8,128)(2,1)S(1)}, u32[]{:S(2)}, u32[]{:S(2)}) collective-permute-start(bf16[24,4096]{1,0:T(8,128)(2,1)} %pick.1), channel_id=1, source_target_pairs={{0,8},{4,12},{8,16},{12,20},{16,24},{20,28},{24,0},{28,4},{1,9},{5... | collective-permute-start | bytes 589832 | tf_op jit(solution)/shard_map/ppermute | solution.py:244
  17.0 21.7 %collective-permute-start.2 = (bf16[24,4096]{1,0:T(8,128)(2,1)}, bf16[24,4096]{1,0:T(8,128)(2,1)S(1)}, u32[]{:S(2)}, u32[]{:S(2)}) collective-permute-start(bf16[24,4096]{1,0:T(8,128)(2,1)} %param.11), channel_id=1, source_target_pairs={{0,24},{4,28},{8,0},{12,4},{16,8},{20,12},{24,16},{28,20},{1,25},{... | collective-permute-start | bytes 589832 | tf_op jit(solution)/shard_map/ppermute | solution.py:244
  34.9 23.5 %collective-permute-start.7 = (bf16[96,4096]{1,0:T(8,128)(2,1)S(1)}, bf16[96,4096]{1,0:T(8,128)(2,1)S(1)}, u32[]{:S(2)}, u32[]{:S(2)}) collective-permute-start(bf16[96,4096]{1,0:T(8,128)(2,1)S(1)} %pad_maximum_fusion.refs_0_), channel_id=1, source_target_pairs={{0,4},{4,0},{8,12},{12,8},{16,20},{20,16},{24,28},{28,24},{1,5},{5... | collective-permute-start | bytes 2359304 | tf_op jit(solution)/shard_map/ppermute | solution.py:248
  35.0 7.8 %collective-permute-start.12 = (bf16[96,1024]{1,0:T(8,128)(2,1)S(1)}, bf16[96,1024]{1,0:T(8,128)(2,1)S(1)}, u32[]{:S(2)}, u32[]{:S(2)}) collective-permute-start(bf16[96,1024]{1,0:T(8,128)(2,1)S(1)} %get-tuple-element.32), channel_id=1, source_target_pairs={{0,1},{1,0},{2,3},{3,2},{4,5},{5,4},{6,7},{7,6},{8,9},{9,8},{10,11... | collective-permute-start | bytes 589832 | tf_op jit(solution)/shard_map/ppermute | solution.py:252
  35.6 12.5 %collective-permute-start.14 = (bf16[96,1024]{1,0:T(8,128)(2,1)S(1)}, bf16[96,1024]{1,0:T(8,128)(2,1)S(1)}, u32[]{:S(2)}, u32[]{:S(2)}) collective-permute-start(bf16[96,1024]{1,0:T(8,128)(2,1)S(1)} %get-tuple-element.31), channel_id=1, source_target_pairs={{0,3},{1,2},{2,1},{3,0},{4,7},{5,6},{6,5},{7,4},{8,11},{9,10},{10,... | collective-permute-start | bytes 589832 | tf_op jit(solution)/shard_map/ppermute | solution.py:252
  38.1 11.0 %collective-permute-start.13 = (bf16[96,1024]{1,0:T(8,128)(2,1)S(1)}, bf16[96,1024]{1,0:T(8,128)(2,1)S(1)}, u32[]{:S(2)}, u32[]{:S(2)}) collective-permute-start(bf16[96,1024]{1,0:T(8,128)(2,1)S(1)} %get-tuple-element.30), channel_id=1, source_target_pairs={{0,2},{1,3},{2,0},{3,1},{4,6},{5,7},{6,4},{7,5},{8,10},{9,11},{10,... | collective-permute-start | bytes 589832 | tf_op jit(solution)/shard_map/ppermute | solution.py:252
  38.8 12.5 %collective-permute-start.26 = (bf16[96,1024]{1,0:T(8,128)(2,1)S(1)}, bf16[96,1024]{1,0:T(8,128)(2,1)S(1)}, u32[]{:S(2)}, u32[]{:S(2)}) collective-permute-start(bf16[96,1024]{1,0:T(8,128)(2,1)S(1)} %get-tuple-element.28), channel_id=1, source_target_pairs={{0,1},{1,0},{2,3},{3,2},{4,5},{5,4},{6,7},{7,6},{8,9},{9,8},{10,11... | collective-permute-start | bytes 589832 | tf_op jit(solution)/shard_map/ppermute | solution.py:252
  42.9 13.3 %collective-permute-start.28 = (bf16[96,1024]{1,0:T(8,128)(2,1)S(1)}, bf16[96,1024]{1,0:T(8,128)(2,1)S(1)}, u32[]{:S(2)}, u32[]{:S(2)}) collective-permute-start(bf16[96,1024]{1,0:T(8,128)(2,1)S(1)} %get-tuple-element.27), channel_id=1, source_target_pairs={{0,3},{1,2},{2,1},{3,0},{4,7},{5,6},{6,5},{7,4},{8,11},{9,10},{10,... | collective-permute-start | bytes 589832 | tf_op jit(solution)/shard_map/ppermute | solution.py:252
  48.1 10.2 %collective-permute-start.27 = (bf16[96,1024]{1,0:T(8,128)(2,1)S(1)}, bf16[96,1024]{1,0:T(8,128)(2,1)S(1)}, u32[]{:S(2)}, u32[]{:S(2)}) collective-permute-start(bf16[96,1024]{1,0:T(8,128)(2,1)S(1)} %get-tuple-element.26), channel_id=1, source_target_pairs={{0,2},{1,3},{2,0},{3,1},{4,6},{5,7},{6,4},{7,5},{8,10},{9,11},{10,... | collective-permute-start | bytes 589832 | tf_op jit(solution)/shard_map/ppermute | solution.py:252
  49.1 20.1 %collective-permute-start.3 = (bf16[96,4096]{1,0:T(8,128)(2,1)S(1)}, bf16[96,4096]{1,0:T(8,128)(2,1)S(1)}, u32[]{:S(2)}, u32[]{:S(2)}) collective-permute-start(bf16[96,4096]{1,0:T(8,128)(2,1)S(1)} %constant_dynamic-update-slice_fusion.refs_0_), channel_id=1, source_target_pairs={{0,4},{4,0},{8,12},{12,8},{16,20},{20,16},{24,28},{28,24},{1,5},{5... | collective-permute-start | bytes 2359304 | tf_op jit(solution)/shard_map/ppermute | solution.py:248
  51.3 32.5 %collective-permute-start.15 = (bf16[288,1024]{1,0:T(8,128)(2,1)S(1)}, bf16[288,1024]{1,0:T(8,128)(2,1)S(1)}, u32[]{:S(2)}, u32[]{:S(2)}) collective-permute-start(bf16[288,1024]{1,0:T(8,128)(2,1)S(1)} %pad_maximum_fusion.1), channel_id=1, source_target_pairs={{0,4},{4,0},{8,12},{12,8},{16,20},{20,16},{24,28},{28,24},{1,5},{5... | collective-permute-start | bytes 1769480 | tf_op jit(solution)/shard_map/ppermute | solution.py:248
  58.3 27.4 %collective-permute-start.29 = (bf16[288,1024]{1,0:T(8,128)(2,1)S(1)}, bf16[288,1024]{1,0:T(8,128)(2,1)S(1)}, u32[]{:S(2)}, u32[]{:S(2)}) collective-permute-start(bf16[288,1024]{1,0:T(8,128)(2,1)S(1)} %pad_maximum_fusion.2), channel_id=1, source_target_pairs={{0,4},{4,0},{8,12},{12,8},{16,20},{20,16},{24,28},{28,24},{1,5},{5... | collective-permute-start | bytes 1769480 | tf_op jit(solution)/shard_map/ppermute | solution.py:248
  81.2 55.0 %collective-permute-start.17 = (bf16[192,1792]{1,0:T(8,128)(2,1)S(1)}, bf16[192,1792]{1,0:T(8,128)(2,1)S(1)}, u32[]{:S(2)}, u32[]{:S(2)}) collective-permute-start(bf16[192,1792]{1,0:T(8,128)(2,1)S(1)} %get-tuple-element.17.refs_0_), channel_id=1, source_target_pairs={{0,2},{1,3},{2,0},{3,1},{4,6},{5,7},{6,4},{7,5},{8,10},{9,11},{10,... | collective-permute-start | bytes 2064392 | tf_op jit(solution)/shard_map/ppermute | solution.py:252
  81.8 61.7 %collective-permute-start.16 = (bf16[192,1792]{1,0:T(8,128)(2,1)S(1)}, bf16[192,1792]{1,0:T(8,128)(2,1)S(1)}, u32[]{:S(2)}, u32[]{:S(2)}) collective-permute-start(bf16[192,1792]{1,0:T(8,128)(2,1)S(1)} %get-tuple-element.17.refs_0_), channel_id=1, source_target_pairs={{0,1},{1,0},{2,3},{3,2},{4,5},{5,4},{6,7},{7,6},{8,9},{9,8},{10,11... | collective-permute-start | bytes 2064392 | tf_op jit(solution)/shard_map/ppermute | solution.py:252
  82.3 32.5 %collective-permute-start.22 = (bf16[192,1792]{1,0:T(8,128)(2,1)S(1)}, bf16[192,1792]{1,0:T(8,128)(2,1)S(1)}, u32[]{:S(2)}, u32[]{:S(2)}) collective-permute-start(bf16[192,1792]{1,0:T(8,128)(2,1)S(1)} %get-tuple-element.14.refs_3_), channel_id=1, source_target_pairs={{0,1},{1,0},{2,3},{3,2},{4,5},{5,4},{6,7},{7,6},{8,9},{9,8},{10,11... | collective-permute-start | bytes 2064392 | tf_op jit(solution)/shard_map/ppermute | solution.py:252
  83.9 30.0 %collective-permute-start.23 = (bf16[192,1792]{1,0:T(8,128)(2,1)S(1)}, bf16[192,1792]{1,0:T(8,128)(2,1)S(1)}, u32[]{:S(2)}, u32[]{:S(2)}) collective-permute-start(bf16[192,1792]{1,0:T(8,128)(2,1)S(1)} %get-tuple-element.14.refs_3_), channel_id=1, source_target_pairs={{0,2},{1,3},{2,0},{3,1},{4,6},{5,7},{6,4},{7,5},{8,10},{9,11},{10,... | collective-permute-start | bytes 2064392 | tf_op jit(solution)/shard_map/ppermute | solution.py:252
  85.7 52.1 %collective-permute-start.19 = (bf16[192,1792]{1,0:T(8,128)(2,1)S(1)}, bf16[192,1792]{1,0:T(8,128)(2,1)S(1)}, u32[]{:S(2)}, u32[]{:S(2)}) collective-permute-start(bf16[192,1792]{1,0:T(8,128)(2,1)S(1)} %get-tuple-element.18.refs_1_), channel_id=1, source_target_pairs={{0,1},{1,0},{2,3},{3,2},{4,5},{5,4},{6,7},{7,6},{8,9},{9,8},{10,11... | collective-permute-start | bytes 2064392 | tf_op jit(solution)/shard_map/ppermute | solution.py:252
  113.9 22.3 %collective-permute-start.24 = (bf16[96,1792]{1,0:T(8,128)(2,1)S(1)}, bf16[96,1792]{1,0:T(8,128)(2,1)S(1)}, u32[]{:S(2)}, u32[]{:S(2)}) collective-permute-start(bf16[96,1792]{1,0:T(8,128)(2,1)S(1)} %slice.65), channel_id=1, source_target_pairs={{0,1},{1,0},{2,3},{3,2},{4,5},{5,4},{6,7},{7,6},{8,9},{9,8},{10,11... | collective-permute-start | bytes 1032200 | tf_op jit(solution)/shard_map/ppermute | solution.py:252
  114.9 23.5 %collective-permute-start.25 = (bf16[96,1792]{1,0:T(8,128)(2,1)S(1)}, bf16[96,1792]{1,0:T(8,128)(2,1)S(1)}, u32[]{:S(2)}, u32[]{:S(2)}) collective-permute-start(bf16[96,1792]{1,0:T(8,128)(2,1)S(1)} %slice.66), channel_id=1, source_target_pairs={{0,2},{1,3},{2,0},{3,1},{4,6},{5,7},{6,4},{7,5},{8,10},{9,11},{10,... | collective-permute-start | bytes 1032200 | tf_op jit(solution)/shard_map/ppermute | solution.py:252
  136.2 24.1 %collective-permute-start.8 = (bf16[2,96,4096]{2,1,0:T(8,128)(2,1)S(1)}, bf16[2,96,4096]{2,1,0:T(8,128)(2,1)S(1)}, u32[]{:S(2)}, u32[]{:S(2)}) collective-permute-start(bf16[2,96,4096]{2,1,0:T(8,128)(2,1)S(1)} %get-tuple-element.22), channel_id=1, source_target_pairs={{0,4},{4,0},{8,12},{12,8},{16,20},{20,16},{24,28},{28,24},{1,5},{5... | collective-permute-start | bytes 4718600 | tf_op jit(solution)/shard_map/ppermute | solution.py:248
  136.3 29.9 %collective-permute-start.20 = (bf16[192,1792]{1,0:T(8,128)(2,1)S(1)}, bf16[192,1792]{1,0:T(8,128)(2,1)S(1)}, u32[]{:S(2)}, u32[]{:S(2)}) collective-permute-start(bf16[192,1792]{1,0:T(8,128)(2,1)S(1)} %get-tuple-element.18.refs_1_), channel_id=1, source_target_pairs={{0,2},{1,3},{2,0},{3,1},{4,6},{5,7},{6,4},{7,5},{8,10},{9,11},{10,... | collective-permute-start | bytes 2064392 | tf_op jit(solution)/shard_map/ppermute | solution.py:252
  137.8 17.6 %collective-permute-start.18 = (bf16[192,1792]{1,0:T(8,128)(2,1)S(1)}, bf16[192,1792]{1,0:T(8,128)(2,1)S(1)}, u32[]{:S(2)}, u32[]{:S(2)}) collective-permute-start(bf16[192,1792]{1,0:T(8,128)(2,1)S(1)} %collective-permute-done.17), channel_id=1, source_target_pairs={{0,1},{1,0},{2,3},{3,2},{4,5},{5,4},{6,7},{7,6},{8,9},{9,8},{10,11... | collective-permute-start | bytes 2064392 | tf_op jit(solution)/shard_map/ppermute | solution.py:252
  138.4 30.5 %collective-permute-start.21 = (bf16[192,1792]{1,0:T(8,128)(2,1)S(1)}, bf16[192,1792]{1,0:T(8,128)(2,1)S(1)}, u32[]{:S(2)}, u32[]{:S(2)}) collective-permute-start(bf16[192,1792]{1,0:T(8,128)(2,1)S(1)} %collective-permute-done.19), channel_id=1, source_target_pairs={{0,2},{1,3},{2,0},{3,1},{4,6},{5,7},{6,4},{7,5},{8,10},{9,11},{10,... | collective-permute-start | bytes 2064392 | tf_op jit(solution)/shard_map/ppermute | solution.py:252
  161.0 12.9 %collective-permute-start.11 = (bf16[2,24,4096]{2,1,0:T(8,128)(2,1)S(1)}, bf16[2,24,4096]{2,1,0:T(8,128)(2,1)S(1)}, u32[]{:S(2)}, u32[]{:S(2)}) collective-permute-start(bf16[2,24,4096]{2,1,0:T(8,128)(2,1)S(1)} %get-tuple-element.25), channel_id=1, source_target_pairs={{0,8},{4,12},{8,16},{12,20},{16,24},{20,28},{24,0},{28,4},{1,9},{5... | collective-permute-start | bytes 1179656 | tf_op jit(solution)/shard_map/ppermute | solution.py:244
  162.2 37.6 %collective-permute-start.10 = (bf16[2,24,4096]{2,1,0:T(8,128)(2,1)S(1)}, bf16[2,24,4096]{2,1,0:T(8,128)(2,1)S(1)}, u32[]{:S(2)}, u32[]{:S(2)}) collective-permute-start(bf16[2,24,4096]{2,1,0:T(8,128)(2,1)S(1)} %get-tuple-element.24), channel_id=1, source_target_pairs={{0,16},{4,20},{8,24},{12,28},{16,0},{20,4},{24,8},{28,12},{1,17},{... | collective-permute-start | bytes 1179656 | tf_op jit(solution)/shard_map/ppermute | solution.py:244
  166.2 33.6 %collective-permute-start.9 = (bf16[2,24,4096]{2,1,0:T(8,128)(2,1)S(1)}, bf16[2,24,4096]{2,1,0:T(8,128)(2,1)S(1)}, u32[]{:S(2)}, u32[]{:S(2)}) collective-permute-start(bf16[2,24,4096]{2,1,0:T(8,128)(2,1)S(1)} %get-tuple-element.23), channel_id=1, source_target_pairs={{0,24},{4,28},{8,0},{12,4},{16,8},{20,12},{24,16},{28,20},{1,25},{... | collective-permute-start | bytes 1179656 | tf_op jit(solution)/shard_map/ppermute | solution.py:244

commit v3 on v1

--- a/solution.py
+++ b/solution.py
@@ -227,7 +227,6 @@
 
 
 def rows_dot(left, right):
-    left, right = jnp.concatenate(left, axis=0), jnp.concatenate(right, axis=0)
     return lax.dot_general(
         left, right, (((0,), (0,)), ((), ())), preferred_element_type=F32
     ).astype(BF)
@@ -257,49 +256,73 @@
     def cut(matrix, group):
         return lax.dynamic_slice_in_dim(matrix, group * part, part, axis=1)
 
-    def slices_of(own):
-        half = own.shape[0]
-        far = [across(cut(own, me ^ m), m) for m in range(1, groups)]
-        got = jnp.concatenate(far, axis=0)
-        mate = swap(got)
-        pairs = []
+    def slices_of(tok_block, cot_block):
+        def both(group):
+            return jnp.concatenate([cut(tok_block, group), cut(cot_block, group)], axis=1)
+
+        small = jnp.stack(
+            [both(me)] + [across(both(me ^ m), m) for m in range(1, groups)])
+        pieces = [small] + [shift(small, k) for k in range(1, ring)]
+        own = jnp.stack(pieces, axis=1)
+        mate = swap(own)
+        both_cores = jnp.stack([own, mate], axis=1)
+        return (both_cores[..., :part].reshape(-1, part), both_cores[..., part:].reshape(-1, part))
+
+    def near(value):
+        held = [[value]] + [None] * (groups - 1)
         for m in range(1, groups):
-            pairs += [got[(m - 1) * half:m * half], mate[(m - 1) * half:m * half]]
-        return pairs
-
-    def spread(value, low):
-        held = [value]
+            if m & (m - 1) == 0:
+                held[m] = [across(value, m)]
+        return held
+
+    def relay(held):
+        half = held[0][0].shape[0] // 2
+        held = list(held)
         for m in range(1, groups):
-            bit = m & -m if low else 1 << (m.bit_length() - 1)
-            held.append(across(held[m ^ bit], bit))
+            low, high = m & -m, 1 << (m.bit_length() - 1)
+            if low != high:
+                a = jnp.concatenate(held[m ^ low], axis=0)
+                b = jnp.concatenate(held[m ^ high], axis=0)
+                held[m] = [across(a[:half], low), across(b[half:], high)]
         return held
+
+    def after(values, others):
+        leaves, tree = jax.tree.flatten(values)
+        return jax.tree.unflatten(
+            tree, lax.optimization_barrier((*leaves, *others))[:len(leaves)])
+
+    def stack(held):
+        return jnp.concatenate(sum(held, []), axis=0)
 
     block = pick(modality, tokens, count)
     tok = gathered(block)
     tok_mate = swap(tok)
+    tok_all, cot_all = slices_of(block, out_grad)
     cot = gathered(out_grad)
     cot_mate = swap(cot)
-    tok_far = slices_of(tok)
     hid, active, factor = enter(tok, tok_mate, gate, up)
-    all_hid = spread(hid, True)
-    cot_far = slices_of(cot)
+    all_hid = relay(near(hid))
     gb, ub, own, other = turn(cot, cot_mate, down, hid, active, factor)
-    all_gb = spread(gb, True)
-    all_ub = spread(ub, False)
+    all_gb = near(gb)
+    all_ub = near(ub)
     own, other = leave(gb, ub, gate, up, own, other)
 
     mate = swap(other)
-    pieces = (own.astype(F32) + mate.astype(F32)).astype(BF).reshape(2, ring, count, width)
-    total = pieces[:, 0].astype(F32)
-    for k in range(1, ring):
-        total = total + shift(pieces[:, k], -k).astype(F32)
+    sums = (own.astype(F32) + mate.astype(F32)).astype(BF).reshape(2, ring, count, width)
+    sums = [sums[:, k] for k in range(ring)]
+    terms = [shift(sums[k], -k) for k in range(1, ring)]
+
+    all_hid = after(all_hid, sums[1:])
+    all_gb = relay(after(all_gb, sums[1:]))
+    all_ub = relay(after(all_ub, sums[1:]))
+    down_grad = rows_dot(stack(all_hid), cot_all)
+    gate_grad = rows_dot(tok_all, stack(all_gb))
+    up_grad = rows_dot(tok_all, stack(all_ub))
+    terms = after(terms, [gate_grad])
+    total = sums[0].astype(F32)
+    for term in terms:
+        total = total + term.astype(F32)
     total = total.astype(BF)
-
-    tok_all = [cut(tok, me), cut(tok_mate, me)] + tok_far
-    cot_all = [cut(cot, me), cut(cot_mate, me)] + cot_far
-    down_grad = rows_dot(all_hid, cot_all)
-    gate_grad = rows_dot(tok_all, all_gb)
-    up_grad = rows_dot(tok_all, all_ub)
     return total[0], total[1], gate_grad, up_grad, down_grad
 
 

time: 203 us -> 190 us (0.936)
  the two profiles are of different devices: /device:TPU:26 before, /device:TPU:0 now
where the time goes in v3:
time: 190 us
  waiting for transfers between devices  83.5 us (44%)
  starting transfers between devices  48.2 us (25%)
  Pallas kernels  37.7 us (20%)
  matrix products  13.7 us (7%)
  local copies, waits for them, and re-layouts  4.69 us (2%)
    ppermute x15, waiting for transfers between devices, across(): return lax.ppermute(value, 'seq', [(g, g ^ mask) for g in range(groups)])  51.6 us
    ppermute x12, waiting for transfers between devices, shift(): lax.ppermute(value, 'dp', [(z * CORES + c, (z + k) % ring * CORES + c) fo...  31.8 us
    ppermute x12, starting transfers between devices, shift(): lax.ppermute(value, 'dp', [(z * CORES + c, (z + k) % ring * CORES + c) fo...  30.9 us
    ppermute x15, starting transfers between devices, across(): return lax.ppermute(value, 'seq', [(g, g ^ mask) for g in range(groups)])  16 us
    dot_general x3, matrix products, rows_dot(): lax.dot_general(left, right, (((0,), (0,)), ((), ())), preferred_element_...  13.7 us
    pallas_call x1, Pallas kernels, leave(): pl.pallas_call(lambda *refs: leave_kernel(step, *refs), grid=(1,), in_spe...  12.9 us
    pallas_call x1, Pallas kernels, turn(): pl.pallas_call(lambda *refs: turn_kernel(tile, step, *refs), grid=(1,), i...  12 us
    pallas_call x1, Pallas kernels, enter(): pl.pallas_call(lambda *refs: enter_kernel(tile, *refs), in_specs=[VMEM, V...  10.8 us
  transfers between devices with their start and end apart: 31, of which 16 were waited for; matrix products, arithmetic and copies ran while one was open for 10% of the time, Pallas kernels for 20%

profile of v3, /device:TPU:0, one launch (start us, length us, event | category | flops | bytes accessed | tf_op | source)
XLA Modules:
  0.0 190.3 jit_solution(8482409884763937685)
XLA Ops:
  0.6 3.1 %collective-permute-start = (bf16[24,4096]{1,0:T(8,128)(2,1)}, bf16[24,4096]{1,0:T(8,128)(2,1)S(1)}, u32[]{:S(2)}, u32[]{:S(2)}) collective-permute-start(bf16[24,4096]{1,0:T(8,128)(2,1)} %param.11), channel_id=1, source_target_pairs={{0,8},{4,12},{8,16},{12,20},{16,24},{20,28},{24,0},{28,4},{1,9},{5... | collective-permute-start | bytes 589832 | tf_op jit(solution)/shard_map/ppermute | solution.py:243
  3.7 2.6 %collective-permute-start.1 = (bf16[24,4096]{1,0:T(8,128)(2,1)}, bf16[24,4096]{1,0:T(8,128)(2,1)S(1)}, u32[]{:S(2)}, u32[]{:S(2)}) collective-permute-start(bf16[24,4096]{1,0:T(8,128)(2,1)} %param.11), channel_id=1, source_target_pairs={{0,16},{4,20},{8,24},{12,28},{16,0},{20,4},{24,8},{28,12},{1,17},{... | collective-permute-start | bytes 589832 | tf_op jit(solution)/shard_map/ppermute | solution.py:243
  6.3 2.0 %pick.1 = bf16[24,4096]{1,0:T(8,128)(2,1)} custom-call(s32[1,32]{1,0:T(1,128)} %bitcast.58, bf16[32,4096]{1,0:T(8,128)(2,1)} %tokens_ref.1), custom_call_target="tpu_custom_call" | custom-call | tf_op jit(solution)/shard_map/pick/pallas_call | solution.py:62
  8.3 0.9 constant_dynamic-slice_fusion.6
  9.2 0.9 constant_dynamic-slice_fusion.7
  10.2 2.5 %collective-permute-start.14 = (bf16[24,2048]{1,0:T(8,128)(2,1)S(1)}, bf16[24,2048]{1,0:T(8,128)(2,1)S(1)}, u32[]{:S(2)}, u32[]{:S(2)}) collective-permute-start(bf16[24,2048]{1,0:T(8,128)(2,1)S(1)} %pad_maximum_fusion.6), channel_id=1, source_target_pairs={{0,3},{1,2},{2,1},{3,0},{4,7},{5,6},{6,5},{7,4},{8,11},{9,10},{10,... | collective-permute-start | bytes 294920 | tf_op jit(solution)/shard_map/ppermute | solution.py:251
  12.7 0.6 collective-permute-start.13
  13.3 0.6 collective-permute-start.12
  13.8 0.9 constant_dynamic-update-slice_fusion.3
  14.8 1.1 collective-permute-done.14
  15.9 1.3 collective-permute-start.6
  17.2 0.2 collective-permute-done.13
  17.5 0.3 collective-permute-start.5
  17.8 0.1 collective-permute-done.12
  17.9 1.5 collective-permute-start.4
  19.4 0.1 fusion.4
  19.5 4.1 %collective-permute-done.6 = bf16[24,4096]{1,0:T(8,128)(2,1)S(1)} collective-permute-done((bf16[24,4096]{1,0:T(8,128)(2,1)}, bf16[24,4096]{1,0:T(8,128)(2,1)S(1)}, u32[]{:S(2)}, u32[]{:S(2)}) %collective-permute-start.6) | collective-permute-done | bytes 196640 | tf_op jit(solution)/shard_map/ppermute | solution.py:243
  23.5 3.6 %collective-permute-start.2 = (bf16[24,4096]{1,0:T(8,128)(2,1)S(1)}, bf16[24,4096]{1,0:T(8,128)(2,1)S(1)}, u32[]{:S(2)}, u32[]{:S(2)}) collective-permute-start(bf16[24,4096]{1,0:T(8,128)(2,1)S(1)} %copy-done.1), channel_id=1, source_target_pairs={{0,24},{4,28},{8,0},{12,4},{16,8},{20,12},{24,16},{28,20},{1,25},{... | collective-permute-start | bytes 589832 | tf_op jit(solution)/shard_map/ppermute | solution.py:243
  27.1 9.3 %collective-permute-done.5 = bf16[24,4096]{1,0:T(8,128)(2,1)S(1)} collective-permute-done((bf16[24,4096]{1,0:T(8,128)(2,1)}, bf16[24,4096]{1,0:T(8,128)(2,1)S(1)}, u32[]{:S(2)}, u32[]{:S(2)}) %collective-permute-start.5) | collective-permute-done | bytes 196640 | tf_op jit(solution)/shard_map/ppermute | solution.py:243
  36.4 2.5 %collective-permute-start.17 = (bf16[4,24,2048]{2,1,0:T(8,128)(2,1)S(1)}, bf16[4,24,2048]{2,1,0:T(8,128)(2,1)S(1)}, u32[]{:S(2)}, u32[]{:S(2)}) collective-permute-start(bf16[4,24,2048]{2,1,0:T(8,128)(2,1)S(1)} %get-tuple-element.61), channel_id=1, source_target_pairs={{0,24},{4,28},{8,0},{12,4},{16,8},{20,12},{24,16},{28,20},{1,25},{... | collective-permute-start | bytes 1179656 | tf_op jit(solution)/shard_map/ppermute | solution.py:243
  38.9 16.0 %collective-permute-start.16 = (bf16[4,24,2048]{2,1,0:T(8,128)(2,1)S(1)}, bf16[4,24,2048]{2,1,0:T(8,128)(2,1)S(1)}, u32[]{:S(2)}, u32[]{:S(2)}) collective-permute-start(bf16[4,24,2048]{2,1,0:T(8,128)(2,1)S(1)} %get-tuple-element.61), channel_id=1, source_target_pairs={{0,16},{4,20},{8,24},{12,28},{16,0},{20,4},{24,8},{28,12},{1,17},{... | collective-permute-start | bytes 1179656 | tf_op jit(solution)/shard_map/ppermute | solution.py:243
  54.8 0.1 pad_maximum_fusion.2.refs_0_
  54.9 0.1 collective-permute-start.15
  55.0 0.1 collective-permute-start.7
  55.1 0.6 collective-permute-start.3
  55.7 18.5 %collective-permute-done.16 = bf16[4,24,2048]{2,1,0:T(8,128)(2,1)S(1)} collective-permute-done((bf16[4,24,2048]{2,1,0:T(8,128)(2,1)S(1)}, bf16[4,24,2048]{2,1,0:T(8,128)(2,1)S(1)}, u32[]{:S(2)}, u32[]{:S(2)}) %collective-permute-start.16) | collective-permute-done | bytes 393248 | tf_op jit(solution)/shard_map/ppermute | solution.py:243
  74.2 0.3 pad_maximum_fusion.1
  74.4 0.1 collective-permute-start.18
  74.5 10.8 %enter.1 = (bf16[192,1792]{1,0:T(8,128)(2,1)S(1)}, f32[192,1792]{1,0:T(8,128)S(1)}, f32[192,1792]{1,0:T(8,128)S(1)}) custom-call(bf16[96,4096]{1,0:T(8,128)(2,1)S(1)} %pad_maximum_fusion.2.refs_0_, bf16[96,4096]{1,0:T(8,128)(2,1)S(1)} %collective-permute-done.7.refs_1_, bf16[4096,1792]{1,0:T(8,128)(2,1)} %refs_2_.5, bf16[4096,1792]{1,0:T(8,128)(2,1)} %refs_3_.3), custom_call_target="tpu_custom_call" | custom-call | flops 5637144576 | bytes 29360128 | tf_op jit(solution)/shard_map/enter/pallas_call | solution.py:107
  85.3 12.0 %turn.1 = (bf16[192,1792]{1,0:T(8,128)(2,1)S(1)}, bf16[192,1792]{1,0:T(8,128)(2,1)S(1)}, bf16[2,96,4096]{2,1,0:T(8,128)(2,1)S(1)}, bf16[2,96,4096]{2,1,0:T(8,128)(2,1)S(1)}) custom-call(bf16[96,4096]{1,0:T(8,128)(2,1)S(1)} %constant_dynamic-update-slice_fusion.refs_0_, bf16[96,4096]{1,0:T(8,128)(2,1)S(1)} %collective-permute-done.3.refs_1_, ...), custom_call_target="tpu_custom_call" | custom-call | flops 5637144576 | bytes 14680064 | tf_op jit(solution)/shard_map/turn/pallas_call | solution.py:162
  97.4 12.9 %leave.1 = (bf16[2,96,4096]{2,1,0:T(8,128)(2,1)S(1)}, bf16[2,96,4096]{2,1,0:T(8,128)(2,1)S(1)}) custom-call(bf16[192,1792]{1,0:T(8,128)(2,1)S(1)} %get-tuple-element.37.refs_0_, bf16[192,1792]{1,0:T(8,128)(2,1)S(1)} %get-tuple-element.43.refs_1_, bf16[4096,1792]{1,0:T(8,128)(2,1)} %refs_2_.5, ...), custom_call_target="tpu_custom_call", output_to_operand_aliasing={{0}: (4, {}), {1}: (5, {})} | custom-call | flops 5637144576 | bytes 29360128 | tf_op jit(solution)/shard_map/leave/pallas_call | solution.py:211
  110.3 0.6 collective-permute-start.8
  110.9 2.2 %collective-permute-start.28 = (bf16[192,1792]{1,0:T(8,128)(2,1)S(1)}, bf16[192,1792]{1,0:T(8,128)(2,1)S(1)}, u32[]{:S(2)}, u32[]{:S(2)}) collective-permute-start(bf16[192,1792]{1,0:T(8,128)(2,1)S(1)} %get-tuple-element.46.refs_3_), channel_id=1, source_target_pairs={{0,2},{1,3},{2,0},{3,1},{4,6},{5,7},{6,4},{7,5},{8,10},{9,11},{10,... | collective-permute-start | bytes 2064392 | tf_op jit(solution)/shard_map/ppermute | solution.py:251
  113.1 0.8 collective-permute-start.27
  113.9 1.2 collective-permute-start.19
  115.1 13.7 %collective-permute-done.28 = bf16[192,1792]{1,0:T(8,128)(2,1)S(1)} collective-permute-done((bf16[192,1792]{1,0:T(8,128)(2,1)S(1)}, bf16[192,1792]{1,0:T(8,128)(2,1)S(1)}, u32[]{:S(2)}, u32[]{:S(2)}) %collective-permute-start.28) | collective-permute-done | bytes 688160 | tf_op jit(solution)/shard_map/ppermute | solution.py:251
  128.7 1.7 collective-permute-start.20
  130.5 0.9 collective-permute-done.27
  131.4 0.8 collective-permute-start.23
  132.2 1.2 collective-permute-start.24
  133.5 0.4 pad_maximum_fusion
  133.8 0.2 copy.21
  134.0 0.2 copy.22
  134.2 0.1 collective-permute-start.29
  134.3 0.5 add_convert_fusion
  134.8 0.1 slice_bitcast_fusion
  134.9 11.2 %collective-permute-done.19 = bf16[192,1792]{1,0:T(8,128)(2,1)S(1)} collective-permute-done((bf16[192,1792]{1,0:T(8,128)(2,1)S(1)}, bf16[192,1792]{1,0:T(8,128)(2,1)S(1)}, u32[]{:S(2)}, u32[]{:S(2)}) %collective-permute-start.19) | collective-permute-done | bytes 688160 | tf_op jit(solution)/shard_map/ppermute | solution.py:251
  146.1 0.9 collective-permute-done.20
  147.3 13.6 %collective-permute-done.23 = bf16[192,1792]{1,0:T(8,128)(2,1)S(1)} collective-permute-done((bf16[192,1792]{1,0:T(8,128)(2,1)S(1)}, bf16[192,1792]{1,0:T(8,128)(2,1)S(1)}, u32[]{:S(2)}, u32[]{:S(2)}) %collective-permute-start.23) | collective-permute-done | bytes 688160 | tf_op jit(solution)/shard_map/ppermute | solution.py:251
  160.9 0.0 collective-permute-start.10
  160.9 0.9 collective-permute-done.24
  161.8 5.2 %collective-permute-done.29 = bf16[96,1792]{1,0:T(8,128)(2,1)S(1)} collective-permute-done((bf16[96,1792]{1,0:T(8,128)(2,1)S(1)}, bf16[96,1792]{1,0:T(8,128)(2,1)S(1)}, u32[]{:S(2)}, u32[]{:S(2)}) %collective-permute-start.29) | collective-permute-done | bytes 344096 | tf_op jit(solution)/shard_map/ppermute | solution.py:251
  167.1 0.8 collective-permute-start.21
  167.9 1.3 collective-permute-start.22
  169.4 4.5 %convolution_convert_fusion = bf16[1792,1024]{1,0:T(8,128)(2,1)} fusion(bf16[768,1792]{1,0:T(8,128)(2,1)S(1)} %constant_dynamic-update-slice_fusion.14, bf16[768,1024]{1,0:T(8,128)(2,1)S(1)} %bitcast.50), kind=kOutput, calls=%fused_computation | convolution fusion | flops 2820407296 | bytes 7995392 | tf_op jit(solution)/shard_map/dot_general | solution.py:230
  174.1 1.9 collective-permute-done.21
  176.0 0.8 collective-permute-start.25
  176.8 1.2 collective-permute-start.26
  178.1 4.6 %convolution_convert_fusion.2 = bf16[1024,1792]{1,0:T(8,128)(2,1)} fusion(bf16[768,1024]{1,0:T(8,128)(2,1)S(1)} %bitcast.48, bf16[768,1792]{1,0:T(8,128)(2,1)S(1)} %constant_dynamic-update-slice_fusion.4), kind=kOutput, calls=%fused_computation.2 | convolution fusion | flops 2820407296 | bytes 7995392 | tf_op jit(solution)/shard_map/dot_general | solution.py:230
  182.7 1.3 collective-permute-done.25
  184.0 0.6 collective-permute-done.26
  184.7 4.6 %convolution_convert_fusion.1 = bf16[1024,1792]{1,0:T(8,128)(2,1)} fusion(bf16[768,1024]{1,0:T(8,128)(2,1)S(1)} %bitcast.49, bf16[768,1792]{1,0:T(8,128)(2,1)S(1)} %constant_dynamic-update-slice_fusion.9), kind=kOutput, calls=%fused_computation.1 | convolution fusion | flops 2820407296 | bytes 7995392 | tf_op jit(solution)/shard_map/dot_general | solution.py:230
  189.3 0.2 fusion.3
  189.5 0.8 slice_bitcast_fusion.4
  (50 shorter events, 0.8 us)
Async XLA Ops:
  0.6 22.9 %copy-start.1 = (bf16[24,4096]{1,0:T(8,128)(2,1)S(1)}, bf16[24,4096]{1,0:T(8,128)(2,1)}, u32[]{:S(2)}) copy-start(bf16[24,4096]{1,0:T(8,128)(2,1)} %param.11) | copy-start | bytes 589828
  0.6 54.3 %collective-permute-start = (bf16[24,4096]{1,0:T(8,128)(2,1)}, bf16[24,4096]{1,0:T(8,128)(2,1)S(1)}, u32[]{:S(2)}, u32[]{:S(2)}) collective-permute-start(bf16[24,4096]{1,0:T(8,128)(2,1)} %param.11), channel_id=1, source_target_pairs={{0,8},{4,12},{8,16},{12,20},{16,24},{20,28},{24,0},{28,4},{1,9},{5... | collective-permute-start | bytes 589832 | tf_op jit(solution)/shard_map/ppermute | solution.py:243
  3.7 51.3 %collective-permute-start.1 = (bf16[24,4096]{1,0:T(8,128)(2,1)}, bf16[24,4096]{1,0:T(8,128)(2,1)S(1)}, u32[]{:S(2)}, u32[]{:S(2)}) collective-permute-start(bf16[24,4096]{1,0:T(8,128)(2,1)} %param.11), channel_id=1, source_target_pairs={{0,16},{4,20},{8,24},{12,28},{16,0},{20,4},{24,8},{28,12},{1,17},{... | collective-permute-start | bytes 589832 | tf_op jit(solution)/shard_map/ppermute | solution.py:243
  8.3 46.5 %copy-start = (bf16[24,4096]{1,0:T(8,128)(2,1)S(1)}, bf16[24,4096]{1,0:T(8,128)(2,1)}, u32[]{:S(2)}) copy-start(bf16[24,4096]{1,0:T(8,128)(2,1)} %pick.1) | copy-start | bytes 589828
  10.2 5.7 %collective-permute-start.14 = (bf16[24,2048]{1,0:T(8,128)(2,1)S(1)}, bf16[24,2048]{1,0:T(8,128)(2,1)S(1)}, u32[]{:S(2)}, u32[]{:S(2)}) collective-permute-start(bf16[24,2048]{1,0:T(8,128)(2,1)S(1)} %pad_maximum_fusion.6), channel_id=1, source_target_pairs={{0,3},{1,2},{2,1},{3,0},{4,7},{5,6},{6,5},{7,4},{8,11},{9,10},{10,... | collective-permute-start | bytes 294920 | tf_op jit(solution)/shard_map/ppermute | solution.py:251
  12.7 4.8 %collective-permute-start.13 = (bf16[24,2048]{1,0:T(8,128)(2,1)S(1)}, bf16[24,2048]{1,0:T(8,128)(2,1)S(1)}, u32[]{:S(2)}, u32[]{:S(2)}) collective-permute-start(bf16[24,2048]{1,0:T(8,128)(2,1)S(1)} %pad_maximum_fusion.5), channel_id=1, source_target_pairs={{0,2},{1,3},{2,0},{3,1},{4,6},{5,7},{6,4},{7,5},{8,10},{9,11},{10,... | collective-permute-start | bytes 294920 | tf_op jit(solution)/shard_map/ppermute | solution.py:251
  13.3 4.7 %collective-permute-start.12 = (bf16[24,2048]{1,0:T(8,128)(2,1)S(1)}, bf16[24,2048]{1,0:T(8,128)(2,1)S(1)}, u32[]{:S(2)}, u32[]{:S(2)}) collective-permute-start(bf16[24,2048]{1,0:T(8,128)(2,1)S(1)} %pad_maximum_fusion.4), channel_id=1, source_target_pairs={{0,1},{1,0},{2,3},{3,2},{4,5},{5,4},{6,7},{7,6},{8,9},{9,8},{10,11... | collective-permute-start | bytes 294920 | tf_op jit(solution)/shard_map/ppermute | solution.py:251
  15.9 7.6 %collective-permute-start.6 = (bf16[24,4096]{1,0:T(8,128)(2,1)}, bf16[24,4096]{1,0:T(8,128)(2,1)S(1)}, u32[]{:S(2)}, u32[]{:S(2)}) collective-permute-start(bf16[24,4096]{1,0:T(8,128)(2,1)} %pick.1), channel_id=1, source_target_pairs={{0,24},{4,28},{8,0},{12,4},{16,8},{20,12},{24,16},{28,20},{1,25},{... | collective-permute-start | bytes 589832 | tf_op jit(solution)/shard_map/ppermute | solution.py:243
  17.5 18.9 %collective-permute-start.5 = (bf16[24,4096]{1,0:T(8,128)(2,1)}, bf16[24,4096]{1,0:T(8,128)(2,1)S(1)}, u32[]{:S(2)}, u32[]{:S(2)}) collective-permute-start(bf16[24,4096]{1,0:T(8,128)(2,1)} %pick.1), channel_id=1, source_target_pairs={{0,16},{4,20},{8,24},{12,28},{16,0},{20,4},{24,8},{28,12},{1,17},{... | collective-permute-start | bytes 589832 | tf_op jit(solution)/shard_map/ppermute | solution.py:243
  17.9 20.9 %collective-permute-start.4 = (bf16[24,4096]{1,0:T(8,128)(2,1)}, bf16[24,4096]{1,0:T(8,128)(2,1)S(1)}, u32[]{:S(2)}, u32[]{:S(2)}) collective-permute-start(bf16[24,4096]{1,0:T(8,128)(2,1)} %pick.1), channel_id=1, source_target_pairs={{0,8},{4,12},{8,16},{12,20},{16,24},{20,28},{24,0},{28,4},{1,9},{5... | collective-permute-start | bytes 589832 | tf_op jit(solution)/shard_map/ppermute | solution.py:243
  23.5 31.6 %collective-permute-start.2 = (bf16[24,4096]{1,0:T(8,128)(2,1)S(1)}, bf16[24,4096]{1,0:T(8,128)(2,1)S(1)}, u32[]{:S(2)}, u32[]{:S(2)}) collective-permute-start(bf16[24,4096]{1,0:T(8,128)(2,1)S(1)} %copy-done.1), channel_id=1, source_target_pairs={{0,24},{4,28},{8,0},{12,4},{16,8},{20,12},{24,16},{28,20},{1,25},{... | collective-permute-start | bytes 589832 | tf_op jit(solution)/shard_map/ppermute | solution.py:243
  36.4 19.3 %collective-permute-start.17 = (bf16[4,24,2048]{2,1,0:T(8,128)(2,1)S(1)}, bf16[4,24,2048]{2,1,0:T(8,128)(2,1)S(1)}, u32[]{:S(2)}, u32[]{:S(2)}) collective-permute-start(bf16[4,24,2048]{2,1,0:T(8,128)(2,1)S(1)} %get-tuple-element.61), channel_id=1, source_target_pairs={{0,24},{4,28},{8,0},{12,4},{16,8},{20,12},{24,16},{28,20},{1,25},{... | collective-permute-start | bytes 1179656 | tf_op jit(solution)/shard_map/ppermute | solution.py:243
  38.9 35.3 %collective-permute-start.16 = (bf16[4,24,2048]{2,1,0:T(8,128)(2,1)S(1)}, bf16[4,24,2048]{2,1,0:T(8,128)(2,1)S(1)}, u32[]{:S(2)}, u32[]{:S(2)}) collective-permute-start(bf16[4,24,2048]{2,1,0:T(8,128)(2,1)S(1)} %get-tuple-element.61), channel_id=1, source_target_pairs={{0,16},{4,20},{8,24},{12,28},{16,0},{20,4},{24,8},{28,12},{1,17},{... | collective-permute-start | bytes 1179656 | tf_op jit(solution)/shard_map/ppermute | solution.py:243
  54.9 19.3 %collective-permute-start.15 = (bf16[4,24,2048]{2,1,0:T(8,128)(2,1)S(1)}, bf16[4,24,2048]{2,1,0:T(8,128)(2,1)S(1)}, u32[]{:S(2)}, u32[]{:S(2)}) collective-permute-start(bf16[4,24,2048]{2,1,0:T(8,128)(2,1)S(1)} %get-tuple-element.61), channel_id=1, source_target_pairs={{0,8},{4,12},{8,16},{12,20},{16,24},{20,28},{24,0},{28,4},{1,9},{5... | collective-permute-start | bytes 1179656 | tf_op jit(solution)/shard_map/ppermute | solution.py:243
  55.0 19.5 %collective-permute-start.7 = (bf16[96,4096]{1,0:T(8,128)(2,1)S(1)}, bf16[96,4096]{1,0:T(8,128)(2,1)S(1)}, u32[]{:S(2)}, u32[]{:S(2)}) collective-permute-start(bf16[96,4096]{1,0:T(8,128)(2,1)S(1)} %pad_maximum_fusion.2.refs_0_), channel_id=1, source_target_pairs={{0,4},{4,0},{8,12},{12,8},{16,20},{20,16},{24,28},{28,24},{1,5},{5... | collective-permute-start | bytes 2359304 | tf_op jit(solution)/shard_map/ppermute | solution.py:247
  55.1 30.2 %collective-permute-start.3 = (bf16[96,4096]{1,0:T(8,128)(2,1)S(1)}, bf16[96,4096]{1,0:T(8,128)(2,1)S(1)}, u32[]{:S(2)}, u32[]{:S(2)}) collective-permute-start(bf16[96,4096]{1,0:T(8,128)(2,1)S(1)} %constant_dynamic-update-slice_fusion.refs_0_), channel_id=1, source_target_pairs={{0,4},{4,0},{8,12},{12,8},{16,20},{20,16},{24,28},{28,24},{1,5},{5... | collective-permute-start | bytes 2359304 | tf_op jit(solution)/shard_map/ppermute | solution.py:247
  74.4 57.8 %collective-permute-start.18 = (bf16[4,4,24,2048]{3,2,0,1:T(8,128)(2,1)S(1)}, bf16[4,4,24,2048]{3,2,0,1:T(8,128)(2,1)S(1)}, u32[]{:S(2)}, u32[]{:S(2)}) collective-permute-start(bf16[4,4,24,2048]{3,2,0,1:T(8,128)(2,1)S(1)} %get-tuple-element.53), channel_id=1, source_target_pairs={{0,4},{4,0},{8,12},{12,8},{16,20},{20,16},{24,28},{28,24},{1,5},{5... | collective-permute-start | bytes 4718600 | tf_op jit(solution)/shard_map/ppermute | solution.py:247
  110.3 23.9 %collective-permute-start.8 = (bf16[2,96,4096]{2,1,0:T(8,128)(2,1)S(1)}, bf16[2,96,4096]{2,1,0:T(8,128)(2,1)S(1)}, u32[]{:S(2)}, u32[]{:S(2)}) collective-permute-start(bf16[2,96,4096]{2,1,0:T(8,128)(2,1)S(1)} %get-tuple-element.36), channel_id=1, source_target_pairs={{0,4},{4,0},{8,12},{12,8},{16,20},{20,16},{24,28},{28,24},{1,5},{5... | collective-permute-start | bytes 4718600 | tf_op jit(solution)/shard_map/ppermute | solution.py:247
  110.9 17.9 %collective-permute-start.28 = (bf16[192,1792]{1,0:T(8,128)(2,1)S(1)}, bf16[192,1792]{1,0:T(8,128)(2,1)S(1)}, u32[]{:S(2)}, u32[]{:S(2)}) collective-permute-start(bf16[192,1792]{1,0:T(8,128)(2,1)S(1)} %get-tuple-element.46.refs_3_), channel_id=1, source_target_pairs={{0,2},{1,3},{2,0},{3,1},{4,6},{5,7},{6,4},{7,5},{8,10},{9,11},{10,... | collective-permute-start | bytes 2064392 | tf_op jit(solution)/shard_map/ppermute | solution.py:251
  113.1 18.3 %collective-permute-start.27 = (bf16[192,1792]{1,0:T(8,128)(2,1)S(1)}, bf16[192,1792]{1,0:T(8,128)(2,1)S(1)}, u32[]{:S(2)}, u32[]{:S(2)}) collective-permute-start(bf16[192,1792]{1,0:T(8,128)(2,1)S(1)} %get-tuple-element.46.refs_3_), channel_id=1, source_target_pairs={{0,1},{1,0},{2,3},{3,2},{4,5},{5,4},{6,7},{7,6},{8,9},{9,8},{10,11... | collective-permute-start | bytes 2064392 | tf_op jit(solution)/shard_map/ppermute | solution.py:251
  113.9 32.2 %collective-permute-start.19 = (bf16[192,1792]{1,0:T(8,128)(2,1)S(1)}, bf16[192,1792]{1,0:T(8,128)(2,1)S(1)}, u32[]{:S(2)}, u32[]{:S(2)}) collective-permute-start(bf16[192,1792]{1,0:T(8,128)(2,1)S(1)} %get-tuple-element.37.refs_0_), channel_id=1, source_target_pairs={{0,1},{1,0},{2,3},{3,2},{4,5},{5,4},{6,7},{7,6},{8,9},{9,8},{10,11... | collective-permute-start | bytes 2064392 | tf_op jit(solution)/shard_map/ppermute | solution.py:251
  128.7 18.3 %collective-permute-start.20 = (bf16[192,1792]{1,0:T(8,128)(2,1)S(1)}, bf16[192,1792]{1,0:T(8,128)(2,1)S(1)}, u32[]{:S(2)}, u32[]{:S(2)}) collective-permute-start(bf16[192,1792]{1,0:T(8,128)(2,1)S(1)} %get-tuple-element.37.refs_0_), channel_id=1, source_target_pairs={{0,2},{1,3},{2,0},{3,1},{4,6},{5,7},{6,4},{7,5},{8,10},{9,11},{10,... | collective-permute-start | bytes 2064392 | tf_op jit(solution)/shard_map/ppermute | solution.py:251
  131.4 29.5 %collective-permute-start.23 = (bf16[192,1792]{1,0:T(8,128)(2,1)S(1)}, bf16[192,1792]{1,0:T(8,128)(2,1)S(1)}, u32[]{:S(2)}, u32[]{:S(2)}) collective-permute-start(bf16[192,1792]{1,0:T(8,128)(2,1)S(1)} %get-tuple-element.43.refs_1_), channel_id=1, source_target_pairs={{0,1},{1,0},{2,3},{3,2},{4,5},{5,4},{6,7},{7,6},{8,9},{9,8},{10,11... | collective-permute-start | bytes 2064392 | tf_op jit(solution)/shard_map/ppermute | solution.py:251
  132.2 29.6 %collective-permute-start.24 = (bf16[192,1792]{1,0:T(8,128)(2,1)S(1)}, bf16[192,1792]{1,0:T(8,128)(2,1)S(1)}, u32[]{:S(2)}, u32[]{:S(2)}) collective-permute-start(bf16[192,1792]{1,0:T(8,128)(2,1)S(1)} %get-tuple-element.43.refs_1_), channel_id=1, source_target_pairs={{0,2},{1,3},{2,0},{3,1},{4,6},{5,7},{6,4},{7,5},{8,10},{9,11},{10,... | collective-permute-start | bytes 2064392 | tf_op jit(solution)/shard_map/ppermute | solution.py:251
  134.2 32.9 %collective-permute-start.29 = (bf16[96,1792]{1,0:T(8,128)(2,1)S(1)}, bf16[96,1792]{1,0:T(8,128)(2,1)S(1)}, u32[]{:S(2)}, u32[]{:S(2)}) collective-permute-start(bf16[96,1792]{1,0:T(8,128)(2,1)S(1)} %slice.64), channel_id=1, source_target_pairs={{0,1},{1,0},{2,3},{3,2},{4,5},{5,4},{6,7},{7,6},{8,9},{9,8},{10,11... | collective-permute-start | bytes 1032200 | tf_op jit(solution)/shard_map/ppermute | solution.py:251
  146.1 21.8 %collective-permute-start.30 = (bf16[96,1792]{1,0:T(8,128)(2,1)S(1)}, bf16[96,1792]{1,0:T(8,128)(2,1)S(1)}, u32[]{:S(2)}, u32[]{:S(2)}) collective-permute-start(bf16[96,1792]{1,0:T(8,128)(2,1)S(1)} %slice.65), channel_id=1, source_target_pairs={{0,2},{1,3},{2,0},{3,1},{4,6},{5,7},{6,4},{7,5},{8,10},{9,11},{10,... | collective-permute-start | bytes 1032200 | tf_op jit(solution)/shard_map/ppermute | solution.py:251
  147.0 42.2 %collective-permute-start.9 = (bf16[2,24,4096]{2,1,0:T(8,128)(2,1)S(1)}, bf16[2,24,4096]{2,1,0:T(8,128)(2,1)S(1)}, u32[]{:S(2)}, u32[]{:S(2)}) collective-permute-start(bf16[2,24,4096]{2,1,0:T(8,128)(2,1)S(1)} %get-tuple-element.57), channel_id=1, source_target_pairs={{0,24},{4,28},{8,0},{12,4},{16,8},{20,12},{24,16},{28,20},{1,25},{... | collective-permute-start | bytes 1179656 | tf_op jit(solution)/shard_map/ppermute | solution.py:243
  160.9 28.4 %collective-permute-start.10 = (bf16[2,24,4096]{2,1,0:T(8,128)(2,1)S(1)}, bf16[2,24,4096]{2,1,0:T(8,128)(2,1)S(1)}, u32[]{:S(2)}, u32[]{:S(2)}) collective-permute-start(bf16[2,24,4096]{2,1,0:T(8,128)(2,1)S(1)} %get-tuple-element.56), channel_id=1, source_target_pairs={{0,16},{4,20},{8,24},{12,28},{16,0},{20,4},{24,8},{28,12},{1,17},{... | collective-permute-start | bytes 1179656 | tf_op jit(solution)/shard_map/ppermute | solution.py:243
  161.8 27.5 %collective-permute-start.11 = (bf16[2,24,4096]{2,1,0:T(8,128)(2,1)S(1)}, bf16[2,24,4096]{2,1,0:T(8,128)(2,1)S(1)}, u32[]{:S(2)}, u32[]{:S(2)}) collective-permute-start(bf16[2,24,4096]{2,1,0:T(8,128)(2,1)S(1)} %get-tuple-element.55), channel_id=1, source_target_pairs={{0,8},{4,12},{8,16},{12,20},{16,24},{20,28},{24,0},{28,4},{1,9},{5... | collective-permute-start | bytes 1179656 | tf_op jit(solution)/shard_map/ppermute | solution.py:243
  167.1 8.9 %collective-permute-start.21 = (bf16[96,1792]{1,0:T(8,128)(2,1)S(1)}, bf16[96,1792]{1,0:T(8,128)(2,1)S(1)}, u32[]{:S(2)}, u32[]{:S(2)}) collective-permute-start(bf16[96,1792]{1,0:T(8,128)(2,1)S(1)} %slice.47), channel_id=1, source_target_pairs={{0,1},{1,0},{2,3},{3,2},{4,5},{5,4},{6,7},{7,6},{8,9},{9,8},{10,11... | collective-permute-start | bytes 1032200 | tf_op jit(solution)/shard_map/ppermute | solution.py:251
  167.9 8.9 %collective-permute-start.22 = (bf16[96,1792]{1,0:T(8,128)(2,1)S(1)}, bf16[96,1792]{1,0:T(8,128)(2,1)S(1)}, u32[]{:S(2)}, u32[]{:S(2)}) collective-permute-start(bf16[96,1792]{1,0:T(8,128)(2,1)S(1)} %slice.48), channel_id=1, source_target_pairs={{0,2},{1,3},{2,0},{3,1},{4,6},{5,7},{6,4},{7,5},{8,10},{9,11},{10,... | collective-permute-start | bytes 1032200 | tf_op jit(solution)/shard_map/ppermute | solution.py:251
  176.0 8.1 %collective-permute-start.25 = (bf16[96,1792]{1,0:T(8,128)(2,1)S(1)}, bf16[96,1792]{1,0:T(8,128)(2,1)S(1)}, u32[]{:S(2)}, u32[]{:S(2)}) collective-permute-start(bf16[96,1792]{1,0:T(8,128)(2,1)S(1)} %slice.51), channel_id=1, source_target_pairs={{0,1},{1,0},{2,3},{3,2},{4,5},{5,4},{6,7},{7,6},{8,9},{9,8},{10,11... | collective-permute-start | bytes 1032200 | tf_op jit(solution)/shard_map/ppermute | solution.py:251
  176.8 7.8 %collective-permute-start.26 = (bf16[96,1792]{1,0:T(8,128)(2,1)S(1)}, bf16[96,1792]{1,0:T(8,128)(2,1)S(1)}, u32[]{:S(2)}, u32[]{:S(2)}) collective-permute-start(bf16[96,1792]{1,0:T(8,128)(2,1)S(1)} %slice.52), channel_id=1, source_target_pairs={{0,2},{1,3},{2,0},{3,1},{4,6},{5,7},{6,4},{7,5},{8,10},{9,11},{10,... | collective-permute-start | bytes 1032200 | tf_op jit(solution)/shard_map/ppermute | solution.py:251

commit v4 on v3

--- a/solution.py
+++ b/solution.py
@@ -12,7 +12,7 @@
 MIB = 1 << 20
 
 
-ANY = pl.BlockSpec(memory_space=pl.ANY)
+HBM = pl.BlockSpec(memory_space=pltpu.HBM)
 VMEM = pl.BlockSpec(memory_space=pltpu.VMEM)
 
 
@@ -62,168 +62,172 @@
     return pl.pallas_call(
         pick_kernel,
         out_shape=shape((rows, tokens.shape[1])),
+        compiler_params=grant(),
         name="pick",
     )(modality.reshape(1, -1), tokens)
+
+
+def streamed(steps, depth, copies, body):
+    depth = min(depth, steps)
+
+    def start(j):
+        for copy in copies(j, lax.rem(j, depth)):
+            copy.start()
+
+    for j in range(depth):
+        start(jnp.int32(j))
+
+    @pl.loop(0, steps)
+    def _(j):
+        slot = lax.rem(j, depth)
+        for copy in copies(j, slot):
+            copy.wait()
+        body(j, slot)
+
+        @pl.when(j + depth < steps)
+        def _():
+            start(j + depth)
+
+
+DEPTH = 4
 
 
 def enter_kernel(tile, xa_ref, xb_ref, gate_hbm, up_hbm, hid_ref, active_ref, turn_ref,
                  x_ref, gate_ref, up_ref, sems):
     half = xa_ref.shape[0]
-    tiles = gate_ref.shape[0]
-
-    def copies(j):
+    x_ref[:half] = xa_ref[...]
+    x_ref[half:] = xb_ref[...]
+
+    def copies(j, slot):
         column = pl.ds(pl.multiple_of(j * tile, tile), tile)
         return (
-            pltpu.make_async_copy(gate_hbm.at[:, column], gate_ref.at[j], sems.at[0, j]),
-            pltpu.make_async_copy(up_hbm.at[:, column], up_ref.at[j], sems.at[1, j]),
+            pltpu.make_async_copy(gate_hbm.at[:, column], gate_ref.at[slot], sems.at[0, slot]),
+            pltpu.make_async_copy(up_hbm.at[:, column], up_ref.at[slot], sems.at[1, slot]),
         )
 
-    for j in range(tiles):
-        for copy in copies(j):
-            copy.start()
-    x_ref[:half] = xa_ref[...]
-    x_ref[half:] = xb_ref[...]
-
-    @pl.loop(0, tiles)
-    def _(j):
+    def body(j, slot):
         column = pl.ds(pl.multiple_of(j * tile, tile), tile)
-        for copy in copies(j):
-            copy.wait()
-        gate_proj = nn_dot(x_ref[...], gate_ref[j])
-        up_proj = nn_dot(x_ref[...], up_ref[j])
+        gate_proj = nn_dot(x_ref[...], gate_ref[slot])
+        up_proj = nn_dot(x_ref[...], up_ref[slot])
         sig = jax.nn.sigmoid(gate_proj)
         active = gate_proj * sig
         hid_ref[:, column] = (active * up_proj).astype(BF)
         active_ref[:, column] = active
         turn_ref[:, column] = up_proj * (sig * (1.0 + gate_proj * (1.0 - sig)))
 
+    streamed(gate_hbm.shape[1] // tile, gate_ref.shape[0], copies, body)
+
 
 def enter(own, other, gate, up):
     half, width = own.shape
     units = gate.shape[1]
     rows = 2 * half
     tile = tile_of(units, (256, 128))
-    tiles = units // tile
+    depth = min(DEPTH, units // tile)
     return pl.pallas_call(
         lambda *refs: enter_kernel(tile, *refs),
-        in_specs=[VMEM, VMEM, ANY, ANY],
+        in_specs=[VMEM, VMEM, HBM, HBM],
         out_specs=[VMEM] * 3,
         out_shape=[shape((rows, units)), shape((rows, units), F32), shape((rows, units), F32)],
         scratch_shapes=[
             pltpu.VMEM((rows, width), BF),
-            pltpu.VMEM((tiles, width, tile), BF),
-            pltpu.VMEM((tiles, width, tile), BF),
-            pltpu.SemaphoreType.DMA((2, tiles)),
+            pltpu.VMEM((depth, width, tile), BF),
+            pltpu.VMEM((depth, width, tile), BF),
+            pltpu.SemaphoreType.DMA((2, depth)),
         ],
-        compiler_params=grant((2 * width, units, BF), (2 * rows, width, BF),
-                              (rows, units, BF), (2 * rows, units, F32)),
+        compiler_params=grant((rows, width, BF), (2 * depth * tile, width, BF)),
         cost_estimate=cost(4 * rows * width * units, 4 * width * units),
         name="enter",
     )(own, other, gate, up)
 
 
-def turn_kernel(tile, step, ca_ref, cb_ref, down_hbm, hid_ref, active_ref, factor_ref,
-                gb_ref, ub_ref, own_ref, other_ref, c_ref, down_ref, sems):
+def turn_kernel(tile, ca_ref, cb_ref, down_hbm, active_ref, factor_ref, gb_ref, ub_ref,
+                c_ref, down_ref, sems):
     half = ca_ref.shape[0]
-    units, width = down_ref.shape
-    tiles = units // tile
-
-    def copy(j):
-        row = pl.ds(pl.multiple_of(j * tile, tile), tile)
-        return pltpu.make_async_copy(down_hbm.at[row, :], down_ref.at[row, :], sems.at[j])
-
-    for j in range(tiles):
-        copy(j).start()
     c_ref[:half] = ca_ref[...]
     c_ref[half:] = cb_ref[...]
 
-    @pl.loop(0, tiles)
-    def _(j):
+    def copies(j, slot):
+        row = pl.ds(pl.multiple_of(j * tile, tile), tile)
+        return (pltpu.make_async_copy(down_hbm.at[row, :], down_ref.at[slot], sems.at[slot]),)
+
+    def body(j, slot):
         span = pl.ds(pl.multiple_of(j * tile, tile), tile)
-        copy(j).wait()
-        back = nt_dot(c_ref[...], down_ref[span, :])
+        back = nt_dot(c_ref[...], down_ref[slot])
         gb_ref[:, span] = (back * factor_ref[:, span]).astype(BF)
         ub_ref[:, span] = (back * active_ref[:, span]).astype(BF)
 
-    @pl.loop(0, width // step)
-    def _(j):
-        span = pl.ds(pl.multiple_of(j * step, step), step)
-        result = nn_dot(hid_ref[...], down_ref[:, span]).astype(BF)
-        own_ref[0, :, span] = result[:half]
-        other_ref[0, :, span] = result[half:]
-
-
-def turn(own, other, down, hid, active, factor):
+    streamed(down_hbm.shape[0] // tile, down_ref.shape[0], copies, body)
+
+
+def turn(own, other, down, active, factor):
     half, width = own.shape
     units = down.shape[0]
     rows = 2 * half
     tile = tile_of(units, (256, 128))
-    step = tile_of(width, (512, 256, 128))
+    depth = min(DEPTH, units // tile)
     return pl.pallas_call(
-        lambda *refs: turn_kernel(tile, step, *refs),
-        grid=(1,),
-        in_specs=[VMEM, VMEM, ANY, VMEM, VMEM, VMEM],
-        out_specs=[VMEM, VMEM] + [pl.BlockSpec((1, half, width), lambda i: (0, 0, 0))] * 2,
-        out_shape=[shape((rows, units))] * 2 + [shape((2, half, width))] * 2,
+        lambda *refs: turn_kernel(tile, *refs),
+        in_specs=[VMEM, VMEM, HBM, VMEM, VMEM],
+        out_specs=[VMEM] * 2,
+        out_shape=[shape((rows, units))] * 2,
         scratch_shapes=[
             pltpu.VMEM((rows, width), BF),
-            pltpu.VMEM((units, width), BF),
-            pltpu.SemaphoreType.DMA((units // tile,)),
+            pltpu.VMEM((depth, tile, width), BF),
+            pltpu.SemaphoreType.DMA((depth,)),
         ],
-        compiler_params=grant((width, units, BF), (4 * rows, width, BF),
-                              (4 * rows, units, BF), (2 * rows, units, F32)),
-        cost_estimate=cost(4 * rows * width * units, 2 * width * units),
+        compiler_params=grant((rows, width, BF), (depth * tile, width, BF)),
+        cost_estimate=cost(2 * rows * width * units, 2 * width * units),
         name="turn",
-    )(own, other, down, hid, active, factor)
-
-
-def leave_kernel(step, gb_ref, ub_ref, gate_hbm, up_hbm, own_in, other_in, own_ref, other_ref,
-                 gate_ref, up_ref, sems):
+    )(own, other, down, active, factor)
+
+
+def leave_kernel(step, hid_ref, gb_ref, ub_ref, gate_hbm, up_hbm, down_hbm, own_ref, other_ref,
+                 gate_ref, up_ref, down_ref, sems):
     half = own_ref.shape[1]
-    steps = gate_ref.shape[0] // step
-
-    def copies(j):
-        row = pl.ds(pl.multiple_of(j * step, step), step)
+
+    def copies(j, slot):
+        span = pl.ds(pl.multiple_of(j * step, step), step)
         return (
-            pltpu.make_async_copy(gate_hbm.at[row, :], gate_ref.at[row, :], sems.at[0, j]),
-            pltpu.make_async_copy(up_hbm.at[row, :], up_ref.at[row, :], sems.at[1, j]),
+            pltpu.make_async_copy(down_hbm.at[:, span], down_ref.at[slot], sems.at[0, slot]),
+            pltpu.make_async_copy(gate_hbm.at[span, :], gate_ref.at[slot], sems.at[1, slot]),
+            pltpu.make_async_copy(up_hbm.at[span, :], up_ref.at[slot], sems.at[2, slot]),
         )
 
-    for j in range(steps):
-        for copy in copies(j):
-            copy.start()
-
-    @pl.loop(0, steps)
-    def _(j):
+    def body(j, slot):
         span = pl.ds(pl.multiple_of(j * step, step), step)
-        for copy in copies(j):
-            copy.wait()
-        result = nt_dot(gb_ref[...], gate_ref[span, :]) + nt_dot(ub_ref[...], up_ref[span, :])
-        result = result.astype(BF)
+        result = nn_dot(hid_ref[...], down_ref[slot]).astype(BF)
         own_ref[0, :, span] = result[:half]
         other_ref[0, :, span] = result[half:]
-
-
-def leave(gb, ub, gate, up, own, other):
+        result = nt_dot(gb_ref[...], gate_ref[slot]) + nt_dot(ub_ref[...], up_ref[slot])
+        result = result.astype(BF)
+        own_ref[1, :, span] = result[:half]
+        other_ref[1, :, span] = result[half:]
+
+    streamed(gate_hbm.shape[0] // step, gate_ref.shape[0], copies, body)
+
+
+def leave(hid, gb, ub, gate, up, down):
     rows, units = gb.shape
-    half, width = own.shape[1:]
+    width = gate.shape[0]
+    half = rows // 2
     step = tile_of(width, (512, 256, 128))
+    depth = min(DEPTH, width // step)
     return pl.pallas_call(
         lambda *refs: leave_kernel(step, *refs),
-        grid=(1,),
-        in_specs=[VMEM, VMEM, ANY, ANY, ANY, ANY],
-        out_specs=[pl.BlockSpec((1, half, width), lambda i: (1, 0, 0))] * 2,
+        in_specs=[VMEM] * 3 + [HBM] * 3,
+        out_specs=[VMEM] * 2,
         out_shape=[shape((2, half, width))] * 2,
         scratch_shapes=[
-            pltpu.VMEM((width, units), BF),
-            pltpu.VMEM((width, units), BF),
-            pltpu.SemaphoreType.DMA((2, width // step)),
+            pltpu.VMEM((depth, step, units), BF),
+            pltpu.VMEM((depth, step, units), BF),
+            pltpu.VMEM((depth, units, step), BF),
+            pltpu.SemaphoreType.DMA((3, depth)),
         ],
-        input_output_aliases={4: 0, 5: 1},
-        compiler_params=grant((2 * width, units, BF), (2 * rows, width, BF), (2 * rows, units, BF)),
-        cost_estimate=cost(4 * rows * width * units, 4 * width * units),
+        compiler_params=grant((3 * depth * step, units, BF)),
+        cost_estimate=cost(6 * rows * width * units, 6 * width * units),
         name="leave",
-    )(gb, ub, gate, up, own, other)
+    )(hid, gb, ub, gate, up, down)
 
 
 def rows_dot(left, right):
@@ -302,10 +306,10 @@
     cot_mate = swap(cot)
     hid, active, factor = enter(tok, tok_mate, gate, up)
     all_hid = relay(near(hid))
-    gb, ub, own, other = turn(cot, cot_mate, down, hid, active, factor)
+    gb, ub = turn(cot, cot_mate, down, active, factor)
     all_gb = near(gb)
     all_ub = near(ub)
-    own, other = leave(gb, ub, gate, up, own, other)
+    own, other = leave(hid, gb, ub, gate, up, down)
 
     mate = swap(other)
     sums = (own.astype(F32) + mate.astype(F32)).astype(BF).reshape(2, ring, count, width)
@@ -318,7 +322,7 @@
     down_grad = rows_dot(stack(all_hid), cot_all)
     gate_grad = rows_dot(tok_all, stack(all_gb))
     up_grad = rows_dot(tok_all, stack(all_ub))
-    terms = after(terms, [gate_grad])
+    terms = after(terms, [up_grad])
     total = sums[0].astype(F32)
     for term in terms:
         total = total + term.astype(F32)

time: 190 us -> 200 us (1.053)
  local copies, waits for them, and re-layouts: 4.69 us -> 15.7 us
  starting transfers between devices: 48.2 us -> 58.6 us
  waiting for transfers between devices: 83.5 us -> 74.8 us
  Pallas kernels: 37.7 us -> 33.3 us
    unnamed x19 -> x33, local copies, waits for them, and re-layouts: 1.47 us -> 13.4 us
    ppermute x12, starting transfers between devices: 30.9 us -> 41.3 us  [shift(): lax.ppermute(value, 'dp', [(z * CORES + c, (z + k) % ring * CORES + c) fo...]
    ppermute x15, waiting for transfers between devices: 51.6 us -> 44.3 us  [across(): return lax.ppermute(value, 'seq', [(g, g ^ mask) for g in range(groups)])]
    pallas_call x3, Pallas kernels: 26.9 us -> 23.8 us  [the longest x1 16.3 us: leave(): pl.pallas_call(lambda *refs: leave_kernel(step, *refs), in_specs=[VMEM] *...]
  transfers between devices with their start and end apart: 31 -> 31, of which waited for: 16 -> 13; matrix products, arithmetic and copies ran while one was open for 10% -> 10% of each run, Pallas kernels for 20% -> 17%
where the time goes in v4:
time: 200 us
  waiting for transfers between devices  74.8 us (37%)
  starting transfers between devices  58.6 us (29%)
  Pallas kernels  33.3 us (17%)
  local copies, waits for them, and re-layouts  15.7 us (8%)
  matrix products  13.6 us (7%)
  other arithmetic  2.72 us (1%)
    ppermute x15, waiting for transfers between devices, across(): return lax.ppermute(value, 'seq', [(g, g ^ mask) for g in range(groups)])  44.3 us
    ppermute x12, starting transfers between devices, shift(): lax.ppermute(value, 'dp', [(z * CORES + c, (z + k) % ring * CORES + c) fo...  41.3 us
    ppermute x12, waiting for transfers between devices, shift(): lax.ppermute(value, 'dp', [(z * CORES + c, (z + k) % ring * CORES + c) fo...  30.5 us
    pallas_call x1, Pallas kernels, leave(): pl.pallas_call(lambda *refs: leave_kernel(step, *refs), in_specs=[VMEM] *...  16.3 us
    ppermute x15, starting transfers between devices, across(): return lax.ppermute(value, 'seq', [(g, g ^ mask) for g in range(groups)])  16.1 us
    dot_general x3, matrix products, rows_dot(): lax.dot_general(left, right, (((0,), (0,)), ((), ())), preferred_element_...  13.6 us
    unnamed x33, local copies, waits for them, and re-layouts  13.4 us
    pallas_call x1, Pallas kernels, enter(): pl.pallas_call(lambda *refs: enter_kernel(tile, *refs), in_specs=[VMEM, V...  9.56 us
  transfers between devices with their start and end apart: 31, of which 13 were waited for; matrix products, arithmetic and copies ran while one was open for 10% of the time, Pallas kernels for 17%

profile of v4, /device:TPU:0, one launch (start us, length us, event | category | flops | bytes accessed | tf_op | source)
XLA Modules:
  0.0 199.8 jit_solution(463914366375891543)
XLA Ops:
  0.6 0.9 copy-done.2
  1.6 0.7 copy-done.3
  2.2 0.3 pick.1
  2.6 5.1 %collective-permute-start.2 = (bf16[24,4096]{1,0:T(8,128)(2,1)S(1)}, bf16[24,4096]{1,0:T(8,128)(2,1)S(1)}, u32[]{:S(2)}, u32[]{:S(2)}) collective-permute-start(bf16[24,4096]{1,0:T(8,128)(2,1)S(1)} %pick.1), channel_id=1, source_target_pairs={{0,24},{4,28},{8,0},{12,4},{16,8},{20,12},{24,16},{28,20},{1,25},{... | collective-permute-start | bytes 589832 | tf_op jit(solution)/shard_map/ppermute | solution.py:247
  7.7 0.9 constant_dynamic-slice_fusion.6
  8.6 2.5 %collective-permute-start.14 = (bf16[24,2048]{1,0:T(8,128)(2,1)S(1)}, bf16[24,2048]{1,0:T(8,128)(2,1)S(1)}, u32[]{:S(2)}, u32[]{:S(2)}) collective-permute-start(bf16[24,2048]{1,0:T(8,128)(2,1)S(1)} %pad_maximum_fusion.6), channel_id=1, source_target_pairs={{0,3},{1,2},{2,1},{3,0},{4,7},{5,6},{6,5},{7,4},{8,11},{9,10},{10,... | collective-permute-start | bytes 294920 | tf_op jit(solution)/shard_map/ppermute | solution.py:255
  11.2 0.6 collective-permute-start.13
  11.7 0.6 collective-permute-start.12
  12.3 0.9 constant_dynamic-update-slice_fusion.3
  13.3 1.0 collective-permute-done.14
  14.3 1.1 collective-permute-start
  15.4 0.9 collective-permute-done.13
  16.2 1.6 collective-permute-start.4
  17.9 1.5 collective-permute-start.5
  19.3 0.1 fusion.4
  19.4 2.5 %collective-permute-start.6 = (bf16[24,4096]{1,0:T(8,128)(2,1)S(1)}, bf16[24,4096]{1,0:T(8,128)(2,1)S(1)}, u32[]{:S(2)}, u32[]{:S(2)}) collective-permute-start(bf16[24,4096]{1,0:T(8,128)(2,1)S(1)} %copy-done.4), channel_id=1, source_target_pairs={{0,24},{4,28},{8,0},{12,4},{16,8},{20,12},{24,16},{28,20},{1,25},{... | collective-permute-start | bytes 589832 | tf_op jit(solution)/shard_map/ppermute | solution.py:247
  22.0 11.9 %collective-permute-done.1 = bf16[24,4096]{1,0:T(8,128)(2,1)S(1)} collective-permute-done((bf16[24,4096]{1,0:T(8,128)(2,1)S(1)}, bf16[24,4096]{1,0:T(8,128)(2,1)S(1)}, u32[]{:S(2)}, u32[]{:S(2)}) %collective-permute-start.1) | collective-permute-done | bytes 196640 | tf_op jit(solution)/shard_map/ppermute | solution.py:247
  33.9 0.1 pad_maximum_fusion.2.refs_0_
  33.9 21.8 %collective-permute-start.15 = (bf16[4,24,2048]{2,1,0:T(8,128)(2,1)S(1)}, bf16[4,24,2048]{2,1,0:T(8,128)(2,1)S(1)}, u32[]{:S(2)}, u32[]{:S(2)}) collective-permute-start(bf16[4,24,2048]{2,1,0:T(8,128)(2,1)S(1)} %get-tuple-element.57), channel_id=1, source_target_pairs={{0,8},{4,12},{8,16},{12,20},{16,24},{20,28},{24,0},{28,4},{1,9},{5... | collective-permute-start | bytes 1179656 | tf_op jit(solution)/shard_map/ppermute | solution.py:247
  55.7 0.1 collective-permute-start.3
  55.9 0.6 collective-permute-start.7
  56.4 18.6 %collective-permute-done.16 = bf16[4,24,2048]{2,1,0:T(8,128)(2,1)S(1)} collective-permute-done((bf16[4,24,2048]{2,1,0:T(8,128)(2,1)S(1)}, bf16[4,24,2048]{2,1,0:T(8,128)(2,1)S(1)}, u32[]{:S(2)}, u32[]{:S(2)}) %collective-permute-start.16) | collective-permute-done | bytes 393248 | tf_op jit(solution)/shard_map/ppermute | solution.py:247
  75.0 1.4 pad_maximum_fusion.1
  76.4 5.2 %copy-done = bf16[4096,1792]{1,0:T(8,128)(2,1)S(1)} copy-done((bf16[4096,1792]{1,0:T(8,128)(2,1)S(1)}, bf16[4096,1792]{1,0:T(8,128)(2,1)}, u32[]{:S(2)}) %copy-start) | copy-done | bytes 14680088
  81.6 9.6 %enter.1 = (bf16[192,1792]{1,0:T(8,128)(2,1)S(1)}, f32[192,1792]{1,0:T(8,128)S(1)}, f32[192,1792]{1,0:T(8,128)S(1)}) custom-call(bf16[96,4096]{1,0:T(8,128)(2,1)S(1)} %pad_maximum_fusion.2.refs_0_, bf16[96,4096]{1,0:T(8,128)(2,1)S(1)} %collective-permute-done.3.refs_1_, bf16[4096,1792]{1,0:T(8,128)(2,1)S(1)} %copy-done, bf16[4096,1792]{1,0:T(8,128)(2,1)} %refs_4_.1), custom_call_target="tpu_custom_call" | custom-call | flops 5637144576 | bytes 29360128 | tf_op jit(solution)/shard_map/enter/pallas_call | solution.py:127
  91.2 0.0 copy-start.1
  91.2 5.2 %copy-done.1 = bf16[1792,4096]{1,0:T(8,128)(2,1)S(1)} copy-done((bf16[1792,4096]{1,0:T(8,128)(2,1)S(1)}, bf16[1792,4096]{1,0:T(8,128)(2,1)}, u32[]{:S(2)}) %copy-start.1) | copy-done | bytes 14680088
  96.3 7.1 %turn.1 = (bf16[192,1792]{1,0:T(8,128)(2,1)S(1)}, bf16[192,1792]{1,0:T(8,128)(2,1)S(1)}) custom-call(bf16[96,4096]{1,0:T(8,128)(2,1)S(1)} %constant_dynamic-update-slice_fusion.refs_0_, bf16[96,4096]{1,0:T(8,128)(2,1)S(1)} %collective-permute-done.7.refs_1_, bf16[1792,4096]{1,0:T(8,128)(2,1)S(1)} %copy-done.1, f32[192,1792]{1,0:T(8,128)S(1)} %get-tuple-element.27.refs_3_, ...), custom_call_target="tpu_custom_call" | custom-call | flops 2818572288 | bytes 14680064 | tf_op jit(solution)/shard_map/turn/pallas_call | solution.py:169
  103.5 16.3 %leave.1 = (bf16[2,96,4096]{2,1,0:T(8,128)(2,1)S(1)}, bf16[2,96,4096]{2,1,0:T(8,128)(2,1)S(1)}) custom-call(bf16[192,1792]{1,0:T(8,128)(2,1)S(1)} %get-tuple-element.42.refs_0_, bf16[192,1792]{1,0:T(8,128)(2,1)S(1)} %get-tuple-element.39.refs_1_, bf16[192,1792]{1,0:T(8,128)(2,1)S(1)} %get-tuple-element.33.refs_2_, bf16[4096,1792]{1,0:T(8,128)(2,1)S(1)} %bitcast.47, ...), custom_call_target="tpu_custom_call" | custom-call | flops 8455716864 | bytes 44040192 | tf_op jit(solution)/shard_map/leave/pallas_call | solution.py:216
  119.9 0.6 collective-permute-start.8
  120.4 1.5 collective-permute-start.28
  122.0 1.5 collective-permute-start.27
  123.5 0.5 collective-permute-start.19
  124.0 13.9 %collective-permute-done.28 = bf16[192,1792]{1,0:T(8,128)(2,1)S(1)} collective-permute-done((bf16[192,1792]{1,0:T(8,128)(2,1)S(1)}, bf16[192,1792]{1,0:T(8,128)(2,1)S(1)}, u32[]{:S(2)}, u32[]{:S(2)}) %collective-permute-start.28) | collective-permute-done | bytes 688160 | tf_op jit(solution)/shard_map/ppermute | solution.py:255
  137.9 1.5 collective-permute-start.20
  139.4 0.9 collective-permute-done.27
  140.3 1.5 collective-permute-start.23
  141.8 0.5 collective-permute-start.24
  142.4 0.4 pad_maximum_fusion
  142.8 0.2 copy.19
  143.0 0.2 copy.20
  143.1 0.6 collective-permute-start.29
  143.7 0.5 add_convert_fusion
  144.3 0.1 slice_bitcast_fusion
  144.4 10.6 %collective-permute-done.19 = bf16[192,1792]{1,0:T(8,128)(2,1)S(1)} collective-permute-done((bf16[192,1792]{1,0:T(8,128)(2,1)S(1)}, bf16[192,1792]{1,0:T(8,128)(2,1)S(1)}, u32[]{:S(2)}, u32[]{:S(2)}) %collective-permute-start.19) | collective-permute-done | bytes 688160 | tf_op jit(solution)/shard_map/ppermute | solution.py:255
  155.0 0.5 collective-permute-start.30
  155.5 0.6 collective-permute-done.20
  156.2 3.6 %collective-permute-start.9 = (bf16[2,24,4096]{2,1,0:T(8,128)(2,1)S(1)}, bf16[2,24,4096]{2,1,0:T(8,128)(2,1)S(1)}, u32[]{:S(2)}, u32[]{:S(2)}) collective-permute-start(bf16[2,24,4096]{2,1,0:T(8,128)(2,1)S(1)} %get-tuple-element.53), channel_id=1, source_target_pairs={{0,24},{4,28},{8,0},{12,4},{16,8},{20,12},{24,16},{28,20},{1,25},{... | collective-permute-start | bytes 1179656 | tf_op jit(solution)/shard_map/ppermute | solution.py:247
  160.0 9.8 %collective-permute-done.23 = bf16[192,1792]{1,0:T(8,128)(2,1)S(1)} collective-permute-done((bf16[192,1792]{1,0:T(8,128)(2,1)S(1)}, bf16[192,1792]{1,0:T(8,128)(2,1)S(1)}, u32[]{:S(2)}, u32[]{:S(2)}) %collective-permute-start.23) | collective-permute-done | bytes 688160 | tf_op jit(solution)/shard_map/ppermute | solution.py:255
  169.8 2.8 %collective-permute-start.10 = (bf16[2,24,4096]{2,1,0:T(8,128)(2,1)S(1)}, bf16[2,24,4096]{2,1,0:T(8,128)(2,1)S(1)}, u32[]{:S(2)}, u32[]{:S(2)}) collective-permute-start(bf16[2,24,4096]{2,1,0:T(8,128)(2,1)S(1)} %get-tuple-element.52), channel_id=1, source_target_pairs={{0,16},{4,20},{8,24},{12,28},{16,0},{20,4},{24,8},{28,12},{1,17},{... | collective-permute-start | bytes 1179656 | tf_op jit(solution)/shard_map/ppermute | solution.py:247
  172.6 1.4 collective-permute-start.11
  174.0 2.0 collective-permute-done.29
  176.0 1.5 collective-permute-start.21
  177.5 0.6 collective-permute-start.22
  178.3 4.5 %convolution_convert_fusion = bf16[1792,1024]{1,0:T(8,128)(2,1)} fusion(bf16[768,1792]{1,0:T(8,128)(2,1)S(1)} %constant_dynamic-update-slice_fusion.14, bf16[768,1024]{1,0:T(8,128)(2,1)S(1)} %bitcast.53), kind=kOutput, calls=%fused_computation | convolution fusion | flops 2820407296 | bytes 7995392 | tf_op jit(solution)/shard_map/dot_general | solution.py:234
  183.0 1.9 collective-permute-done.21
  184.9 1.5 collective-permute-start.25
  186.4 0.5 collective-permute-start.26
  187.0 4.5 %convolution_convert_fusion.2 = bf16[1024,1792]{1,0:T(8,128)(2,1)} fusion(bf16[768,1024]{1,0:T(8,128)(2,1)S(1)} %bitcast.51, bf16[768,1792]{1,0:T(8,128)(2,1)S(1)} %constant_dynamic-update-slice_fusion.4), kind=kOutput, calls=%fused_computation.2 | convolution fusion | flops 2820407296 | bytes 7995392 | tf_op jit(solution)/shard_map/dot_general | solution.py:234
  191.5 1.4 collective-permute-done.25
  192.9 1.3 collective-permute-done.26
  194.3 4.5 %convolution_convert_fusion.1 = bf16[1024,1792]{1,0:T(8,128)(2,1)} fusion(bf16[768,1024]{1,0:T(8,128)(2,1)S(1)} %bitcast.52, bf16[768,1792]{1,0:T(8,128)(2,1)S(1)} %constant_dynamic-update-slice_fusion.9), kind=kOutput, calls=%fused_computation.1 | convolution fusion | flops 2820407296 | bytes 7995392 | tf_op jit(solution)/shard_map/dot_general | solution.py:234
  198.9 0.2 fusion.3
  199.1 0.8 slice_bitcast_fusion.4
  (65 shorter events, 0.9 us)
Async XLA Ops:
  0.6 1.0 copy-start.2
  1.6 0.7 copy-start.3
  2.2 17.2 %copy-start.4 = (bf16[24,4096]{1,0:T(8,128)(2,1)S(1)}, bf16[24,4096]{1,0:T(8,128)(2,1)}, u32[]{:S(2)}) copy-start(bf16[24,4096]{1,0:T(8,128)(2,1)} %param.11) | copy-start | bytes 589828
  2.6 16.8 %collective-permute-start.2 = (bf16[24,4096]{1,0:T(8,128)(2,1)S(1)}, bf16[24,4096]{1,0:T(8,128)(2,1)S(1)}, u32[]{:S(2)}, u32[]{:S(2)}) collective-permute-start(bf16[24,4096]{1,0:T(8,128)(2,1)S(1)} %pick.1), channel_id=1, source_target_pairs={{0,24},{4,28},{8,0},{12,4},{16,8},{20,12},{24,16},{28,20},{1,25},{... | collective-permute-start | bytes 589832 | tf_op jit(solution)/shard_map/ppermute | solution.py:247
  7.7 26.2 %collective-permute-start.1 = (bf16[24,4096]{1,0:T(8,128)(2,1)S(1)}, bf16[24,4096]{1,0:T(8,128)(2,1)S(1)}, u32[]{:S(2)}, u32[]{:S(2)}) collective-permute-start(bf16[24,4096]{1,0:T(8,128)(2,1)S(1)} %pick.1), channel_id=1, source_target_pairs={{0,16},{4,20},{8,24},{12,28},{16,0},{20,4},{24,8},{28,12},{1,17},{... | collective-permute-start | bytes 589832 | tf_op jit(solution)/shard_map/ppermute | solution.py:247
  8.6 5.7 %collective-permute-start.14 = (bf16[24,2048]{1,0:T(8,128)(2,1)S(1)}, bf16[24,2048]{1,0:T(8,128)(2,1)S(1)}, u32[]{:S(2)}, u32[]{:S(2)}) collective-permute-start(bf16[24,2048]{1,0:T(8,128)(2,1)S(1)} %pad_maximum_fusion.6), channel_id=1, source_target_pairs={{0,3},{1,2},{2,1},{3,0},{4,7},{5,6},{6,5},{7,4},{8,11},{9,10},{10,... | collective-permute-start | bytes 294920 | tf_op jit(solution)/shard_map/ppermute | solution.py:255
  11.2 5.1 %collective-permute-start.13 = (bf16[24,2048]{1,0:T(8,128)(2,1)S(1)}, bf16[24,2048]{1,0:T(8,128)(2,1)S(1)}, u32[]{:S(2)}, u32[]{:S(2)}) collective-permute-start(bf16[24,2048]{1,0:T(8,128)(2,1)S(1)} %pad_maximum_fusion.5), channel_id=1, source_target_pairs={{0,2},{1,3},{2,0},{3,1},{4,6},{5,7},{6,4},{7,5},{8,10},{9,11},{10,... | collective-permute-start | bytes 294920 | tf_op jit(solution)/shard_map/ppermute | solution.py:255
  11.7 6.1 %collective-permute-start.12 = (bf16[24,2048]{1,0:T(8,128)(2,1)S(1)}, bf16[24,2048]{1,0:T(8,128)(2,1)S(1)}, u32[]{:S(2)}, u32[]{:S(2)}) collective-permute-start(bf16[24,2048]{1,0:T(8,128)(2,1)S(1)} %pad_maximum_fusion.4), channel_id=1, source_target_pairs={{0,1},{1,0},{2,3},{3,2},{4,5},{5,4},{6,7},{7,6},{8,9},{9,8},{10,11... | collective-permute-start | bytes 294920 | tf_op jit(solution)/shard_map/ppermute | solution.py:255
  14.3 19.5 %collective-permute-start = (bf16[24,4096]{1,0:T(8,128)(2,1)S(1)}, bf16[24,4096]{1,0:T(8,128)(2,1)S(1)}, u32[]{:S(2)}, u32[]{:S(2)}) collective-permute-start(bf16[24,4096]{1,0:T(8,128)(2,1)S(1)} %pick.1), channel_id=1, source_target_pairs={{0,8},{4,12},{8,16},{12,20},{16,24},{20,28},{24,0},{28,4},{1,9},{5... | collective-permute-start | bytes 589832 | tf_op jit(solution)/shard_map/ppermute | solution.py:247
  16.2 17.7 %collective-permute-start.4 = (bf16[24,4096]{1,0:T(8,128)(2,1)}, bf16[24,4096]{1,0:T(8,128)(2,1)S(1)}, u32[]{:S(2)}, u32[]{:S(2)}) collective-permute-start(bf16[24,4096]{1,0:T(8,128)(2,1)} %param.11), channel_id=1, source_target_pairs={{0,8},{4,12},{8,16},{12,20},{16,24},{20,28},{24,0},{28,4},{1,9},{5... | collective-permute-start | bytes 589832 | tf_op jit(solution)/shard_map/ppermute | solution.py:247
  17.9 37.9 %collective-permute-start.5 = (bf16[24,4096]{1,0:T(8,128)(2,1)}, bf16[24,4096]{1,0:T(8,128)(2,1)S(1)}, u32[]{:S(2)}, u32[]{:S(2)}) collective-permute-start(bf16[24,4096]{1,0:T(8,128)(2,1)} %param.11), channel_id=1, source_target_pairs={{0,16},{4,20},{8,24},{12,28},{16,0},{20,4},{24,8},{28,12},{1,17},{... | collective-permute-start | bytes 589832 | tf_op jit(solution)/shard_map/ppermute | solution.py:247
  19.4 36.4 %collective-permute-start.6 = (bf16[24,4096]{1,0:T(8,128)(2,1)S(1)}, bf16[24,4096]{1,0:T(8,128)(2,1)S(1)}, u32[]{:S(2)}, u32[]{:S(2)}) collective-permute-start(bf16[24,4096]{1,0:T(8,128)(2,1)S(1)} %copy-done.4), channel_id=1, source_target_pairs={{0,24},{4,28},{8,0},{12,4},{16,8},{20,12},{24,16},{28,20},{1,25},{... | collective-permute-start | bytes 589832 | tf_op jit(solution)/shard_map/ppermute | solution.py:247
  33.9 22.6 %collective-permute-start.17 = (bf16[4,24,2048]{2,1,0:T(8,128)(2,1)S(1)}, bf16[4,24,2048]{2,1,0:T(8,128)(2,1)S(1)}, u32[]{:S(2)}, u32[]{:S(2)}) collective-permute-start(bf16[4,24,2048]{2,1,0:T(8,128)(2,1)S(1)} %get-tuple-element.57), channel_id=1, source_target_pairs={{0,24},{4,28},{8,0},{12,4},{16,8},{20,12},{24,16},{28,20},{1,25},{... | collective-permute-start | bytes 1179656 | tf_op jit(solution)/shard_map/ppermute | solution.py:247
  33.9 41.1 %collective-permute-start.16 = (bf16[4,24,2048]{2,1,0:T(8,128)(2,1)S(1)}, bf16[4,24,2048]{2,1,0:T(8,128)(2,1)S(1)}, u32[]{:S(2)}, u32[]{:S(2)}) collective-permute-start(bf16[4,24,2048]{2,1,0:T(8,128)(2,1)S(1)} %get-tuple-element.57), channel_id=1, source_target_pairs={{0,16},{4,20},{8,24},{12,28},{16,0},{20,4},{24,8},{28,12},{1,17},{... | collective-permute-start | bytes 1179656 | tf_op jit(solution)/shard_map/ppermute | solution.py:247
  33.9 41.1 %collective-permute-start.15 = (bf16[4,24,2048]{2,1,0:T(8,128)(2,1)S(1)}, bf16[4,24,2048]{2,1,0:T(8,128)(2,1)S(1)}, u32[]{:S(2)}, u32[]{:S(2)}) collective-permute-start(bf16[4,24,2048]{2,1,0:T(8,128)(2,1)S(1)} %get-tuple-element.57), channel_id=1, source_target_pairs={{0,8},{4,12},{8,16},{12,20},{16,24},{20,28},{24,0},{28,4},{1,9},{5... | collective-permute-start | bytes 1179656 | tf_op jit(solution)/shard_map/ppermute | solution.py:247
  55.7 20.7 %collective-permute-start.3 = (bf16[96,4096]{1,0:T(8,128)(2,1)S(1)}, bf16[96,4096]{1,0:T(8,128)(2,1)S(1)}, u32[]{:S(2)}, u32[]{:S(2)}) collective-permute-start(bf16[96,4096]{1,0:T(8,128)(2,1)S(1)} %pad_maximum_fusion.2.refs_0_), channel_id=1, source_target_pairs={{0,4},{4,0},{8,12},{12,8},{16,20},{20,16},{24,28},{28,24},{1,5},{5... | collective-permute-start | bytes 2359304 | tf_op jit(solution)/shard_map/ppermute | solution.py:251
  55.9 35.3 %collective-permute-start.7 = (bf16[96,4096]{1,0:T(8,128)(2,1)S(1)}, bf16[96,4096]{1,0:T(8,128)(2,1)S(1)}, u32[]{:S(2)}, u32[]{:S(2)}) collective-permute-start(bf16[96,4096]{1,0:T(8,128)(2,1)S(1)} %constant_dynamic-update-slice_fusion.refs_0_), channel_id=1, source_target_pairs={{0,4},{4,0},{8,12},{12,8},{16,20},{20,16},{24,28},{28,24},{1,5},{5... | collective-permute-start | bytes 2359304 | tf_op jit(solution)/shard_map/ppermute | solution.py:251
  76.4 65.4 %collective-permute-start.18 = (bf16[4,4,24,2048]{3,2,0,1:T(8,128)(2,1)}, bf16[4,4,24,2048]{3,2,0,1:T(8,128)(2,1)S(1)}, u32[]{:S(2)}, u32[]{:S(2)}) collective-permute-start(bf16[4,4,24,2048]{3,2,0,1:T(8,128)(2,1)} %get-tuple-element.49), channel_id=1, source_target_pairs={{0,4},{4,0},{8,12},{12,8},{16,20},{20,16},{24,28},{28,24},{1,5},{5... | collective-permute-start | bytes 4718600 | tf_op jit(solution)/shard_map/ppermute | solution.py:251
  76.4 5.2 %copy-start = (bf16[4096,1792]{1,0:T(8,128)(2,1)S(1)}, bf16[4096,1792]{1,0:T(8,128)(2,1)}, u32[]{:S(2)}) copy-start(bf16[4096,1792]{1,0:T(8,128)(2,1)} %refs_3_.3) | copy-start | bytes 44040196
  81.6 21.9 %slice-start = ((s8[14680064]{0:T(1024)(128)(4,1)}), s8[4194304]{0:T(1024)(128)(4,1)S(1)}, s32[]{:S(2)}) async-start(s8[14680064]{0:T(1024)(128)(4,1)} %bitcast.46), calls=%async_computation | async-start | bytes 8388608
  81.6 21.9 %slice-start.1 = ((s8[14680064]{0:T(1024)(128)(4,1)}), s8[4194304]{0:T(1024)(128)(4,1)S(1)}, s32[]{:S(2)}) async-start(s8[14680064]{0:T(1024)(128)(4,1)} %bitcast.46), calls=%async_computation.1 | async-start | bytes 8388608
  81.6 21.9 %slice-start.2 = ((s8[14680064]{0:T(1024)(128)(4,1)}), s8[4194304]{0:T(1024)(128)(4,1)S(1)}, s32[]{:S(2)}) async-start(s8[14680064]{0:T(1024)(128)(4,1)} %bitcast.46), calls=%async_computation.2 | async-start | bytes 8388608
  91.2 5.2 %copy-start.1 = (bf16[1792,4096]{1,0:T(8,128)(2,1)S(1)}, bf16[1792,4096]{1,0:T(8,128)(2,1)}, u32[]{:S(2)}) copy-start(bf16[1792,4096]{1,0:T(8,128)(2,1)} %refs_5_.1) | copy-start | bytes 44040196
  96.3 7.2 %slice-start.3 = ((s8[14680064]{0:T(1024)(128)(4,1)}), s8[2097152]{0:T(1024)(128)(4,1)S(1)}, s32[]{:S(2)}) async-start(s8[14680064]{0:T(1024)(128)(4,1)} %bitcast.46), calls=%async_computation.3 | async-start | bytes 4194304
  119.9 23.3 %collective-permute-start.8 = (bf16[2,96,4096]{2,1,0:T(8,128)(2,1)S(1)}, bf16[2,96,4096]{2,1,0:T(8,128)(2,1)S(1)}, u32[]{:S(2)}, u32[]{:S(2)}) collective-permute-start(bf16[2,96,4096]{2,1,0:T(8,128)(2,1)S(1)} %get-tuple-element.32), channel_id=1, source_target_pairs={{0,4},{4,0},{8,12},{12,8},{16,20},{20,16},{24,28},{28,24},{1,5},{5... | collective-permute-start | bytes 4718600 | tf_op jit(solution)/shard_map/ppermute | solution.py:251
  120.4 17.4 %collective-permute-start.28 = (bf16[192,1792]{1,0:T(8,128)(2,1)S(1)}, bf16[192,1792]{1,0:T(8,128)(2,1)S(1)}, u32[]{:S(2)}, u32[]{:S(2)}) collective-permute-start(bf16[192,1792]{1,0:T(8,128)(2,1)S(1)} %get-tuple-element.42.refs_0_), channel_id=1, source_target_pairs={{0,2},{1,3},{2,0},{3,1},{4,6},{5,7},{6,4},{7,5},{8,10},{9,11},{10,... | collective-permute-start | bytes 2064392 | tf_op jit(solution)/shard_map/ppermute | solution.py:255
  122.0 18.3 %collective-permute-start.27 = (bf16[192,1792]{1,0:T(8,128)(2,1)S(1)}, bf16[192,1792]{1,0:T(8,128)(2,1)S(1)}, u32[]{:S(2)}, u32[]{:S(2)}) collective-permute-start(bf16[192,1792]{1,0:T(8,128)(2,1)S(1)} %get-tuple-element.42.refs_0_), channel_id=1, source_target_pairs={{0,1},{1,0},{2,3},{3,2},{4,5},{5,4},{6,7},{7,6},{8,9},{9,8},{10,11... | collective-permute-start | bytes 2064392 | tf_op jit(solution)/shard_map/ppermute | solution.py:255
  123.5 31.5 %collective-permute-start.19 = (bf16[192,1792]{1,0:T(8,128)(2,1)S(1)}, bf16[192,1792]{1,0:T(8,128)(2,1)S(1)}, u32[]{:S(2)}, u32[]{:S(2)}) collective-permute-start(bf16[192,1792]{1,0:T(8,128)(2,1)S(1)} %get-tuple-element.33.refs_2_), channel_id=1, source_target_pairs={{0,1},{1,0},{2,3},{3,2},{4,5},{5,4},{6,7},{7,6},{8,9},{9,8},{10,11... | collective-permute-start | bytes 2064392 | tf_op jit(solution)/shard_map/ppermute | solution.py:255
  137.9 18.3 %collective-permute-start.20 = (bf16[192,1792]{1,0:T(8,128)(2,1)S(1)}, bf16[192,1792]{1,0:T(8,128)(2,1)S(1)}, u32[]{:S(2)}, u32[]{:S(2)}) collective-permute-start(bf16[192,1792]{1,0:T(8,128)(2,1)S(1)} %get-tuple-element.33.refs_2_), channel_id=1, source_target_pairs={{0,2},{1,3},{2,0},{3,1},{4,6},{5,7},{6,4},{7,5},{8,10},{9,11},{10,... | collective-permute-start | bytes 2064392 | tf_op jit(solution)/shard_map/ppermute | solution.py:255
  140.3 29.5 %collective-permute-start.23 = (bf16[192,1792]{1,0:T(8,128)(2,1)S(1)}, bf16[192,1792]{1,0:T(8,128)(2,1)S(1)}, u32[]{:S(2)}, u32[]{:S(2)}) collective-permute-start(bf16[192,1792]{1,0:T(8,128)(2,1)S(1)} %get-tuple-element.39.refs_1_), channel_id=1, source_target_pairs={{0,1},{1,0},{2,3},{3,2},{4,5},{5,4},{6,7},{7,6},{8,9},{9,8},{10,11... | collective-permute-start | bytes 2064392 | tf_op jit(solution)/shard_map/ppermute | solution.py:255
  141.8 30.7 %collective-permute-start.24 = (bf16[192,1792]{1,0:T(8,128)(2,1)S(1)}, bf16[192,1792]{1,0:T(8,128)(2,1)S(1)}, u32[]{:S(2)}, u32[]{:S(2)}) collective-permute-start(bf16[192,1792]{1,0:T(8,128)(2,1)S(1)} %get-tuple-element.39.refs_1_), channel_id=1, source_target_pairs={{0,2},{1,3},{2,0},{3,1},{4,6},{5,7},{6,4},{7,5},{8,10},{9,11},{10,... | collective-permute-start | bytes 2064392 | tf_op jit(solution)/shard_map/ppermute | solution.py:255
  143.1 32.8 %collective-permute-start.29 = (bf16[96,1792]{1,0:T(8,128)(2,1)S(1)}, bf16[96,1792]{1,0:T(8,128)(2,1)S(1)}, u32[]{:S(2)}, u32[]{:S(2)}) collective-permute-start(bf16[96,1792]{1,0:T(8,128)(2,1)S(1)} %slice.64), channel_id=1, source_target_pairs={{0,1},{1,0},{2,3},{3,2},{4,5},{5,4},{6,7},{7,6},{8,9},{9,8},{10,11... | collective-permute-start | bytes 1032200 | tf_op jit(solution)/shard_map/ppermute | solution.py:255
  155.0 22.5 %collective-permute-start.30 = (bf16[96,1792]{1,0:T(8,128)(2,1)S(1)}, bf16[96,1792]{1,0:T(8,128)(2,1)S(1)}, u32[]{:S(2)}, u32[]{:S(2)}) collective-permute-start(bf16[96,1792]{1,0:T(8,128)(2,1)S(1)} %slice.65), channel_id=1, source_target_pairs={{0,2},{1,3},{2,0},{3,1},{4,6},{5,7},{6,4},{7,5},{8,10},{9,11},{10,... | collective-permute-start | bytes 1032200 | tf_op jit(solution)/shard_map/ppermute | solution.py:255
  156.2 42.7 %collective-permute-start.9 = (bf16[2,24,4096]{2,1,0:T(8,128)(2,1)S(1)}, bf16[2,24,4096]{2,1,0:T(8,128)(2,1)S(1)}, u32[]{:S(2)}, u32[]{:S(2)}) collective-permute-start(bf16[2,24,4096]{2,1,0:T(8,128)(2,1)S(1)} %get-tuple-element.53), channel_id=1, source_target_pairs={{0,24},{4,28},{8,0},{12,4},{16,8},{20,12},{24,16},{28,20},{1,25},{... | collective-permute-start | bytes 1179656 | tf_op jit(solution)/shard_map/ppermute | solution.py:247
  169.8 29.1 %collective-permute-start.10 = (bf16[2,24,4096]{2,1,0:T(8,128)(2,1)S(1)}, bf16[2,24,4096]{2,1,0:T(8,128)(2,1)S(1)}, u32[]{:S(2)}, u32[]{:S(2)}) collective-permute-start(bf16[2,24,4096]{2,1,0:T(8,128)(2,1)S(1)} %get-tuple-element.52), channel_id=1, source_target_pairs={{0,16},{4,20},{8,24},{12,28},{16,0},{20,4},{24,8},{28,12},{1,17},{... | collective-permute-start | bytes 1179656 | tf_op jit(solution)/shard_map/ppermute | solution.py:247
  172.6 26.3 %collective-permute-start.11 = (bf16[2,24,4096]{2,1,0:T(8,128)(2,1)S(1)}, bf16[2,24,4096]{2,1,0:T(8,128)(2,1)S(1)}, u32[]{:S(2)}, u32[]{:S(2)}) collective-permute-start(bf16[2,24,4096]{2,1,0:T(8,128)(2,1)S(1)} %get-tuple-element.51), channel_id=1, source_target_pairs={{0,8},{4,12},{8,16},{12,20},{16,24},{20,28},{24,0},{28,4},{1,9},{5... | collective-permute-start | bytes 1179656 | tf_op jit(solution)/shard_map/ppermute | solution.py:247
  176.0 8.9 %collective-permute-start.21 = (bf16[96,1792]{1,0:T(8,128)(2,1)S(1)}, bf16[96,1792]{1,0:T(8,128)(2,1)S(1)}, u32[]{:S(2)}, u32[]{:S(2)}) collective-permute-start(bf16[96,1792]{1,0:T(8,128)(2,1)S(1)} %slice.47), channel_id=1, source_target_pairs={{0,1},{1,0},{2,3},{3,2},{4,5},{5,4},{6,7},{7,6},{8,9},{9,8},{10,11... | collective-permute-start | bytes 1032200 | tf_op jit(solution)/shard_map/ppermute | solution.py:255
  177.5 8.9 %collective-permute-start.22 = (bf16[96,1792]{1,0:T(8,128)(2,1)S(1)}, bf16[96,1792]{1,0:T(8,128)(2,1)S(1)}, u32[]{:S(2)}, u32[]{:S(2)}) collective-permute-start(bf16[96,1792]{1,0:T(8,128)(2,1)S(1)} %slice.48), channel_id=1, source_target_pairs={{0,2},{1,3},{2,0},{3,1},{4,6},{5,7},{6,4},{7,5},{8,10},{9,11},{10,... | collective-permute-start | bytes 1032200 | tf_op jit(solution)/shard_map/ppermute | solution.py:255
  184.9 8.1 %collective-permute-start.25 = (bf16[96,1792]{1,0:T(8,128)(2,1)S(1)}, bf16[96,1792]{1,0:T(8,128)(2,1)S(1)}, u32[]{:S(2)}, u32[]{:S(2)}) collective-permute-start(bf16[96,1792]{1,0:T(8,128)(2,1)S(1)} %slice.51), channel_id=1, source_target_pairs={{0,1},{1,0},{2,3},{3,2},{4,5},{5,4},{6,7},{7,6},{8,9},{9,8},{10,11... | collective-permute-start | bytes 1032200 | tf_op jit(solution)/shard_map/ppermute | solution.py:255
  186.4 7.8 %collective-permute-start.26 = (bf16[96,1792]{1,0:T(8,128)(2,1)S(1)}, bf16[96,1792]{1,0:T(8,128)(2,1)S(1)}, u32[]{:S(2)}, u32[]{:S(2)}) collective-permute-start(bf16[96,1792]{1,0:T(8,128)(2,1)S(1)} %slice.52), channel_id=1, source_target_pairs={{0,2},{1,3},{2,0},{3,1},{4,6},{5,7},{6,4},{7,5},{8,10},{9,11},{10,... | collective-permute-start | bytes 1032200 | tf_op jit(solution)/shard_map/ppermute | solution.py:255

commit v5 on v4

--- a/solution.py
+++ b/solution.py
@@ -10,6 +10,7 @@
 F32 = jnp.float32
 CORES = 2
 MIB = 1 << 20
+ALL_VMEM = 67043328
 
 
 HBM = pl.BlockSpec(memory_space=pltpu.HBM)
@@ -31,9 +32,9 @@
     return jax.ShapeDtypeStruct(dims, dtype)
 
 
-def grant(*arrays):
+def grant(*arrays, least=0):
     total = sum(2 * r * c if d == BF else 4 * r * c for r, c, d in arrays)
-    return pltpu.CompilerParams(vmem_limit_bytes=min(total + 6 * MIB, 60 * MIB))
+    return pltpu.CompilerParams(vmem_limit_bytes=min(max(total + 6 * MIB, least), ALL_VMEM))
 
 
 def nt_dot(left, right):
@@ -44,9 +45,15 @@
     return jnp.dot(left, right, preferred_element_type=F32)
 
 
-def pick_kernel(flag_ref, tokens_ref, out_ref):
+def pick_kernel(flag_hbm, tokens_hbm, out_ref, flag_ref, tokens_ref, sems):
     rows = out_ref.shape[0]
     count = tokens_ref.shape[0]
+    copies = (pltpu.make_async_copy(flag_hbm, flag_ref, sems.at[0]),
+              pltpu.make_async_copy(tokens_hbm, tokens_ref, sems.at[1]))
+    for copy in copies:
+        copy.start()
+    for copy in copies:
+        copy.wait()
     flags = (flag_ref[...] == 1).astype(F32)
     before = lax.broadcasted_iota(jnp.int32, (count, count), 0)
     after = lax.broadcasted_iota(jnp.int32, (count, count), 1)
@@ -61,8 +68,15 @@
 def pick(modality, tokens, rows):
     return pl.pallas_call(
         pick_kernel,
+        in_specs=[HBM, HBM],
+        out_specs=VMEM,
         out_shape=shape((rows, tokens.shape[1])),
-        compiler_params=grant(),
+        scratch_shapes=[
+            pltpu.VMEM((1, modality.shape[0]), modality.dtype),
+            pltpu.VMEM(tokens.shape, BF),
+            pltpu.SemaphoreType.DMA((2,)),
+        ],
+        compiler_params=grant(least=ALL_VMEM),
         name="pick",
     )(modality.reshape(1, -1), tokens)
 
@@ -89,7 +103,7 @@
             start(j + depth)
 
 
-DEPTH = 4
+DEPTH = 5
 
 
 def enter_kernel(tile, xa_ref, xb_ref, gate_hbm, up_hbm, hid_ref, active_ref, turn_ref,
@@ -135,7 +149,7 @@
             pltpu.VMEM((depth, width, tile), BF),
             pltpu.SemaphoreType.DMA((2, depth)),
         ],
-        compiler_params=grant((rows, width, BF), (2 * depth * tile, width, BF)),
+        compiler_params=grant((rows, width, BF), (2 * depth * tile, width, BF), least=46 * MIB),
         cost_estimate=cost(4 * rows * width * units, 4 * width * units),
         name="enter",
     )(own, other, gate, up)
@@ -176,7 +190,7 @@
             pltpu.VMEM((depth, tile, width), BF),
             pltpu.SemaphoreType.DMA((depth,)),
         ],
-        compiler_params=grant((rows, width, BF), (depth * tile, width, BF)),
+        compiler_params=grant((rows, width, BF), (depth * tile, width, BF), least=46 * MIB),
         cost_estimate=cost(2 * rows * width * units, 2 * width * units),
         name="turn",
     )(own, other, down, active, factor)
@@ -224,7 +238,7 @@
             pltpu.VMEM((depth, units, step), BF),
             pltpu.SemaphoreType.DMA((3, depth)),
         ],
-        compiler_params=grant((3 * depth * step, units, BF)),
+        compiler_params=grant((3 * depth * step, units, BF), least=46 * MIB),
         cost_estimate=cost(6 * rows * width * units, 6 * width * units),
         name="leave",
     )(hid, gb, ub, gate, up, down)
@@ -323,11 +337,15 @@
     gate_grad = rows_dot(tok_all, stack(all_gb))
     up_grad = rows_dot(tok_all, stack(all_ub))
     terms = after(terms, [up_grad])
-    total = sums[0].astype(F32)
-    for term in terms:
-        total = total + term.astype(F32)
-    total = total.astype(BF)
-    return total[0], total[1], gate_grad, up_grad, down_grad
+
+    def total(side):
+        value = sums[0][side].astype(F32)
+        for term in terms:
+            value = value + term[side].astype(F32)
+        return value.astype(BF)
+
+    output, in_grad = total(0), total(1)
+    return output, in_grad, gate_grad, up_grad, down_grad
 
 
 def solution(mesh):

time: 200 us -> 191 us (0.955)
  local copies, waits for them, and re-layouts: 15.7 us -> 3.93 us
  Pallas kernels: 33.3 us -> 37 us
    unnamed x33 -> x19, local copies, waits for them, and re-layouts: 13.4 us -> 1.47 us
  transfers between devices with their start and end apart: 31 -> 31, of which waited for: 13 -> 13; matrix products, arithmetic and copies ran while one was open for 10% -> 10% of each run, Pallas kernels for 17% -> 18%
where the time goes in v5:
time: 191 us
  waiting for transfers between devices  74.2 us (39%)
  starting transfers between devices  58.5 us (31%)
  Pallas kernels  37 us (19%)
  matrix products  13.6 us (7%)
  local copies, waits for them, and re-layouts  3.93 us (2%)
  other arithmetic  2.31 us (1%)
    ppermute x15, waiting for transfers between devices, across(): return lax.ppermute(value, 'seq', [(g, g ^ mask) for g in range(groups)])  44.2 us
    ppermute x12, starting transfers between devices, shift(): lax.ppermute(value, 'dp', [(z * CORES + c, (z + k) % ring * CORES + c) fo...  41.2 us
    ppermute x12, waiting for transfers between devices, shift(): lax.ppermute(value, 'dp', [(z * CORES + c, (z + k) % ring * CORES + c) fo...  29.9 us
    pallas_call x1, Pallas kernels, leave(): pl.pallas_call(lambda *refs: leave_kernel(step, *refs), in_specs=[VMEM] *...  16.4 us
    ppermute x15, starting transfers between devices, across(): return lax.ppermute(value, 'seq', [(g, g ^ mask) for g in range(groups)])  16.1 us
    dot_general x3, matrix products, rows_dot(): lax.dot_general(left, right, (((0,), (0,)), ((), ())), preferred_element_...  13.6 us
    pallas_call x1, Pallas kernels, enter(): pl.pallas_call(lambda *refs: enter_kernel(tile, *refs), in_specs=[VMEM, V...  11 us
    pallas_call x1, Pallas kernels, turn(): pl.pallas_call(lambda *refs: turn_kernel(tile, *refs), in_specs=[VMEM, VM...  7.65 us
  transfers between devices with their start and end apart: 31, of which 13 were waited for; matrix products, arithmetic and copies ran while one was open for 10% of the time, Pallas kernels for 18%

profile of v5, /device:TPU:0, one launch (start us, length us, event | category | flops | bytes accessed | tf_op | source)
XLA Modules:
  0.0 190.5 jit_solution(10165290592734964901)
XLA Ops:
  0.6 2.0 %pick.1 = bf16[24,4096]{1,0:T(8,128)(2,1)} custom-call(s32[1,32]{1,0:T(1,128)} %bitcast.69, bf16[32,4096]{1,0:T(8,128)(2,1)} %tokens_hbm.1), custom_call_target="tpu_custom_call" | custom-call | tf_op jit(solution)/shard_map/pick/pallas_call | solution.py:69
  2.6 0.0 copy-start.1
  2.6 0.0 copy-start
  2.7 5.1 %collective-permute-start.2 = (bf16[24,4096]{1,0:T(8,128)(2,1)}, bf16[24,4096]{1,0:T(8,128)(2,1)S(1)}, u32[]{:S(2)}, u32[]{:S(2)}) collective-permute-start(bf16[24,4096]{1,0:T(8,128)(2,1)} %pick.1), channel_id=1, source_target_pairs={{0,24},{4,28},{8,0},{12,4},{16,8},{20,12},{24,16},{28,20},{1,25},{... | collective-permute-start | bytes 589832 | tf_op jit(solution)/shard_map/ppermute | solution.py:261
  7.8 0.9 constant_dynamic-slice_fusion.7
  8.7 0.9 constant_dynamic-slice_fusion.6
  9.6 2.5 %collective-permute-start.14 = (bf16[24,2048]{1,0:T(8,128)(2,1)S(1)}, bf16[24,2048]{1,0:T(8,128)(2,1)S(1)}, u32[]{:S(2)}, u32[]{:S(2)}) collective-permute-start(bf16[24,2048]{1,0:T(8,128)(2,1)S(1)} %pad_maximum_fusion.6), channel_id=1, source_target_pairs={{0,3},{1,2},{2,1},{3,0},{4,7},{5,6},{6,5},{7,4},{8,11},{9,10},{10,... | collective-permute-start | bytes 294920 | tf_op jit(solution)/shard_map/ppermute | solution.py:269
  12.1 0.6 collective-permute-start.13
  12.7 0.6 collective-permute-start.12
  13.3 0.9 constant_dynamic-update-slice_fusion.3
  14.3 1.0 collective-permute-done.14
  15.3 1.0 collective-permute-start
  16.3 0.9 collective-permute-done.13
  17.2 1.6 collective-permute-start.4
  18.8 0.0 collective-permute-done.12
  18.8 1.5 collective-permute-start.5
  20.3 0.1 fusion.3
  20.4 2.5 %collective-permute-start.6 = (bf16[24,4096]{1,0:T(8,128)(2,1)S(1)}, bf16[24,4096]{1,0:T(8,128)(2,1)S(1)}, u32[]{:S(2)}, u32[]{:S(2)}) collective-permute-start(bf16[24,4096]{1,0:T(8,128)(2,1)S(1)} %copy-done.1), channel_id=1, source_target_pairs={{0,24},{4,28},{8,0},{12,4},{16,8},{20,12},{24,16},{28,20},{1,25},{... | collective-permute-start | bytes 589832 | tf_op jit(solution)/shard_map/ppermute | solution.py:261
  22.9 11.3 %collective-permute-done.1 = bf16[24,4096]{1,0:T(8,128)(2,1)S(1)} collective-permute-done((bf16[24,4096]{1,0:T(8,128)(2,1)}, bf16[24,4096]{1,0:T(8,128)(2,1)S(1)}, u32[]{:S(2)}, u32[]{:S(2)}) %collective-permute-start.1) | collective-permute-done | bytes 196640 | tf_op jit(solution)/shard_map/ppermute | solution.py:261
  34.2 0.1 pad_maximum_fusion.2.refs_0_
  34.3 0.0 collective-permute-done.4
  34.3 21.7 %collective-permute-start.15 = (bf16[4,24,2048]{2,1,0:T(8,128)(2,1)S(1)}, bf16[4,24,2048]{2,1,0:T(8,128)(2,1)S(1)}, u32[]{:S(2)}, u32[]{:S(2)}) collective-permute-start(bf16[4,24,2048]{2,1,0:T(8,128)(2,1)S(1)} %get-tuple-element.57), channel_id=1, source_target_pairs={{0,8},{4,12},{8,16},{12,20},{16,24},{20,28},{24,0},{28,4},{1,9},{5... | collective-permute-start | bytes 1179656 | tf_op jit(solution)/shard_map/ppermute | solution.py:261
  56.0 0.1 collective-permute-start.3
  56.2 0.6 collective-permute-start.7
  56.7 18.6 %collective-permute-done.16 = bf16[4,24,2048]{2,1,0:T(8,128)(2,1)S(1)} collective-permute-done((bf16[4,24,2048]{2,1,0:T(8,128)(2,1)S(1)}, bf16[4,24,2048]{2,1,0:T(8,128)(2,1)S(1)}, u32[]{:S(2)}, u32[]{:S(2)}) %collective-permute-start.16) | collective-permute-done | bytes 393248 | tf_op jit(solution)/shard_map/ppermute | solution.py:261
  75.3 0.3 pad_maximum_fusion.1
  75.6 0.1 collective-permute-start.18
  75.7 11.0 %enter.1 = (bf16[192,1792]{1,0:T(8,128)(2,1)S(1)}, f32[192,1792]{1,0:T(8,128)S(1)}, f32[192,1792]{1,0:T(8,128)S(1)}) custom-call(bf16[96,4096]{1,0:T(8,128)(2,1)S(1)} %pad_maximum_fusion.2.refs_0_, bf16[96,4096]{1,0:T(8,128)(2,1)S(1)} %collective-permute-done.3.refs_1_, bf16[4096,1792]{1,0:T(8,128)(2,1)} %refs_3_.3, bf16[4096,1792]{1,0:T(8,128)(2,1)} %refs_4_.1), custom_call_target="tpu_custom_call" | custom-call | flops 5637144576 | bytes 29360128 | tf_op jit(solution)/shard_map/enter/pallas_call | solution.py:141
  86.7 7.7 %turn.1 = (bf16[192,1792]{1,0:T(8,128)(2,1)S(1)}, bf16[192,1792]{1,0:T(8,128)(2,1)S(1)}) custom-call(bf16[96,4096]{1,0:T(8,128)(2,1)S(1)} %constant_dynamic-update-slice_fusion.refs_0_, bf16[96,4096]{1,0:T(8,128)(2,1)S(1)} %collective-permute-done.7.refs_1_, bf16[1792,4096]{1,0:T(8,128)(2,1)} %refs_5_.1, f32[192,1792]{1,0:T(8,128)S(1)} %get-tuple-element.27.refs_3_, ...), custom_call_target="tpu_custom_call" | custom-call | flops 2818572288 | bytes 14680064 | tf_op jit(solution)/shard_map/turn/pallas_call | solution.py:183
  94.3 16.4 %leave.1 = (bf16[2,96,4096]{2,1,0:T(8,128)(2,1)S(1)}, bf16[2,96,4096]{2,1,0:T(8,128)(2,1)S(1)}) custom-call(bf16[192,1792]{1,0:T(8,128)(2,1)S(1)} %get-tuple-element.42.refs_0_, bf16[192,1792]{1,0:T(8,128)(2,1)S(1)} %get-tuple-element.39.refs_1_, bf16[192,1792]{1,0:T(8,128)(2,1)S(1)} %get-tuple-element.33.refs_2_, bf16[4096,1792]{1,0:T(8,128)(2,1)} %refs_3_.3, ...), custom_call_target="tpu_custom_call" | custom-call | flops 8455716864 | bytes 44040192 | tf_op jit(solution)/shard_map/leave/pallas_call | solution.py:230
  110.7 0.6 collective-permute-start.8
  111.3 1.5 collective-permute-start.28
  112.7 1.5 collective-permute-start.27
  114.2 0.5 collective-permute-start.19
  114.8 13.9 %collective-permute-done.28 = bf16[192,1792]{1,0:T(8,128)(2,1)S(1)} collective-permute-done((bf16[192,1792]{1,0:T(8,128)(2,1)S(1)}, bf16[192,1792]{1,0:T(8,128)(2,1)S(1)}, u32[]{:S(2)}, u32[]{:S(2)}) %collective-permute-start.28) | collective-permute-done | bytes 688160 | tf_op jit(solution)/shard_map/ppermute | solution.py:269
  128.7 1.5 collective-permute-start.20
  130.2 0.9 collective-permute-done.27
  131.0 1.5 collective-permute-start.23
  132.6 0.6 collective-permute-start.24
  133.1 0.4 pad_maximum_fusion
  133.6 0.2 copy.11
  133.7 0.2 copy.12
  133.9 0.7 collective-permute-start.29
  134.6 0.5 add_convert_fusion
  135.1 0.1 slice_bitcast_fusion
  135.2 10.6 %collective-permute-done.19 = bf16[192,1792]{1,0:T(8,128)(2,1)S(1)} collective-permute-done((bf16[192,1792]{1,0:T(8,128)(2,1)S(1)}, bf16[192,1792]{1,0:T(8,128)(2,1)S(1)}, u32[]{:S(2)}, u32[]{:S(2)}) %collective-permute-start.19) | collective-permute-done | bytes 688160 | tf_op jit(solution)/shard_map/ppermute | solution.py:269
  145.8 0.6 collective-permute-start.30
  146.3 0.6 collective-permute-done.20
  147.0 3.5 %collective-permute-start.9 = (bf16[2,24,4096]{2,1,0:T(8,128)(2,1)S(1)}, bf16[2,24,4096]{2,1,0:T(8,128)(2,1)S(1)}, u32[]{:S(2)}, u32[]{:S(2)}) collective-permute-start(bf16[2,24,4096]{2,1,0:T(8,128)(2,1)S(1)} %get-tuple-element.55), channel_id=1, source_target_pairs={{0,24},{4,28},{8,0},{12,4},{16,8},{20,12},{24,16},{28,20},{1,25},{... | collective-permute-start | bytes 1179656 | tf_op jit(solution)/shard_map/ppermute | solution.py:261
  150.8 9.8 %collective-permute-done.23 = bf16[192,1792]{1,0:T(8,128)(2,1)S(1)} collective-permute-done((bf16[192,1792]{1,0:T(8,128)(2,1)S(1)}, bf16[192,1792]{1,0:T(8,128)(2,1)S(1)}, u32[]{:S(2)}, u32[]{:S(2)}) %collective-permute-start.23) | collective-permute-done | bytes 688160 | tf_op jit(solution)/shard_map/ppermute | solution.py:269
  160.5 2.8 %collective-permute-start.10 = (bf16[2,24,4096]{2,1,0:T(8,128)(2,1)S(1)}, bf16[2,24,4096]{2,1,0:T(8,128)(2,1)S(1)}, u32[]{:S(2)}, u32[]{:S(2)}) collective-permute-start(bf16[2,24,4096]{2,1,0:T(8,128)(2,1)S(1)} %get-tuple-element.54), channel_id=1, source_target_pairs={{0,16},{4,20},{8,24},{12,28},{16,0},{20,4},{24,8},{28,12},{1,17},{... | collective-permute-start | bytes 1179656 | tf_op jit(solution)/shard_map/ppermute | solution.py:261
  163.3 1.4 collective-permute-start.11
  164.7 2.0 %collective-permute-done.29 = bf16[96,1792]{1,0:T(8,128)(2,1)S(1)} collective-permute-done((bf16[96,1792]{1,0:T(8,128)(2,1)S(1)}, bf16[96,1792]{1,0:T(8,128)(2,1)S(1)}, u32[]{:S(2)}, u32[]{:S(2)}) %collective-permute-start.29) | collective-permute-done | bytes 344096 | tf_op jit(solution)/shard_map/ppermute | solution.py:269
  166.7 1.5 collective-permute-start.21
  168.2 0.6 collective-permute-start.22
  169.1 4.5 %convolution_convert_fusion = bf16[1792,1024]{1,0:T(8,128)(2,1)} fusion(bf16[768,1792]{1,0:T(8,128)(2,1)S(1)} %constant_dynamic-update-slice_fusion.14, bf16[768,1024]{1,0:T(8,128)(2,1)S(1)} %bitcast.61), kind=kOutput, calls=%fused_computation | convolution fusion | flops 2820407296 | bytes 7995392 | tf_op jit(solution)/shard_map/dot_general | solution.py:248
  173.8 1.9 collective-permute-done.21
  175.6 1.5 collective-permute-start.25
  177.2 0.6 collective-permute-start.26
  177.8 4.5 %convolution_convert_fusion.2 = bf16[1024,1792]{1,0:T(8,128)(2,1)} fusion(bf16[768,1024]{1,0:T(8,128)(2,1)S(1)} %bitcast.59, bf16[768,1792]{1,0:T(8,128)(2,1)S(1)} %constant_dynamic-update-slice_fusion.4), kind=kOutput, calls=%fused_computation.2 | convolution fusion | flops 2820407296 | bytes 7995392 | tf_op jit(solution)/shard_map/dot_general | solution.py:248
  182.3 1.4 collective-permute-done.25
  183.7 1.3 collective-permute-done.26
  185.0 4.5 %convolution_convert_fusion.1 = bf16[1024,1792]{1,0:T(8,128)(2,1)} fusion(bf16[768,1024]{1,0:T(8,128)(2,1)S(1)} %bitcast.60, bf16[768,1792]{1,0:T(8,128)(2,1)S(1)} %constant_dynamic-update-slice_fusion.9), kind=kOutput, calls=%fused_computation.1 | convolution fusion | flops 2820407296 | bytes 7995392 | tf_op jit(solution)/shard_map/dot_general | solution.py:248
  189.6 0.9 fusion.1
  (49 shorter events, 0.8 us)
Async XLA Ops:
  2.6 17.7 %copy-start.1 = (bf16[24,4096]{1,0:T(8,128)(2,1)S(1)}, bf16[24,4096]{1,0:T(8,128)(2,1)}, u32[]{:S(2)}) copy-start(bf16[24,4096]{1,0:T(8,128)(2,1)} %param.11) | copy-start | bytes 589828
  2.6 31.6 %copy-start = (bf16[24,4096]{1,0:T(8,128)(2,1)S(1)}, bf16[24,4096]{1,0:T(8,128)(2,1)}, u32[]{:S(2)}) copy-start(bf16[24,4096]{1,0:T(8,128)(2,1)} %pick.1) | copy-start | bytes 589828
  2.7 17.7 %collective-permute-start.2 = (bf16[24,4096]{1,0:T(8,128)(2,1)}, bf16[24,4096]{1,0:T(8,128)(2,1)S(1)}, u32[]{:S(2)}, u32[]{:S(2)}) collective-permute-start(bf16[24,4096]{1,0:T(8,128)(2,1)} %pick.1), channel_id=1, source_target_pairs={{0,24},{4,28},{8,0},{12,4},{16,8},{20,12},{24,16},{28,20},{1,25},{... | collective-permute-start | bytes 589832 | tf_op jit(solution)/shard_map/ppermute | solution.py:261
  7.8 26.4 %collective-permute-start.1 = (bf16[24,4096]{1,0:T(8,128)(2,1)}, bf16[24,4096]{1,0:T(8,128)(2,1)S(1)}, u32[]{:S(2)}, u32[]{:S(2)}) collective-permute-start(bf16[24,4096]{1,0:T(8,128)(2,1)} %pick.1), channel_id=1, source_target_pairs={{0,16},{4,20},{8,24},{12,28},{16,0},{20,4},{24,8},{28,12},{1,17},{... | collective-permute-start | bytes 589832 | tf_op jit(solution)/shard_map/ppermute | solution.py:261
  9.6 5.7 %collective-permute-start.14 = (bf16[24,2048]{1,0:T(8,128)(2,1)S(1)}, bf16[24,2048]{1,0:T(8,128)(2,1)S(1)}, u32[]{:S(2)}, u32[]{:S(2)}) collective-permute-start(bf16[24,2048]{1,0:T(8,128)(2,1)S(1)} %pad_maximum_fusion.6), channel_id=1, source_target_pairs={{0,3},{1,2},{2,1},{3,0},{4,7},{5,6},{6,5},{7,4},{8,11},{9,10},{10,... | collective-permute-start | bytes 294920 | tf_op jit(solution)/shard_map/ppermute | solution.py:269
  12.1 5.1 %collective-permute-start.13 = (bf16[24,2048]{1,0:T(8,128)(2,1)S(1)}, bf16[24,2048]{1,0:T(8,128)(2,1)S(1)}, u32[]{:S(2)}, u32[]{:S(2)}) collective-permute-start(bf16[24,2048]{1,0:T(8,128)(2,1)S(1)} %pad_maximum_fusion.5), channel_id=1, source_target_pairs={{0,2},{1,3},{2,0},{3,1},{4,6},{5,7},{6,4},{7,5},{8,10},{9,11},{10,... | collective-permute-start | bytes 294920 | tf_op jit(solution)/shard_map/ppermute | solution.py:269
  12.7 6.1 %collective-permute-start.12 = (bf16[24,2048]{1,0:T(8,128)(2,1)S(1)}, bf16[24,2048]{1,0:T(8,128)(2,1)S(1)}, u32[]{:S(2)}, u32[]{:S(2)}) collective-permute-start(bf16[24,2048]{1,0:T(8,128)(2,1)S(1)} %pad_maximum_fusion.4), channel_id=1, source_target_pairs={{0,1},{1,0},{2,3},{3,2},{4,5},{5,4},{6,7},{7,6},{8,9},{9,8},{10,11... | collective-permute-start | bytes 294920 | tf_op jit(solution)/shard_map/ppermute | solution.py:269
  15.3 18.9 %collective-permute-start = (bf16[24,4096]{1,0:T(8,128)(2,1)}, bf16[24,4096]{1,0:T(8,128)(2,1)S(1)}, u32[]{:S(2)}, u32[]{:S(2)}) collective-permute-start(bf16[24,4096]{1,0:T(8,128)(2,1)} %pick.1), channel_id=1, source_target_pairs={{0,8},{4,12},{8,16},{12,20},{16,24},{20,28},{24,0},{28,4},{1,9},{5... | collective-permute-start | bytes 589832 | tf_op jit(solution)/shard_map/ppermute | solution.py:261
  17.2 17.1 %collective-permute-start.4 = (bf16[24,4096]{1,0:T(8,128)(2,1)}, bf16[24,4096]{1,0:T(8,128)(2,1)S(1)}, u32[]{:S(2)}, u32[]{:S(2)}) collective-permute-start(bf16[24,4096]{1,0:T(8,128)(2,1)} %param.11), channel_id=1, source_target_pairs={{0,8},{4,12},{8,16},{12,20},{16,24},{20,28},{24,0},{28,4},{1,9},{5... | collective-permute-start | bytes 589832 | tf_op jit(solution)/shard_map/ppermute | solution.py:261
  18.8 37.2 %collective-permute-start.5 = (bf16[24,4096]{1,0:T(8,128)(2,1)}, bf16[24,4096]{1,0:T(8,128)(2,1)S(1)}, u32[]{:S(2)}, u32[]{:S(2)}) collective-permute-start(bf16[24,4096]{1,0:T(8,128)(2,1)} %param.11), channel_id=1, source_target_pairs={{0,16},{4,20},{8,24},{12,28},{16,0},{20,4},{24,8},{28,12},{1,17},{... | collective-permute-start | bytes 589832 | tf_op jit(solution)/shard_map/ppermute | solution.py:261
  20.4 35.7 %collective-permute-start.6 = (bf16[24,4096]{1,0:T(8,128)(2,1)S(1)}, bf16[24,4096]{1,0:T(8,128)(2,1)S(1)}, u32[]{:S(2)}, u32[]{:S(2)}) collective-permute-start(bf16[24,4096]{1,0:T(8,128)(2,1)S(1)} %copy-done.1), channel_id=1, source_target_pairs={{0,24},{4,28},{8,0},{12,4},{16,8},{20,12},{24,16},{28,20},{1,25},{... | collective-permute-start | bytes 589832 | tf_op jit(solution)/shard_map/ppermute | solution.py:261
  34.2 22.5 %collective-permute-start.17 = (bf16[4,24,2048]{2,1,0:T(8,128)(2,1)S(1)}, bf16[4,24,2048]{2,1,0:T(8,128)(2,1)S(1)}, u32[]{:S(2)}, u32[]{:S(2)}) collective-permute-start(bf16[4,24,2048]{2,1,0:T(8,128)(2,1)S(1)} %get-tuple-element.57), channel_id=1, source_target_pairs={{0,24},{4,28},{8,0},{12,4},{16,8},{20,12},{24,16},{28,20},{1,25},{... | collective-permute-start | bytes 1179656 | tf_op jit(solution)/shard_map/ppermute | solution.py:261
  34.2 41.1 %collective-permute-start.16 = (bf16[4,24,2048]{2,1,0:T(8,128)(2,1)S(1)}, bf16[4,24,2048]{2,1,0:T(8,128)(2,1)S(1)}, u32[]{:S(2)}, u32[]{:S(2)}) collective-permute-start(bf16[4,24,2048]{2,1,0:T(8,128)(2,1)S(1)} %get-tuple-element.57), channel_id=1, source_target_pairs={{0,16},{4,20},{8,24},{12,28},{16,0},{20,4},{24,8},{28,12},{1,17},{... | collective-permute-start | bytes 1179656 | tf_op jit(solution)/shard_map/ppermute | solution.py:261
  34.3 41.0 %collective-permute-start.15 = (bf16[4,24,2048]{2,1,0:T(8,128)(2,1)S(1)}, bf16[4,24,2048]{2,1,0:T(8,128)(2,1)S(1)}, u32[]{:S(2)}, u32[]{:S(2)}) collective-permute-start(bf16[4,24,2048]{2,1,0:T(8,128)(2,1)S(1)} %get-tuple-element.57), channel_id=1, source_target_pairs={{0,8},{4,12},{8,16},{12,20},{16,24},{20,28},{24,0},{28,4},{1,9},{5... | collective-permute-start | bytes 1179656 | tf_op jit(solution)/shard_map/ppermute | solution.py:261
  56.0 19.7 %collective-permute-start.3 = (bf16[96,4096]{1,0:T(8,128)(2,1)S(1)}, bf16[96,4096]{1,0:T(8,128)(2,1)S(1)}, u32[]{:S(2)}, u32[]{:S(2)}) collective-permute-start(bf16[96,4096]{1,0:T(8,128)(2,1)S(1)} %pad_maximum_fusion.2.refs_0_), channel_id=1, source_target_pairs={{0,4},{4,0},{8,12},{12,8},{16,20},{20,16},{24,28},{28,24},{1,5},{5... | collective-permute-start | bytes 2359304 | tf_op jit(solution)/shard_map/ppermute | solution.py:265
  56.2 30.5 %collective-permute-start.7 = (bf16[96,4096]{1,0:T(8,128)(2,1)S(1)}, bf16[96,4096]{1,0:T(8,128)(2,1)S(1)}, u32[]{:S(2)}, u32[]{:S(2)}) collective-permute-start(bf16[96,4096]{1,0:T(8,128)(2,1)S(1)} %constant_dynamic-update-slice_fusion.refs_0_), channel_id=1, source_target_pairs={{0,4},{4,0},{8,12},{12,8},{16,20},{20,16},{24,28},{28,24},{1,5},{5... | collective-permute-start | bytes 2359304 | tf_op jit(solution)/shard_map/ppermute | solution.py:265
  75.6 57.0 %collective-permute-start.18 = (bf16[4,4,24,2048]{3,2,0,1:T(8,128)(2,1)S(1)}, bf16[4,4,24,2048]{3,2,0,1:T(8,128)(2,1)S(1)}, u32[]{:S(2)}, u32[]{:S(2)}) collective-permute-start(bf16[4,4,24,2048]{3,2,0,1:T(8,128)(2,1)S(1)} %get-tuple-element.51), channel_id=1, source_target_pairs={{0,4},{4,0},{8,12},{12,8},{16,20},{20,16},{24,28},{28,24},{1,5},{5... | collective-permute-start | bytes 4718600 | tf_op jit(solution)/shard_map/ppermute | solution.py:265
  110.7 23.2 %collective-permute-start.8 = (bf16[2,96,4096]{2,1,0:T(8,128)(2,1)S(1)}, bf16[2,96,4096]{2,1,0:T(8,128)(2,1)S(1)}, u32[]{:S(2)}, u32[]{:S(2)}) collective-permute-start(bf16[2,96,4096]{2,1,0:T(8,128)(2,1)S(1)} %get-tuple-element.32), channel_id=1, source_target_pairs={{0,4},{4,0},{8,12},{12,8},{16,20},{20,16},{24,28},{28,24},{1,5},{5... | collective-permute-start | bytes 4718600 | tf_op jit(solution)/shard_map/ppermute | solution.py:265
  111.3 17.4 %collective-permute-start.28 = (bf16[192,1792]{1,0:T(8,128)(2,1)S(1)}, bf16[192,1792]{1,0:T(8,128)(2,1)S(1)}, u32[]{:S(2)}, u32[]{:S(2)}) collective-permute-start(bf16[192,1792]{1,0:T(8,128)(2,1)S(1)} %get-tuple-element.42.refs_0_), channel_id=1, source_target_pairs={{0,2},{1,3},{2,0},{3,1},{4,6},{5,7},{6,4},{7,5},{8,10},{9,11},{10,... | collective-permute-start | bytes 2064392 | tf_op jit(solution)/shard_map/ppermute | solution.py:269
  112.7 18.3 %collective-permute-start.27 = (bf16[192,1792]{1,0:T(8,128)(2,1)S(1)}, bf16[192,1792]{1,0:T(8,128)(2,1)S(1)}, u32[]{:S(2)}, u32[]{:S(2)}) collective-permute-start(bf16[192,1792]{1,0:T(8,128)(2,1)S(1)} %get-tuple-element.42.refs_0_), channel_id=1, source_target_pairs={{0,1},{1,0},{2,3},{3,2},{4,5},{5,4},{6,7},{7,6},{8,9},{9,8},{10,11... | collective-permute-start | bytes 2064392 | tf_op jit(solution)/shard_map/ppermute | solution.py:269
  114.2 31.6 %collective-permute-start.19 = (bf16[192,1792]{1,0:T(8,128)(2,1)S(1)}, bf16[192,1792]{1,0:T(8,128)(2,1)S(1)}, u32[]{:S(2)}, u32[]{:S(2)}) collective-permute-start(bf16[192,1792]{1,0:T(8,128)(2,1)S(1)} %get-tuple-element.33.refs_2_), channel_id=1, source_target_pairs={{0,1},{1,0},{2,3},{3,2},{4,5},{5,4},{6,7},{7,6},{8,9},{9,8},{10,11... | collective-permute-start | bytes 2064392 | tf_op jit(solution)/shard_map/ppermute | solution.py:269
  128.7 18.3 %collective-permute-start.20 = (bf16[192,1792]{1,0:T(8,128)(2,1)S(1)}, bf16[192,1792]{1,0:T(8,128)(2,1)S(1)}, u32[]{:S(2)}, u32[]{:S(2)}) collective-permute-start(bf16[192,1792]{1,0:T(8,128)(2,1)S(1)} %get-tuple-element.33.refs_2_), channel_id=1, source_target_pairs={{0,2},{1,3},{2,0},{3,1},{4,6},{5,7},{6,4},{7,5},{8,10},{9,11},{10,... | collective-permute-start | bytes 2064392 | tf_op jit(solution)/shard_map/ppermute | solution.py:269
  131.0 29.5 %collective-permute-start.23 = (bf16[192,1792]{1,0:T(8,128)(2,1)S(1)}, bf16[192,1792]{1,0:T(8,128)(2,1)S(1)}, u32[]{:S(2)}, u32[]{:S(2)}) collective-permute-start(bf16[192,1792]{1,0:T(8,128)(2,1)S(1)} %get-tuple-element.39.refs_1_), channel_id=1, source_target_pairs={{0,1},{1,0},{2,3},{3,2},{4,5},{5,4},{6,7},{7,6},{8,9},{9,8},{10,11... | collective-permute-start | bytes 2064392 | tf_op jit(solution)/shard_map/ppermute | solution.py:269
  132.6 30.8 %collective-permute-start.24 = (bf16[192,1792]{1,0:T(8,128)(2,1)S(1)}, bf16[192,1792]{1,0:T(8,128)(2,1)S(1)}, u32[]{:S(2)}, u32[]{:S(2)}) collective-permute-start(bf16[192,1792]{1,0:T(8,128)(2,1)S(1)} %get-tuple-element.39.refs_1_), channel_id=1, source_target_pairs={{0,2},{1,3},{2,0},{3,1},{4,6},{5,7},{6,4},{7,5},{8,10},{9,11},{10,... | collective-permute-start | bytes 2064392 | tf_op jit(solution)/shard_map/ppermute | solution.py:269
  133.9 32.8 %collective-permute-start.29 = (bf16[96,1792]{1,0:T(8,128)(2,1)S(1)}, bf16[96,1792]{1,0:T(8,128)(2,1)S(1)}, u32[]{:S(2)}, u32[]{:S(2)}) collective-permute-start(bf16[96,1792]{1,0:T(8,128)(2,1)S(1)} %slice.88), channel_id=1, source_target_pairs={{0,1},{1,0},{2,3},{3,2},{4,5},{5,4},{6,7},{7,6},{8,9},{9,8},{10,11... | collective-permute-start | bytes 1032200 | tf_op jit(solution)/shard_map/ppermute | solution.py:269
  145.8 22.4 %collective-permute-start.30 = (bf16[96,1792]{1,0:T(8,128)(2,1)S(1)}, bf16[96,1792]{1,0:T(8,128)(2,1)S(1)}, u32[]{:S(2)}, u32[]{:S(2)}) collective-permute-start(bf16[96,1792]{1,0:T(8,128)(2,1)S(1)} %slice.89), channel_id=1, source_target_pairs={{0,2},{1,3},{2,0},{3,1},{4,6},{5,7},{6,4},{7,5},{8,10},{9,11},{10,... | collective-permute-start | bytes 1032200 | tf_op jit(solution)/shard_map/ppermute | solution.py:269
  147.0 42.6 %collective-permute-start.9 = (bf16[2,24,4096]{2,1,0:T(8,128)(2,1)S(1)}, bf16[2,24,4096]{2,1,0:T(8,128)(2,1)S(1)}, u32[]{:S(2)}, u32[]{:S(2)}) collective-permute-start(bf16[2,24,4096]{2,1,0:T(8,128)(2,1)S(1)} %get-tuple-element.55), channel_id=1, source_target_pairs={{0,24},{4,28},{8,0},{12,4},{16,8},{20,12},{24,16},{28,20},{1,25},{... | collective-permute-start | bytes 1179656 | tf_op jit(solution)/shard_map/ppermute | solution.py:261
  160.5 29.1 %collective-permute-start.10 = (bf16[2,24,4096]{2,1,0:T(8,128)(2,1)S(1)}, bf16[2,24,4096]{2,1,0:T(8,128)(2,1)S(1)}, u32[]{:S(2)}, u32[]{:S(2)}) collective-permute-start(bf16[2,24,4096]{2,1,0:T(8,128)(2,1)S(1)} %get-tuple-element.54), channel_id=1, source_target_pairs={{0,16},{4,20},{8,24},{12,28},{16,0},{20,4},{24,8},{28,12},{1,17},{... | collective-permute-start | bytes 1179656 | tf_op jit(solution)/shard_map/ppermute | solution.py:261
  163.3 26.2 %collective-permute-start.11 = (bf16[2,24,4096]{2,1,0:T(8,128)(2,1)S(1)}, bf16[2,24,4096]{2,1,0:T(8,128)(2,1)S(1)}, u32[]{:S(2)}, u32[]{:S(2)}) collective-permute-start(bf16[2,24,4096]{2,1,0:T(8,128)(2,1)S(1)} %get-tuple-element.53), channel_id=1, source_target_pairs={{0,8},{4,12},{8,16},{12,20},{16,24},{20,28},{24,0},{28,4},{1,9},{5... | collective-permute-start | bytes 1179656 | tf_op jit(solution)/shard_map/ppermute | solution.py:261
  166.7 8.9 %collective-permute-start.21 = (bf16[96,1792]{1,0:T(8,128)(2,1)S(1)}, bf16[96,1792]{1,0:T(8,128)(2,1)S(1)}, u32[]{:S(2)}, u32[]{:S(2)}) collective-permute-start(bf16[96,1792]{1,0:T(8,128)(2,1)S(1)} %slice.67), channel_id=1, source_target_pairs={{0,1},{1,0},{2,3},{3,2},{4,5},{5,4},{6,7},{7,6},{8,9},{9,8},{10,11... | collective-permute-start | bytes 1032200 | tf_op jit(solution)/shard_map/ppermute | solution.py:269
  168.2 8.9 %collective-permute-start.22 = (bf16[96,1792]{1,0:T(8,128)(2,1)S(1)}, bf16[96,1792]{1,0:T(8,128)(2,1)S(1)}, u32[]{:S(2)}, u32[]{:S(2)}) collective-permute-start(bf16[96,1792]{1,0:T(8,128)(2,1)S(1)} %slice.68), channel_id=1, source_target_pairs={{0,2},{1,3},{2,0},{3,1},{4,6},{5,7},{6,4},{7,5},{8,10},{9,11},{10,... | collective-permute-start | bytes 1032200 | tf_op jit(solution)/shard_map/ppermute | solution.py:269
  175.6 8.1 %collective-permute-start.25 = (bf16[96,1792]{1,0:T(8,128)(2,1)S(1)}, bf16[96,1792]{1,0:T(8,128)(2,1)S(1)}, u32[]{:S(2)}, u32[]{:S(2)}) collective-permute-start(bf16[96,1792]{1,0:T(8,128)(2,1)S(1)} %slice.76), channel_id=1, source_target_pairs={{0,1},{1,0},{2,3},{3,2},{4,5},{5,4},{6,7},{7,6},{8,9},{9,8},{10,11... | collective-permute-start | bytes 1032200 | tf_op jit(solution)/shard_map/ppermute | solution.py:269
  177.2 7.8 %collective-permute-start.26 = (bf16[96,1792]{1,0:T(8,128)(2,1)S(1)}, bf16[96,1792]{1,0:T(8,128)(2,1)S(1)}, u32[]{:S(2)}, u32[]{:S(2)}) collective-permute-start(bf16[96,1792]{1,0:T(8,128)(2,1)S(1)} %slice.77), channel_id=1, source_target_pairs={{0,2},{1,3},{2,0},{3,1},{4,6},{5,7},{6,4},{7,5},{8,10},{9,11},{10,... | collective-permute-start | bytes 1032200 | tf_op jit(solution)/shard_map/ppermute | solution.py:269

commit v6 on v5

--- a/solution.py
+++ b/solution.py
@@ -45,7 +45,7 @@
     return jnp.dot(left, right, preferred_element_type=F32)
 
 
-def pick_kernel(flag_hbm, tokens_hbm, out_ref, flag_ref, tokens_ref, sems):
+def pick_kernel(flag_hbm, tokens_hbm, out_ref, left_ref, right_ref, flag_ref, tokens_ref, sems):
     rows = out_ref.shape[0]
     count = tokens_ref.shape[0]
     copies = (pltpu.make_async_copy(flag_hbm, flag_ref, sems.at[0]),
@@ -62,15 +62,20 @@
     chosen = (jnp.broadcast_to(ranks, (rows, count)) == slots) & (
         jnp.broadcast_to(flags, (rows, count)) == 1.0
     )
-    out_ref[...] = nn_dot(chosen.astype(BF), tokens_ref[...]).astype(BF)
+    picked = nn_dot(chosen.astype(BF), tokens_ref[...]).astype(BF)
+    middle = left_ref.shape[1]
+    out_ref[...] = picked
+    left_ref[...] = picked[:, :middle]
+    right_ref[...] = picked[:, middle:]
 
 
 def pick(modality, tokens, rows):
+    width = tokens.shape[1]
     return pl.pallas_call(
         pick_kernel,
         in_specs=[HBM, HBM],
-        out_specs=VMEM,
-        out_shape=shape((rows, tokens.shape[1])),
+        out_specs=[VMEM] * 3,
+        out_shape=[shape((rows, width)), shape((rows, width // 2)), shape((rows, width // 2))],
         scratch_shapes=[
             pltpu.VMEM((1, modality.shape[0]), modality.dtype),
             pltpu.VMEM(tokens.shape, BF),
@@ -81,7 +86,7 @@
     )(modality.reshape(1, -1), tokens)
 
 
-def streamed(steps, depth, copies, body):
+def streamed(steps, depth, copies, body, first):
     depth = min(depth, steps)
 
     def start(j):
@@ -90,6 +95,7 @@
 
     for j in range(depth):
         start(jnp.int32(j))
+    first()
 
     @pl.loop(0, steps)
     def _(j):
@@ -106,43 +112,56 @@
 DEPTH = 5
 
 
-def enter_kernel(tile, xa_ref, xb_ref, gate_hbm, up_hbm, hid_ref, active_ref, turn_ref,
-                 x_ref, gate_ref, up_ref, sems):
-    half = xa_ref.shape[0]
-    x_ref[:half] = xa_ref[...]
-    x_ref[half:] = xb_ref[...]
+def enter_kernel(tile, last, xa_ref, xb_ref, gate_hbm, up_hbm, *refs):
+    (*before, hid_ref, active_ref, turn_ref) = refs[:5] if last else (None, *refs[:2])
+    x_ref, gate_ref, up_ref, sems = refs[5:] if last else refs[2:]
+    half, depth = xa_ref.shape
+    rows = pl.ds(depth if last else 0, depth)
+
+    def first():
+        x_ref[:half] = xa_ref[...]
+        x_ref[half:] = xb_ref[...]
 
     def copies(j, slot):
         column = pl.ds(pl.multiple_of(j * tile, tile), tile)
         return (
-            pltpu.make_async_copy(gate_hbm.at[:, column], gate_ref.at[slot], sems.at[0, slot]),
-            pltpu.make_async_copy(up_hbm.at[:, column], up_ref.at[slot], sems.at[1, slot]),
+            pltpu.make_async_copy(gate_hbm.at[rows, column], gate_ref.at[slot], sems.at[0, slot]),
+            pltpu.make_async_copy(up_hbm.at[rows, column], up_ref.at[slot], sems.at[1, slot]),
         )
 
     def body(j, slot):
         column = pl.ds(pl.multiple_of(j * tile, tile), tile)
         gate_proj = nn_dot(x_ref[...], gate_ref[slot])
         up_proj = nn_dot(x_ref[...], up_ref[slot])
+        if not last:
+            active_ref[:, column] = gate_proj
+            turn_ref[:, column] = up_proj
+            return
+        gate_proj = gate_proj + before[0][:, column]
+        up_proj = up_proj + before[1][:, column]
         sig = jax.nn.sigmoid(gate_proj)
         active = gate_proj * sig
         hid_ref[:, column] = (active * up_proj).astype(BF)
         active_ref[:, column] = active
         turn_ref[:, column] = up_proj * (sig * (1.0 + gate_proj * (1.0 - sig)))
 
-    streamed(gate_hbm.shape[1] // tile, gate_ref.shape[0], copies, body)
-
-
-def enter(own, other, gate, up):
+    streamed(gate_hbm.shape[1] // tile, gate_ref.shape[0], copies, body, first)
+
+
+def enter(own, other, gate, up, *before):
     half, width = own.shape
     units = gate.shape[1]
     rows = 2 * half
     tile = tile_of(units, (256, 128))
     depth = min(DEPTH, units // tile)
+    last = len(before) > 0
+    wide = shape((rows, units), F32)
+    outs = [shape((rows, units)), wide, wide] if last else [wide, wide]
     return pl.pallas_call(
-        lambda *refs: enter_kernel(tile, *refs),
-        in_specs=[VMEM, VMEM, HBM, HBM],
-        out_specs=[VMEM] * 3,
-        out_shape=[shape((rows, units)), shape((rows, units), F32), shape((rows, units), F32)],
+        lambda *refs: enter_kernel(tile, last, *refs),
+        in_specs=[VMEM, VMEM, HBM, HBM] + [VMEM] * len(before),
+        out_specs=[VMEM] * len(outs),
+        out_shape=outs,
         scratch_shapes=[
             pltpu.VMEM((rows, width), BF),
             pltpu.VMEM((depth, width, tile), BF),
@@ -152,14 +171,16 @@
         compiler_params=grant((rows, width, BF), (2 * depth * tile, width, BF), least=46 * MIB),
         cost_estimate=cost(4 * rows * width * units, 4 * width * units),
         name="enter",
-    )(own, other, gate, up)
+    )(own, other, gate, up, *before)
 
 
 def turn_kernel(tile, ca_ref, cb_ref, down_hbm, active_ref, factor_ref, gb_ref, ub_ref,
                 c_ref, down_ref, sems):
     half = ca_ref.shape[0]
-    c_ref[:half] = ca_ref[...]
-    c_ref[half:] = cb_ref[...]
+
+    def first():
+        c_ref[:half] = ca_ref[...]
+        c_ref[half:] = cb_ref[...]
 
     def copies(j, slot):
         row = pl.ds(pl.multiple_of(j * tile, tile), tile)
@@ -171,7 +192,7 @@
         gb_ref[:, span] = (back * factor_ref[:, span]).astype(BF)
         ub_ref[:, span] = (back * active_ref[:, span]).astype(BF)
 
-    streamed(down_hbm.shape[0] // tile, down_ref.shape[0], copies, body)
+    streamed(down_hbm.shape[0] // tile, down_ref.shape[0], copies, body, first)
 
 
 def turn(own, other, down, active, factor):
@@ -218,7 +239,7 @@
         own_ref[1, :, span] = result[:half]
         other_ref[1, :, span] = result[half:]
 
-    streamed(gate_hbm.shape[0] // step, gate_ref.shape[0], copies, body)
+    streamed(gate_hbm.shape[0] // step, gate_ref.shape[0], copies, body, lambda: None)
 
 
 def leave(hid, gb, ub, gate, up, down):
@@ -312,13 +333,16 @@
     def stack(held):
         return jnp.concatenate(sum(held, []), axis=0)
 
-    block = pick(modality, tokens, count)
-    tok = gathered(block)
-    tok_mate = swap(tok)
+    block, *sides = pick(modality, tokens, count)
+    tok = [gathered(side) for side in sides]
+    tok_mate = []
+    for side in tok:
+        tok_mate.append(swap(side))
     tok_all, cot_all = slices_of(block, out_grad)
     cot = gathered(out_grad)
     cot_mate = swap(cot)
-    hid, active, factor = enter(tok, tok_mate, gate, up)
+    before = enter(tok[0], tok_mate[0], gate, up)
+    hid, active, factor = enter(tok[1], tok_mate[1], gate, up, *before)
     all_hid = relay(near(hid))
     gb, ub = turn(cot, cot_mate, down, active, factor)
     all_gb = near(gb)

time: 191 us -> 197 us (1.031)
    pallas_call x2 -> x3, Pallas kernels: 13 us -> 14.6 us  [the longest x2 12.6 us: enter(): pl.pallas_call(lambda *refs: enter_kernel(tile, last, *refs), in_specs=[V...]
    ppermute x12 -> x15, starting transfers between devices: 41.2 us -> 42.5 us  [shift(): lax.ppermute(value, 'dp', [(z * CORES + c, (z + k) % ring * CORES + c) fo...]
    ppermute x12 -> x15, waiting for transfers between devices: 29.9 us -> 29.9 us  [shift(): lax.ppermute(value, 'dp', [(z * CORES + c, (z + k) % ring * CORES + c) fo...]
  transfers between devices with their start and end apart: 31 -> 35, of which waited for: 13 -> 13; matrix products, arithmetic and copies ran while one was open for 10% -> 10% of each run, Pallas kernels for 18% -> 19%
where the time goes in v6:
time: 197 us
  waiting for transfers between devices  75.9 us (39%)
  starting transfers between devices  59.9 us (30%)
  Pallas kernels  38.6 us (20%)
  matrix products  13.6 us (7%)
  local copies, waits for them, and re-layouts  5.74 us (3%)
  other arithmetic  2.25 us (1%)
    ppermute x15, waiting for transfers between devices, across(): return lax.ppermute(value, 'seq', [(g, g ^ mask) for g in range(groups)])  46 us
    ppermute x15, starting transfers between devices, shift(): lax.ppermute(value, 'dp', [(z * CORES + c, (z + k) % ring * CORES + c) fo...  42.5 us
    ppermute x15, waiting for transfers between devices, shift(): lax.ppermute(value, 'dp', [(z * CORES + c, (z + k) % ring * CORES + c) fo...  29.9 us
    pallas_call x1, Pallas kernels, leave(): pl.pallas_call(lambda *refs: leave_kernel(step, *refs), in_specs=[VMEM] *...  16.4 us
    ppermute x15, starting transfers between devices, across(): return lax.ppermute(value, 'seq', [(g, g ^ mask) for g in range(groups)])  16.1 us
    dot_general x3, matrix products, rows_dot(): lax.dot_general(left, right, (((0,), (0,)), ((), ())), preferred_element_...  13.6 us
    pallas_call x2, Pallas kernels, enter(): pl.pallas_call(lambda *refs: enter_kernel(tile, last, *refs), in_specs=[V...  12.6 us
    pallas_call x1, Pallas kernels, turn(): pl.pallas_call(lambda *refs: turn_kernel(tile, *refs), in_specs=[VMEM, VM...  7.65 us
  transfers between devices with their start and end apart: 35, of which 13 were waited for; matrix products, arithmetic and copies ran while one was open for 10% of the time, Pallas kernels for 19%

profile of v6, /device:TPU:0, one launch (start us, length us, event | category | flops | bytes accessed | tf_op | source)
XLA Modules:
  0.0 197.1 jit_solution(1996248455909524288)
XLA Ops:
  0.6 2.0 %pick.1 = (bf16[24,4096]{1,0:T(8,128)(2,1)}, bf16[24,2048]{1,0:T(8,128)(2,1)}, bf16[24,2048]{1,0:T(8,128)(2,1)}) custom-call(s32[1,32]{1,0:T(1,128)} %bitcast.69, bf16[32,4096]{1,0:T(8,128)(2,1)} %tokens_hbm.1), custom_call_target="tpu_custom_call" | custom-call | tf_op jit(solution)/shard_map/pick/pallas_call | solution.py:74
  2.7 3.1 %collective-permute-start = (bf16[24,2048]{1,0:T(8,128)(2,1)}, bf16[24,2048]{1,0:T(8,128)(2,1)S(1)}, u32[]{:S(2)}, u32[]{:S(2)}) collective-permute-start(bf16[24,2048]{1,0:T(8,128)(2,1)} %get-tuple-element.31), channel_id=1, source_target_pairs={{0,8},{4,12},{8,16},{12,20},{16,24},{20,28},{24,0},{28,4},{1,9},{5... | collective-permute-start | bytes 294920 | tf_op jit(solution)/shard_map/ppermute | solution.py:282
  5.8 2.6 %collective-permute-start.1 = (bf16[24,2048]{1,0:T(8,128)(2,1)}, bf16[24,2048]{1,0:T(8,128)(2,1)S(1)}, u32[]{:S(2)}, u32[]{:S(2)}) collective-permute-start(bf16[24,2048]{1,0:T(8,128)(2,1)} %get-tuple-element.31), channel_id=1, source_target_pairs={{0,16},{4,20},{8,24},{12,28},{16,0},{20,4},{24,8},{28,12},{1,17},{... | collective-permute-start | bytes 294920 | tf_op jit(solution)/shard_map/ppermute | solution.py:282
  8.4 0.9 constant_dynamic-slice_fusion.6
  9.3 0.9 constant_dynamic-slice_fusion.7
  10.2 2.5 %collective-permute-start.18 = (bf16[24,2048]{1,0:T(8,128)(2,1)S(1)}, bf16[24,2048]{1,0:T(8,128)(2,1)S(1)}, u32[]{:S(2)}, u32[]{:S(2)}) collective-permute-start(bf16[24,2048]{1,0:T(8,128)(2,1)S(1)} %pad_maximum_fusion.5), channel_id=1, source_target_pairs={{0,3},{1,2},{2,1},{3,0},{4,7},{5,6},{6,5},{7,4},{8,11},{9,10},{10,... | collective-permute-start | bytes 294920 | tf_op jit(solution)/shard_map/ppermute | solution.py:290
  12.7 0.6 collective-permute-start.17
  13.3 0.6 collective-permute-start.16
  13.9 0.9 constant_dynamic-update-slice_fusion.3
  14.8 0.9 constant_dynamic-update-slice_fusion.11
  15.7 0.9 constant_dynamic-update-slice_fusion.7
  16.6 1.4 collective-permute-start.2
  18.0 0.7 collective-permute-start.4
  18.7 0.7 collective-permute-start.5
  19.5 2.5 %collective-permute-start.6 = (bf16[24,2048]{1,0:T(8,128)(2,1)S(1)}, bf16[24,2048]{1,0:T(8,128)(2,1)S(1)}, u32[]{:S(2)}, u32[]{:S(2)}) collective-permute-start(bf16[24,2048]{1,0:T(8,128)(2,1)S(1)} %copy-done.1), channel_id=1, source_target_pairs={{0,24},{4,28},{8,0},{12,4},{16,8},{20,12},{24,16},{28,20},{1,25},{... | collective-permute-start | bytes 294920 | tf_op jit(solution)/shard_map/ppermute | solution.py:282
  22.0 0.6 collective-permute-start.8
  22.7 0.7 collective-permute-done.2
  23.4 0.8 collective-permute-start.9
  24.2 1.5 collective-permute-done.4
  25.8 1.4 collective-permute-start.10
  27.2 6.9 %collective-permute-done.5 = bf16[24,2048]{1,0:T(8,128)(2,1)S(1)} collective-permute-done((bf16[24,2048]{1,0:T(8,128)(2,1)}, bf16[24,2048]{1,0:T(8,128)(2,1)S(1)}, u32[]{:S(2)}, u32[]{:S(2)}) %collective-permute-start.5) | collective-permute-done | bytes 98336 | tf_op jit(solution)/shard_map/ppermute | solution.py:282
  34.1 3.2 %collective-permute-start.20 = (bf16[4,24,2048]{2,1,0:T(8,128)(2,1)S(1)}, bf16[4,24,2048]{2,1,0:T(8,128)(2,1)S(1)}, u32[]{:S(2)}, u32[]{:S(2)}) collective-permute-start(bf16[4,24,2048]{2,1,0:T(8,128)(2,1)S(1)} %get-tuple-element.67), channel_id=1, source_target_pairs={{0,16},{4,20},{8,24},{12,28},{16,0},{20,4},{24,8},{28,12},{1,17},{... | collective-permute-start | bytes 1179656 | tf_op jit(solution)/shard_map/ppermute | solution.py:282
  37.4 21.3 %collective-permute-start.19 = (bf16[4,24,2048]{2,1,0:T(8,128)(2,1)S(1)}, bf16[4,24,2048]{2,1,0:T(8,128)(2,1)S(1)}, u32[]{:S(2)}, u32[]{:S(2)}) collective-permute-start(bf16[4,24,2048]{2,1,0:T(8,128)(2,1)S(1)} %get-tuple-element.67), channel_id=1, source_target_pairs={{0,8},{4,12},{8,16},{12,20},{16,24},{20,28},{24,0},{28,4},{1,9},{5... | collective-permute-start | bytes 1179656 | tf_op jit(solution)/shard_map/ppermute | solution.py:282
  58.8 0.6 collective-permute-start.7
  59.5 20.7 %collective-permute-done.20 = bf16[4,24,2048]{2,1,0:T(8,128)(2,1)S(1)} collective-permute-done((bf16[4,24,2048]{2,1,0:T(8,128)(2,1)S(1)}, bf16[4,24,2048]{2,1,0:T(8,128)(2,1)S(1)}, u32[]{:S(2)}, u32[]{:S(2)}) %collective-permute-start.20) | collective-permute-done | bytes 393248 | tf_op jit(solution)/shard_map/ppermute | solution.py:282
  80.1 0.3 pad_maximum_fusion.1
  80.5 6.3 %enter.2 = (f32[192,1792]{1,0:T(8,128)S(1)}, f32[192,1792]{1,0:T(8,128)S(1)}) custom-call(bf16[96,2048]{1,0:T(8,128)(2,1)S(1)} %constant_dynamic-update-slice_fusion.4.refs_0_, bf16[96,2048]{1,0:T(8,128)(2,1)S(1)} %collective-permute-done.7.refs_1_, bf16[4096,1792]{1,0:T(8,128)(2,1)} %refs_3_.5, bf16[4096,1792]{1,0:T(8,128)(2,1)} %refs_4_.1), custom_call_target="tpu_custom_call" | custom-call | flops 2818572288 | bytes 14680064 | tf_op jit(solution)/shard_map/enter/pallas_call | solution.py:160
  86.8 6.3 %enter.3 = (bf16[192,1792]{1,0:T(8,128)(2,1)S(1)}, f32[192,1792]{1,0:T(8,128)S(1)}, f32[192,1792]{1,0:T(8,128)S(1)}) custom-call(bf16[96,2048]{1,0:T(8,128)(2,1)S(1)} %constant_dynamic-update-slice_fusion.refs_0_, bf16[96,2048]{1,0:T(8,128)(2,1)S(1)} %collective-permute-done.3.refs_1_, bf16[4096,1792]{1,0:T(8,128)(2,1)} %refs_3_.5, ...), custom_call_target="tpu_custom_call" | custom-call | flops 2818572288 | bytes 14680064 | tf_op jit(solution)/shard_map/enter/pallas_call | solution.py:160
  93.1 7.6 %turn.1 = (bf16[192,1792]{1,0:T(8,128)(2,1)S(1)}, bf16[192,1792]{1,0:T(8,128)(2,1)S(1)}) custom-call(bf16[96,4096]{1,0:T(8,128)(2,1)S(1)} %constant_dynamic-update-slice_fusion.8.refs_0_, bf16[96,4096]{1,0:T(8,128)(2,1)S(1)} %collective-permute-done.11.refs_1_, bf16[1792,4096]{1,0:T(8,128)(2,1)} %refs_5_.1, f32[192,1792]{1,0:T(8,128)S(1)} %get-tuple-element.36.refs_3_, ...), custom_call_target="tpu_custom_call" | custom-call | flops 2818572288 | bytes 14680064 | tf_op jit(solution)/shard_map/turn/pallas_call | solution.py:204
  100.8 16.4 %leave.1 = (bf16[2,96,4096]{2,1,0:T(8,128)(2,1)S(1)}, bf16[2,96,4096]{2,1,0:T(8,128)(2,1)S(1)}) custom-call(bf16[192,1792]{1,0:T(8,128)(2,1)S(1)} %get-tuple-element.52.refs_0_, bf16[192,1792]{1,0:T(8,128)(2,1)S(1)} %get-tuple-element.49.refs_1_, bf16[192,1792]{1,0:T(8,128)(2,1)S(1)} %get-tuple-element.43.refs_2_, bf16[4096,1792]{1,0:T(8,128)(2,1)} %refs_3_.5, ...), custom_call_target="tpu_custom_call" | custom-call | flops 8455716864 | bytes 44040192 | tf_op jit(solution)/shard_map/leave/pallas_call | solution.py:251
  117.1 0.6 collective-permute-start.12
  117.7 1.7 collective-permute-start.32
  119.3 1.4 collective-permute-start.31
  120.8 0.6 collective-permute-start.23
  121.4 13.7 %collective-permute-done.32 = bf16[192,1792]{1,0:T(8,128)(2,1)S(1)} collective-permute-done((bf16[192,1792]{1,0:T(8,128)(2,1)S(1)}, bf16[192,1792]{1,0:T(8,128)(2,1)S(1)}, u32[]{:S(2)}, u32[]{:S(2)}) %collective-permute-start.32) | collective-permute-done | bytes 688160 | tf_op jit(solution)/shard_map/ppermute | solution.py:290
  135.1 1.7 collective-permute-start.24
  136.8 0.9 collective-permute-done.31
  137.7 1.4 collective-permute-start.27
  139.1 0.6 collective-permute-start.28
  139.8 0.4 pad_maximum_fusion
  140.2 0.2 copy.11
  140.4 0.2 copy.12
  140.5 0.5 collective-permute-start.33
  141.0 0.5 add_convert_fusion
  141.5 0.1 slice_bitcast_fusion
  141.6 10.8 %collective-permute-done.23 = bf16[192,1792]{1,0:T(8,128)(2,1)S(1)} collective-permute-done((bf16[192,1792]{1,0:T(8,128)(2,1)S(1)}, bf16[192,1792]{1,0:T(8,128)(2,1)S(1)}, u32[]{:S(2)}, u32[]{:S(2)}) %collective-permute-start.23) | collective-permute-done | bytes 688160 | tf_op jit(solution)/shard_map/ppermute | solution.py:290
  152.4 0.4 collective-permute-start.34
  152.8 0.6 collective-permute-done.24
  153.4 1.8 collective-permute-start.13
  155.4 11.7 %collective-permute-done.27 = bf16[192,1792]{1,0:T(8,128)(2,1)S(1)} collective-permute-done((bf16[192,1792]{1,0:T(8,128)(2,1)S(1)}, bf16[192,1792]{1,0:T(8,128)(2,1)S(1)}, u32[]{:S(2)}, u32[]{:S(2)}) %collective-permute-start.27) | collective-permute-done | bytes 688160 | tf_op jit(solution)/shard_map/ppermute | solution.py:290
  167.1 1.1 collective-permute-start.14
  168.2 1.3 collective-permute-start.15
  169.6 3.8 %collective-permute-done.33 = bf16[96,1792]{1,0:T(8,128)(2,1)S(1)} collective-permute-done((bf16[96,1792]{1,0:T(8,128)(2,1)S(1)}, bf16[96,1792]{1,0:T(8,128)(2,1)S(1)}, u32[]{:S(2)}, u32[]{:S(2)}) %collective-permute-start.33) | collective-permute-done | bytes 344096 | tf_op jit(solution)/shard_map/ppermute | solution.py:290
  173.3 1.4 collective-permute-start.25
  174.8 0.7 collective-permute-start.26
  175.7 4.5 %convolution_convert_fusion = bf16[1792,1024]{1,0:T(8,128)(2,1)} fusion(bf16[768,1792]{1,0:T(8,128)(2,1)S(1)} %constant_dynamic-update-slice_fusion.22, bf16[768,1024]{1,0:T(8,128)(2,1)S(1)} %bitcast.61), kind=kOutput, calls=%fused_computation | convolution fusion | flops 2820407296 | bytes 7995392 | tf_op jit(solution)/shard_map/dot_general | solution.py:269
  180.4 1.9 collective-permute-done.25
  182.3 1.4 collective-permute-start.29
  183.7 0.6 collective-permute-start.30
  184.4 4.5 %convolution_convert_fusion.2 = bf16[1024,1792]{1,0:T(8,128)(2,1)} fusion(bf16[768,1024]{1,0:T(8,128)(2,1)S(1)} %bitcast.59, bf16[768,1792]{1,0:T(8,128)(2,1)S(1)} %constant_dynamic-update-slice_fusion.12), kind=kOutput, calls=%fused_computation.2 | convolution fusion | flops 2820407296 | bytes 7995392 | tf_op jit(solution)/shard_map/dot_general | solution.py:269
  188.9 1.4 collective-permute-done.29
  190.3 1.2 collective-permute-done.30
  191.6 4.5 %convolution_convert_fusion.1 = bf16[1024,1792]{1,0:T(8,128)(2,1)} fusion(bf16[768,1024]{1,0:T(8,128)(2,1)S(1)} %bitcast.60, bf16[768,1792]{1,0:T(8,128)(2,1)S(1)} %constant_dynamic-update-slice_fusion.17), kind=kOutput, calls=%fused_computation.1 | convolution fusion | flops 2820407296 | bytes 7995392 | tf_op jit(solution)/shard_map/dot_general | solution.py:269
  196.2 0.9 fusion.1
  (65 shorter events, 1.2 us)
Async XLA Ops:
  2.6 16.9 %copy-start.1 = (bf16[24,2048]{1,0:T(8,128)(2,1)S(1)}, bf16[24,2048]{1,0:T(8,128)(2,1)}, u32[]{:S(2)}) copy-start(bf16[24,2048]{1,0:T(8,128)(2,1)} %get-tuple-element.32) | copy-start | bytes 294916
  2.7 19.4 %copy-start = (bf16[24,4096]{1,0:T(8,128)(2,1)S(1)}, bf16[24,4096]{1,0:T(8,128)(2,1)}, u32[]{:S(2)}) copy-start(bf16[24,4096]{1,0:T(8,128)(2,1)} %param.11) | copy-start | bytes 589828
  2.7 16.8 %collective-permute-start = (bf16[24,2048]{1,0:T(8,128)(2,1)}, bf16[24,2048]{1,0:T(8,128)(2,1)S(1)}, u32[]{:S(2)}, u32[]{:S(2)}) collective-permute-start(bf16[24,2048]{1,0:T(8,128)(2,1)} %get-tuple-element.31), channel_id=1, source_target_pairs={{0,8},{4,12},{8,16},{12,20},{16,24},{20,28},{24,0},{28,4},{1,9},{5... | collective-permute-start | bytes 294920 | tf_op jit(solution)/shard_map/ppermute | solution.py:282
  5.8 16.2 %collective-permute-start.1 = (bf16[24,2048]{1,0:T(8,128)(2,1)}, bf16[24,2048]{1,0:T(8,128)(2,1)S(1)}, u32[]{:S(2)}, u32[]{:S(2)}) collective-permute-start(bf16[24,2048]{1,0:T(8,128)(2,1)} %get-tuple-element.31), channel_id=1, source_target_pairs={{0,16},{4,20},{8,24},{12,28},{16,0},{20,4},{24,8},{28,12},{1,17},{... | collective-permute-start | bytes 294920 | tf_op jit(solution)/shard_map/ppermute | solution.py:282
  10.2 6.5 %collective-permute-start.18 = (bf16[24,2048]{1,0:T(8,128)(2,1)S(1)}, bf16[24,2048]{1,0:T(8,128)(2,1)S(1)}, u32[]{:S(2)}, u32[]{:S(2)}) collective-permute-start(bf16[24,2048]{1,0:T(8,128)(2,1)S(1)} %pad_maximum_fusion.5), channel_id=1, source_target_pairs={{0,3},{1,2},{2,1},{3,0},{4,7},{5,6},{6,5},{7,4},{8,11},{9,10},{10,... | collective-permute-start | bytes 294920 | tf_op jit(solution)/shard_map/ppermute | solution.py:290
  12.7 5.3 %collective-permute-start.17 = (bf16[24,2048]{1,0:T(8,128)(2,1)S(1)}, bf16[24,2048]{1,0:T(8,128)(2,1)S(1)}, u32[]{:S(2)}, u32[]{:S(2)}) collective-permute-start(bf16[24,2048]{1,0:T(8,128)(2,1)S(1)} %pad_maximum_fusion.4), channel_id=1, source_target_pairs={{0,2},{1,3},{2,0},{3,1},{4,6},{5,7},{6,4},{7,5},{8,10},{9,11},{10,... | collective-permute-start | bytes 294920 | tf_op jit(solution)/shard_map/ppermute | solution.py:290
  13.3 5.5 %collective-permute-start.16 = (bf16[24,2048]{1,0:T(8,128)(2,1)S(1)}, bf16[24,2048]{1,0:T(8,128)(2,1)S(1)}, u32[]{:S(2)}, u32[]{:S(2)}) collective-permute-start(bf16[24,2048]{1,0:T(8,128)(2,1)S(1)} %pad_maximum_fusion.3), channel_id=1, source_target_pairs={{0,1},{1,0},{2,3},{3,2},{4,5},{5,4},{6,7},{7,6},{8,9},{9,8},{10,11... | collective-permute-start | bytes 294920 | tf_op jit(solution)/shard_map/ppermute | solution.py:290
  16.6 6.8 %collective-permute-start.2 = (bf16[24,2048]{1,0:T(8,128)(2,1)}, bf16[24,2048]{1,0:T(8,128)(2,1)S(1)}, u32[]{:S(2)}, u32[]{:S(2)}) collective-permute-start(bf16[24,2048]{1,0:T(8,128)(2,1)} %get-tuple-element.31), channel_id=1, source_target_pairs={{0,24},{4,28},{8,0},{12,4},{16,8},{20,12},{24,16},{28,20},{1,25},{... | collective-permute-start | bytes 294920 | tf_op jit(solution)/shard_map/ppermute | solution.py:282
  18.0 7.7 %collective-permute-start.4 = (bf16[24,2048]{1,0:T(8,128)(2,1)}, bf16[24,2048]{1,0:T(8,128)(2,1)S(1)}, u32[]{:S(2)}, u32[]{:S(2)}) collective-permute-start(bf16[24,2048]{1,0:T(8,128)(2,1)} %get-tuple-element.32), channel_id=1, source_target_pairs={{0,8},{4,12},{8,16},{12,20},{16,24},{20,28},{24,0},{28,4},{1,9},{5... | collective-permute-start | bytes 294920 | tf_op jit(solution)/shard_map/ppermute | solution.py:282
  18.7 15.4 %collective-permute-start.5 = (bf16[24,2048]{1,0:T(8,128)(2,1)}, bf16[24,2048]{1,0:T(8,128)(2,1)S(1)}, u32[]{:S(2)}, u32[]{:S(2)}) collective-permute-start(bf16[24,2048]{1,0:T(8,128)(2,1)} %get-tuple-element.32), channel_id=1, source_target_pairs={{0,16},{4,20},{8,24},{12,28},{16,0},{20,4},{24,8},{28,12},{1,17},{... | collective-permute-start | bytes 294920 | tf_op jit(solution)/shard_map/ppermute | solution.py:282
  19.5 14.6 %collective-permute-start.6 = (bf16[24,2048]{1,0:T(8,128)(2,1)S(1)}, bf16[24,2048]{1,0:T(8,128)(2,1)S(1)}, u32[]{:S(2)}, u32[]{:S(2)}) collective-permute-start(bf16[24,2048]{1,0:T(8,128)(2,1)S(1)} %copy-done.1), channel_id=1, source_target_pairs={{0,24},{4,28},{8,0},{12,4},{16,8},{20,12},{24,16},{28,20},{1,25},{... | collective-permute-start | bytes 294920 | tf_op jit(solution)/shard_map/ppermute | solution.py:282
  22.0 15.3 %collective-permute-start.8 = (bf16[24,4096]{1,0:T(8,128)(2,1)S(1)}, bf16[24,4096]{1,0:T(8,128)(2,1)S(1)}, u32[]{:S(2)}, u32[]{:S(2)}) collective-permute-start(bf16[24,4096]{1,0:T(8,128)(2,1)S(1)} %copy-done), channel_id=1, source_target_pairs={{0,8},{4,12},{8,16},{12,20},{16,24},{20,28},{24,0},{28,4},{1,9},{5... | collective-permute-start | bytes 589832 | tf_op jit(solution)/shard_map/ppermute | solution.py:282
  23.4 35.2 %collective-permute-start.9 = (bf16[24,4096]{1,0:T(8,128)(2,1)S(1)}, bf16[24,4096]{1,0:T(8,128)(2,1)S(1)}, u32[]{:S(2)}, u32[]{:S(2)}) collective-permute-start(bf16[24,4096]{1,0:T(8,128)(2,1)S(1)} %copy-done), channel_id=1, source_target_pairs={{0,16},{4,20},{8,24},{12,28},{16,0},{20,4},{24,8},{28,12},{1,17},{... | collective-permute-start | bytes 589832 | tf_op jit(solution)/shard_map/ppermute | solution.py:282
  25.8 33.0 %collective-permute-start.10 = (bf16[24,4096]{1,0:T(8,128)(2,1)S(1)}, bf16[24,4096]{1,0:T(8,128)(2,1)S(1)}, u32[]{:S(2)}, u32[]{:S(2)}) collective-permute-start(bf16[24,4096]{1,0:T(8,128)(2,1)S(1)} %copy-done), channel_id=1, source_target_pairs={{0,24},{4,28},{8,0},{12,4},{16,8},{20,12},{24,16},{28,20},{1,25},{... | collective-permute-start | bytes 589832 | tf_op jit(solution)/shard_map/ppermute | solution.py:282
  34.1 25.3 %collective-permute-start.21 = (bf16[4,24,2048]{2,1,0:T(8,128)(2,1)S(1)}, bf16[4,24,2048]{2,1,0:T(8,128)(2,1)S(1)}, u32[]{:S(2)}, u32[]{:S(2)}) collective-permute-start(bf16[4,24,2048]{2,1,0:T(8,128)(2,1)S(1)} %get-tuple-element.67), channel_id=1, source_target_pairs={{0,24},{4,28},{8,0},{12,4},{16,8},{20,12},{24,16},{28,20},{1,25},{... | collective-permute-start | bytes 1179656 | tf_op jit(solution)/shard_map/ppermute | solution.py:282
  34.1 46.0 %collective-permute-start.20 = (bf16[4,24,2048]{2,1,0:T(8,128)(2,1)S(1)}, bf16[4,24,2048]{2,1,0:T(8,128)(2,1)S(1)}, u32[]{:S(2)}, u32[]{:S(2)}) collective-permute-start(bf16[4,24,2048]{2,1,0:T(8,128)(2,1)S(1)} %get-tuple-element.67), channel_id=1, source_target_pairs={{0,16},{4,20},{8,24},{12,28},{16,0},{20,4},{24,8},{28,12},{1,17},{... | collective-permute-start | bytes 1179656 | tf_op jit(solution)/shard_map/ppermute | solution.py:282
  37.4 42.7 %collective-permute-start.19 = (bf16[4,24,2048]{2,1,0:T(8,128)(2,1)S(1)}, bf16[4,24,2048]{2,1,0:T(8,128)(2,1)S(1)}, u32[]{:S(2)}, u32[]{:S(2)}) collective-permute-start(bf16[4,24,2048]{2,1,0:T(8,128)(2,1)S(1)} %get-tuple-element.67), channel_id=1, source_target_pairs={{0,8},{4,12},{8,16},{12,20},{16,24},{20,28},{24,0},{28,4},{1,9},{5... | collective-permute-start | bytes 1179656 | tf_op jit(solution)/shard_map/ppermute | solution.py:282
  58.7 28.1 %collective-permute-start.3 = (bf16[96,2048]{1,0:T(8,128)(2,1)S(1)}, bf16[96,2048]{1,0:T(8,128)(2,1)S(1)}, u32[]{:S(2)}, u32[]{:S(2)}) collective-permute-start(bf16[96,2048]{1,0:T(8,128)(2,1)S(1)} %constant_dynamic-update-slice_fusion.refs_0_), channel_id=1, source_target_pairs={{0,4},{4,0},{8,12},{12,8},{16,20},{20,16},{24,28},{28,24},{1,5},{5... | collective-permute-start | bytes 1179656 | tf_op jit(solution)/shard_map/ppermute | solution.py:286
  58.8 21.7 %collective-permute-start.7 = (bf16[96,2048]{1,0:T(8,128)(2,1)S(1)}, bf16[96,2048]{1,0:T(8,128)(2,1)S(1)}, u32[]{:S(2)}, u32[]{:S(2)}) collective-permute-start(bf16[96,2048]{1,0:T(8,128)(2,1)S(1)} %constant_dynamic-update-slice_fusion.4.refs_0_), channel_id=1, source_target_pairs={{0,4},{4,0},{8,12},{12,8},{16,20},{20,16},{24,28},{28,24},{1,5},{5... | collective-permute-start | bytes 1179656 | tf_op jit(solution)/shard_map/ppermute | solution.py:286
  59.4 33.7 %collective-permute-start.11 = (bf16[96,4096]{1,0:T(8,128)(2,1)S(1)}, bf16[96,4096]{1,0:T(8,128)(2,1)S(1)}, u32[]{:S(2)}, u32[]{:S(2)}) collective-permute-start(bf16[96,4096]{1,0:T(8,128)(2,1)S(1)} %constant_dynamic-update-slice_fusion.8.refs_0_), channel_id=1, source_target_pairs={{0,4},{4,0},{8,12},{12,8},{16,20},{20,16},{24,28},{28,24},{1,5},{5... | collective-permute-start | bytes 2359304 | tf_op jit(solution)/shard_map/ppermute | solution.py:286
  80.4 58.7 %collective-permute-start.22 = (bf16[4,4,24,2048]{3,2,0,1:T(8,128)(2,1)S(1)}, bf16[4,4,24,2048]{3,2,0,1:T(8,128)(2,1)S(1)}, u32[]{:S(2)}, u32[]{:S(2)}) collective-permute-start(bf16[4,4,24,2048]{3,2,0,1:T(8,128)(2,1)S(1)} %get-tuple-element.61), channel_id=1, source_target_pairs={{0,4},{4,0},{8,12},{12,8},{16,20},{20,16},{24,28},{28,24},{1,5},{5... | collective-permute-start | bytes 4718600 | tf_op jit(solution)/shard_map/ppermute | solution.py:286
  117.1 23.4 %collective-permute-start.12 = (bf16[2,96,4096]{2,1,0:T(8,128)(2,1)S(1)}, bf16[2,96,4096]{2,1,0:T(8,128)(2,1)S(1)}, u32[]{:S(2)}, u32[]{:S(2)}) collective-permute-start(bf16[2,96,4096]{2,1,0:T(8,128)(2,1)S(1)} %get-tuple-element.41), channel_id=1, source_target_pairs={{0,4},{4,0},{8,12},{12,8},{16,20},{20,16},{24,28},{28,24},{1,5},{5... | collective-permute-start | bytes 4718600 | tf_op jit(solution)/shard_map/ppermute | solution.py:286
  117.7 17.4 %collective-permute-start.32 = (bf16[192,1792]{1,0:T(8,128)(2,1)S(1)}, bf16[192,1792]{1,0:T(8,128)(2,1)S(1)}, u32[]{:S(2)}, u32[]{:S(2)}) collective-permute-start(bf16[192,1792]{1,0:T(8,128)(2,1)S(1)} %get-tuple-element.52.refs_0_), channel_id=1, source_target_pairs={{0,2},{1,3},{2,0},{3,1},{4,6},{5,7},{6,4},{7,5},{8,10},{9,11},{10,... | collective-permute-start | bytes 2064392 | tf_op jit(solution)/shard_map/ppermute | solution.py:290
  119.3 18.3 %collective-permute-start.31 = (bf16[192,1792]{1,0:T(8,128)(2,1)S(1)}, bf16[192,1792]{1,0:T(8,128)(2,1)S(1)}, u32[]{:S(2)}, u32[]{:S(2)}) collective-permute-start(bf16[192,1792]{1,0:T(8,128)(2,1)S(1)} %get-tuple-element.52.refs_0_), channel_id=1, source_target_pairs={{0,1},{1,0},{2,3},{3,2},{4,5},{5,4},{6,7},{7,6},{8,9},{9,8},{10,11... | collective-permute-start | bytes 2064392 | tf_op jit(solution)/shard_map/ppermute | solution.py:290
  120.8 31.6 %collective-permute-start.23 = (bf16[192,1792]{1,0:T(8,128)(2,1)S(1)}, bf16[192,1792]{1,0:T(8,128)(2,1)S(1)}, u32[]{:S(2)}, u32[]{:S(2)}) collective-permute-start(bf16[192,1792]{1,0:T(8,128)(2,1)S(1)} %get-tuple-element.43.refs_2_), channel_id=1, source_target_pairs={{0,1},{1,0},{2,3},{3,2},{4,5},{5,4},{6,7},{7,6},{8,9},{9,8},{10,11... | collective-permute-start | bytes 2064392 | tf_op jit(solution)/shard_map/ppermute | solution.py:290
  135.1 18.3 %collective-permute-start.24 = (bf16[192,1792]{1,0:T(8,128)(2,1)S(1)}, bf16[192,1792]{1,0:T(8,128)(2,1)S(1)}, u32[]{:S(2)}, u32[]{:S(2)}) collective-permute-start(bf16[192,1792]{1,0:T(8,128)(2,1)S(1)} %get-tuple-element.43.refs_2_), channel_id=1, source_target_pairs={{0,2},{1,3},{2,0},{3,1},{4,6},{5,7},{6,4},{7,5},{8,10},{9,11},{10,... | collective-permute-start | bytes 2064392 | tf_op jit(solution)/shard_map/ppermute | solution.py:290
  137.7 29.5 %collective-permute-start.27 = (bf16[192,1792]{1,0:T(8,128)(2,1)S(1)}, bf16[192,1792]{1,0:T(8,128)(2,1)S(1)}, u32[]{:S(2)}, u32[]{:S(2)}) collective-permute-start(bf16[192,1792]{1,0:T(8,128)(2,1)S(1)} %get-tuple-element.49.refs_1_), channel_id=1, source_target_pairs={{0,1},{1,0},{2,3},{3,2},{4,5},{5,4},{6,7},{7,6},{8,9},{9,8},{10,11... | collective-permute-start | bytes 2064392 | tf_op jit(solution)/shard_map/ppermute | solution.py:290
  139.1 29.1 %collective-permute-start.28 = (bf16[192,1792]{1,0:T(8,128)(2,1)S(1)}, bf16[192,1792]{1,0:T(8,128)(2,1)S(1)}, u32[]{:S(2)}, u32[]{:S(2)}) collective-permute-start(bf16[192,1792]{1,0:T(8,128)(2,1)S(1)} %get-tuple-element.49.refs_1_), channel_id=1, source_target_pairs={{0,2},{1,3},{2,0},{3,1},{4,6},{5,7},{6,4},{7,5},{8,10},{9,11},{10,... | collective-permute-start | bytes 2064392 | tf_op jit(solution)/shard_map/ppermute | solution.py:290
  140.5 32.8 %collective-permute-start.33 = (bf16[96,1792]{1,0:T(8,128)(2,1)S(1)}, bf16[96,1792]{1,0:T(8,128)(2,1)S(1)}, u32[]{:S(2)}, u32[]{:S(2)}) collective-permute-start(bf16[96,1792]{1,0:T(8,128)(2,1)S(1)} %slice.88), channel_id=1, source_target_pairs={{0,1},{1,0},{2,3},{3,2},{4,5},{5,4},{6,7},{7,6},{8,9},{9,8},{10,11... | collective-permute-start | bytes 1032200 | tf_op jit(solution)/shard_map/ppermute | solution.py:290
  152.4 22.4 %collective-permute-start.34 = (bf16[96,1792]{1,0:T(8,128)(2,1)S(1)}, bf16[96,1792]{1,0:T(8,128)(2,1)S(1)}, u32[]{:S(2)}, u32[]{:S(2)}) collective-permute-start(bf16[96,1792]{1,0:T(8,128)(2,1)S(1)} %slice.89), channel_id=1, source_target_pairs={{0,2},{1,3},{2,0},{3,1},{4,6},{5,7},{6,4},{7,5},{8,10},{9,11},{10,... | collective-permute-start | bytes 1032200 | tf_op jit(solution)/shard_map/ppermute | solution.py:290
  153.4 42.7 %collective-permute-start.13 = (bf16[2,24,4096]{2,1,0:T(8,128)(2,1)S(1)}, bf16[2,24,4096]{2,1,0:T(8,128)(2,1)S(1)}, u32[]{:S(2)}, u32[]{:S(2)}) collective-permute-start(bf16[2,24,4096]{2,1,0:T(8,128)(2,1)S(1)} %get-tuple-element.65), channel_id=1, source_target_pairs={{0,24},{4,28},{8,0},{12,4},{16,8},{20,12},{24,16},{28,20},{1,25},{... | collective-permute-start | bytes 1179656 | tf_op jit(solution)/shard_map/ppermute | solution.py:282
  167.1 29.0 %collective-permute-start.14 = (bf16[2,24,4096]{2,1,0:T(8,128)(2,1)S(1)}, bf16[2,24,4096]{2,1,0:T(8,128)(2,1)S(1)}, u32[]{:S(2)}, u32[]{:S(2)}) collective-permute-start(bf16[2,24,4096]{2,1,0:T(8,128)(2,1)S(1)} %get-tuple-element.64), channel_id=1, source_target_pairs={{0,16},{4,20},{8,24},{12,28},{16,0},{20,4},{24,8},{28,12},{1,17},{... | collective-permute-start | bytes 1179656 | tf_op jit(solution)/shard_map/ppermute | solution.py:282
  168.2 27.9 %collective-permute-start.15 = (bf16[2,24,4096]{2,1,0:T(8,128)(2,1)S(1)}, bf16[2,24,4096]{2,1,0:T(8,128)(2,1)S(1)}, u32[]{:S(2)}, u32[]{:S(2)}) collective-permute-start(bf16[2,24,4096]{2,1,0:T(8,128)(2,1)S(1)} %get-tuple-element.63), channel_id=1, source_target_pairs={{0,8},{4,12},{8,16},{12,20},{16,24},{20,28},{24,0},{28,4},{1,9},{5... | collective-permute-start | bytes 1179656 | tf_op jit(solution)/shard_map/ppermute | solution.py:282
  173.3 8.9 %collective-permute-start.25 = (bf16[96,1792]{1,0:T(8,128)(2,1)S(1)}, bf16[96,1792]{1,0:T(8,128)(2,1)S(1)}, u32[]{:S(2)}, u32[]{:S(2)}) collective-permute-start(bf16[96,1792]{1,0:T(8,128)(2,1)S(1)} %slice.67), channel_id=1, source_target_pairs={{0,1},{1,0},{2,3},{3,2},{4,5},{5,4},{6,7},{7,6},{8,9},{9,8},{10,11... | collective-permute-start | bytes 1032200 | tf_op jit(solution)/shard_map/ppermute | solution.py:290
  174.8 8.9 %collective-permute-start.26 = (bf16[96,1792]{1,0:T(8,128)(2,1)S(1)}, bf16[96,1792]{1,0:T(8,128)(2,1)S(1)}, u32[]{:S(2)}, u32[]{:S(2)}) collective-permute-start(bf16[96,1792]{1,0:T(8,128)(2,1)S(1)} %slice.68), channel_id=1, source_target_pairs={{0,2},{1,3},{2,0},{3,1},{4,6},{5,7},{6,4},{7,5},{8,10},{9,11},{10,... | collective-permute-start | bytes 1032200 | tf_op jit(solution)/shard_map/ppermute | solution.py:290
  182.3 8.1 %collective-permute-start.29 = (bf16[96,1792]{1,0:T(8,128)(2,1)S(1)}, bf16[96,1792]{1,0:T(8,128)(2,1)S(1)}, u32[]{:S(2)}, u32[]{:S(2)}) collective-permute-start(bf16[96,1792]{1,0:T(8,128)(2,1)S(1)} %slice.76), channel_id=1, source_target_pairs={{0,1},{1,0},{2,3},{3,2},{4,5},{5,4},{6,7},{7,6},{8,9},{9,8},{10,11... | collective-permute-start | bytes 1032200 | tf_op jit(solution)/shard_map/ppermute | solution.py:290
  183.7 7.8 %collective-permute-start.30 = (bf16[96,1792]{1,0:T(8,128)(2,1)S(1)}, bf16[96,1792]{1,0:T(8,128)(2,1)S(1)}, u32[]{:S(2)}, u32[]{:S(2)}) collective-permute-start(bf16[96,1792]{1,0:T(8,128)(2,1)S(1)} %slice.77), channel_id=1, source_target_pairs={{0,2},{1,3},{2,0},{3,1},{4,6},{5,7},{6,4},{7,5},{8,10},{9,11},{10,... | collective-permute-start | bytes 1032200 | tf_op jit(solution)/shard_map/ppermute | solution.py:290

commit v7 on v6

--- a/solution.py
+++ b/solution.py
@@ -259,10 +259,40 @@
             pltpu.VMEM((depth, units, step), BF),
             pltpu.SemaphoreType.DMA((3, depth)),
         ],
-        compiler_params=grant((3 * depth * step, units, BF), least=46 * MIB),
+        compiler_params=grant((3 * depth * step, units, BF), least=40 * MIB),
         cost_estimate=cost(6 * rows * width * units, 6 * width * units),
         name="leave",
     )(hid, gb, ub, gate, up, down)
+
+
+def fold_kernel(first_ref, own_ref, mate_ref, *chunks):
+    count = chunks[0].shape[1]
+    ring = own_ref.shape[1] // count
+    for k in range(ring):
+        span = slice(k * count, (k + 1) * count)
+        both = own_ref[:, span].astype(F32) + mate_ref[:, span].astype(F32)
+        chunks[k][...] = both.astype(BF)
+    if len(chunks) > ring:
+        @pl.when(first_ref[0] == 1)
+        def _():
+            chunks[ring][...] = chunks[1][...]
+
+        @pl.when(first_ref[0] != 1)
+        def _():
+            chunks[ring][...] = chunks[ring - 1][...]
+
+
+def fold(first, own, mate, ring, chunks):
+    sides, rows, width = own.shape
+    return pl.pallas_call(
+        fold_kernel,
+        in_specs=[pl.BlockSpec(memory_space=pltpu.SMEM), VMEM, VMEM],
+        out_specs=[VMEM] * chunks,
+        out_shape=[shape((sides, rows // ring, width))] * chunks,
+        compiler_params=grant(),
+        cost_estimate=cost(own.size, 6 * own.size),
+        name="fold",
+    )(first, own, mate)
 
 
 def rows_dot(left, right):
@@ -275,8 +305,11 @@
     count, width = out_grad.shape
     groups = lax.axis_size("seq")
     ring = lax.axis_size("dp") // CORES
-    me = lax.axis_index("seq")
     part = width // groups
+    starts = [(lax.axis_index("seq") ^ m) * part for m in range(groups)]
+    first = (lax.axis_index("dp") < CORES).astype(jnp.int32).reshape(1)
+    tokens, modality, first, *starts = lax.optimization_barrier(
+        (tokens, modality, first, *starts))
 
     def shift(value, k):
         return lax.ppermute(value, "dp", [
@@ -292,15 +325,14 @@
     def gathered(block):
         return jnp.concatenate([block] + [shift(block, k) for k in range(1, ring)], axis=0)
 
-    def cut(matrix, group):
-        return lax.dynamic_slice_in_dim(matrix, group * part, part, axis=1)
+    def cut(matrix, m):
+        return lax.dynamic_slice_in_dim(matrix, starts[m], part, axis=1)
 
     def slices_of(tok_block, cot_block):
-        def both(group):
-            return jnp.concatenate([cut(tok_block, group), cut(cot_block, group)], axis=1)
-
-        small = jnp.stack(
-            [both(me)] + [across(both(me ^ m), m) for m in range(1, groups)])
+        def both(m):
+            return jnp.concatenate([cut(tok_block, m), cut(cot_block, m)], axis=1)
+
+        small = jnp.stack([both(0)] + [across(both(m), m) for m in range(1, groups)])
         pieces = [small] + [shift(small, k) for k in range(1, ring)]
         own = jnp.stack(pieces, axis=1)
         mate = swap(own)
@@ -329,6 +361,22 @@
         leaves, tree = jax.tree.flatten(values)
         return jax.tree.unflatten(
             tree, lax.optimization_barrier((*leaves, *others))[:len(leaves)])
+
+    def returned(own, mate):
+        line = ring == 4
+        sums = fold(first, own, mate, ring, ring + line)
+        if not line:
+            return [sums[0]] + [shift(sums[k], -k) for k in range(1, ring)]
+
+        def along(value, pairs):
+            return lax.ppermute(value, "dp", [
+                (a * CORES + c, b * CORES + c) for a, b in pairs for c in range(CORES)])
+
+        far = along(sums[4], [(0, 1), (3, 2)])
+        terms = [along(sums[1], [(1, 0), (2, 1), (3, 2)]),
+                 along(sums[3], [(0, 1), (1, 2), (2, 3)])]
+        mid = (sums[2].astype(F32) + far.astype(F32)).astype(BF)
+        return [sums[0], *terms, shift(mid, 2)]
 
     def stack(held):
         return jnp.concatenate(sum(held, []), axis=0)
@@ -350,21 +398,18 @@
     own, other = leave(hid, gb, ub, gate, up, down)
 
     mate = swap(other)
-    sums = (own.astype(F32) + mate.astype(F32)).astype(BF).reshape(2, ring, count, width)
-    sums = [sums[:, k] for k in range(ring)]
-    terms = [shift(sums[k], -k) for k in range(1, ring)]
-
-    all_hid = after(all_hid, sums[1:])
-    all_gb = relay(after(all_gb, sums[1:]))
-    all_ub = relay(after(all_ub, sums[1:]))
+    terms = returned(own, mate)
+    all_hid = after(all_hid, terms[:1])
+    all_gb = relay(all_gb)
+    all_ub = relay(after(all_ub, terms[:1]))
     down_grad = rows_dot(stack(all_hid), cot_all)
     gate_grad = rows_dot(tok_all, stack(all_gb))
     up_grad = rows_dot(tok_all, stack(all_ub))
     terms = after(terms, [up_grad])
 
     def total(side):
-        value = sums[0][side].astype(F32)
-        for term in terms:
+        value = terms[0][side].astype(F32)
+        for term in terms[1:]:
             value = value + term[side].astype(F32)
         return value.astype(BF)
 

time: 197 us -> 184 us (0.934)
  waiting for transfers between devices: 75.9 us -> 55.5 us
  starting transfers between devices: 59.9 us -> 66.6 us
    ppermute x15, waiting for transfers between devices: 46 us -> 29.5 us  [across(): return lax.ppermute(value, 'seq', [(g, g ^ mask) for g in range(groups)])]
    ppermute x0 -> x3, starting transfers between devices: none -> 8.29 us  [along(): lax.ppermute(value, 'dp', [(a * CORES + c, b * CORES + c) for a, b in pai...]
    ppermute x15 -> x13, waiting for transfers between devices: 29.9 us -> 24.3 us  [shift(): lax.ppermute(value, 'dp', [(z * CORES + c, (z + k) % ring * CORES + c) fo...]
    ppermute x15 -> x13, starting transfers between devices: 42.5 us -> 39.4 us  [shift(): lax.ppermute(value, 'dp', [(z * CORES + c, (z + k) % ring * CORES + c) fo...]
    ppermute x15, starting transfers between devices: 16.1 us -> 18 us  [across(): return lax.ppermute(value, 'seq', [(g, g ^ mask) for g in range(groups)])]
  transfers between devices with their start and end apart: 35 -> 36, of which waited for: 13 -> 10; matrix products, arithmetic and copies ran while one was open for 10% -> 11% of each run, Pallas kernels for 19% -> 20%
where the time goes in v7:
time: 184 us
  starting transfers between devices  66.6 us (36%)
  waiting for transfers between devices  55.5 us (30%)
  Pallas kernels  39 us (21%)
  matrix products  13.6 us (7%)
  local copies, waits for them, and re-layouts  5.89 us (3%)
    ppermute x13, starting transfers between devices, shift(): lax.ppermute(value, 'dp', [(z * CORES + c, (z + k) % ring * CORES + c) fo...  39.4 us
    ppermute x15, waiting for transfers between devices, across(): return lax.ppermute(value, 'seq', [(g, g ^ mask) for g in range(groups)])  29.5 us
    ppermute x13, waiting for transfers between devices, shift(): lax.ppermute(value, 'dp', [(z * CORES + c, (z + k) % ring * CORES + c) fo...  24.3 us
    ppermute x15, starting transfers between devices, across(): return lax.ppermute(value, 'seq', [(g, g ^ mask) for g in range(groups)])  18 us
    pallas_call x1, Pallas kernels, leave(): pl.pallas_call(lambda *refs: leave_kernel(step, *refs), in_specs=[VMEM] *...  16.4 us
    dot_general x3, matrix products, rows_dot(): lax.dot_general(left, right, (((0,), (0,)), ((), ())), preferred_element_...  13.6 us
    pallas_call x2, Pallas kernels, enter(): pl.pallas_call(lambda *refs: enter_kernel(tile, last, *refs), in_specs=[V...  12.6 us
    ppermute x3, starting transfers between devices, along(): lax.ppermute(value, 'dp', [(a * CORES + c, b * CORES + c) for a, b in pai...  8.29 us
  transfers between devices with their start and end apart: 36, of which 10 were waited for; matrix products, arithmetic and copies ran while one was open for 11% of the time, Pallas kernels for 20%

profile of v7, /device:TPU:0, one launch (start us, length us, event | category | flops | bytes accessed | tf_op | source)
XLA Modules:
  0.0 183.5 jit_solution(10822489171357666429)
XLA Ops:
  0.6 2.0 %pick.1 = (bf16[24,4096]{1,0:T(8,128)(2,1)}, bf16[24,2048]{1,0:T(8,128)(2,1)}, bf16[24,2048]{1,0:T(8,128)(2,1)}) custom-call(s32[1,32]{1,0:T(1,128)} %bitcast.37, bf16[32,4096]{1,0:T(8,128)(2,1)} %tokens_hbm), custom_call_target="tpu_custom_call" | custom-call | tf_op jit(solution)/shard_map/pick/pallas_call | solution.py:74
  2.7 3.1 %collective-permute-start = (bf16[24,2048]{1,0:T(8,128)(2,1)}, bf16[24,2048]{1,0:T(8,128)(2,1)S(1)}, u32[]{:S(2)}, u32[]{:S(2)}) collective-permute-start(bf16[24,2048]{1,0:T(8,128)(2,1)} %get-tuple-element.44), channel_id=1, source_target_pairs={{0,8},{4,12},{8,16},{12,20},{16,24},{20,28},{24,0},{28,4},{1,9},{5... | collective-permute-start | bytes 294920 | tf_op jit(solution)/shard_map/ppermute | solution.py:315
  5.8 2.6 %collective-permute-start.1 = (bf16[24,2048]{1,0:T(8,128)(2,1)}, bf16[24,2048]{1,0:T(8,128)(2,1)S(1)}, u32[]{:S(2)}, u32[]{:S(2)}) collective-permute-start(bf16[24,2048]{1,0:T(8,128)(2,1)} %get-tuple-element.44), channel_id=1, source_target_pairs={{0,16},{4,20},{8,24},{12,28},{16,0},{20,4},{24,8},{28,12},{1,17},{... | collective-permute-start | bytes 294920 | tf_op jit(solution)/shard_map/ppermute | solution.py:315
  8.4 1.0 constant_dynamic-slice_fusion.6
  9.4 1.0 constant_dynamic-slice_fusion.7
  10.5 2.5 %collective-permute-start.19 = (bf16[24,2048]{1,0:T(8,128)(2,1)S(1)}, bf16[24,2048]{1,0:T(8,128)(2,1)S(1)}, u32[]{:S(2)}, u32[]{:S(2)}) collective-permute-start(bf16[24,2048]{1,0:T(8,128)(2,1)S(1)} %pad_maximum_fusion.5), channel_id=1, source_target_pairs={{0,3},{1,2},{2,1},{3,0},{4,7},{5,6},{6,5},{7,4},{8,11},{9,10},{10,... | collective-permute-start | bytes 294920 | tf_op jit(solution)/shard_map/ppermute | solution.py:323
  13.0 0.5 collective-permute-start.18
  13.6 0.6 collective-permute-start.17
  14.2 0.9 constant_dynamic-update-slice_fusion.3
  15.1 0.9 constant_dynamic-update-slice_fusion.11
  16.0 0.9 constant_dynamic-update-slice_fusion.7
  16.9 1.4 collective-permute-start.2
  18.3 0.7 collective-permute-start.4
  19.0 0.7 collective-permute-start.5
  19.8 2.5 %collective-permute-start.6 = (bf16[24,2048]{1,0:T(8,128)(2,1)S(1)}, bf16[24,2048]{1,0:T(8,128)(2,1)S(1)}, u32[]{:S(2)}, u32[]{:S(2)}) collective-permute-start(bf16[24,2048]{1,0:T(8,128)(2,1)S(1)} %copy-done.1), channel_id=1, source_target_pairs={{0,24},{4,28},{8,0},{12,4},{16,8},{20,12},{24,16},{28,20},{1,25},{... | collective-permute-start | bytes 294920 | tf_op jit(solution)/shard_map/ppermute | solution.py:315
  22.3 0.6 collective-permute-start.8
  23.0 0.7 collective-permute-done.2
  23.7 0.8 collective-permute-start.9
  24.5 1.5 collective-permute-done.4
  26.1 1.4 collective-permute-start.10
  27.5 6.9 %collective-permute-done.5 = bf16[24,2048]{1,0:T(8,128)(2,1)S(1)} collective-permute-done((bf16[24,2048]{1,0:T(8,128)(2,1)}, bf16[24,2048]{1,0:T(8,128)(2,1)S(1)}, u32[]{:S(2)}, u32[]{:S(2)}) %collective-permute-start.5) | collective-permute-done | bytes 98336 | tf_op jit(solution)/shard_map/ppermute | solution.py:315
  34.4 3.2 %collective-permute-start.21 = (bf16[4,24,2048]{2,1,0:T(8,128)(2,1)S(1)}, bf16[4,24,2048]{2,1,0:T(8,128)(2,1)S(1)}, u32[]{:S(2)}, u32[]{:S(2)}) collective-permute-start(bf16[4,24,2048]{2,1,0:T(8,128)(2,1)S(1)} %get-tuple-element.84), channel_id=1, source_target_pairs={{0,16},{4,20},{8,24},{12,28},{16,0},{20,4},{24,8},{28,12},{1,17},{... | collective-permute-start | bytes 1179656 | tf_op jit(solution)/shard_map/ppermute | solution.py:315
  37.7 21.3 %collective-permute-start.20 = (bf16[4,24,2048]{2,1,0:T(8,128)(2,1)S(1)}, bf16[4,24,2048]{2,1,0:T(8,128)(2,1)S(1)}, u32[]{:S(2)}, u32[]{:S(2)}) collective-permute-start(bf16[4,24,2048]{2,1,0:T(8,128)(2,1)S(1)} %get-tuple-element.84), channel_id=1, source_target_pairs={{0,8},{4,12},{8,16},{12,20},{16,24},{20,28},{24,0},{28,4},{1,9},{5... | collective-permute-start | bytes 1179656 | tf_op jit(solution)/shard_map/ppermute | solution.py:315
  59.1 0.6 collective-permute-start.7
  59.6 1.7 collective-permute-done.7.refs_1_
  61.3 0.1 collective-permute-start.11
  61.5 6.3 %enter.2 = (f32[192,1792]{1,0:T(8,128)S(1)}, f32[192,1792]{1,0:T(8,128)S(1)}) custom-call(bf16[96,2048]{1,0:T(8,128)(2,1)S(1)} %constant_dynamic-update-slice_fusion.4.refs_0_, bf16[96,2048]{1,0:T(8,128)(2,1)S(1)} %collective-permute-done.7.refs_1_, bf16[4096,1792]{1,0:T(8,128)(2,1)} %refs_3_.5, bf16[4096,1792]{1,0:T(8,128)(2,1)} %refs_4_.1), custom_call_target="tpu_custom_call" | custom-call | flops 2818572288 | bytes 14680064 | tf_op jit(solution)/shard_map/enter/pallas_call | solution.py:160
  67.8 6.3 %enter.3 = (bf16[192,1792]{1,0:T(8,128)(2,1)S(1)}, f32[192,1792]{1,0:T(8,128)S(1)}, f32[192,1792]{1,0:T(8,128)S(1)}) custom-call(bf16[96,2048]{1,0:T(8,128)(2,1)S(1)} %constant_dynamic-update-slice_fusion.refs_0_, bf16[96,2048]{1,0:T(8,128)(2,1)S(1)} %collective-permute-done.3.refs_1_, bf16[4096,1792]{1,0:T(8,128)(2,1)} %refs_3_.5, ...), custom_call_target="tpu_custom_call" | custom-call | flops 2818572288 | bytes 14680064 | tf_op jit(solution)/shard_map/enter/pallas_call | solution.py:160
  74.1 2.0 %collective-permute-start.32 = (bf16[192,1792]{1,0:T(8,128)(2,1)S(1)}, bf16[192,1792]{1,0:T(8,128)(2,1)S(1)}, u32[]{:S(2)}, u32[]{:S(2)}) collective-permute-start(bf16[192,1792]{1,0:T(8,128)(2,1)S(1)} %get-tuple-element.72.refs_0_), channel_id=1, source_target_pairs={{0,1},{1,0},{2,3},{3,2},{4,5},{5,4},{6,7},{7,6},{8,9},{9,8},{10,11... | collective-permute-start | bytes 2064392 | tf_op jit(solution)/shard_map/ppermute | solution.py:323
  76.1 1.4 collective-permute-start.33
  77.4 3.0 %collective-permute-done.21 = bf16[4,24,2048]{2,1,0:T(8,128)(2,1)S(1)} collective-permute-done((bf16[4,24,2048]{2,1,0:T(8,128)(2,1)S(1)}, bf16[4,24,2048]{2,1,0:T(8,128)(2,1)S(1)}, u32[]{:S(2)}, u32[]{:S(2)}) %collective-permute-start.21) | collective-permute-done | bytes 393248 | tf_op jit(solution)/shard_map/ppermute | solution.py:315
  80.4 0.3 pad_maximum_fusion.1
  80.7 0.1 collective-permute-start.23
  80.7 7.6 %turn.1 = (bf16[192,1792]{1,0:T(8,128)(2,1)S(1)}, bf16[192,1792]{1,0:T(8,128)(2,1)S(1)}) custom-call(bf16[96,4096]{1,0:T(8,128)(2,1)S(1)} %constant_dynamic-update-slice_fusion.8.refs_0_, bf16[96,4096]{1,0:T(8,128)(2,1)S(1)} %collective-permute-done.11.refs_1_, bf16[1792,4096]{1,0:T(8,128)(2,1)} %refs_5_.1, f32[192,1792]{1,0:T(8,128)S(1)} %get-tuple-element.49.refs_3_, ...), custom_call_target="tpu_custom_call" | custom-call | flops 2818572288 | bytes 14680064 | tf_op jit(solution)/shard_map/turn/pallas_call | solution.py:204
  88.5 1.7 collective-permute-start.28
  90.1 1.5 collective-permute-start.29
  91.6 16.4 %leave.1 = (bf16[2,96,4096]{2,1,0:T(8,128)(2,1)S(1)}, bf16[2,96,4096]{2,1,0:T(8,128)(2,1)S(1)}) custom-call(bf16[192,1792]{1,0:T(8,128)(2,1)S(1)} %get-tuple-element.72.refs_0_, bf16[192,1792]{1,0:T(8,128)(2,1)S(1)} %get-tuple-element.51.refs_1_, bf16[192,1792]{1,0:T(8,128)(2,1)S(1)} %get-tuple-element.65.refs_2_, bf16[4096,1792]{1,0:T(8,128)(2,1)} %refs_3_.5, ...), custom_call_target="tpu_custom_call" | custom-call | flops 8455716864 | bytes 44040192 | tf_op jit(solution)/shard_map/leave/pallas_call | solution.py:251
  108.0 0.7 collective-permute-start.24
  108.7 0.1 collective-permute-start.12
  108.9 1.5 collective-permute-start.30
  110.4 0.6 collective-permute-start.31
  111.1 21.6 %collective-permute-done.30 = bf16[96,1792]{1,0:T(8,128)(2,1)S(1)} collective-permute-done((bf16[96,1792]{1,0:T(8,128)(2,1)S(1)}, bf16[96,1792]{1,0:T(8,128)(2,1)S(1)}, u32[]{:S(2)}, u32[]{:S(2)}) %collective-permute-start.30) | collective-permute-done | bytes 344096 | tf_op jit(solution)/shard_map/ppermute | solution.py:323
  132.7 0.5 collective-permute-start.25
  133.3 0.5 collective-permute-start.34
  133.8 1.7 collective-permute-start.35
  135.5 0.3 pad_maximum_fusion
  135.9 0.1 copy.11
  136.0 4.5 %convolution_convert_fusion.1 = bf16[1024,1792]{1,0:T(8,128)(2,1)} fusion(bf16[768,1024]{1,0:T(8,128)(2,1)S(1)} %bitcast.27, bf16[768,1792]{1,0:T(8,128)(2,1)S(1)} %constant_dynamic-update-slice_fusion.17), kind=kOutput, calls=%fused_computation.1 | convolution fusion | flops 2820407296 | bytes 7995392 | tf_op jit(solution)/shard_map/dot_general | solution.py:299
  140.6 0.2 copy.12
  140.8 0.4 fold.1
  141.2 1.3 collective-permute-start.13
  142.5 4.6 %collective-permute-start.14 = (bf16[2,24,4096]{2,1,0:T(8,128)(2,1)S(1)}, bf16[2,24,4096]{2,1,0:T(8,128)(2,1)S(1)}, u32[]{:S(2)}, u32[]{:S(2)}) collective-permute-start(bf16[2,24,4096]{2,1,0:T(8,128)(2,1)S(1)} %get-tuple-element.57), channel_id=1, source_target_pairs={{0,8},{4,12},{8,16},{12,20},{16,24},{20,28},{1,9},{5,13},{9,17},{1... | collective-permute-start | bytes 1179656 | tf_op jit(solution)/shard_map/ppermute | solution.py:372
  147.1 4.0 %collective-permute-done.25 = bf16[192,1792]{1,0:T(8,128)(2,1)S(1)} collective-permute-done((bf16[192,1792]{1,0:T(8,128)(2,1)S(1)}, bf16[192,1792]{1,0:T(8,128)(2,1)S(1)}, u32[]{:S(2)}, u32[]{:S(2)}) %collective-permute-start.25) | collective-permute-done | bytes 688160 | tf_op jit(solution)/shard_map/ppermute | solution.py:323
  151.0 2.4 %collective-permute-start.15 = (bf16[2,24,4096]{2,1,0:T(8,128)(2,1)S(1)}, bf16[2,24,4096]{2,1,0:T(8,128)(2,1)S(1)}, u32[]{:S(2)}, u32[]{:S(2)}) collective-permute-start(bf16[2,24,4096]{2,1,0:T(8,128)(2,1)S(1)} %get-tuple-element.59), channel_id=1, source_target_pairs={{0,8},{4,12},{24,16},{28,20},{1,9},{5,13},{25,17},{29,21},{2,10},{... | collective-permute-start | bytes 1179656 | tf_op jit(solution)/shard_map/ppermute | solution.py:372
  153.6 1.8 collective-permute-start.26
  155.4 1.1 collective-permute-done.35
  156.5 0.5 collective-permute-start.27
  157.3 4.5 %convolution_convert_fusion = bf16[1792,1024]{1,0:T(8,128)(2,1)} fusion(bf16[768,1792]{1,0:T(8,128)(2,1)S(1)} %constant_dynamic-update-slice_fusion.22, bf16[768,1024]{1,0:T(8,128)(2,1)S(1)} %bitcast.29), kind=kOutput, calls=%fused_computation | convolution fusion | flops 2820407296 | bytes 7995392 | tf_op jit(solution)/shard_map/dot_general | solution.py:299
  161.9 2.7 %collective-permute-done.27 = bf16[96,1792]{1,0:T(8,128)(2,1)S(1)} collective-permute-done((bf16[96,1792]{1,0:T(8,128)(2,1)S(1)}, bf16[96,1792]{1,0:T(8,128)(2,1)S(1)}, u32[]{:S(2)}, u32[]{:S(2)}) %collective-permute-start.27) | collective-permute-done | bytes 344096 | tf_op jit(solution)/shard_map/ppermute | solution.py:323
  164.7 0.1 add_convert_fusion
  164.8 1.0 collective-permute-start.16
  165.9 4.5 %convolution_convert_fusion.2 = bf16[1024,1792]{1,0:T(8,128)(2,1)} fusion(bf16[768,1024]{1,0:T(8,128)(2,1)S(1)} %bitcast.28, bf16[768,1792]{1,0:T(8,128)(2,1)S(1)} %constant_dynamic-update-slice_fusion.12), kind=kOutput, calls=%fused_computation.2 | convolution fusion | flops 2820407296 | bytes 7995392 | tf_op jit(solution)/shard_map/dot_general | solution.py:299
  170.4 12.2 %collective-permute-done.16 = bf16[2,24,4096]{2,1,0:T(8,128)(2,1)S(1)} collective-permute-done((bf16[2,24,4096]{2,1,0:T(8,128)(2,1)S(1)}, bf16[2,24,4096]{2,1,0:T(8,128)(2,1)S(1)}, u32[]{:S(2)}, u32[]{:S(2)}) %collective-permute-start.16) | collective-permute-done | bytes 393248 | tf_op jit(solution)/shard_map/ppermute | solution.py:315
  182.6 0.9 fusion.2
  (67 shorter events, 1.0 us)
Async XLA Ops:
  2.7 17.1 %copy-start.1 = (bf16[24,2048]{1,0:T(8,128)(2,1)S(1)}, bf16[24,2048]{1,0:T(8,128)(2,1)}, u32[]{:S(2)}) copy-start(bf16[24,2048]{1,0:T(8,128)(2,1)} %get-tuple-element.45) | copy-start | bytes 294916
  2.7 19.6 %copy-start = (bf16[24,4096]{1,0:T(8,128)(2,1)S(1)}, bf16[24,4096]{1,0:T(8,128)(2,1)}, u32[]{:S(2)}) copy-start(bf16[24,4096]{1,0:T(8,128)(2,1)} %param.11) | copy-start | bytes 589828
  2.7 17.1 %collective-permute-start = (bf16[24,2048]{1,0:T(8,128)(2,1)}, bf16[24,2048]{1,0:T(8,128)(2,1)S(1)}, u32[]{:S(2)}, u32[]{:S(2)}) collective-permute-start(bf16[24,2048]{1,0:T(8,128)(2,1)} %get-tuple-element.44), channel_id=1, source_target_pairs={{0,8},{4,12},{8,16},{12,20},{16,24},{20,28},{24,0},{28,4},{1,9},{5... | collective-permute-start | bytes 294920 | tf_op jit(solution)/shard_map/ppermute | solution.py:315
  5.8 16.5 %collective-permute-start.1 = (bf16[24,2048]{1,0:T(8,128)(2,1)}, bf16[24,2048]{1,0:T(8,128)(2,1)S(1)}, u32[]{:S(2)}, u32[]{:S(2)}) collective-permute-start(bf16[24,2048]{1,0:T(8,128)(2,1)} %get-tuple-element.44), channel_id=1, source_target_pairs={{0,16},{4,20},{8,24},{12,28},{16,0},{20,4},{24,8},{28,12},{1,17},{... | collective-permute-start | bytes 294920 | tf_op jit(solution)/shard_map/ppermute | solution.py:315
  10.5 6.5 %collective-permute-start.19 = (bf16[24,2048]{1,0:T(8,128)(2,1)S(1)}, bf16[24,2048]{1,0:T(8,128)(2,1)S(1)}, u32[]{:S(2)}, u32[]{:S(2)}) collective-permute-start(bf16[24,2048]{1,0:T(8,128)(2,1)S(1)} %pad_maximum_fusion.5), channel_id=1, source_target_pairs={{0,3},{1,2},{2,1},{3,0},{4,7},{5,6},{6,5},{7,4},{8,11},{9,10},{10,... | collective-permute-start | bytes 294920 | tf_op jit(solution)/shard_map/ppermute | solution.py:323
  13.0 5.3 %collective-permute-start.18 = (bf16[24,2048]{1,0:T(8,128)(2,1)S(1)}, bf16[24,2048]{1,0:T(8,128)(2,1)S(1)}, u32[]{:S(2)}, u32[]{:S(2)}) collective-permute-start(bf16[24,2048]{1,0:T(8,128)(2,1)S(1)} %pad_maximum_fusion.4), channel_id=1, source_target_pairs={{0,2},{1,3},{2,0},{3,1},{4,6},{5,7},{6,4},{7,5},{8,10},{9,11},{10,... | collective-permute-start | bytes 294920 | tf_op jit(solution)/shard_map/ppermute | solution.py:323
  13.6 5.5 %collective-permute-start.17 = (bf16[24,2048]{1,0:T(8,128)(2,1)S(1)}, bf16[24,2048]{1,0:T(8,128)(2,1)S(1)}, u32[]{:S(2)}, u32[]{:S(2)}) collective-permute-start(bf16[24,2048]{1,0:T(8,128)(2,1)S(1)} %pad_maximum_fusion.3), channel_id=1, source_target_pairs={{0,1},{1,0},{2,3},{3,2},{4,5},{5,4},{6,7},{7,6},{8,9},{9,8},{10,11... | collective-permute-start | bytes 294920 | tf_op jit(solution)/shard_map/ppermute | solution.py:323
  16.9 6.8 %collective-permute-start.2 = (bf16[24,2048]{1,0:T(8,128)(2,1)}, bf16[24,2048]{1,0:T(8,128)(2,1)S(1)}, u32[]{:S(2)}, u32[]{:S(2)}) collective-permute-start(bf16[24,2048]{1,0:T(8,128)(2,1)} %get-tuple-element.44), channel_id=1, source_target_pairs={{0,24},{4,28},{8,0},{12,4},{16,8},{20,12},{24,16},{28,20},{1,25},{... | collective-permute-start | bytes 294920 | tf_op jit(solution)/shard_map/ppermute | solution.py:315
  18.3 7.7 %collective-permute-start.4 = (bf16[24,2048]{1,0:T(8,128)(2,1)}, bf16[24,2048]{1,0:T(8,128)(2,1)S(1)}, u32[]{:S(2)}, u32[]{:S(2)}) collective-permute-start(bf16[24,2048]{1,0:T(8,128)(2,1)} %get-tuple-element.45), channel_id=1, source_target_pairs={{0,8},{4,12},{8,16},{12,20},{16,24},{20,28},{24,0},{28,4},{1,9},{5... | collective-permute-start | bytes 294920 | tf_op jit(solution)/shard_map/ppermute | solution.py:315
  19.0 15.4 %collective-permute-start.5 = (bf16[24,2048]{1,0:T(8,128)(2,1)}, bf16[24,2048]{1,0:T(8,128)(2,1)S(1)}, u32[]{:S(2)}, u32[]{:S(2)}) collective-permute-start(bf16[24,2048]{1,0:T(8,128)(2,1)} %get-tuple-element.45), channel_id=1, source_target_pairs={{0,16},{4,20},{8,24},{12,28},{16,0},{20,4},{24,8},{28,12},{1,17},{... | collective-permute-start | bytes 294920 | tf_op jit(solution)/shard_map/ppermute | solution.py:315
  19.8 14.6 %collective-permute-start.6 = (bf16[24,2048]{1,0:T(8,128)(2,1)S(1)}, bf16[24,2048]{1,0:T(8,128)(2,1)S(1)}, u32[]{:S(2)}, u32[]{:S(2)}) collective-permute-start(bf16[24,2048]{1,0:T(8,128)(2,1)S(1)} %copy-done.1), channel_id=1, source_target_pairs={{0,24},{4,28},{8,0},{12,4},{16,8},{20,12},{24,16},{28,20},{1,25},{... | collective-permute-start | bytes 294920 | tf_op jit(solution)/shard_map/ppermute | solution.py:315
  22.3 15.3 %collective-permute-start.8 = (bf16[24,4096]{1,0:T(8,128)(2,1)S(1)}, bf16[24,4096]{1,0:T(8,128)(2,1)S(1)}, u32[]{:S(2)}, u32[]{:S(2)}) collective-permute-start(bf16[24,4096]{1,0:T(8,128)(2,1)S(1)} %copy-done), channel_id=1, source_target_pairs={{0,8},{4,12},{8,16},{12,20},{16,24},{20,28},{24,0},{28,4},{1,9},{5... | collective-permute-start | bytes 589832 | tf_op jit(solution)/shard_map/ppermute | solution.py:315
  23.7 35.3 %collective-permute-start.9 = (bf16[24,4096]{1,0:T(8,128)(2,1)S(1)}, bf16[24,4096]{1,0:T(8,128)(2,1)S(1)}, u32[]{:S(2)}, u32[]{:S(2)}) collective-permute-start(bf16[24,4096]{1,0:T(8,128)(2,1)S(1)} %copy-done), channel_id=1, source_target_pairs={{0,16},{4,20},{8,24},{12,28},{16,0},{20,4},{24,8},{28,12},{1,17},{... | collective-permute-start | bytes 589832 | tf_op jit(solution)/shard_map/ppermute | solution.py:315
  26.1 33.0 %collective-permute-start.10 = (bf16[24,4096]{1,0:T(8,128)(2,1)S(1)}, bf16[24,4096]{1,0:T(8,128)(2,1)S(1)}, u32[]{:S(2)}, u32[]{:S(2)}) collective-permute-start(bf16[24,4096]{1,0:T(8,128)(2,1)S(1)} %copy-done), channel_id=1, source_target_pairs={{0,24},{4,28},{8,0},{12,4},{16,8},{20,12},{24,16},{28,20},{1,25},{... | collective-permute-start | bytes 589832 | tf_op jit(solution)/shard_map/ppermute | solution.py:315
  34.4 41.7 %collective-permute-start.22 = (bf16[4,24,2048]{2,1,0:T(8,128)(2,1)S(1)}, bf16[4,24,2048]{2,1,0:T(8,128)(2,1)S(1)}, u32[]{:S(2)}, u32[]{:S(2)}) collective-permute-start(bf16[4,24,2048]{2,1,0:T(8,128)(2,1)S(1)} %get-tuple-element.84), channel_id=1, source_target_pairs={{0,24},{4,28},{8,0},{12,4},{16,8},{20,12},{24,16},{28,20},{1,25},{... | collective-permute-start | bytes 1179656 | tf_op jit(solution)/shard_map/ppermute | solution.py:315
  34.4 46.0 %collective-permute-start.21 = (bf16[4,24,2048]{2,1,0:T(8,128)(2,1)S(1)}, bf16[4,24,2048]{2,1,0:T(8,128)(2,1)S(1)}, u32[]{:S(2)}, u32[]{:S(2)}) collective-permute-start(bf16[4,24,2048]{2,1,0:T(8,128)(2,1)S(1)} %get-tuple-element.84), channel_id=1, source_target_pairs={{0,16},{4,20},{8,24},{12,28},{16,0},{20,4},{24,8},{28,12},{1,17},{... | collective-permute-start | bytes 1179656 | tf_op jit(solution)/shard_map/ppermute | solution.py:315
  37.7 42.7 %collective-permute-start.20 = (bf16[4,24,2048]{2,1,0:T(8,128)(2,1)S(1)}, bf16[4,24,2048]{2,1,0:T(8,128)(2,1)S(1)}, u32[]{:S(2)}, u32[]{:S(2)}) collective-permute-start(bf16[4,24,2048]{2,1,0:T(8,128)(2,1)S(1)} %get-tuple-element.84), channel_id=1, source_target_pairs={{0,8},{4,12},{8,16},{12,20},{16,24},{20,28},{24,0},{28,4},{1,9},{5... | collective-permute-start | bytes 1179656 | tf_op jit(solution)/shard_map/ppermute | solution.py:315
  59.0 8.8 %collective-permute-start.3 = (bf16[96,2048]{1,0:T(8,128)(2,1)S(1)}, bf16[96,2048]{1,0:T(8,128)(2,1)S(1)}, u32[]{:S(2)}, u32[]{:S(2)}) collective-permute-start(bf16[96,2048]{1,0:T(8,128)(2,1)S(1)} %constant_dynamic-update-slice_fusion.refs_0_), channel_id=1, source_target_pairs={{0,4},{4,0},{8,12},{12,8},{16,20},{20,16},{24,28},{28,24},{1,5},{5... | collective-permute-start | bytes 1179656 | tf_op jit(solution)/shard_map/ppermute | solution.py:319
  59.1 2.2 %collective-permute-start.7 = (bf16[96,2048]{1,0:T(8,128)(2,1)S(1)}, bf16[96,2048]{1,0:T(8,128)(2,1)S(1)}, u32[]{:S(2)}, u32[]{:S(2)}) collective-permute-start(bf16[96,2048]{1,0:T(8,128)(2,1)S(1)} %constant_dynamic-update-slice_fusion.4.refs_0_), channel_id=1, source_target_pairs={{0,4},{4,0},{8,12},{12,8},{16,20},{20,16},{24,28},{28,24},{1,5},{5... | collective-permute-start | bytes 1179656 | tf_op jit(solution)/shard_map/ppermute | solution.py:319
  61.3 19.4 %collective-permute-start.11 = (bf16[96,4096]{1,0:T(8,128)(2,1)S(1)}, bf16[96,4096]{1,0:T(8,128)(2,1)S(1)}, u32[]{:S(2)}, u32[]{:S(2)}) collective-permute-start(bf16[96,4096]{1,0:T(8,128)(2,1)S(1)} %constant_dynamic-update-slice_fusion.8.refs_0_), channel_id=1, source_target_pairs={{0,4},{4,0},{8,12},{12,8},{16,20},{20,16},{24,28},{28,24},{1,5},{5... | collective-permute-start | bytes 2359304 | tf_op jit(solution)/shard_map/ppermute | solution.py:319
  74.1 34.6 %collective-permute-start.32 = (bf16[192,1792]{1,0:T(8,128)(2,1)S(1)}, bf16[192,1792]{1,0:T(8,128)(2,1)S(1)}, u32[]{:S(2)}, u32[]{:S(2)}) collective-permute-start(bf16[192,1792]{1,0:T(8,128)(2,1)S(1)} %get-tuple-element.72.refs_0_), channel_id=1, source_target_pairs={{0,1},{1,0},{2,3},{3,2},{4,5},{5,4},{6,7},{7,6},{8,9},{9,8},{10,11... | collective-permute-start | bytes 2064392 | tf_op jit(solution)/shard_map/ppermute | solution.py:323
  76.1 32.0 %collective-permute-start.33 = (bf16[192,1792]{1,0:T(8,128)(2,1)S(1)}, bf16[192,1792]{1,0:T(8,128)(2,1)S(1)}, u32[]{:S(2)}, u32[]{:S(2)}) collective-permute-start(bf16[192,1792]{1,0:T(8,128)(2,1)S(1)} %get-tuple-element.72.refs_0_), channel_id=1, source_target_pairs={{0,2},{1,3},{2,0},{3,1},{4,6},{5,7},{6,4},{7,5},{8,10},{9,11},{10,... | collective-permute-start | bytes 2064392 | tf_op jit(solution)/shard_map/ppermute | solution.py:323
  80.7 53.1 %collective-permute-start.23 = (bf16[4,4,24,2048]{3,2,0,1:T(8,128)(2,1)S(1)}, bf16[4,4,24,2048]{3,2,0,1:T(8,128)(2,1)S(1)}, u32[]{:S(2)}, u32[]{:S(2)}) collective-permute-start(bf16[4,4,24,2048]{3,2,0,1:T(8,128)(2,1)S(1)} %get-tuple-element.81), channel_id=1, source_target_pairs={{0,4},{4,0},{8,12},{12,8},{16,20},{20,16},{24,28},{28,24},{1,5},{5... | collective-permute-start | bytes 4718600 | tf_op jit(solution)/shard_map/ppermute | solution.py:319
  88.5 21.9 %collective-permute-start.28 = (bf16[192,1792]{1,0:T(8,128)(2,1)S(1)}, bf16[192,1792]{1,0:T(8,128)(2,1)S(1)}, u32[]{:S(2)}, u32[]{:S(2)}) collective-permute-start(bf16[192,1792]{1,0:T(8,128)(2,1)S(1)} %get-tuple-element.51.refs_1_), channel_id=1, source_target_pairs={{0,1},{1,0},{2,3},{3,2},{4,5},{5,4},{6,7},{7,6},{8,9},{9,8},{10,11... | collective-permute-start | bytes 2064392 | tf_op jit(solution)/shard_map/ppermute | solution.py:323
  90.1 18.7 %collective-permute-start.29 = (bf16[192,1792]{1,0:T(8,128)(2,1)S(1)}, bf16[192,1792]{1,0:T(8,128)(2,1)S(1)}, u32[]{:S(2)}, u32[]{:S(2)}) collective-permute-start(bf16[192,1792]{1,0:T(8,128)(2,1)S(1)} %get-tuple-element.51.refs_1_), channel_id=1, source_target_pairs={{0,2},{1,3},{2,0},{3,1},{4,6},{5,7},{6,4},{7,5},{8,10},{9,11},{10,... | collective-permute-start | bytes 2064392 | tf_op jit(solution)/shard_map/ppermute | solution.py:323
  108.0 34.5 %collective-permute-start.24 = (bf16[192,1792]{1,0:T(8,128)(2,1)S(1)}, bf16[192,1792]{1,0:T(8,128)(2,1)S(1)}, u32[]{:S(2)}, u32[]{:S(2)}) collective-permute-start(bf16[192,1792]{1,0:T(8,128)(2,1)S(1)} %get-tuple-element.65.refs_2_), channel_id=1, source_target_pairs={{0,1},{1,0},{2,3},{3,2},{4,5},{5,4},{6,7},{7,6},{8,9},{9,8},{10,11... | collective-permute-start | bytes 2064392 | tf_op jit(solution)/shard_map/ppermute | solution.py:323
  108.7 32.1 %collective-permute-start.12 = (bf16[2,96,4096]{2,1,0:T(8,128)(2,1)S(1)}, bf16[2,96,4096]{2,1,0:T(8,128)(2,1)S(1)}, u32[]{:S(2)}, u32[]{:S(2)}) collective-permute-start(bf16[2,96,4096]{2,1,0:T(8,128)(2,1)S(1)} %get-tuple-element.54), channel_id=1, source_target_pairs={{0,4},{4,0},{8,12},{12,8},{16,20},{20,16},{24,28},{28,24},{1,5},{5... | collective-permute-start | bytes 4718600 | tf_op jit(solution)/shard_map/ppermute | solution.py:319
  108.9 23.9 %collective-permute-start.30 = (bf16[96,1792]{1,0:T(8,128)(2,1)S(1)}, bf16[96,1792]{1,0:T(8,128)(2,1)S(1)}, u32[]{:S(2)}, u32[]{:S(2)}) collective-permute-start(bf16[96,1792]{1,0:T(8,128)(2,1)S(1)} %slice.66), channel_id=1, source_target_pairs={{0,1},{1,0},{2,3},{3,2},{4,5},{5,4},{6,7},{7,6},{8,9},{9,8},{10,11... | collective-permute-start | bytes 1032200 | tf_op jit(solution)/shard_map/ppermute | solution.py:323
  110.4 22.9 %collective-permute-start.31 = (bf16[96,1792]{1,0:T(8,128)(2,1)S(1)}, bf16[96,1792]{1,0:T(8,128)(2,1)S(1)}, u32[]{:S(2)}, u32[]{:S(2)}) collective-permute-start(bf16[96,1792]{1,0:T(8,128)(2,1)S(1)} %slice.67), channel_id=1, source_target_pairs={{0,2},{1,3},{2,0},{3,1},{4,6},{5,7},{6,4},{7,5},{8,10},{9,11},{10,... | collective-permute-start | bytes 1032200 | tf_op jit(solution)/shard_map/ppermute | solution.py:323
  132.7 18.3 %collective-permute-start.25 = (bf16[192,1792]{1,0:T(8,128)(2,1)S(1)}, bf16[192,1792]{1,0:T(8,128)(2,1)S(1)}, u32[]{:S(2)}, u32[]{:S(2)}) collective-permute-start(bf16[192,1792]{1,0:T(8,128)(2,1)S(1)} %get-tuple-element.65.refs_2_), channel_id=1, source_target_pairs={{0,2},{1,3},{2,0},{3,1},{4,6},{5,7},{6,4},{7,5},{8,10},{9,11},{10,... | collective-permute-start | bytes 2064392 | tf_op jit(solution)/shard_map/ppermute | solution.py:323
  133.3 20.3 %collective-permute-start.34 = (bf16[96,1792]{1,0:T(8,128)(2,1)S(1)}, bf16[96,1792]{1,0:T(8,128)(2,1)S(1)}, u32[]{:S(2)}, u32[]{:S(2)}) collective-permute-start(bf16[96,1792]{1,0:T(8,128)(2,1)S(1)} %slice.68), channel_id=1, source_target_pairs={{0,1},{1,0},{2,3},{3,2},{4,5},{5,4},{6,7},{7,6},{8,9},{9,8},{10,11... | collective-permute-start | bytes 1032200 | tf_op jit(solution)/shard_map/ppermute | solution.py:323
  133.8 22.7 %collective-permute-start.35 = (bf16[96,1792]{1,0:T(8,128)(2,1)S(1)}, bf16[96,1792]{1,0:T(8,128)(2,1)S(1)}, u32[]{:S(2)}, u32[]{:S(2)}) collective-permute-start(bf16[96,1792]{1,0:T(8,128)(2,1)S(1)} %slice.69), channel_id=1, source_target_pairs={{0,2},{1,3},{2,0},{3,1},{4,6},{5,7},{6,4},{7,5},{8,10},{9,11},{10,... | collective-permute-start | bytes 1032200 | tf_op jit(solution)/shard_map/ppermute | solution.py:323
  141.2 29.2 %collective-permute-start.13 = (bf16[2,24,4096]{2,1,0:T(8,128)(2,1)S(1)}, bf16[2,24,4096]{2,1,0:T(8,128)(2,1)S(1)}, u32[]{:S(2)}, u32[]{:S(2)}) collective-permute-start(bf16[2,24,4096]{2,1,0:T(8,128)(2,1)S(1)} %get-tuple-element.56), channel_id=1, source_target_pairs={{8,0},{12,4},{16,8},{20,12},{24,16},{28,20},{9,1},{13,5},{17,9},{2... | collective-permute-start | bytes 1179656 | tf_op jit(solution)/shard_map/ppermute | solution.py:372
  142.5 27.9 %collective-permute-start.14 = (bf16[2,24,4096]{2,1,0:T(8,128)(2,1)S(1)}, bf16[2,24,4096]{2,1,0:T(8,128)(2,1)S(1)}, u32[]{:S(2)}, u32[]{:S(2)}) collective-permute-start(bf16[2,24,4096]{2,1,0:T(8,128)(2,1)S(1)} %get-tuple-element.57), channel_id=1, source_target_pairs={{0,8},{4,12},{8,16},{12,20},{16,24},{20,28},{1,9},{5,13},{9,17},{1... | collective-permute-start | bytes 1179656 | tf_op jit(solution)/shard_map/ppermute | solution.py:372
  151.0 13.7 %collective-permute-start.15 = (bf16[2,24,4096]{2,1,0:T(8,128)(2,1)S(1)}, bf16[2,24,4096]{2,1,0:T(8,128)(2,1)S(1)}, u32[]{:S(2)}, u32[]{:S(2)}) collective-permute-start(bf16[2,24,4096]{2,1,0:T(8,128)(2,1)S(1)} %get-tuple-element.59), channel_id=1, source_target_pairs={{0,8},{4,12},{24,16},{28,20},{1,9},{5,13},{25,17},{29,21},{2,10},{... | collective-permute-start | bytes 1179656 | tf_op jit(solution)/shard_map/ppermute | solution.py:372
  153.6 8.3 %collective-permute-start.26 = (bf16[96,1792]{1,0:T(8,128)(2,1)S(1)}, bf16[96,1792]{1,0:T(8,128)(2,1)S(1)}, u32[]{:S(2)}, u32[]{:S(2)}) collective-permute-start(bf16[96,1792]{1,0:T(8,128)(2,1)S(1)} %slice.49), channel_id=1, source_target_pairs={{0,1},{1,0},{2,3},{3,2},{4,5},{5,4},{6,7},{7,6},{8,9},{9,8},{10,11... | collective-permute-start | bytes 1032200 | tf_op jit(solution)/shard_map/ppermute | solution.py:323
  156.5 8.2 %collective-permute-start.27 = (bf16[96,1792]{1,0:T(8,128)(2,1)S(1)}, bf16[96,1792]{1,0:T(8,128)(2,1)S(1)}, u32[]{:S(2)}, u32[]{:S(2)}) collective-permute-start(bf16[96,1792]{1,0:T(8,128)(2,1)S(1)} %slice.50), channel_id=1, source_target_pairs={{0,2},{1,3},{2,0},{3,1},{4,6},{5,7},{6,4},{7,5},{8,10},{9,11},{10,... | collective-permute-start | bytes 1032200 | tf_op jit(solution)/shard_map/ppermute | solution.py:323
  164.8 17.8 %collective-permute-start.16 = (bf16[2,24,4096]{2,1,0:T(8,128)(2,1)S(1)}, bf16[2,24,4096]{2,1,0:T(8,128)(2,1)S(1)}, u32[]{:S(2)}, u32[]{:S(2)}) collective-permute-start(bf16[2,24,4096]{2,1,0:T(8,128)(2,1)S(1)} %add_convert_fusion), channel_id=1, source_target_pairs={{0,16},{4,20},{8,24},{12,28},{16,0},{20,4},{24,8},{28,12},{1,17},{... | collective-permute-start | bytes 1179656 | tf_op jit(solution)/shard_map/ppermute | solution.py:315

commit v8 on v7

--- a/solution.py
+++ b/solution.py
@@ -45,15 +45,10 @@
     return jnp.dot(left, right, preferred_element_type=F32)
 
 
-def pick_kernel(flag_hbm, tokens_hbm, out_ref, left_ref, right_ref, flag_ref, tokens_ref, sems):
-    rows = out_ref.shape[0]
+def pick_kernel(seat_ref, flag_ref, tokens_ref, cot_ref, left_ref, right_ref, *refs):
+    blocks, picked_ref = refs[:-1], refs[-1]
+    rows = cot_ref.shape[0]
     count = tokens_ref.shape[0]
-    copies = (pltpu.make_async_copy(flag_hbm, flag_ref, sems.at[0]),
-              pltpu.make_async_copy(tokens_hbm, tokens_ref, sems.at[1]))
-    for copy in copies:
-        copy.start()
-    for copy in copies:
-        copy.wait()
     flags = (flag_ref[...] == 1).astype(F32)
     before = lax.broadcasted_iota(jnp.int32, (count, count), 0)
     after = lax.broadcasted_iota(jnp.int32, (count, count), 1)
@@ -62,28 +57,29 @@
     chosen = (jnp.broadcast_to(ranks, (rows, count)) == slots) & (
         jnp.broadcast_to(flags, (rows, count)) == 1.0
     )
-    picked = nn_dot(chosen.astype(BF), tokens_ref[...]).astype(BF)
+    picked_ref[...] = nn_dot(chosen.astype(BF), tokens_ref[...]).astype(BF)
     middle = left_ref.shape[1]
-    out_ref[...] = picked
-    left_ref[...] = picked[:, :middle]
-    right_ref[...] = picked[:, middle:]
-
-
-def pick(modality, tokens, rows):
-    width = tokens.shape[1]
+    left_ref[...] = picked_ref[:, :middle]
+    right_ref[...] = picked_ref[:, middle:]
+    part = picked_ref.shape[1] // len(blocks)
+    for m, block in enumerate(blocks):
+        span = pl.ds(pl.multiple_of((seat_ref[0] ^ m) * part, part), part)
+        block[:, :part] = picked_ref[:, span]
+        block[:, part:] = cot_ref[:, span]
+
+
+def pick(seat, modality, tokens, out_grad, groups):
+    rows, width = out_grad.shape
+    half, block = shape((rows, width // 2)), shape((rows, 2 * width // groups))
     return pl.pallas_call(
         pick_kernel,
-        in_specs=[HBM, HBM],
-        out_specs=[VMEM] * 3,
-        out_shape=[shape((rows, width)), shape((rows, width // 2)), shape((rows, width // 2))],
-        scratch_shapes=[
-            pltpu.VMEM((1, modality.shape[0]), modality.dtype),
-            pltpu.VMEM(tokens.shape, BF),
-            pltpu.SemaphoreType.DMA((2,)),
-        ],
-        compiler_params=grant(least=ALL_VMEM),
+        in_specs=[pl.BlockSpec(memory_space=pltpu.SMEM)] + [VMEM] * 3,
+        out_specs=[VMEM] * (2 + groups),
+        out_shape=[half, half] + [block] * groups,
+        scratch_shapes=[pltpu.VMEM((rows, width), BF)],
+        compiler_params=grant(),
         name="pick",
-    )(modality.reshape(1, -1), tokens)
+    )(seat, modality.reshape(1, -1), tokens, out_grad)
 
 
 def streamed(steps, depth, copies, body, first):
@@ -302,14 +298,13 @@
 
 
 def on_device(tokens, modality, gate, up, down, out_grad):
-    count, width = out_grad.shape
+    _, width = out_grad.shape
     groups = lax.axis_size("seq")
     ring = lax.axis_size("dp") // CORES
     part = width // groups
-    starts = [(lax.axis_index("seq") ^ m) * part for m in range(groups)]
+    seat = lax.axis_index("seq").reshape(1)
     first = (lax.axis_index("dp") < CORES).astype(jnp.int32).reshape(1)
-    tokens, modality, first, *starts = lax.optimization_barrier(
-        (tokens, modality, first, *starts))
+    tokens, modality, first, seat = lax.optimization_barrier((tokens, modality, first, seat))
 
     def shift(value, k):
         return lax.ppermute(value, "dp", [
@@ -325,14 +320,8 @@
     def gathered(block):
         return jnp.concatenate([block] + [shift(block, k) for k in range(1, ring)], axis=0)
 
-    def cut(matrix, m):
-        return lax.dynamic_slice_in_dim(matrix, starts[m], part, axis=1)
-
-    def slices_of(tok_block, cot_block):
-        def both(m):
-            return jnp.concatenate([cut(tok_block, m), cut(cot_block, m)], axis=1)
-
-        small = jnp.stack([both(0)] + [across(both(m), m) for m in range(1, groups)])
+    def slices_of(blocks):
+        small = jnp.stack([blocks[0]] + [across(blocks[m], m) for m in range(1, groups)])
         pieces = [small] + [shift(small, k) for k in range(1, ring)]
         own = jnp.stack(pieces, axis=1)
         mate = swap(own)
@@ -381,12 +370,12 @@
     def stack(held):
         return jnp.concatenate(sum(held, []), axis=0)
 
-    block, *sides = pick(modality, tokens, count)
-    tok = [gathered(side) for side in sides]
+    left, right, *blocks = pick(seat, modality, tokens, out_grad, groups)
+    tok = [gathered(side) for side in (left, right)]
     tok_mate = []
     for side in tok:
         tok_mate.append(swap(side))
-    tok_all, cot_all = slices_of(block, out_grad)
+    tok_all, cot_all = slices_of(blocks)
     cot = gathered(out_grad)
     cot_mate = swap(cot)
     before = enter(tok[0], tok_mate[0], gate, up)

time: 184 us -> 181 us (0.984)
  local copies, waits for them, and re-layouts: 5.89 us -> 3.64 us
    dynamic_slice x2 -> x0, local copies, waits for them, and re-layouts: 2.05 us -> none  [cut(): return lax.dynamic_slice_in_dim(matrix, starts[m], part, axis=1)]
  transfers between devices with their start and end apart: 36 -> 36, of which waited for: 10 -> 11; matrix products, arithmetic and copies ran while one was open for 11% -> 9% of each run, Pallas kernels for 20% -> 20%
where the time goes in v8:
time: 181 us
  starting transfers between devices  67.6 us (37%)
  waiting for transfers between devices  56.1 us (31%)
  Pallas kernels  37.3 us (21%)
  matrix products  13.6 us (8%)
  local copies, waits for them, and re-layouts  3.64 us (2%)
    ppermute x13, starting transfers between devices, shift(): lax.ppermute(value, 'dp', [(z * CORES + c, (z + k) % ring * CORES + c) fo...  38.5 us
    ppermute x15, waiting for transfers between devices, across(): return lax.ppermute(value, 'seq', [(g, g ^ mask) for g in range(groups)])  29.3 us
    ppermute x13, waiting for transfers between devices, shift(): lax.ppermute(value, 'dp', [(z * CORES + c, (z + k) % ring * CORES + c) fo...  25.2 us
    ppermute x15, starting transfers between devices, across(): return lax.ppermute(value, 'seq', [(g, g ^ mask) for g in range(groups)])  19.6 us
    pallas_call x1, Pallas kernels, leave(): pl.pallas_call(lambda *refs: leave_kernel(step, *refs), in_specs=[VMEM] *...  16.4 us
    dot_general x3, matrix products, rows_dot(): lax.dot_general(left, right, (((0,), (0,)), ((), ())), preferred_element_...  13.6 us
    pallas_call x2, Pallas kernels, enter(): pl.pallas_call(lambda *refs: enter_kernel(tile, last, *refs), in_specs=[V...  12.6 us
    ppermute x3, starting transfers between devices, along(): lax.ppermute(value, 'dp', [(a * CORES + c, b * CORES + c) for a, b in pai...  8.6 us
  transfers between devices with their start and end apart: 36, of which 11 were waited for; matrix products, arithmetic and copies ran while one was open for 9% of the time, Pallas kernels for 20%

profile of v8, /device:TPU:0, one launch (start us, length us, event | category | flops | bytes accessed | tf_op | source)
XLA Modules:
  0.0 181.1 jit_solution(8630041497967833656)
XLA Ops:
  0.6 0.9 copy-done
  1.6 0.9 copy-done.1
  2.5 0.7 copy-done.2
  3.2 0.3 pick.1
  3.5 3.1 %collective-permute-start = (bf16[24,2048]{1,0:T(8,128)(2,1)S(1)}, bf16[24,2048]{1,0:T(8,128)(2,1)S(1)}, u32[]{:S(2)}, u32[]{:S(2)}) collective-permute-start(bf16[24,2048]{1,0:T(8,128)(2,1)S(1)} %get-tuple-element.45), channel_id=1, source_target_pairs={{0,8},{4,12},{8,16},{12,20},{16,24},{20,28},{24,0},{28,4},{1,9},{5... | collective-permute-start | bytes 294920 | tf_op jit(solution)/shard_map/ppermute | solution.py:310
  6.6 2.6 %collective-permute-start.1 = (bf16[24,2048]{1,0:T(8,128)(2,1)S(1)}, bf16[24,2048]{1,0:T(8,128)(2,1)S(1)}, u32[]{:S(2)}, u32[]{:S(2)}) collective-permute-start(bf16[24,2048]{1,0:T(8,128)(2,1)S(1)} %get-tuple-element.45), channel_id=1, source_target_pairs={{0,16},{4,20},{8,24},{12,28},{16,0},{20,4},{24,8},{28,12},{1,17},{... | collective-permute-start | bytes 294920 | tf_op jit(solution)/shard_map/ppermute | solution.py:310
  9.2 2.4 %collective-permute-start.19 = (bf16[24,2048]{1,0:T(8,128)(2,1)S(1)}, bf16[24,2048]{1,0:T(8,128)(2,1)S(1)}, u32[]{:S(2)}, u32[]{:S(2)}) collective-permute-start(bf16[24,2048]{1,0:T(8,128)(2,1)S(1)} %get-tuple-element.64), channel_id=1, source_target_pairs={{0,3},{1,2},{2,1},{3,0},{4,7},{5,6},{6,5},{7,4},{8,11},{9,10},{10,... | collective-permute-start | bytes 294920 | tf_op jit(solution)/shard_map/ppermute | solution.py:318
  11.7 0.5 collective-permute-start.18
  12.2 0.5 collective-permute-start.17
  12.7 2.3 %collective-permute-done.19 = bf16[24,2048]{1,0:T(8,128)(2,1)S(1)} collective-permute-done((bf16[24,2048]{1,0:T(8,128)(2,1)S(1)}, bf16[24,2048]{1,0:T(8,128)(2,1)S(1)}, u32[]{:S(2)}, u32[]{:S(2)}) %collective-permute-start.19) | collective-permute-done | bytes 98336 | tf_op jit(solution)/shard_map/ppermute | solution.py:318
  15.0 1.3 collective-permute-start.2
  16.4 0.6 collective-permute-start.4
  17.1 1.3 collective-permute-start.5
  18.4 2.0 %collective-permute-start.6 = (bf16[24,2048]{1,0:T(8,128)(2,1)S(1)}, bf16[24,2048]{1,0:T(8,128)(2,1)S(1)}, u32[]{:S(2)}, u32[]{:S(2)}) collective-permute-start(bf16[24,2048]{1,0:T(8,128)(2,1)S(1)} %get-tuple-element.46), channel_id=1, source_target_pairs={{0,24},{4,28},{8,0},{12,4},{16,8},{20,12},{24,16},{28,20},{1,25},{... | collective-permute-start | bytes 294920 | tf_op jit(solution)/shard_map/ppermute | solution.py:310
  20.4 0.6 collective-permute-start.8
  21.0 0.7 collective-permute-done.2
  21.7 0.9 collective-permute-start.9
  22.6 1.4 collective-permute-done.4
  23.9 1.6 collective-permute-start.10
  25.5 7.8 %collective-permute-done.5 = bf16[24,2048]{1,0:T(8,128)(2,1)S(1)} collective-permute-done((bf16[24,2048]{1,0:T(8,128)(2,1)S(1)}, bf16[24,2048]{1,0:T(8,128)(2,1)S(1)}, u32[]{:S(2)}, u32[]{:S(2)}) %collective-permute-start.5) | collective-permute-done | bytes 98336 | tf_op jit(solution)/shard_map/ppermute | solution.py:310
  33.3 3.1 %collective-permute-start.21 = (bf16[4,24,2048]{2,1,0:T(8,128)(2,1)S(1)}, bf16[4,24,2048]{2,1,0:T(8,128)(2,1)S(1)}, u32[]{:S(2)}, u32[]{:S(2)}) collective-permute-start(bf16[4,24,2048]{2,1,0:T(8,128)(2,1)S(1)} %get-tuple-element.84), channel_id=1, source_target_pairs={{0,16},{4,20},{8,24},{12,28},{16,0},{20,4},{24,8},{28,12},{1,17},{... | collective-permute-start | bytes 1179656 | tf_op jit(solution)/shard_map/ppermute | solution.py:310
  36.4 20.4 %collective-permute-start.20 = (bf16[4,24,2048]{2,1,0:T(8,128)(2,1)S(1)}, bf16[4,24,2048]{2,1,0:T(8,128)(2,1)S(1)}, u32[]{:S(2)}, u32[]{:S(2)}) collective-permute-start(bf16[4,24,2048]{2,1,0:T(8,128)(2,1)S(1)} %get-tuple-element.84), channel_id=1, source_target_pairs={{0,8},{4,12},{8,16},{12,20},{16,24},{20,28},{24,0},{28,4},{1,9},{5... | collective-permute-start | bytes 1179656 | tf_op jit(solution)/shard_map/ppermute | solution.py:310
  56.9 0.1 collective-permute-start.3
  57.0 0.6 collective-permute-start.7
  57.6 1.7 collective-permute-done.7.refs_1_
  59.2 0.1 collective-permute-start.11
  59.4 6.3 %enter.2 = (f32[192,1792]{1,0:T(8,128)S(1)}, f32[192,1792]{1,0:T(8,128)S(1)}) custom-call(bf16[96,2048]{1,0:T(8,128)(2,1)S(1)} %constant_dynamic-update-slice_fusion.4.refs_0_, bf16[96,2048]{1,0:T(8,128)(2,1)S(1)} %collective-permute-done.7.refs_1_, bf16[4096,1792]{1,0:T(8,128)(2,1)} %refs_3_.5, bf16[4096,1792]{1,0:T(8,128)(2,1)} %refs_4_.1), custom_call_target="tpu_custom_call" | custom-call | flops 2818572288 | bytes 14680064 | tf_op jit(solution)/shard_map/enter/pallas_call | solution.py:156
  65.7 6.3 %enter.3 = (bf16[192,1792]{1,0:T(8,128)(2,1)S(1)}, f32[192,1792]{1,0:T(8,128)S(1)}, f32[192,1792]{1,0:T(8,128)S(1)}) custom-call(bf16[96,2048]{1,0:T(8,128)(2,1)S(1)} %constant_dynamic-update-slice_fusion.refs_0_, bf16[96,2048]{1,0:T(8,128)(2,1)S(1)} %collective-permute-done.3.refs_1_, bf16[4096,1792]{1,0:T(8,128)(2,1)} %refs_3_.5, ...), custom_call_target="tpu_custom_call" | custom-call | flops 2818572288 | bytes 14680064 | tf_op jit(solution)/shard_map/enter/pallas_call | solution.py:156
  72.0 1.9 %collective-permute-start.32 = (bf16[192,1792]{1,0:T(8,128)(2,1)S(1)}, bf16[192,1792]{1,0:T(8,128)(2,1)S(1)}, u32[]{:S(2)}, u32[]{:S(2)}) collective-permute-start(bf16[192,1792]{1,0:T(8,128)(2,1)S(1)} %get-tuple-element.72.refs_0_), channel_id=1, source_target_pairs={{0,1},{1,0},{2,3},{3,2},{4,5},{5,4},{6,7},{7,6},{8,9},{9,8},{10,11... | collective-permute-start | bytes 2064392 | tf_op jit(solution)/shard_map/ppermute | solution.py:318
  73.9 1.4 collective-permute-start.33
  75.3 3.1 %collective-permute-done.21 = bf16[4,24,2048]{2,1,0:T(8,128)(2,1)S(1)} collective-permute-done((bf16[4,24,2048]{2,1,0:T(8,128)(2,1)S(1)}, bf16[4,24,2048]{2,1,0:T(8,128)(2,1)S(1)}, u32[]{:S(2)}, u32[]{:S(2)}) %collective-permute-start.21) | collective-permute-done | bytes 393248 | tf_op jit(solution)/shard_map/ppermute | solution.py:310
  78.4 0.3 pad_maximum_fusion.1
  78.7 0.1 collective-permute-start.23
  78.8 7.7 %turn.1 = (bf16[192,1792]{1,0:T(8,128)(2,1)S(1)}, bf16[192,1792]{1,0:T(8,128)(2,1)S(1)}) custom-call(bf16[96,4096]{1,0:T(8,128)(2,1)S(1)} %constant_dynamic-update-slice_fusion.8.refs_0_, bf16[96,4096]{1,0:T(8,128)(2,1)S(1)} %collective-permute-done.11.refs_1_, bf16[1792,4096]{1,0:T(8,128)(2,1)} %refs_5_.1, f32[192,1792]{1,0:T(8,128)S(1)} %get-tuple-element.50.refs_3_, ...), custom_call_target="tpu_custom_call" | custom-call | flops 2818572288 | bytes 14680064 | tf_op jit(solution)/shard_map/turn/pallas_call | solution.py:200
  86.5 2.0 %collective-permute-start.28 = (bf16[192,1792]{1,0:T(8,128)(2,1)S(1)}, bf16[192,1792]{1,0:T(8,128)(2,1)S(1)}, u32[]{:S(2)}, u32[]{:S(2)}) collective-permute-start(bf16[192,1792]{1,0:T(8,128)(2,1)S(1)} %get-tuple-element.52.refs_1_), channel_id=1, source_target_pairs={{0,1},{1,0},{2,3},{3,2},{4,5},{5,4},{6,7},{7,6},{8,9},{9,8},{10,11... | collective-permute-start | bytes 2064392 | tf_op jit(solution)/shard_map/ppermute | solution.py:318
  88.5 0.8 collective-permute-start.29
  89.2 16.4 %leave.1 = (bf16[2,96,4096]{2,1,0:T(8,128)(2,1)S(1)}, bf16[2,96,4096]{2,1,0:T(8,128)(2,1)S(1)}) custom-call(bf16[192,1792]{1,0:T(8,128)(2,1)S(1)} %get-tuple-element.72.refs_0_, bf16[192,1792]{1,0:T(8,128)(2,1)S(1)} %get-tuple-element.52.refs_1_, bf16[192,1792]{1,0:T(8,128)(2,1)S(1)} %get-tuple-element.65.refs_2_, bf16[4096,1792]{1,0:T(8,128)(2,1)} %refs_3_.5, ...), custom_call_target="tpu_custom_call" | custom-call | flops 8455716864 | bytes 44040192 | tf_op jit(solution)/shard_map/leave/pallas_call | solution.py:247
  105.6 1.4 collective-permute-start.24
  107.1 0.1 collective-permute-start.12
  107.2 0.7 collective-permute-start.30
  108.0 1.3 collective-permute-start.31
  109.4 20.9 %collective-permute-done.30 = bf16[96,1792]{1,0:T(8,128)(2,1)S(1)} collective-permute-done((bf16[96,1792]{1,0:T(8,128)(2,1)S(1)}, bf16[96,1792]{1,0:T(8,128)(2,1)S(1)}, u32[]{:S(2)}, u32[]{:S(2)}) %collective-permute-start.30) | collective-permute-done | bytes 344096 | tf_op jit(solution)/shard_map/ppermute | solution.py:318
  130.3 1.3 collective-permute-start.25
  131.6 0.4 collective-permute-start.34
  132.1 1.8 collective-permute-start.35
  133.9 0.3 pad_maximum_fusion
  134.2 0.1 copy.11
  134.4 4.5 %convolution_convert_fusion.1 = bf16[1024,1792]{1,0:T(8,128)(2,1)} fusion(bf16[768,1024]{1,0:T(8,128)(2,1)S(1)} %bitcast.29, bf16[768,1792]{1,0:T(8,128)(2,1)S(1)} %constant_dynamic-update-slice_fusion.17), kind=kOutput, calls=%fused_computation.1 | convolution fusion | flops 2820407296 | bytes 7995392 | tf_op jit(solution)/shard_map/dot_general | solution.py:295
  138.9 0.2 copy.12
  139.1 0.4 fold.1
  139.5 1.3 collective-permute-start.13
  140.8 4.6 %collective-permute-start.14 = (bf16[2,24,4096]{2,1,0:T(8,128)(2,1)S(1)}, bf16[2,24,4096]{2,1,0:T(8,128)(2,1)S(1)}, u32[]{:S(2)}, u32[]{:S(2)}) collective-permute-start(bf16[2,24,4096]{2,1,0:T(8,128)(2,1)S(1)} %get-tuple-element.58), channel_id=1, source_target_pairs={{0,8},{4,12},{8,16},{12,20},{16,24},{20,28},{1,9},{5,13},{9,17},{1... | collective-permute-start | bytes 1179656 | tf_op jit(solution)/shard_map/ppermute | solution.py:361
  145.4 3.2 %collective-permute-done.25 = bf16[192,1792]{1,0:T(8,128)(2,1)S(1)} collective-permute-done((bf16[192,1792]{1,0:T(8,128)(2,1)S(1)}, bf16[192,1792]{1,0:T(8,128)(2,1)S(1)}, u32[]{:S(2)}, u32[]{:S(2)}) %collective-permute-start.25) | collective-permute-done | bytes 688160 | tf_op jit(solution)/shard_map/ppermute | solution.py:318
  148.6 2.7 %collective-permute-start.15 = (bf16[2,24,4096]{2,1,0:T(8,128)(2,1)S(1)}, bf16[2,24,4096]{2,1,0:T(8,128)(2,1)S(1)}, u32[]{:S(2)}, u32[]{:S(2)}) collective-permute-start(bf16[2,24,4096]{2,1,0:T(8,128)(2,1)S(1)} %get-tuple-element.60), channel_id=1, source_target_pairs={{0,8},{4,12},{24,16},{28,20},{1,9},{5,13},{25,17},{29,21},{2,10},{... | collective-permute-start | bytes 1179656 | tf_op jit(solution)/shard_map/ppermute | solution.py:361
  151.5 1.8 collective-permute-start.26
  153.3 0.8 collective-permute-done.35
  154.1 1.3 collective-permute-start.27
  155.6 4.5 %convolution_convert_fusion = bf16[1792,1024]{1,0:T(8,128)(2,1)} fusion(bf16[768,1792]{1,0:T(8,128)(2,1)S(1)} %constant_dynamic-update-slice_fusion.22, bf16[768,1024]{1,0:T(8,128)(2,1)S(1)} %bitcast.31), kind=kOutput, calls=%fused_computation | convolution fusion | flops 2820407296 | bytes 7995392 | tf_op jit(solution)/shard_map/dot_general | solution.py:295
  160.3 2.0 %collective-permute-done.27 = bf16[96,1792]{1,0:T(8,128)(2,1)S(1)} collective-permute-done((bf16[96,1792]{1,0:T(8,128)(2,1)S(1)}, bf16[96,1792]{1,0:T(8,128)(2,1)S(1)}, u32[]{:S(2)}, u32[]{:S(2)}) %collective-permute-start.27) | collective-permute-done | bytes 344096 | tf_op jit(solution)/shard_map/ppermute | solution.py:318
  162.3 0.1 add_convert_fusion
  162.4 1.0 collective-permute-start.16
  163.4 4.5 %convolution_convert_fusion.2 = bf16[1024,1792]{1,0:T(8,128)(2,1)} fusion(bf16[768,1024]{1,0:T(8,128)(2,1)S(1)} %bitcast.30, bf16[768,1792]{1,0:T(8,128)(2,1)S(1)} %constant_dynamic-update-slice_fusion.12), kind=kOutput, calls=%fused_computation.2 | convolution fusion | flops 2820407296 | bytes 7995392 | tf_op jit(solution)/shard_map/dot_general | solution.py:295
  167.9 12.2 %collective-permute-done.16 = bf16[2,24,4096]{2,1,0:T(8,128)(2,1)S(1)} collective-permute-done((bf16[2,24,4096]{2,1,0:T(8,128)(2,1)S(1)}, bf16[2,24,4096]{2,1,0:T(8,128)(2,1)S(1)}, u32[]{:S(2)}, u32[]{:S(2)}) %collective-permute-start.16) | collective-permute-done | bytes 393248 | tf_op jit(solution)/shard_map/ppermute | solution.py:310
  180.2 0.9 fusion.2
  (63 shorter events, 1.0 us)
Async XLA Ops:
  0.6 0.9 copy-start
  1.6 0.9 copy-start.1
  2.5 0.7 copy-start.2
  3.5 14.9 %collective-permute-start = (bf16[24,2048]{1,0:T(8,128)(2,1)S(1)}, bf16[24,2048]{1,0:T(8,128)(2,1)S(1)}, u32[]{:S(2)}, u32[]{:S(2)}) collective-permute-start(bf16[24,2048]{1,0:T(8,128)(2,1)S(1)} %get-tuple-element.45), channel_id=1, source_target_pairs={{0,8},{4,12},{8,16},{12,20},{16,24},{20,28},{24,0},{28,4},{1,9},{5... | collective-permute-start | bytes 294920 | tf_op jit(solution)/shard_map/ppermute | solution.py:310
  6.6 13.8 %collective-permute-start.1 = (bf16[24,2048]{1,0:T(8,128)(2,1)S(1)}, bf16[24,2048]{1,0:T(8,128)(2,1)S(1)}, u32[]{:S(2)}, u32[]{:S(2)}) collective-permute-start(bf16[24,2048]{1,0:T(8,128)(2,1)S(1)} %get-tuple-element.45), channel_id=1, source_target_pairs={{0,16},{4,20},{8,24},{12,28},{16,0},{20,4},{24,8},{28,12},{1,17},{... | collective-permute-start | bytes 294920 | tf_op jit(solution)/shard_map/ppermute | solution.py:310
  9.2 5.8 %collective-permute-start.19 = (bf16[24,2048]{1,0:T(8,128)(2,1)S(1)}, bf16[24,2048]{1,0:T(8,128)(2,1)S(1)}, u32[]{:S(2)}, u32[]{:S(2)}) collective-permute-start(bf16[24,2048]{1,0:T(8,128)(2,1)S(1)} %get-tuple-element.64), channel_id=1, source_target_pairs={{0,3},{1,2},{2,1},{3,0},{4,7},{5,6},{6,5},{7,4},{8,11},{9,10},{10,... | collective-permute-start | bytes 294920 | tf_op jit(solution)/shard_map/ppermute | solution.py:318
  11.7 4.7 %collective-permute-start.18 = (bf16[24,2048]{1,0:T(8,128)(2,1)S(1)}, bf16[24,2048]{1,0:T(8,128)(2,1)S(1)}, u32[]{:S(2)}, u32[]{:S(2)}) collective-permute-start(bf16[24,2048]{1,0:T(8,128)(2,1)S(1)} %get-tuple-element.63), channel_id=1, source_target_pairs={{0,2},{1,3},{2,0},{3,1},{4,6},{5,7},{6,4},{7,5},{8,10},{9,11},{10,... | collective-permute-start | bytes 294920 | tf_op jit(solution)/shard_map/ppermute | solution.py:318
  12.2 4.9 %collective-permute-start.17 = (bf16[24,2048]{1,0:T(8,128)(2,1)S(1)}, bf16[24,2048]{1,0:T(8,128)(2,1)S(1)}, u32[]{:S(2)}, u32[]{:S(2)}) collective-permute-start(bf16[24,2048]{1,0:T(8,128)(2,1)S(1)} %get-tuple-element.62), channel_id=1, source_target_pairs={{0,1},{1,0},{2,3},{3,2},{4,5},{5,4},{6,7},{7,6},{8,9},{9,8},{10,11... | collective-permute-start | bytes 294920 | tf_op jit(solution)/shard_map/ppermute | solution.py:318
  15.0 6.7 %collective-permute-start.2 = (bf16[24,2048]{1,0:T(8,128)(2,1)S(1)}, bf16[24,2048]{1,0:T(8,128)(2,1)S(1)}, u32[]{:S(2)}, u32[]{:S(2)}) collective-permute-start(bf16[24,2048]{1,0:T(8,128)(2,1)S(1)} %get-tuple-element.45), channel_id=1, source_target_pairs={{0,24},{4,28},{8,0},{12,4},{16,8},{20,12},{24,16},{28,20},{1,25},{... | collective-permute-start | bytes 294920 | tf_op jit(solution)/shard_map/ppermute | solution.py:310
  16.4 7.5 %collective-permute-start.4 = (bf16[24,2048]{1,0:T(8,128)(2,1)S(1)}, bf16[24,2048]{1,0:T(8,128)(2,1)S(1)}, u32[]{:S(2)}, u32[]{:S(2)}) collective-permute-start(bf16[24,2048]{1,0:T(8,128)(2,1)S(1)} %get-tuple-element.46), channel_id=1, source_target_pairs={{0,8},{4,12},{8,16},{12,20},{16,24},{20,28},{24,0},{28,4},{1,9},{5... | collective-permute-start | bytes 294920 | tf_op jit(solution)/shard_map/ppermute | solution.py:310
  17.1 16.3 %collective-permute-start.5 = (bf16[24,2048]{1,0:T(8,128)(2,1)S(1)}, bf16[24,2048]{1,0:T(8,128)(2,1)S(1)}, u32[]{:S(2)}, u32[]{:S(2)}) collective-permute-start(bf16[24,2048]{1,0:T(8,128)(2,1)S(1)} %get-tuple-element.46), channel_id=1, source_target_pairs={{0,16},{4,20},{8,24},{12,28},{16,0},{20,4},{24,8},{28,12},{1,17},{... | collective-permute-start | bytes 294920 | tf_op jit(solution)/shard_map/ppermute | solution.py:310
  18.4 14.9 %collective-permute-start.6 = (bf16[24,2048]{1,0:T(8,128)(2,1)S(1)}, bf16[24,2048]{1,0:T(8,128)(2,1)S(1)}, u32[]{:S(2)}, u32[]{:S(2)}) collective-permute-start(bf16[24,2048]{1,0:T(8,128)(2,1)S(1)} %get-tuple-element.46), channel_id=1, source_target_pairs={{0,24},{4,28},{8,0},{12,4},{16,8},{20,12},{24,16},{28,20},{1,25},{... | collective-permute-start | bytes 294920 | tf_op jit(solution)/shard_map/ppermute | solution.py:310
  20.4 16.1 %collective-permute-start.8 = (bf16[24,4096]{1,0:T(8,128)(2,1)S(1)}, bf16[24,4096]{1,0:T(8,128)(2,1)S(1)}, u32[]{:S(2)}, u32[]{:S(2)}) collective-permute-start(bf16[24,4096]{1,0:T(8,128)(2,1)S(1)} %copy-done), channel_id=1, source_target_pairs={{0,8},{4,12},{8,16},{12,20},{16,24},{20,28},{24,0},{28,4},{1,9},{5... | collective-permute-start | bytes 589832 | tf_op jit(solution)/shard_map/ppermute | solution.py:310
  21.7 35.2 %collective-permute-start.9 = (bf16[24,4096]{1,0:T(8,128)(2,1)S(1)}, bf16[24,4096]{1,0:T(8,128)(2,1)S(1)}, u32[]{:S(2)}, u32[]{:S(2)}) collective-permute-start(bf16[24,4096]{1,0:T(8,128)(2,1)S(1)} %copy-done), channel_id=1, source_target_pairs={{0,16},{4,20},{8,24},{12,28},{16,0},{20,4},{24,8},{28,12},{1,17},{... | collective-permute-start | bytes 589832 | tf_op jit(solution)/shard_map/ppermute | solution.py:310
  23.9 33.1 %collective-permute-start.10 = (bf16[24,4096]{1,0:T(8,128)(2,1)S(1)}, bf16[24,4096]{1,0:T(8,128)(2,1)S(1)}, u32[]{:S(2)}, u32[]{:S(2)}) collective-permute-start(bf16[24,4096]{1,0:T(8,128)(2,1)S(1)} %copy-done), channel_id=1, source_target_pairs={{0,24},{4,28},{8,0},{12,4},{16,8},{20,12},{24,16},{28,20},{1,25},{... | collective-permute-start | bytes 589832 | tf_op jit(solution)/shard_map/ppermute | solution.py:310
  33.3 40.6 %collective-permute-start.22 = (bf16[4,24,2048]{2,1,0:T(8,128)(2,1)S(1)}, bf16[4,24,2048]{2,1,0:T(8,128)(2,1)S(1)}, u32[]{:S(2)}, u32[]{:S(2)}) collective-permute-start(bf16[4,24,2048]{2,1,0:T(8,128)(2,1)S(1)} %get-tuple-element.84), channel_id=1, source_target_pairs={{0,24},{4,28},{8,0},{12,4},{16,8},{20,12},{24,16},{28,20},{1,25},{... | collective-permute-start | bytes 1179656 | tf_op jit(solution)/shard_map/ppermute | solution.py:310
  33.3 45.1 %collective-permute-start.21 = (bf16[4,24,2048]{2,1,0:T(8,128)(2,1)S(1)}, bf16[4,24,2048]{2,1,0:T(8,128)(2,1)S(1)}, u32[]{:S(2)}, u32[]{:S(2)}) collective-permute-start(bf16[4,24,2048]{2,1,0:T(8,128)(2,1)S(1)} %get-tuple-element.84), channel_id=1, source_target_pairs={{0,16},{4,20},{8,24},{12,28},{16,0},{20,4},{24,8},{28,12},{1,17},{... | collective-permute-start | bytes 1179656 | tf_op jit(solution)/shard_map/ppermute | solution.py:310
  36.4 42.0 %collective-permute-start.20 = (bf16[4,24,2048]{2,1,0:T(8,128)(2,1)S(1)}, bf16[4,24,2048]{2,1,0:T(8,128)(2,1)S(1)}, u32[]{:S(2)}, u32[]{:S(2)}) collective-permute-start(bf16[4,24,2048]{2,1,0:T(8,128)(2,1)S(1)} %get-tuple-element.84), channel_id=1, source_target_pairs={{0,8},{4,12},{8,16},{12,20},{16,24},{20,28},{24,0},{28,4},{1,9},{5... | collective-permute-start | bytes 1179656 | tf_op jit(solution)/shard_map/ppermute | solution.py:310
  56.9 8.8 %collective-permute-start.3 = (bf16[96,2048]{1,0:T(8,128)(2,1)S(1)}, bf16[96,2048]{1,0:T(8,128)(2,1)S(1)}, u32[]{:S(2)}, u32[]{:S(2)}) collective-permute-start(bf16[96,2048]{1,0:T(8,128)(2,1)S(1)} %constant_dynamic-update-slice_fusion.refs_0_), channel_id=1, source_target_pairs={{0,4},{4,0},{8,12},{12,8},{16,20},{20,16},{24,28},{28,24},{1,5},{5... | collective-permute-start | bytes 1179656 | tf_op jit(solution)/shard_map/ppermute | solution.py:314
  57.0 2.2 %collective-permute-start.7 = (bf16[96,2048]{1,0:T(8,128)(2,1)S(1)}, bf16[96,2048]{1,0:T(8,128)(2,1)S(1)}, u32[]{:S(2)}, u32[]{:S(2)}) collective-permute-start(bf16[96,2048]{1,0:T(8,128)(2,1)S(1)} %constant_dynamic-update-slice_fusion.4.refs_0_), channel_id=1, source_target_pairs={{0,4},{4,0},{8,12},{12,8},{16,20},{20,16},{24,28},{28,24},{1,5},{5... | collective-permute-start | bytes 1179656 | tf_op jit(solution)/shard_map/ppermute | solution.py:314
  59.2 19.5 %collective-permute-start.11 = (bf16[96,4096]{1,0:T(8,128)(2,1)S(1)}, bf16[96,4096]{1,0:T(8,128)(2,1)S(1)}, u32[]{:S(2)}, u32[]{:S(2)}) collective-permute-start(bf16[96,4096]{1,0:T(8,128)(2,1)S(1)} %constant_dynamic-update-slice_fusion.8.refs_0_), channel_id=1, source_target_pairs={{0,4},{4,0},{8,12},{12,8},{16,20},{20,16},{24,28},{28,24},{1,5},{5... | collective-permute-start | bytes 2359304 | tf_op jit(solution)/shard_map/ppermute | solution.py:314
  72.0 35.0 %collective-permute-start.32 = (bf16[192,1792]{1,0:T(8,128)(2,1)S(1)}, bf16[192,1792]{1,0:T(8,128)(2,1)S(1)}, u32[]{:S(2)}, u32[]{:S(2)}) collective-permute-start(bf16[192,1792]{1,0:T(8,128)(2,1)S(1)} %get-tuple-element.72.refs_0_), channel_id=1, source_target_pairs={{0,1},{1,0},{2,3},{3,2},{4,5},{5,4},{6,7},{7,6},{8,9},{9,8},{10,11... | collective-permute-start | bytes 2064392 | tf_op jit(solution)/shard_map/ppermute | solution.py:318
  73.9 31.6 %collective-permute-start.33 = (bf16[192,1792]{1,0:T(8,128)(2,1)S(1)}, bf16[192,1792]{1,0:T(8,128)(2,1)S(1)}, u32[]{:S(2)}, u32[]{:S(2)}) collective-permute-start(bf16[192,1792]{1,0:T(8,128)(2,1)S(1)} %get-tuple-element.72.refs_0_), channel_id=1, source_target_pairs={{0,2},{1,3},{2,0},{3,1},{4,6},{5,7},{6,4},{7,5},{8,10},{9,11},{10,... | collective-permute-start | bytes 2064392 | tf_op jit(solution)/shard_map/ppermute | solution.py:318
  78.7 53.4 %collective-permute-start.23 = (bf16[4,4,24,2048]{3,2,0,1:T(8,128)(2,1)S(1)}, bf16[4,4,24,2048]{3,2,0,1:T(8,128)(2,1)S(1)}, u32[]{:S(2)}, u32[]{:S(2)}) collective-permute-start(bf16[4,4,24,2048]{3,2,0,1:T(8,128)(2,1)S(1)} %get-tuple-element.81), channel_id=1, source_target_pairs={{0,4},{4,0},{8,12},{12,8},{16,20},{20,16},{24,28},{28,24},{1,5},{5... | collective-permute-start | bytes 4718600 | tf_op jit(solution)/shard_map/ppermute | solution.py:314
  86.5 21.5 %collective-permute-start.28 = (bf16[192,1792]{1,0:T(8,128)(2,1)S(1)}, bf16[192,1792]{1,0:T(8,128)(2,1)S(1)}, u32[]{:S(2)}, u32[]{:S(2)}) collective-permute-start(bf16[192,1792]{1,0:T(8,128)(2,1)S(1)} %get-tuple-element.52.refs_1_), channel_id=1, source_target_pairs={{0,1},{1,0},{2,3},{3,2},{4,5},{5,4},{6,7},{7,6},{8,9},{9,8},{10,11... | collective-permute-start | bytes 2064392 | tf_op jit(solution)/shard_map/ppermute | solution.py:318
  88.5 18.7 %collective-permute-start.29 = (bf16[192,1792]{1,0:T(8,128)(2,1)S(1)}, bf16[192,1792]{1,0:T(8,128)(2,1)S(1)}, u32[]{:S(2)}, u32[]{:S(2)}) collective-permute-start(bf16[192,1792]{1,0:T(8,128)(2,1)S(1)} %get-tuple-element.52.refs_1_), channel_id=1, source_target_pairs={{0,2},{1,3},{2,0},{3,1},{4,6},{5,7},{6,4},{7,5},{8,10},{9,11},{10,... | collective-permute-start | bytes 2064392 | tf_op jit(solution)/shard_map/ppermute | solution.py:318
  105.6 35.2 %collective-permute-start.24 = (bf16[192,1792]{1,0:T(8,128)(2,1)S(1)}, bf16[192,1792]{1,0:T(8,128)(2,1)S(1)}, u32[]{:S(2)}, u32[]{:S(2)}) collective-permute-start(bf16[192,1792]{1,0:T(8,128)(2,1)S(1)} %get-tuple-element.65.refs_2_), channel_id=1, source_target_pairs={{0,1},{1,0},{2,3},{3,2},{4,5},{5,4},{6,7},{7,6},{8,9},{9,8},{10,11... | collective-permute-start | bytes 2064392 | tf_op jit(solution)/shard_map/ppermute | solution.py:318
  107.1 32.0 %collective-permute-start.12 = (bf16[2,96,4096]{2,1,0:T(8,128)(2,1)S(1)}, bf16[2,96,4096]{2,1,0:T(8,128)(2,1)S(1)}, u32[]{:S(2)}, u32[]{:S(2)}) collective-permute-start(bf16[2,96,4096]{2,1,0:T(8,128)(2,1)S(1)} %get-tuple-element.55), channel_id=1, source_target_pairs={{0,4},{4,0},{8,12},{12,8},{16,20},{20,16},{24,28},{28,24},{1,5},{5... | collective-permute-start | bytes 4718600 | tf_op jit(solution)/shard_map/ppermute | solution.py:314
  107.2 23.1 %collective-permute-start.30 = (bf16[96,1792]{1,0:T(8,128)(2,1)S(1)}, bf16[96,1792]{1,0:T(8,128)(2,1)S(1)}, u32[]{:S(2)}, u32[]{:S(2)}) collective-permute-start(bf16[96,1792]{1,0:T(8,128)(2,1)S(1)} %slice.66), channel_id=1, source_target_pairs={{0,1},{1,0},{2,3},{3,2},{4,5},{5,4},{6,7},{7,6},{8,9},{9,8},{10,11... | collective-permute-start | bytes 1032200 | tf_op jit(solution)/shard_map/ppermute | solution.py:318
  108.0 23.6 %collective-permute-start.31 = (bf16[96,1792]{1,0:T(8,128)(2,1)S(1)}, bf16[96,1792]{1,0:T(8,128)(2,1)S(1)}, u32[]{:S(2)}, u32[]{:S(2)}) collective-permute-start(bf16[96,1792]{1,0:T(8,128)(2,1)S(1)} %slice.67), channel_id=1, source_target_pairs={{0,2},{1,3},{2,0},{3,1},{4,6},{5,7},{6,4},{7,5},{8,10},{9,11},{10,... | collective-permute-start | bytes 1032200 | tf_op jit(solution)/shard_map/ppermute | solution.py:318
  130.3 18.3 %collective-permute-start.25 = (bf16[192,1792]{1,0:T(8,128)(2,1)S(1)}, bf16[192,1792]{1,0:T(8,128)(2,1)S(1)}, u32[]{:S(2)}, u32[]{:S(2)}) collective-permute-start(bf16[192,1792]{1,0:T(8,128)(2,1)S(1)} %get-tuple-element.65.refs_2_), channel_id=1, source_target_pairs={{0,2},{1,3},{2,0},{3,1},{4,6},{5,7},{6,4},{7,5},{8,10},{9,11},{10,... | collective-permute-start | bytes 2064392 | tf_op jit(solution)/shard_map/ppermute | solution.py:318
  131.6 19.9 %collective-permute-start.34 = (bf16[96,1792]{1,0:T(8,128)(2,1)S(1)}, bf16[96,1792]{1,0:T(8,128)(2,1)S(1)}, u32[]{:S(2)}, u32[]{:S(2)}) collective-permute-start(bf16[96,1792]{1,0:T(8,128)(2,1)S(1)} %slice.68), channel_id=1, source_target_pairs={{0,1},{1,0},{2,3},{3,2},{4,5},{5,4},{6,7},{7,6},{8,9},{9,8},{10,11... | collective-permute-start | bytes 1032200 | tf_op jit(solution)/shard_map/ppermute | solution.py:318
  132.1 22.0 %collective-permute-start.35 = (bf16[96,1792]{1,0:T(8,128)(2,1)S(1)}, bf16[96,1792]{1,0:T(8,128)(2,1)S(1)}, u32[]{:S(2)}, u32[]{:S(2)}) collective-permute-start(bf16[96,1792]{1,0:T(8,128)(2,1)S(1)} %slice.69), channel_id=1, source_target_pairs={{0,2},{1,3},{2,0},{3,1},{4,6},{5,7},{6,4},{7,5},{8,10},{9,11},{10,... | collective-permute-start | bytes 1032200 | tf_op jit(solution)/shard_map/ppermute | solution.py:318
  139.5 28.5 %collective-permute-start.13 = (bf16[2,24,4096]{2,1,0:T(8,128)(2,1)S(1)}, bf16[2,24,4096]{2,1,0:T(8,128)(2,1)S(1)}, u32[]{:S(2)}, u32[]{:S(2)}) collective-permute-start(bf16[2,24,4096]{2,1,0:T(8,128)(2,1)S(1)} %get-tuple-element.57), channel_id=1, source_target_pairs={{8,0},{12,4},{16,8},{20,12},{24,16},{28,20},{9,1},{13,5},{17,9},{2... | collective-permute-start | bytes 1179656 | tf_op jit(solution)/shard_map/ppermute | solution.py:361
  140.8 27.2 %collective-permute-start.14 = (bf16[2,24,4096]{2,1,0:T(8,128)(2,1)S(1)}, bf16[2,24,4096]{2,1,0:T(8,128)(2,1)S(1)}, u32[]{:S(2)}, u32[]{:S(2)}) collective-permute-start(bf16[2,24,4096]{2,1,0:T(8,128)(2,1)S(1)} %get-tuple-element.58), channel_id=1, source_target_pairs={{0,8},{4,12},{8,16},{12,20},{16,24},{20,28},{1,9},{5,13},{9,17},{1... | collective-permute-start | bytes 1179656 | tf_op jit(solution)/shard_map/ppermute | solution.py:361
  148.6 13.7 %collective-permute-start.15 = (bf16[2,24,4096]{2,1,0:T(8,128)(2,1)S(1)}, bf16[2,24,4096]{2,1,0:T(8,128)(2,1)S(1)}, u32[]{:S(2)}, u32[]{:S(2)}) collective-permute-start(bf16[2,24,4096]{2,1,0:T(8,128)(2,1)S(1)} %get-tuple-element.60), channel_id=1, source_target_pairs={{0,8},{4,12},{24,16},{28,20},{1,9},{5,13},{25,17},{29,21},{2,10},{... | collective-permute-start | bytes 1179656 | tf_op jit(solution)/shard_map/ppermute | solution.py:361
  151.5 8.7 %collective-permute-start.26 = (bf16[96,1792]{1,0:T(8,128)(2,1)S(1)}, bf16[96,1792]{1,0:T(8,128)(2,1)S(1)}, u32[]{:S(2)}, u32[]{:S(2)}) collective-permute-start(bf16[96,1792]{1,0:T(8,128)(2,1)S(1)} %slice.49), channel_id=1, source_target_pairs={{0,1},{1,0},{2,3},{3,2},{4,5},{5,4},{6,7},{7,6},{8,9},{9,8},{10,11... | collective-permute-start | bytes 1032200 | tf_op jit(solution)/shard_map/ppermute | solution.py:318
  154.1 8.2 %collective-permute-start.27 = (bf16[96,1792]{1,0:T(8,128)(2,1)S(1)}, bf16[96,1792]{1,0:T(8,128)(2,1)S(1)}, u32[]{:S(2)}, u32[]{:S(2)}) collective-permute-start(bf16[96,1792]{1,0:T(8,128)(2,1)S(1)} %slice.50), channel_id=1, source_target_pairs={{0,2},{1,3},{2,0},{3,1},{4,6},{5,7},{6,4},{7,5},{8,10},{9,11},{10,... | collective-permute-start | bytes 1032200 | tf_op jit(solution)/shard_map/ppermute | solution.py:318
  162.4 17.8 %collective-permute-start.16 = (bf16[2,24,4096]{2,1,0:T(8,128)(2,1)S(1)}, bf16[2,24,4096]{2,1,0:T(8,128)(2,1)S(1)}, u32[]{:S(2)}, u32[]{:S(2)}) collective-permute-start(bf16[2,24,4096]{2,1,0:T(8,128)(2,1)S(1)} %add_convert_fusion), channel_id=1, source_target_pairs={{0,16},{4,20},{8,24},{12,28},{16,0},{20,4},{24,8},{28,12},{1,17},{... | collective-permute-start | bytes 1179656 | tf_op jit(solution)/shard_map/ppermute | solution.py:310

commit v9 on v8

--- a/solution.py
+++ b/solution.py
@@ -355,7 +355,7 @@
         line = ring == 4
         sums = fold(first, own, mate, ring, ring + line)
         if not line:
-            return [sums[0]] + [shift(sums[k], -k) for k in range(1, ring)]
+            return [sums[0]] + [shift(sums[k], -k) for k in range(1, ring)], sums[0]
 
         def along(value, pairs):
             return lax.ppermute(value, "dp", [
@@ -365,7 +365,7 @@
         terms = [along(sums[1], [(1, 0), (2, 1), (3, 2)]),
                  along(sums[3], [(0, 1), (1, 2), (2, 3)])]
         mid = (sums[2].astype(F32) + far.astype(F32)).astype(BF)
-        return [sums[0], *terms, shift(mid, 2)]
+        return [sums[0], *terms, shift(mid, 2)], mid
 
     def stack(held):
         return jnp.concatenate(sum(held, []), axis=0)
@@ -387,10 +387,10 @@
     own, other = leave(hid, gb, ub, gate, up, down)
 
     mate = swap(other)
-    terms = returned(own, mate)
+    terms, last = returned(own, mate)
     all_hid = after(all_hid, terms[:1])
     all_gb = relay(all_gb)
-    all_ub = relay(after(all_ub, terms[:1]))
+    all_ub = relay(after(all_ub, [last]))
     down_grad = rows_dot(stack(all_hid), cot_all)
     gate_grad = rows_dot(tok_all, stack(all_gb))
     up_grad = rows_dot(tok_all, stack(all_ub))

time: 181 us -> 185 us (1.022)
  starting transfers between devices: 67.6 us -> 70.7 us
    ppermute x13, waiting for transfers between devices: 25.2 us -> 15 us  [shift(): lax.ppermute(value, 'dp', [(z * CORES + c, (z + k) % ring * CORES + c) fo...]
    ppermute x15, waiting for transfers between devices: 29.3 us -> 38 us  [across(): return lax.ppermute(value, 'seq', [(g, g ^ mask) for g in range(groups)])]
    ppermute x13, starting transfers between devices: 38.5 us -> 41.1 us  [shift(): lax.ppermute(value, 'dp', [(z * CORES + c, (z + k) % ring * CORES + c) fo...]
    ppermute x3, waiting for transfers between devices: 0.01 us -> 2.35 us  [along(): lax.ppermute(value, 'dp', [(a * CORES + c, b * CORES + c) for a, b in pai...]
  transfers between devices with their start and end apart: 36 -> 36, of which waited for: 11 -> 12; matrix products, arithmetic and copies ran while one was open for 9% -> 8% of each run, Pallas kernels for 20% -> 20%
where the time goes in v9:
time: 185 us
  starting transfers between devices  70.7 us (38%)
  waiting for transfers between devices  57 us (31%)
  Pallas kernels  37.3 us (20%)
  matrix products  13.6 us (7%)
  local copies, waits for them, and re-layouts  3.64 us (2%)
    ppermute x13, starting transfers between devices, shift(): lax.ppermute(value, 'dp', [(z * CORES + c, (z + k) % ring * CORES + c) fo...  41.1 us
    ppermute x15, waiting for transfers between devices, across(): return lax.ppermute(value, 'seq', [(g, g ^ mask) for g in range(groups)])  38 us
    ppermute x15, starting transfers between devices, across(): return lax.ppermute(value, 'seq', [(g, g ^ mask) for g in range(groups)])  19.5 us
    pallas_call x1, Pallas kernels, leave(): pl.pallas_call(lambda *refs: leave_kernel(step, *refs), in_specs=[VMEM] *...  16.4 us
    ppermute x13, waiting for transfers between devices, shift(): lax.ppermute(value, 'dp', [(z * CORES + c, (z + k) % ring * CORES + c) fo...  15 us
    dot_general x3, matrix products, rows_dot(): lax.dot_general(left, right, (((0,), (0,)), ((), ())), preferred_element_...  13.6 us
    pallas_call x2, Pallas kernels, enter(): pl.pallas_call(lambda *refs: enter_kernel(tile, last, *refs), in_specs=[V...  12.6 us
    ppermute x3, starting transfers between devices, along(): lax.ppermute(value, 'dp', [(a * CORES + c, b * CORES + c) for a, b in pai...  9.17 us
  transfers between devices with their start and end apart: 36, of which 12 were waited for; matrix products, arithmetic and copies ran while one was open for 8% of the time, Pallas kernels for 20%

profile of v9, /device:TPU:0, one launch (start us, length us, event | category | flops | bytes accessed | tf_op | source)
XLA Modules:
  0.0 185.1 jit_solution(5413943088364170968)
XLA Ops:
  0.6 0.9 copy-done
  1.6 0.9 copy-done.1
  2.5 0.7 copy-done.2
  3.2 0.3 pick.1
  3.5 3.1 %collective-permute-start = (bf16[24,2048]{1,0:T(8,128)(2,1)S(1)}, bf16[24,2048]{1,0:T(8,128)(2,1)S(1)}, u32[]{:S(2)}, u32[]{:S(2)}) collective-permute-start(bf16[24,2048]{1,0:T(8,128)(2,1)S(1)} %get-tuple-element.45), channel_id=1, source_target_pairs={{0,8},{4,12},{8,16},{12,20},{16,24},{20,28},{24,0},{28,4},{1,9},{5... | collective-permute-start | bytes 294920 | tf_op jit(solution)/shard_map/ppermute | solution.py:310
  6.6 2.6 %collective-permute-start.1 = (bf16[24,2048]{1,0:T(8,128)(2,1)S(1)}, bf16[24,2048]{1,0:T(8,128)(2,1)S(1)}, u32[]{:S(2)}, u32[]{:S(2)}) collective-permute-start(bf16[24,2048]{1,0:T(8,128)(2,1)S(1)} %get-tuple-element.45), channel_id=1, source_target_pairs={{0,16},{4,20},{8,24},{12,28},{16,0},{20,4},{24,8},{28,12},{1,17},{... | collective-permute-start | bytes 294920 | tf_op jit(solution)/shard_map/ppermute | solution.py:310
  9.2 2.4 %collective-permute-start.19 = (bf16[24,2048]{1,0:T(8,128)(2,1)S(1)}, bf16[24,2048]{1,0:T(8,128)(2,1)S(1)}, u32[]{:S(2)}, u32[]{:S(2)}) collective-permute-start(bf16[24,2048]{1,0:T(8,128)(2,1)S(1)} %get-tuple-element.64), channel_id=1, source_target_pairs={{0,3},{1,2},{2,1},{3,0},{4,7},{5,6},{6,5},{7,4},{8,11},{9,10},{10,... | collective-permute-start | bytes 294920 | tf_op jit(solution)/shard_map/ppermute | solution.py:318
  11.7 0.5 collective-permute-start.18
  12.2 0.5 collective-permute-start.17
  12.7 2.3 %collective-permute-done.19 = bf16[24,2048]{1,0:T(8,128)(2,1)S(1)} collective-permute-done((bf16[24,2048]{1,0:T(8,128)(2,1)S(1)}, bf16[24,2048]{1,0:T(8,128)(2,1)S(1)}, u32[]{:S(2)}, u32[]{:S(2)}) %collective-permute-start.19) | collective-permute-done | bytes 98336 | tf_op jit(solution)/shard_map/ppermute | solution.py:318
  15.0 1.3 collective-permute-start.2
  16.4 0.6 collective-permute-start.4
  17.1 1.3 collective-permute-start.5
  18.4 2.0 %collective-permute-start.6 = (bf16[24,2048]{1,0:T(8,128)(2,1)S(1)}, bf16[24,2048]{1,0:T(8,128)(2,1)S(1)}, u32[]{:S(2)}, u32[]{:S(2)}) collective-permute-start(bf16[24,2048]{1,0:T(8,128)(2,1)S(1)} %get-tuple-element.46), channel_id=1, source_target_pairs={{0,24},{4,28},{8,0},{12,4},{16,8},{20,12},{24,16},{28,20},{1,25},{... | collective-permute-start | bytes 294920 | tf_op jit(solution)/shard_map/ppermute | solution.py:310
  20.4 0.6 collective-permute-start.8
  21.0 0.7 collective-permute-done.2
  21.7 0.9 collective-permute-start.9
  22.6 1.4 collective-permute-done.4
  23.9 1.6 collective-permute-start.10
  25.5 7.8 %collective-permute-done.5 = bf16[24,2048]{1,0:T(8,128)(2,1)S(1)} collective-permute-done((bf16[24,2048]{1,0:T(8,128)(2,1)S(1)}, bf16[24,2048]{1,0:T(8,128)(2,1)S(1)}, u32[]{:S(2)}, u32[]{:S(2)}) %collective-permute-start.5) | collective-permute-done | bytes 98336 | tf_op jit(solution)/shard_map/ppermute | solution.py:310
  33.3 3.1 %collective-permute-start.21 = (bf16[4,24,2048]{2,1,0:T(8,128)(2,1)S(1)}, bf16[4,24,2048]{2,1,0:T(8,128)(2,1)S(1)}, u32[]{:S(2)}, u32[]{:S(2)}) collective-permute-start(bf16[4,24,2048]{2,1,0:T(8,128)(2,1)S(1)} %get-tuple-element.84), channel_id=1, source_target_pairs={{0,16},{4,20},{8,24},{12,28},{16,0},{20,4},{24,8},{28,12},{1,17},{... | collective-permute-start | bytes 1179656 | tf_op jit(solution)/shard_map/ppermute | solution.py:310
  36.4 20.4 %collective-permute-start.20 = (bf16[4,24,2048]{2,1,0:T(8,128)(2,1)S(1)}, bf16[4,24,2048]{2,1,0:T(8,128)(2,1)S(1)}, u32[]{:S(2)}, u32[]{:S(2)}) collective-permute-start(bf16[4,24,2048]{2,1,0:T(8,128)(2,1)S(1)} %get-tuple-element.84), channel_id=1, source_target_pairs={{0,8},{4,12},{8,16},{12,20},{16,24},{20,28},{24,0},{28,4},{1,9},{5... | collective-permute-start | bytes 1179656 | tf_op jit(solution)/shard_map/ppermute | solution.py:310
  56.9 0.1 collective-permute-start.3
  57.0 0.6 collective-permute-start.7
  57.6 1.7 collective-permute-done.7.refs_1_
  59.2 0.1 collective-permute-start.11
  59.4 6.3 %enter.2 = (f32[192,1792]{1,0:T(8,128)S(1)}, f32[192,1792]{1,0:T(8,128)S(1)}) custom-call(bf16[96,2048]{1,0:T(8,128)(2,1)S(1)} %constant_dynamic-update-slice_fusion.4.refs_0_, bf16[96,2048]{1,0:T(8,128)(2,1)S(1)} %collective-permute-done.7.refs_1_, bf16[4096,1792]{1,0:T(8,128)(2,1)} %refs_3_.5, bf16[4096,1792]{1,0:T(8,128)(2,1)} %refs_4_.1), custom_call_target="tpu_custom_call" | custom-call | flops 2818572288 | bytes 14680064 | tf_op jit(solution)/shard_map/enter/pallas_call | solution.py:156
  65.7 6.3 %enter.3 = (bf16[192,1792]{1,0:T(8,128)(2,1)S(1)}, f32[192,1792]{1,0:T(8,128)S(1)}, f32[192,1792]{1,0:T(8,128)S(1)}) custom-call(bf16[96,2048]{1,0:T(8,128)(2,1)S(1)} %constant_dynamic-update-slice_fusion.refs_0_, bf16[96,2048]{1,0:T(8,128)(2,1)S(1)} %collective-permute-done.3.refs_1_, bf16[4096,1792]{1,0:T(8,128)(2,1)} %refs_3_.5, ...), custom_call_target="tpu_custom_call" | custom-call | flops 2818572288 | bytes 14680064 | tf_op jit(solution)/shard_map/enter/pallas_call | solution.py:156
  72.0 1.9 %collective-permute-start.32 = (bf16[192,1792]{1,0:T(8,128)(2,1)S(1)}, bf16[192,1792]{1,0:T(8,128)(2,1)S(1)}, u32[]{:S(2)}, u32[]{:S(2)}) collective-permute-start(bf16[192,1792]{1,0:T(8,128)(2,1)S(1)} %get-tuple-element.72.refs_0_), channel_id=1, source_target_pairs={{0,1},{1,0},{2,3},{3,2},{4,5},{5,4},{6,7},{7,6},{8,9},{9,8},{10,11... | collective-permute-start | bytes 2064392 | tf_op jit(solution)/shard_map/ppermute | solution.py:318
  73.9 1.4 collective-permute-start.33
  75.3 3.1 %collective-permute-done.21 = bf16[4,24,2048]{2,1,0:T(8,128)(2,1)S(1)} collective-permute-done((bf16[4,24,2048]{2,1,0:T(8,128)(2,1)S(1)}, bf16[4,24,2048]{2,1,0:T(8,128)(2,1)S(1)}, u32[]{:S(2)}, u32[]{:S(2)}) %collective-permute-start.21) | collective-permute-done | bytes 393248 | tf_op jit(solution)/shard_map/ppermute | solution.py:310
  78.4 0.3 pad_maximum_fusion.1
  78.7 0.1 collective-permute-start.23
  78.8 7.7 %turn.1 = (bf16[192,1792]{1,0:T(8,128)(2,1)S(1)}, bf16[192,1792]{1,0:T(8,128)(2,1)S(1)}) custom-call(bf16[96,4096]{1,0:T(8,128)(2,1)S(1)} %constant_dynamic-update-slice_fusion.8.refs_0_, bf16[96,4096]{1,0:T(8,128)(2,1)S(1)} %collective-permute-done.11.refs_1_, bf16[1792,4096]{1,0:T(8,128)(2,1)} %refs_5_.1, f32[192,1792]{1,0:T(8,128)S(1)} %get-tuple-element.50.refs_3_, ...), custom_call_target="tpu_custom_call" | custom-call | flops 2818572288 | bytes 14680064 | tf_op jit(solution)/shard_map/turn/pallas_call | solution.py:200
  86.5 2.0 %collective-permute-start.28 = (bf16[192,1792]{1,0:T(8,128)(2,1)S(1)}, bf16[192,1792]{1,0:T(8,128)(2,1)S(1)}, u32[]{:S(2)}, u32[]{:S(2)}) collective-permute-start(bf16[192,1792]{1,0:T(8,128)(2,1)S(1)} %get-tuple-element.52.refs_1_), channel_id=1, source_target_pairs={{0,1},{1,0},{2,3},{3,2},{4,5},{5,4},{6,7},{7,6},{8,9},{9,8},{10,11... | collective-permute-start | bytes 2064392 | tf_op jit(solution)/shard_map/ppermute | solution.py:318
  88.5 0.8 collective-permute-start.29
  89.2 16.4 %leave.1 = (bf16[2,96,4096]{2,1,0:T(8,128)(2,1)S(1)}, bf16[2,96,4096]{2,1,0:T(8,128)(2,1)S(1)}) custom-call(bf16[192,1792]{1,0:T(8,128)(2,1)S(1)} %get-tuple-element.72.refs_0_, bf16[192,1792]{1,0:T(8,128)(2,1)S(1)} %get-tuple-element.52.refs_1_, bf16[192,1792]{1,0:T(8,128)(2,1)S(1)} %get-tuple-element.65.refs_2_, bf16[4096,1792]{1,0:T(8,128)(2,1)} %refs_3_.5, ...), custom_call_target="tpu_custom_call" | custom-call | flops 8455716864 | bytes 44040192 | tf_op jit(solution)/shard_map/leave/pallas_call | solution.py:247
  105.6 1.4 collective-permute-start.24
  107.2 0.7 collective-permute-start.30
  108.0 1.3 collective-permute-start.31
  109.4 20.9 %collective-permute-done.30 = bf16[96,1792]{1,0:T(8,128)(2,1)S(1)} collective-permute-done((bf16[96,1792]{1,0:T(8,128)(2,1)S(1)}, bf16[96,1792]{1,0:T(8,128)(2,1)S(1)}, u32[]{:S(2)}, u32[]{:S(2)}) %collective-permute-start.30) | collective-permute-done | bytes 344096 | tf_op jit(solution)/shard_map/ppermute | solution.py:318
  130.3 1.3 collective-permute-start.25
  131.6 0.4 collective-permute-start.34
  132.1 1.8 collective-permute-start.35
  133.9 0.3 pad_maximum_fusion
  134.2 0.2 copy.11
  134.4 0.1 copy.12
  134.5 4.5 %convolution_convert_fusion.1 = bf16[1024,1792]{1,0:T(8,128)(2,1)} fusion(bf16[768,1024]{1,0:T(8,128)(2,1)S(1)} %bitcast.29, bf16[768,1792]{1,0:T(8,128)(2,1)S(1)} %constant_dynamic-update-slice_fusion.17), kind=kOutput, calls=%fused_computation.1 | convolution fusion | flops 2820407296 | bytes 7995392 | tf_op jit(solution)/shard_map/dot_general | solution.py:295
  139.1 0.4 fold.1
  139.5 1.3 collective-permute-start.13
  140.8 4.6 %collective-permute-start.14 = (bf16[2,24,4096]{2,1,0:T(8,128)(2,1)S(1)}, bf16[2,24,4096]{2,1,0:T(8,128)(2,1)S(1)}, u32[]{:S(2)}, u32[]{:S(2)}) collective-permute-start(bf16[2,24,4096]{2,1,0:T(8,128)(2,1)S(1)} %get-tuple-element.58), channel_id=1, source_target_pairs={{0,8},{4,12},{8,16},{12,20},{16,24},{20,28},{1,9},{5,13},{9,17},{1... | collective-permute-start | bytes 1179656 | tf_op jit(solution)/shard_map/ppermute | solution.py:361
  145.4 8.7 %collective-permute-done.35 = bf16[96,1792]{1,0:T(8,128)(2,1)S(1)} collective-permute-done((bf16[96,1792]{1,0:T(8,128)(2,1)S(1)}, bf16[96,1792]{1,0:T(8,128)(2,1)S(1)}, u32[]{:S(2)}, u32[]{:S(2)}) %collective-permute-start.35) | collective-permute-done | bytes 344096 | tf_op jit(solution)/shard_map/ppermute | solution.py:318
  154.1 3.3 %collective-permute-start.15 = (bf16[2,24,4096]{2,1,0:T(8,128)(2,1)S(1)}, bf16[2,24,4096]{2,1,0:T(8,128)(2,1)S(1)}, u32[]{:S(2)}, u32[]{:S(2)}) collective-permute-start(bf16[2,24,4096]{2,1,0:T(8,128)(2,1)S(1)} %get-tuple-element.60), channel_id=1, source_target_pairs={{0,8},{4,12},{24,16},{28,20},{1,9},{5,13},{25,17},{29,21},{2,10},{... | collective-permute-start | bytes 1179656 | tf_op jit(solution)/shard_map/ppermute | solution.py:361
  157.6 4.5 %convolution_convert_fusion = bf16[1792,1024]{1,0:T(8,128)(2,1)} fusion(bf16[768,1792]{1,0:T(8,128)(2,1)S(1)} %constant_dynamic-update-slice_fusion.22, bf16[768,1024]{1,0:T(8,128)(2,1)S(1)} %bitcast.31), kind=kOutput, calls=%fused_computation | convolution fusion | flops 2820407296 | bytes 7995392 | tf_op jit(solution)/shard_map/dot_general | solution.py:295
  162.2 2.3 %collective-permute-done.15 = bf16[2,24,4096]{2,1,0:T(8,128)(2,1)S(1)} collective-permute-done((bf16[2,24,4096]{2,1,0:T(8,128)(2,1)S(1)}, bf16[2,24,4096]{2,1,0:T(8,128)(2,1)S(1)}, u32[]{:S(2)}, u32[]{:S(2)}) %collective-permute-start.15) | collective-permute-done | bytes 393248 | tf_op jit(solution)/shard_map/ppermute | solution.py:361
  164.5 0.1 add_convert_fusion
  164.6 3.6 %collective-permute-start.16 = (bf16[2,24,4096]{2,1,0:T(8,128)(2,1)S(1)}, bf16[2,24,4096]{2,1,0:T(8,128)(2,1)S(1)}, u32[]{:S(2)}, u32[]{:S(2)}) collective-permute-start(bf16[2,24,4096]{2,1,0:T(8,128)(2,1)S(1)} %add_convert_fusion), channel_id=1, source_target_pairs={{0,16},{4,20},{8,24},{12,28},{16,0},{20,4},{24,8},{28,12},{1,17},{... | collective-permute-start | bytes 1179656 | tf_op jit(solution)/shard_map/ppermute | solution.py:310
  168.3 1.5 collective-permute-start.26
  169.9 1.4 collective-permute-start.27
  171.4 4.9 %collective-permute-done.26 = bf16[96,1792]{1,0:T(8,128)(2,1)S(1)} collective-permute-done((bf16[96,1792]{1,0:T(8,128)(2,1)S(1)}, bf16[96,1792]{1,0:T(8,128)(2,1)S(1)}, u32[]{:S(2)}, u32[]{:S(2)}) %collective-permute-start.26) | collective-permute-done | bytes 344096 | tf_op jit(solution)/shard_map/ppermute | solution.py:318
  176.3 1.2 collective-permute-done.27
  177.5 4.5 %convolution_convert_fusion.2 = bf16[1024,1792]{1,0:T(8,128)(2,1)} fusion(bf16[768,1024]{1,0:T(8,128)(2,1)S(1)} %bitcast.30, bf16[768,1792]{1,0:T(8,128)(2,1)S(1)} %constant_dynamic-update-slice_fusion.12), kind=kOutput, calls=%fused_computation.2 | convolution fusion | flops 2820407296 | bytes 7995392 | tf_op jit(solution)/shard_map/dot_general | solution.py:295
  182.1 2.1 %collective-permute-done.16 = bf16[2,24,4096]{2,1,0:T(8,128)(2,1)S(1)} collective-permute-done((bf16[2,24,4096]{2,1,0:T(8,128)(2,1)S(1)}, bf16[2,24,4096]{2,1,0:T(8,128)(2,1)S(1)}, u32[]{:S(2)}, u32[]{:S(2)}) %collective-permute-start.16) | collective-permute-done | bytes 393248 | tf_op jit(solution)/shard_map/ppermute | solution.py:310
  184.2 0.9 fusion.2
  (63 shorter events, 1.1 us)
Async XLA Ops:
  0.6 0.9 copy-start
  1.6 0.9 copy-start.1
  2.5 0.7 copy-start.2
  3.5 14.9 %collective-permute-start = (bf16[24,2048]{1,0:T(8,128)(2,1)S(1)}, bf16[24,2048]{1,0:T(8,128)(2,1)S(1)}, u32[]{:S(2)}, u32[]{:S(2)}) collective-permute-start(bf16[24,2048]{1,0:T(8,128)(2,1)S(1)} %get-tuple-element.45), channel_id=1, source_target_pairs={{0,8},{4,12},{8,16},{12,20},{16,24},{20,28},{24,0},{28,4},{1,9},{5... | collective-permute-start | bytes 294920 | tf_op jit(solution)/shard_map/ppermute | solution.py:310
  6.6 13.8 %collective-permute-start.1 = (bf16[24,2048]{1,0:T(8,128)(2,1)S(1)}, bf16[24,2048]{1,0:T(8,128)(2,1)S(1)}, u32[]{:S(2)}, u32[]{:S(2)}) collective-permute-start(bf16[24,2048]{1,0:T(8,128)(2,1)S(1)} %get-tuple-element.45), channel_id=1, source_target_pairs={{0,16},{4,20},{8,24},{12,28},{16,0},{20,4},{24,8},{28,12},{1,17},{... | collective-permute-start | bytes 294920 | tf_op jit(solution)/shard_map/ppermute | solution.py:310
  9.2 5.8 %collective-permute-start.19 = (bf16[24,2048]{1,0:T(8,128)(2,1)S(1)}, bf16[24,2048]{1,0:T(8,128)(2,1)S(1)}, u32[]{:S(2)}, u32[]{:S(2)}) collective-permute-start(bf16[24,2048]{1,0:T(8,128)(2,1)S(1)} %get-tuple-element.64), channel_id=1, source_target_pairs={{0,3},{1,2},{2,1},{3,0},{4,7},{5,6},{6,5},{7,4},{8,11},{9,10},{10,... | collective-permute-start | bytes 294920 | tf_op jit(solution)/shard_map/ppermute | solution.py:318
  11.7 4.7 %collective-permute-start.18 = (bf16[24,2048]{1,0:T(8,128)(2,1)S(1)}, bf16[24,2048]{1,0:T(8,128)(2,1)S(1)}, u32[]{:S(2)}, u32[]{:S(2)}) collective-permute-start(bf16[24,2048]{1,0:T(8,128)(2,1)S(1)} %get-tuple-element.63), channel_id=1, source_target_pairs={{0,2},{1,3},{2,0},{3,1},{4,6},{5,7},{6,4},{7,5},{8,10},{9,11},{10,... | collective-permute-start | bytes 294920 | tf_op jit(solution)/shard_map/ppermute | solution.py:318
  12.2 4.9 %collective-permute-start.17 = (bf16[24,2048]{1,0:T(8,128)(2,1)S(1)}, bf16[24,2048]{1,0:T(8,128)(2,1)S(1)}, u32[]{:S(2)}, u32[]{:S(2)}) collective-permute-start(bf16[24,2048]{1,0:T(8,128)(2,1)S(1)} %get-tuple-element.62), channel_id=1, source_target_pairs={{0,1},{1,0},{2,3},{3,2},{4,5},{5,4},{6,7},{7,6},{8,9},{9,8},{10,11... | collective-permute-start | bytes 294920 | tf_op jit(solution)/shard_map/ppermute | solution.py:318
  15.0 6.7 %collective-permute-start.2 = (bf16[24,2048]{1,0:T(8,128)(2,1)S(1)}, bf16[24,2048]{1,0:T(8,128)(2,1)S(1)}, u32[]{:S(2)}, u32[]{:S(2)}) collective-permute-start(bf16[24,2048]{1,0:T(8,128)(2,1)S(1)} %get-tuple-element.45), channel_id=1, source_target_pairs={{0,24},{4,28},{8,0},{12,4},{16,8},{20,12},{24,16},{28,20},{1,25},{... | collective-permute-start | bytes 294920 | tf_op jit(solution)/shard_map/ppermute | solution.py:310
  16.4 7.5 %collective-permute-start.4 = (bf16[24,2048]{1,0:T(8,128)(2,1)S(1)}, bf16[24,2048]{1,0:T(8,128)(2,1)S(1)}, u32[]{:S(2)}, u32[]{:S(2)}) collective-permute-start(bf16[24,2048]{1,0:T(8,128)(2,1)S(1)} %get-tuple-element.46), channel_id=1, source_target_pairs={{0,8},{4,12},{8,16},{12,20},{16,24},{20,28},{24,0},{28,4},{1,9},{5... | collective-permute-start | bytes 294920 | tf_op jit(solution)/shard_map/ppermute | solution.py:310
  17.1 16.3 %collective-permute-start.5 = (bf16[24,2048]{1,0:T(8,128)(2,1)S(1)}, bf16[24,2048]{1,0:T(8,128)(2,1)S(1)}, u32[]{:S(2)}, u32[]{:S(2)}) collective-permute-start(bf16[24,2048]{1,0:T(8,128)(2,1)S(1)} %get-tuple-element.46), channel_id=1, source_target_pairs={{0,16},{4,20},{8,24},{12,28},{16,0},{20,4},{24,8},{28,12},{1,17},{... | collective-permute-start | bytes 294920 | tf_op jit(solution)/shard_map/ppermute | solution.py:310
  18.4 14.9 %collective-permute-start.6 = (bf16[24,2048]{1,0:T(8,128)(2,1)S(1)}, bf16[24,2048]{1,0:T(8,128)(2,1)S(1)}, u32[]{:S(2)}, u32[]{:S(2)}) collective-permute-start(bf16[24,2048]{1,0:T(8,128)(2,1)S(1)} %get-tuple-element.46), channel_id=1, source_target_pairs={{0,24},{4,28},{8,0},{12,4},{16,8},{20,12},{24,16},{28,20},{1,25},{... | collective-permute-start | bytes 294920 | tf_op jit(solution)/shard_map/ppermute | solution.py:310
  20.4 16.1 %collective-permute-start.8 = (bf16[24,4096]{1,0:T(8,128)(2,1)S(1)}, bf16[24,4096]{1,0:T(8,128)(2,1)S(1)}, u32[]{:S(2)}, u32[]{:S(2)}) collective-permute-start(bf16[24,4096]{1,0:T(8,128)(2,1)S(1)} %copy-done), channel_id=1, source_target_pairs={{0,8},{4,12},{8,16},{12,20},{16,24},{20,28},{24,0},{28,4},{1,9},{5... | collective-permute-start | bytes 589832 | tf_op jit(solution)/shard_map/ppermute | solution.py:310
  21.7 35.2 %collective-permute-start.9 = (bf16[24,4096]{1,0:T(8,128)(2,1)S(1)}, bf16[24,4096]{1,0:T(8,128)(2,1)S(1)}, u32[]{:S(2)}, u32[]{:S(2)}) collective-permute-start(bf16[24,4096]{1,0:T(8,128)(2,1)S(1)} %copy-done), channel_id=1, source_target_pairs={{0,16},{4,20},{8,24},{12,28},{16,0},{20,4},{24,8},{28,12},{1,17},{... | collective-permute-start | bytes 589832 | tf_op jit(solution)/shard_map/ppermute | solution.py:310
  23.9 33.1 %collective-permute-start.10 = (bf16[24,4096]{1,0:T(8,128)(2,1)S(1)}, bf16[24,4096]{1,0:T(8,128)(2,1)S(1)}, u32[]{:S(2)}, u32[]{:S(2)}) collective-permute-start(bf16[24,4096]{1,0:T(8,128)(2,1)S(1)} %copy-done), channel_id=1, source_target_pairs={{0,24},{4,28},{8,0},{12,4},{16,8},{20,12},{24,16},{28,20},{1,25},{... | collective-permute-start | bytes 589832 | tf_op jit(solution)/shard_map/ppermute | solution.py:310
  33.3 40.6 %collective-permute-start.22 = (bf16[4,24,2048]{2,1,0:T(8,128)(2,1)S(1)}, bf16[4,24,2048]{2,1,0:T(8,128)(2,1)S(1)}, u32[]{:S(2)}, u32[]{:S(2)}) collective-permute-start(bf16[4,24,2048]{2,1,0:T(8,128)(2,1)S(1)} %get-tuple-element.84), channel_id=1, source_target_pairs={{0,24},{4,28},{8,0},{12,4},{16,8},{20,12},{24,16},{28,20},{1,25},{... | collective-permute-start | bytes 1179656 | tf_op jit(solution)/shard_map/ppermute | solution.py:310
  33.3 45.1 %collective-permute-start.21 = (bf16[4,24,2048]{2,1,0:T(8,128)(2,1)S(1)}, bf16[4,24,2048]{2,1,0:T(8,128)(2,1)S(1)}, u32[]{:S(2)}, u32[]{:S(2)}) collective-permute-start(bf16[4,24,2048]{2,1,0:T(8,128)(2,1)S(1)} %get-tuple-element.84), channel_id=1, source_target_pairs={{0,16},{4,20},{8,24},{12,28},{16,0},{20,4},{24,8},{28,12},{1,17},{... | collective-permute-start | bytes 1179656 | tf_op jit(solution)/shard_map/ppermute | solution.py:310
  36.4 42.0 %collective-permute-start.20 = (bf16[4,24,2048]{2,1,0:T(8,128)(2,1)S(1)}, bf16[4,24,2048]{2,1,0:T(8,128)(2,1)S(1)}, u32[]{:S(2)}, u32[]{:S(2)}) collective-permute-start(bf16[4,24,2048]{2,1,0:T(8,128)(2,1)S(1)} %get-tuple-element.84), channel_id=1, source_target_pairs={{0,8},{4,12},{8,16},{12,20},{16,24},{20,28},{24,0},{28,4},{1,9},{5... | collective-permute-start | bytes 1179656 | tf_op jit(solution)/shard_map/ppermute | solution.py:310
  56.9 8.8 %collective-permute-start.3 = (bf16[96,2048]{1,0:T(8,128)(2,1)S(1)}, bf16[96,2048]{1,0:T(8,128)(2,1)S(1)}, u32[]{:S(2)}, u32[]{:S(2)}) collective-permute-start(bf16[96,2048]{1,0:T(8,128)(2,1)S(1)} %constant_dynamic-update-slice_fusion.refs_0_), channel_id=1, source_target_pairs={{0,4},{4,0},{8,12},{12,8},{16,20},{20,16},{24,28},{28,24},{1,5},{5... | collective-permute-start | bytes 1179656 | tf_op jit(solution)/shard_map/ppermute | solution.py:314
  57.0 2.2 %collective-permute-start.7 = (bf16[96,2048]{1,0:T(8,128)(2,1)S(1)}, bf16[96,2048]{1,0:T(8,128)(2,1)S(1)}, u32[]{:S(2)}, u32[]{:S(2)}) collective-permute-start(bf16[96,2048]{1,0:T(8,128)(2,1)S(1)} %constant_dynamic-update-slice_fusion.4.refs_0_), channel_id=1, source_target_pairs={{0,4},{4,0},{8,12},{12,8},{16,20},{20,16},{24,28},{28,24},{1,5},{5... | collective-permute-start | bytes 1179656 | tf_op jit(solution)/shard_map/ppermute | solution.py:314
  59.2 19.5 %collective-permute-start.11 = (bf16[96,4096]{1,0:T(8,128)(2,1)S(1)}, bf16[96,4096]{1,0:T(8,128)(2,1)S(1)}, u32[]{:S(2)}, u32[]{:S(2)}) collective-permute-start(bf16[96,4096]{1,0:T(8,128)(2,1)S(1)} %constant_dynamic-update-slice_fusion.8.refs_0_), channel_id=1, source_target_pairs={{0,4},{4,0},{8,12},{12,8},{16,20},{20,16},{24,28},{28,24},{1,5},{5... | collective-permute-start | bytes 2359304 | tf_op jit(solution)/shard_map/ppermute | solution.py:314
  72.0 35.0 %collective-permute-start.32 = (bf16[192,1792]{1,0:T(8,128)(2,1)S(1)}, bf16[192,1792]{1,0:T(8,128)(2,1)S(1)}, u32[]{:S(2)}, u32[]{:S(2)}) collective-permute-start(bf16[192,1792]{1,0:T(8,128)(2,1)S(1)} %get-tuple-element.72.refs_0_), channel_id=1, source_target_pairs={{0,1},{1,0},{2,3},{3,2},{4,5},{5,4},{6,7},{7,6},{8,9},{9,8},{10,11... | collective-permute-start | bytes 2064392 | tf_op jit(solution)/shard_map/ppermute | solution.py:318
  73.9 31.6 %collective-permute-start.33 = (bf16[192,1792]{1,0:T(8,128)(2,1)S(1)}, bf16[192,1792]{1,0:T(8,128)(2,1)S(1)}, u32[]{:S(2)}, u32[]{:S(2)}) collective-permute-start(bf16[192,1792]{1,0:T(8,128)(2,1)S(1)} %get-tuple-element.72.refs_0_), channel_id=1, source_target_pairs={{0,2},{1,3},{2,0},{3,1},{4,6},{5,7},{6,4},{7,5},{8,10},{9,11},{10,... | collective-permute-start | bytes 2064392 | tf_op jit(solution)/shard_map/ppermute | solution.py:318
  78.7 53.4 %collective-permute-start.23 = (bf16[4,4,24,2048]{3,2,0,1:T(8,128)(2,1)S(1)}, bf16[4,4,24,2048]{3,2,0,1:T(8,128)(2,1)S(1)}, u32[]{:S(2)}, u32[]{:S(2)}) collective-permute-start(bf16[4,4,24,2048]{3,2,0,1:T(8,128)(2,1)S(1)} %get-tuple-element.81), channel_id=1, source_target_pairs={{0,4},{4,0},{8,12},{12,8},{16,20},{20,16},{24,28},{28,24},{1,5},{5... | collective-permute-start | bytes 4718600 | tf_op jit(solution)/shard_map/ppermute | solution.py:314
  86.5 21.5 %collective-permute-start.28 = (bf16[192,1792]{1,0:T(8,128)(2,1)S(1)}, bf16[192,1792]{1,0:T(8,128)(2,1)S(1)}, u32[]{:S(2)}, u32[]{:S(2)}) collective-permute-start(bf16[192,1792]{1,0:T(8,128)(2,1)S(1)} %get-tuple-element.52.refs_1_), channel_id=1, source_target_pairs={{0,1},{1,0},{2,3},{3,2},{4,5},{5,4},{6,7},{7,6},{8,9},{9,8},{10,11... | collective-permute-start | bytes 2064392 | tf_op jit(solution)/shard_map/ppermute | solution.py:318
  88.5 18.7 %collective-permute-start.29 = (bf16[192,1792]{1,0:T(8,128)(2,1)S(1)}, bf16[192,1792]{1,0:T(8,128)(2,1)S(1)}, u32[]{:S(2)}, u32[]{:S(2)}) collective-permute-start(bf16[192,1792]{1,0:T(8,128)(2,1)S(1)} %get-tuple-element.52.refs_1_), channel_id=1, source_target_pairs={{0,2},{1,3},{2,0},{3,1},{4,6},{5,7},{6,4},{7,5},{8,10},{9,11},{10,... | collective-permute-start | bytes 2064392 | tf_op jit(solution)/shard_map/ppermute | solution.py:318
  105.6 62.6 %collective-permute-start.24 = (bf16[192,1792]{1,0:T(8,128)(2,1)S(1)}, bf16[192,1792]{1,0:T(8,128)(2,1)S(1)}, u32[]{:S(2)}, u32[]{:S(2)}) collective-permute-start(bf16[192,1792]{1,0:T(8,128)(2,1)S(1)} %get-tuple-element.65.refs_2_), channel_id=1, source_target_pairs={{0,1},{1,0},{2,3},{3,2},{4,5},{5,4},{6,7},{7,6},{8,9},{9,8},{10,11... | collective-permute-start | bytes 2064392 | tf_op jit(solution)/shard_map/ppermute | solution.py:318
  107.1 32.0 %collective-permute-start.12 = (bf16[2,96,4096]{2,1,0:T(8,128)(2,1)S(1)}, bf16[2,96,4096]{2,1,0:T(8,128)(2,1)S(1)}, u32[]{:S(2)}, u32[]{:S(2)}) collective-permute-start(bf16[2,96,4096]{2,1,0:T(8,128)(2,1)S(1)} %get-tuple-element.55), channel_id=1, source_target_pairs={{0,4},{4,0},{8,12},{12,8},{16,20},{20,16},{24,28},{28,24},{1,5},{5... | collective-permute-start | bytes 4718600 | tf_op jit(solution)/shard_map/ppermute | solution.py:314
  107.2 23.1 %collective-permute-start.30 = (bf16[96,1792]{1,0:T(8,128)(2,1)S(1)}, bf16[96,1792]{1,0:T(8,128)(2,1)S(1)}, u32[]{:S(2)}, u32[]{:S(2)}) collective-permute-start(bf16[96,1792]{1,0:T(8,128)(2,1)S(1)} %slice.66), channel_id=1, source_target_pairs={{0,1},{1,0},{2,3},{3,2},{4,5},{5,4},{6,7},{7,6},{8,9},{9,8},{10,11... | collective-permute-start | bytes 1032200 | tf_op jit(solution)/shard_map/ppermute | solution.py:318
  108.0 23.6 %collective-permute-start.31 = (bf16[96,1792]{1,0:T(8,128)(2,1)S(1)}, bf16[96,1792]{1,0:T(8,128)(2,1)S(1)}, u32[]{:S(2)}, u32[]{:S(2)}) collective-permute-start(bf16[96,1792]{1,0:T(8,128)(2,1)S(1)} %slice.67), channel_id=1, source_target_pairs={{0,2},{1,3},{2,0},{3,1},{4,6},{5,7},{6,4},{7,5},{8,10},{9,11},{10,... | collective-permute-start | bytes 1032200 | tf_op jit(solution)/shard_map/ppermute | solution.py:318
  130.3 37.9 %collective-permute-start.25 = (bf16[192,1792]{1,0:T(8,128)(2,1)S(1)}, bf16[192,1792]{1,0:T(8,128)(2,1)S(1)}, u32[]{:S(2)}, u32[]{:S(2)}) collective-permute-start(bf16[192,1792]{1,0:T(8,128)(2,1)S(1)} %get-tuple-element.65.refs_2_), channel_id=1, source_target_pairs={{0,2},{1,3},{2,0},{3,1},{4,6},{5,7},{6,4},{7,5},{8,10},{9,11},{10,... | collective-permute-start | bytes 2064392 | tf_op jit(solution)/shard_map/ppermute | solution.py:318
  131.6 9.2 %collective-permute-start.34 = (bf16[96,1792]{1,0:T(8,128)(2,1)S(1)}, bf16[96,1792]{1,0:T(8,128)(2,1)S(1)}, u32[]{:S(2)}, u32[]{:S(2)}) collective-permute-start(bf16[96,1792]{1,0:T(8,128)(2,1)S(1)} %slice.68), channel_id=1, source_target_pairs={{0,1},{1,0},{2,3},{3,2},{4,5},{5,4},{6,7},{7,6},{8,9},{9,8},{10,11... | collective-permute-start | bytes 1032200 | tf_op jit(solution)/shard_map/ppermute | solution.py:318
  132.1 22.0 %collective-permute-start.35 = (bf16[96,1792]{1,0:T(8,128)(2,1)S(1)}, bf16[96,1792]{1,0:T(8,128)(2,1)S(1)}, u32[]{:S(2)}, u32[]{:S(2)}) collective-permute-start(bf16[96,1792]{1,0:T(8,128)(2,1)S(1)} %slice.69), channel_id=1, source_target_pairs={{0,2},{1,3},{2,0},{3,1},{4,6},{5,7},{6,4},{7,5},{8,10},{9,11},{10,... | collective-permute-start | bytes 1032200 | tf_op jit(solution)/shard_map/ppermute | solution.py:318
  139.5 42.6 %collective-permute-start.13 = (bf16[2,24,4096]{2,1,0:T(8,128)(2,1)S(1)}, bf16[2,24,4096]{2,1,0:T(8,128)(2,1)S(1)}, u32[]{:S(2)}, u32[]{:S(2)}) collective-permute-start(bf16[2,24,4096]{2,1,0:T(8,128)(2,1)S(1)} %get-tuple-element.57), channel_id=1, source_target_pairs={{8,0},{12,4},{16,8},{20,12},{24,16},{28,20},{9,1},{13,5},{17,9},{2... | collective-permute-start | bytes 1179656 | tf_op jit(solution)/shard_map/ppermute | solution.py:361
  140.8 41.3 %collective-permute-start.14 = (bf16[2,24,4096]{2,1,0:T(8,128)(2,1)S(1)}, bf16[2,24,4096]{2,1,0:T(8,128)(2,1)S(1)}, u32[]{:S(2)}, u32[]{:S(2)}) collective-permute-start(bf16[2,24,4096]{2,1,0:T(8,128)(2,1)S(1)} %get-tuple-element.58), channel_id=1, source_target_pairs={{0,8},{4,12},{8,16},{12,20},{16,24},{20,28},{1,9},{5,13},{9,17},{1... | collective-permute-start | bytes 1179656 | tf_op jit(solution)/shard_map/ppermute | solution.py:361
  154.1 10.4 %collective-permute-start.15 = (bf16[2,24,4096]{2,1,0:T(8,128)(2,1)S(1)}, bf16[2,24,4096]{2,1,0:T(8,128)(2,1)S(1)}, u32[]{:S(2)}, u32[]{:S(2)}) collective-permute-start(bf16[2,24,4096]{2,1,0:T(8,128)(2,1)S(1)} %get-tuple-element.60), channel_id=1, source_target_pairs={{0,8},{4,12},{24,16},{28,20},{1,9},{5,13},{25,17},{29,21},{2,10},{... | collective-permute-start | bytes 1179656 | tf_op jit(solution)/shard_map/ppermute | solution.py:361
  164.6 19.6 %collective-permute-start.16 = (bf16[2,24,4096]{2,1,0:T(8,128)(2,1)S(1)}, bf16[2,24,4096]{2,1,0:T(8,128)(2,1)S(1)}, u32[]{:S(2)}, u32[]{:S(2)}) collective-permute-start(bf16[2,24,4096]{2,1,0:T(8,128)(2,1)S(1)} %add_convert_fusion), channel_id=1, source_target_pairs={{0,16},{4,20},{8,24},{12,28},{16,0},{20,4},{24,8},{28,12},{1,17},{... | collective-permute-start | bytes 1179656 | tf_op jit(solution)/shard_map/ppermute | solution.py:310
  168.3 8.0 %collective-permute-start.26 = (bf16[96,1792]{1,0:T(8,128)(2,1)S(1)}, bf16[96,1792]{1,0:T(8,128)(2,1)S(1)}, u32[]{:S(2)}, u32[]{:S(2)}) collective-permute-start(bf16[96,1792]{1,0:T(8,128)(2,1)S(1)} %slice.49), channel_id=1, source_target_pairs={{0,1},{1,0},{2,3},{3,2},{4,5},{5,4},{6,7},{7,6},{8,9},{9,8},{10,11... | collective-permute-start | bytes 1032200 | tf_op jit(solution)/shard_map/ppermute | solution.py:318
  169.9 7.6 %collective-permute-start.27 = (bf16[96,1792]{1,0:T(8,128)(2,1)S(1)}, bf16[96,1792]{1,0:T(8,128)(2,1)S(1)}, u32[]{:S(2)}, u32[]{:S(2)}) collective-permute-start(bf16[96,1792]{1,0:T(8,128)(2,1)S(1)} %slice.50), channel_id=1, source_target_pairs={{0,2},{1,3},{2,0},{3,1},{4,6},{5,7},{6,4},{7,5},{8,10},{9,11},{10,... | collective-permute-start | bytes 1032200 | tf_op jit(solution)/shard_map/ppermute | solution.py:318

commit v10 on v9

--- a/solution.py
+++ b/solution.py
@@ -170,7 +170,7 @@
     )(own, other, gate, up, *before)
 
 
-def turn_kernel(tile, ca_ref, cb_ref, down_hbm, active_ref, factor_ref, gb_ref, ub_ref,
+def turn_kernel(tile, ca_ref, cb_ref, down_hbm, active_ref, factor_ref, both_ref,
                 c_ref, down_ref, sems):
     half = ca_ref.shape[0]
 
@@ -185,8 +185,8 @@
     def body(j, slot):
         span = pl.ds(pl.multiple_of(j * tile, tile), tile)
         back = nt_dot(c_ref[...], down_ref[slot])
-        gb_ref[:, span] = (back * factor_ref[:, span]).astype(BF)
-        ub_ref[:, span] = (back * active_ref[:, span]).astype(BF)
+        both_ref[0, :, span] = (back * factor_ref[:, span]).astype(BF)
+        both_ref[1, :, span] = (back * active_ref[:, span]).astype(BF)
 
     streamed(down_hbm.shape[0] // tile, down_ref.shape[0], copies, body, first)
 
@@ -200,8 +200,8 @@
     return pl.pallas_call(
         lambda *refs: turn_kernel(tile, *refs),
         in_specs=[VMEM, VMEM, HBM, VMEM, VMEM],
-        out_specs=[VMEM] * 2,
-        out_shape=[shape((rows, units))] * 2,
+        out_specs=VMEM,
+        out_shape=shape((2, rows, units)),
         scratch_shapes=[
             pltpu.VMEM((rows, width), BF),
             pltpu.VMEM((depth, tile, width), BF),
@@ -213,7 +213,7 @@
     )(own, other, down, active, factor)
 
 
-def leave_kernel(step, hid_ref, gb_ref, ub_ref, gate_hbm, up_hbm, down_hbm, own_ref, other_ref,
+def leave_kernel(step, hid_ref, both_ref, gate_hbm, up_hbm, down_hbm, own_ref, other_ref,
                  gate_ref, up_ref, down_ref, sems):
     half = own_ref.shape[1]
 
@@ -230,7 +230,7 @@
         result = nn_dot(hid_ref[...], down_ref[slot]).astype(BF)
         own_ref[0, :, span] = result[:half]
         other_ref[0, :, span] = result[half:]
-        result = nt_dot(gb_ref[...], gate_ref[slot]) + nt_dot(ub_ref[...], up_ref[slot])
+        result = nt_dot(both_ref[0], gate_ref[slot]) + nt_dot(both_ref[1], up_ref[slot])
         result = result.astype(BF)
         own_ref[1, :, span] = result[:half]
         other_ref[1, :, span] = result[half:]
@@ -238,15 +238,15 @@
     streamed(gate_hbm.shape[0] // step, gate_ref.shape[0], copies, body, lambda: None)
 
 
-def leave(hid, gb, ub, gate, up, down):
-    rows, units = gb.shape
+def leave(hid, both, gate, up, down):
+    rows, units = hid.shape
     width = gate.shape[0]
     half = rows // 2
     step = tile_of(width, (512, 256, 128))
     depth = min(DEPTH, width // step)
     return pl.pallas_call(
         lambda *refs: leave_kernel(step, *refs),
-        in_specs=[VMEM] * 3 + [HBM] * 3,
+        in_specs=[VMEM] * 2 + [HBM] * 3,
         out_specs=[VMEM] * 2,
         out_shape=[shape((2, half, width))] * 2,
         scratch_shapes=[
@@ -258,7 +258,7 @@
         compiler_params=grant((3 * depth * step, units, BF), least=40 * MIB),
         cost_estimate=cost(6 * rows * width * units, 6 * width * units),
         name="leave",
-    )(hid, gb, ub, gate, up, down)
+    )(hid, both, gate, up, down)
 
 
 def fold_kernel(first_ref, own_ref, mate_ref, *chunks):
@@ -336,14 +336,11 @@
         return held
 
     def relay(held):
-        half = held[0][0].shape[0] // 2
         held = list(held)
         for m in range(1, groups):
             low, high = m & -m, 1 << (m.bit_length() - 1)
             if low != high:
-                a = jnp.concatenate(held[m ^ low], axis=0)
-                b = jnp.concatenate(held[m ^ high], axis=0)
-                held[m] = [across(a[:half], low), across(b[half:], high)]
+                held[m] = [across(held[m ^ low][0], low), across(held[m ^ high][1], high)]
         return held
 
     def after(values, others):
@@ -380,17 +377,22 @@
     cot_mate = swap(cot)
     before = enter(tok[0], tok_mate[0], gate, up)
     hid, active, factor = enter(tok[1], tok_mate[1], gate, up, *before)
-    all_hid = relay(near(hid))
-    gb, ub = turn(cot, cot_mate, down, active, factor)
-    all_gb = near(gb)
-    all_ub = near(ub)
-    own, other = leave(hid, gb, ub, gate, up, down)
+    rows = hid.shape[0]
+    all_hid = near(hid)
+    all_hid = [v and [v[0][:rows // 2], v[0][rows // 2:]] for v in all_hid]
+    all_hid = relay(all_hid)
+    both = turn(cot, cot_mate, down, active, factor)
+    all_both = near(both)
+    own, other = leave(hid, both, gate, up, down)
 
     mate = swap(other)
     terms, last = returned(own, mate)
-    all_hid = after(all_hid, terms[:1])
+    all_hid = after(all_hid, [last])
+    all_both = after(all_both, [last])
+    all_gb, all_ub = ([v and [v[0][side, :rows // 2], v[0][side, rows // 2:]] for v in all_both]
+                      for side in range(2))
     all_gb = relay(all_gb)
-    all_ub = relay(after(all_ub, [last]))
+    all_ub = relay(all_ub)
     down_grad = rows_dot(stack(all_hid), cot_all)
     gate_grad = rows_dot(tok_all, stack(all_gb))
     up_grad = rows_dot(tok_all, stack(all_ub))

time: 185 us -> 169 us (0.914)
  starting transfers between devices: 70.7 us -> 52.7 us
    ppermute x13, starting transfers between devices: 41.1 us -> 24.8 us  [shift(): lax.ppermute(value, 'dp', [(z * CORES + c, (z + k) % ring * CORES + c) fo...]
    ppermute x3, waiting for transfers between devices: 2.35 us -> 6.15 us  [along(): lax.ppermute(value, 'dp', [(a * CORES + c, b * CORES + c) for a, b in pai...]
    ppermute x15 -> x13, starting transfers between devices: 19.5 us -> 15.9 us  [across(): return lax.ppermute(value, 'seq', [(g, g ^ mask) for g in range(groups)])]
    ppermute x15 -> x13, waiting for transfers between devices: 38 us -> 34.7 us  [across(): return lax.ppermute(value, 'seq', [(g, g ^ mask) for g in range(groups)])]
    ppermute x13, waiting for transfers between devices: 15 us -> 17.2 us  [shift(): lax.ppermute(value, 'dp', [(z * CORES + c, (z + k) % ring * CORES + c) fo...]
  transfers between devices with their start and end apart: 36 -> 34, of which waited for: 12 -> 12; matrix products, arithmetic and copies ran while one was open for 8% -> 9% of each run, Pallas kernels for 20% -> 22%
where the time goes in v10:
time: 169 us; the launch traced here: 168 us
  waiting for transfers between devices  58.1 us (34%)
  starting transfers between devices  52.7 us (31%)
  Pallas kernels  37.3 us (22%)
  matrix products  13.7 us (8%)
  local copies, waits for them, and re-layouts  3.76 us (2%)
  other arithmetic  1.75 us (1%)
    ppermute x13, waiting for transfers between devices, across(): return lax.ppermute(value, 'seq', [(g, g ^ mask) for g in range(groups)])  34.7 us
    ppermute x13, starting transfers between devices, shift(): lax.ppermute(value, 'dp', [(z * CORES + c, (z + k) % ring * CORES + c) fo...  24.8 us
    ppermute x13, waiting for transfers between devices, shift(): lax.ppermute(value, 'dp', [(z * CORES + c, (z + k) % ring * CORES + c) fo...  17.2 us
    pallas_call x1, Pallas kernels, leave(): pl.pallas_call(lambda *refs: leave_kernel(step, *refs), in_specs=[VMEM] *...  16.4 us
    ppermute x13, starting transfers between devices, across(): return lax.ppermute(value, 'seq', [(g, g ^ mask) for g in range(groups)])  15.9 us
    dot_general x3, matrix products, rows_dot(): lax.dot_general(left, right, (((0,), (0,)), ((), ())), preferred_element_...  13.7 us
    pallas_call x2, Pallas kernels, enter(): pl.pallas_call(lambda *refs: enter_kernel(tile, last, *refs), in_specs=[V...  12.6 us
    ppermute x3, starting transfers between devices, along(): lax.ppermute(value, 'dp', [(a * CORES + c, b * CORES + c) for a, b in pai...  11 us
  transfers between devices with their start and end apart: 34, of which 12 were waited for; matrix products, arithmetic and copies ran while one was open for 9% of the time, Pallas kernels for 22%

profile of v10, /device:TPU:0, one launch (start us, length us, event | category | flops | bytes accessed | tf_op | source)
XLA Modules:
  0.0 168.4 jit_solution(15160852312823433185)
XLA Ops:
  0.6 0.9 copy-done
  1.6 0.9 copy-done.1
  2.5 0.7 copy-done.2
  3.2 0.3 pick.1
  3.5 3.1 %collective-permute-start = (bf16[24,2048]{1,0:T(8,128)(2,1)S(1)}, bf16[24,2048]{1,0:T(8,128)(2,1)S(1)}, u32[]{:S(2)}, u32[]{:S(2)}) collective-permute-start(bf16[24,2048]{1,0:T(8,128)(2,1)S(1)} %get-tuple-element.46), channel_id=1, source_target_pairs={{0,8},{4,12},{8,16},{12,20},{16,24},{20,28},{24,0},{28,4},{1,9},{5... | collective-permute-start | bytes 294920 | tf_op jit(solution)/shard_map/ppermute | solution.py:310
  6.6 2.6 %collective-permute-start.1 = (bf16[24,2048]{1,0:T(8,128)(2,1)S(1)}, bf16[24,2048]{1,0:T(8,128)(2,1)S(1)}, u32[]{:S(2)}, u32[]{:S(2)}) collective-permute-start(bf16[24,2048]{1,0:T(8,128)(2,1)S(1)} %get-tuple-element.46), channel_id=1, source_target_pairs={{0,16},{4,20},{8,24},{12,28},{16,0},{20,4},{24,8},{28,12},{1,17},{... | collective-permute-start | bytes 294920 | tf_op jit(solution)/shard_map/ppermute | solution.py:310
  9.2 1.3 collective-permute-start.2
  10.6 0.7 collective-permute-start.4
  11.2 0.3 collective-permute-start.5
  11.6 0.7 collective-permute-done
  12.3 3.0 %collective-permute-start.6 = (bf16[24,2048]{1,0:T(8,128)(2,1)S(1)}, bf16[24,2048]{1,0:T(8,128)(2,1)S(1)}, u32[]{:S(2)}, u32[]{:S(2)}) collective-permute-start(bf16[24,2048]{1,0:T(8,128)(2,1)S(1)} %get-tuple-element.47), channel_id=1, source_target_pairs={{0,24},{4,28},{8,0},{12,4},{16,8},{20,12},{24,16},{28,20},{1,25},{... | collective-permute-start | bytes 294920 | tf_op jit(solution)/shard_map/ppermute | solution.py:310
  15.4 4.0 %collective-permute-done.1 = bf16[24,2048]{1,0:T(8,128)(2,1)S(1)} collective-permute-done((bf16[24,2048]{1,0:T(8,128)(2,1)S(1)}, bf16[24,2048]{1,0:T(8,128)(2,1)S(1)}, u32[]{:S(2)}, u32[]{:S(2)}) %collective-permute-start.1) | collective-permute-done | bytes 98336 | tf_op jit(solution)/shard_map/ppermute | solution.py:310
  19.3 1.7 %collective-permute-start.8 = (bf16[24,4096]{1,0:T(8,128)(2,1)S(1)}, bf16[24,4096]{1,0:T(8,128)(2,1)S(1)}, u32[]{:S(2)}, u32[]{:S(2)}) collective-permute-start(bf16[24,4096]{1,0:T(8,128)(2,1)S(1)} %copy-done), channel_id=1, source_target_pairs={{0,8},{4,12},{8,16},{12,20},{16,24},{20,28},{24,0},{28,4},{1,9},{5... | collective-permute-start | bytes 589832 | tf_op jit(solution)/shard_map/ppermute | solution.py:310
  21.1 4.9 %collective-permute-start.9 = (bf16[24,4096]{1,0:T(8,128)(2,1)S(1)}, bf16[24,4096]{1,0:T(8,128)(2,1)S(1)}, u32[]{:S(2)}, u32[]{:S(2)}) collective-permute-start(bf16[24,4096]{1,0:T(8,128)(2,1)S(1)} %copy-done), channel_id=1, source_target_pairs={{0,16},{4,20},{8,24},{12,28},{16,0},{20,4},{24,8},{28,12},{1,17},{... | collective-permute-start | bytes 589832 | tf_op jit(solution)/shard_map/ppermute | solution.py:310
  25.9 6.7 %collective-permute-done.5 = bf16[24,2048]{1,0:T(8,128)(2,1)S(1)} collective-permute-done((bf16[24,2048]{1,0:T(8,128)(2,1)S(1)}, bf16[24,2048]{1,0:T(8,128)(2,1)S(1)}, u32[]{:S(2)}, u32[]{:S(2)}) %collective-permute-start.5) | collective-permute-done | bytes 98336 | tf_op jit(solution)/shard_map/ppermute | solution.py:310
  32.7 0.0 collective-permute-done.6
  32.7 2.5 %collective-permute-start.19 = (bf16[24,2048]{1,0:T(8,128)(2,1)S(1)}, bf16[24,2048]{1,0:T(8,128)(2,1)S(1)}, u32[]{:S(2)}, u32[]{:S(2)}) collective-permute-start(bf16[24,2048]{1,0:T(8,128)(2,1)S(1)} %get-tuple-element.63), channel_id=1, source_target_pairs={{0,3},{1,2},{2,1},{3,0},{4,7},{5,6},{6,5},{7,4},{8,11},{9,10},{10,... | collective-permute-start | bytes 294920 | tf_op jit(solution)/shard_map/ppermute | solution.py:318
  35.2 0.6 collective-permute-start.18
  35.8 3.2 %collective-permute-done.9 = bf16[24,4096]{1,0:T(8,128)(2,1)S(1)} collective-permute-done((bf16[24,4096]{1,0:T(8,128)(2,1)S(1)}, bf16[24,4096]{1,0:T(8,128)(2,1)S(1)}, u32[]{:S(2)}, u32[]{:S(2)}) %collective-permute-start.9) | collective-permute-done | bytes 196640 | tf_op jit(solution)/shard_map/ppermute | solution.py:310
  39.0 1.5 collective-permute-start.17
  40.5 2.6 %collective-permute-done.10 = bf16[24,4096]{1,0:T(8,128)(2,1)S(1)} collective-permute-done((bf16[24,4096]{1,0:T(8,128)(2,1)S(1)}, bf16[24,4096]{1,0:T(8,128)(2,1)S(1)}, u32[]{:S(2)}, u32[]{:S(2)}) %collective-permute-start.10) | collective-permute-done | bytes 196640 | tf_op jit(solution)/shard_map/ppermute | solution.py:310
  43.1 0.0 collective-permute-start.7
  43.1 0.6 collective-permute-start.11
  43.7 0.1 collective-permute-start.3
  43.8 0.1 fusion.3
  43.9 5.6 %collective-permute-start.22 = (bf16[4,24,2048]{2,1,0:T(8,128)(2,1)S(1)}, bf16[4,24,2048]{2,1,0:T(8,128)(2,1)S(1)}, u32[]{:S(2)}, u32[]{:S(2)}) collective-permute-start(bf16[4,24,2048]{2,1,0:T(8,128)(2,1)S(1)} %get-tuple-element.106), channel_id=1, source_target_pairs={{0,24},{4,28},{8,0},{12,4},{16,8},{20,12},{24,16},{28,20},{1,25},{... | collective-permute-start | bytes 1179656 | tf_op jit(solution)/shard_map/ppermute | solution.py:310
  49.5 0.6 collective-permute-start.20
  50.1 6.3 %enter.2 = (f32[192,1792]{1,0:T(8,128)S(1)}, f32[192,1792]{1,0:T(8,128)S(1)}) custom-call(bf16[96,2048]{1,0:T(8,128)(2,1)S(1)} %constant_dynamic-update-slice_fusion.4.refs_0_, bf16[96,2048]{1,0:T(8,128)(2,1)S(1)} %collective-permute-done.7.refs_1_, bf16[4096,1792]{1,0:T(8,128)(2,1)} %refs_2_.7, bf16[4096,1792]{1,0:T(8,128)(2,1)} %refs_3_.5), custom_call_target="tpu_custom_call" | custom-call | flops 2818572288 | bytes 14680064 | tf_op jit(solution)/shard_map/enter/pallas_call | solution.py:156
  56.4 6.3 %enter.3 = (bf16[192,1792]{1,0:T(8,128)(2,1)S(1)}, f32[192,1792]{1,0:T(8,128)S(1)}, f32[192,1792]{1,0:T(8,128)S(1)}) custom-call(bf16[96,2048]{1,0:T(8,128)(2,1)S(1)} %constant_dynamic-update-slice_fusion.refs_0_, bf16[96,2048]{1,0:T(8,128)(2,1)S(1)} %collective-permute-done.3.refs_1_, bf16[4096,1792]{1,0:T(8,128)(2,1)} %refs_2_.7, ...), custom_call_target="tpu_custom_call" | custom-call | flops 2818572288 | bytes 14680064 | tf_op jit(solution)/shard_map/enter/pallas_call | solution.py:156
  62.7 7.6 %turn.1.refs_1_ = bf16[2,192,1792]{2,1,0:T(8,128)(2,1)S(1)} custom-call(bf16[96,4096]{1,0:T(8,128)(2,1)S(1)} %constant_dynamic-update-slice_fusion.8.refs_0_, bf16[96,4096]{1,0:T(8,128)(2,1)S(1)} %collective-permute-done.11.refs_1_, bf16[1792,4096]{1,0:T(8,128)(2,1)} %refs_4_.1, f32[192,1792]{1,0:T(8,128)S(1)} %get-tuple-element.51.refs_3_, ...), custom_call_target="tpu_custom_call" | custom-call | flops 2818572288 | bytes 14680064 | tf_op jit(solution)/shard_map/turn/pallas_call | solution.py:200
  70.4 16.4 %leave.1 = (bf16[2,96,4096]{2,1,0:T(8,128)(2,1)S(1)}, bf16[2,96,4096]{2,1,0:T(8,128)(2,1)S(1)}) custom-call(bf16[192,1792]{1,0:T(8,128)(2,1)S(1)} %get-tuple-element.50.refs_0_, bf16[2,192,1792]{2,1,0:T(8,128)(2,1)S(1)} %turn.1.refs_1_, bf16[4096,1792]{1,0:T(8,128)(2,1)} %refs_2_.7, bf16[4096,1792]{1,0:T(8,128)(2,1)} %refs_3_.5, bf16[1792,4096]{1,0:T(8,128)(2,1)} %refs_4_.1), custom_call_target="tpu_custom_call" | custom-call | flops 8455716864 | bytes 44040192 | tf_op jit(solution)/shard_map/leave/pallas_call | solution.py:247
  86.8 0.1 collective-permute-start.12
  86.8 1.6 collective-permute-start.31
  88.4 0.3 pad_maximum_fusion.1
  88.7 0.2 collective-permute-start.23
  88.9 1.5 collective-permute-start.30
  90.4 0.6 collective-permute-start.24
  91.0 13.6 %collective-permute-done.31 = bf16[192,1792]{1,0:T(8,128)(2,1)S(1)} collective-permute-done((bf16[192,1792]{1,0:T(8,128)(2,1)S(1)}, bf16[192,1792]{1,0:T(8,128)(2,1)S(1)}, u32[]{:S(2)}, u32[]{:S(2)}) %collective-permute-start.31) | collective-permute-done | bytes 688160 | tf_op jit(solution)/shard_map/ppermute | solution.py:318
  104.7 1.5 collective-permute-start.25
  106.2 1.6 collective-permute-start.32
  107.8 0.4 fold.1
  108.2 4.8 %collective-permute-start.15 = (bf16[2,24,4096]{2,1,0:T(8,128)(2,1)S(1)}, bf16[2,24,4096]{2,1,0:T(8,128)(2,1)S(1)}, u32[]{:S(2)}, u32[]{:S(2)}) collective-permute-start(bf16[2,24,4096]{2,1,0:T(8,128)(2,1)S(1)} %get-tuple-element.59), channel_id=1, source_target_pairs={{0,8},{4,12},{24,16},{28,20},{1,9},{5,13},{25,17},{29,21},{2,10},{... | collective-permute-start | bytes 1179656 | tf_op jit(solution)/shard_map/ppermute | solution.py:358
  113.0 0.6 collective-permute-start.33
  113.6 0.4 pad_maximum_fusion
  114.0 0.2 copy.11
  114.2 0.2 copy.12
  114.4 6.1 %collective-permute-done.15 = bf16[2,24,4096]{2,1,0:T(8,128)(2,1)S(1)} collective-permute-done((bf16[2,24,4096]{2,1,0:T(8,128)(2,1)S(1)}, bf16[2,24,4096]{2,1,0:T(8,128)(2,1)S(1)}, u32[]{:S(2)}, u32[]{:S(2)}) %collective-permute-start.15) | collective-permute-done | bytes 393248 | tf_op jit(solution)/shard_map/ppermute | solution.py:358
  120.5 1.3 collective-permute-start.13
  121.8 0.1 add_convert_fusion
  121.9 14.8 %collective-permute-done.24 = bf16[2,192,1792]{2,1,0:T(8,128)(2,1)S(1)} collective-permute-done((bf16[2,192,1792]{2,1,0:T(8,128)(2,1)S(1)}, bf16[2,192,1792]{2,1,0:T(8,128)(2,1)S(1)}, u32[]{:S(2)}, u32[]{:S(2)}) %collective-permute-start.24) | collective-permute-done | bytes 1376288 | tf_op jit(solution)/shard_map/ppermute | solution.py:318
  136.7 4.9 %collective-permute-start.14 = (bf16[2,24,4096]{2,1,0:T(8,128)(2,1)S(1)}, bf16[2,24,4096]{2,1,0:T(8,128)(2,1)S(1)}, u32[]{:S(2)}, u32[]{:S(2)}) collective-permute-start(bf16[2,24,4096]{2,1,0:T(8,128)(2,1)S(1)} %get-tuple-element.57), channel_id=1, source_target_pairs={{0,8},{4,12},{8,16},{12,20},{16,24},{20,28},{1,9},{5,13},{9,17},{1... | collective-permute-start | bytes 1179656 | tf_op jit(solution)/shard_map/ppermute | solution.py:358
  141.7 0.9 collective-permute-start.16
  143.0 0.5 collective-permute-done.32
  143.5 1.5 collective-permute-start.26
  145.0 0.5 collective-permute-start.27
  145.8 4.5 %convolution_convert_fusion = bf16[1792,1024]{1,0:T(8,128)(2,1)} fusion(bf16[768,1792]{1,0:T(8,128)(2,1)S(1)} %constant_dynamic-update-slice_fusion.20, bf16[768,1024]{1,0:T(8,128)(2,1)S(1)} %bitcast.63), kind=kOutput, calls=%fused_computation | convolution fusion | flops 2820407296 | bytes 7995392 | tf_op jit(solution)/shard_map/dot_general | solution.py:295
  150.3 2.6 %collective-permute-done.26 = bf16[96,1792]{1,0:T(8,128)(2,1)S(1)} collective-permute-done((bf16[96,1792]{1,0:T(8,128)(2,1)S(1)}, bf16[96,1792]{1,0:T(8,128)(2,1)S(1)}, u32[]{:S(2)}, u32[]{:S(2)}) %collective-permute-start.26) | collective-permute-done | bytes 344096 | tf_op jit(solution)/shard_map/ppermute | solution.py:318
  152.9 1.5 collective-permute-start.28
  154.5 0.6 collective-permute-start.29
  155.1 4.6 %convolution_convert_fusion.2 = bf16[1024,1792]{1,0:T(8,128)(2,1)} fusion(bf16[768,1024]{1,0:T(8,128)(2,1)S(1)} %bitcast.61, bf16[768,1792]{1,0:T(8,128)(2,1)S(1)} %constant_dynamic-update-slice_fusion.12), kind=kOutput, calls=%fused_computation.2 | convolution fusion | flops 2820407296 | bytes 7995392 | tf_op jit(solution)/shard_map/dot_general | solution.py:295
  159.6 1.9 %collective-permute-done.28 = bf16[96,1792]{1,0:T(8,128)(2,1)S(1)} collective-permute-done((bf16[96,1792]{1,0:T(8,128)(2,1)S(1)}, bf16[96,1792]{1,0:T(8,128)(2,1)S(1)}, u32[]{:S(2)}, u32[]{:S(2)}) %collective-permute-start.28) | collective-permute-done | bytes 344096 | tf_op jit(solution)/shard_map/ppermute | solution.py:318
  161.6 1.3 collective-permute-done.29
  162.9 4.6 %convolution_convert_fusion.1 = bf16[1024,1792]{1,0:T(8,128)(2,1)} fusion(bf16[768,1024]{1,0:T(8,128)(2,1)S(1)} %bitcast.62, bf16[768,1792]{1,0:T(8,128)(2,1)S(1)} %constant_dynamic-update-slice_fusion.16), kind=kOutput, calls=%fused_computation.1 | convolution fusion | flops 2820407296 | bytes 7995392 | tf_op jit(solution)/shard_map/dot_general | solution.py:295
  167.5 0.9 fusion.2
  (62 shorter events, 1.0 us)
Async XLA Ops:
  0.6 0.9 copy-start
  1.6 0.9 copy-start.1
  2.5 0.7 copy-start.2
  3.5 8.8 %collective-permute-start = (bf16[24,2048]{1,0:T(8,128)(2,1)S(1)}, bf16[24,2048]{1,0:T(8,128)(2,1)S(1)}, u32[]{:S(2)}, u32[]{:S(2)}) collective-permute-start(bf16[24,2048]{1,0:T(8,128)(2,1)S(1)} %get-tuple-element.46), channel_id=1, source_target_pairs={{0,8},{4,12},{8,16},{12,20},{16,24},{20,28},{24,0},{28,4},{1,9},{5... | collective-permute-start | bytes 294920 | tf_op jit(solution)/shard_map/ppermute | solution.py:310
  6.6 12.7 %collective-permute-start.1 = (bf16[24,2048]{1,0:T(8,128)(2,1)S(1)}, bf16[24,2048]{1,0:T(8,128)(2,1)S(1)}, u32[]{:S(2)}, u32[]{:S(2)}) collective-permute-start(bf16[24,2048]{1,0:T(8,128)(2,1)S(1)} %get-tuple-element.46), channel_id=1, source_target_pairs={{0,16},{4,20},{8,24},{12,28},{16,0},{20,4},{24,8},{28,12},{1,17},{... | collective-permute-start | bytes 294920 | tf_op jit(solution)/shard_map/ppermute | solution.py:310
  9.2 33.9 %collective-permute-start.2 = (bf16[24,2048]{1,0:T(8,128)(2,1)S(1)}, bf16[24,2048]{1,0:T(8,128)(2,1)S(1)}, u32[]{:S(2)}, u32[]{:S(2)}) collective-permute-start(bf16[24,2048]{1,0:T(8,128)(2,1)S(1)} %get-tuple-element.46), channel_id=1, source_target_pairs={{0,24},{4,28},{8,0},{12,4},{16,8},{20,12},{24,16},{28,20},{1,25},{... | collective-permute-start | bytes 294920 | tf_op jit(solution)/shard_map/ppermute | solution.py:310
  10.6 10.5 %collective-permute-start.4 = (bf16[24,2048]{1,0:T(8,128)(2,1)S(1)}, bf16[24,2048]{1,0:T(8,128)(2,1)S(1)}, u32[]{:S(2)}, u32[]{:S(2)}) collective-permute-start(bf16[24,2048]{1,0:T(8,128)(2,1)S(1)} %get-tuple-element.47), channel_id=1, source_target_pairs={{0,8},{4,12},{8,16},{12,20},{16,24},{20,28},{24,0},{28,4},{1,9},{5... | collective-permute-start | bytes 294920 | tf_op jit(solution)/shard_map/ppermute | solution.py:310
  11.2 21.4 %collective-permute-start.5 = (bf16[24,2048]{1,0:T(8,128)(2,1)S(1)}, bf16[24,2048]{1,0:T(8,128)(2,1)S(1)}, u32[]{:S(2)}, u32[]{:S(2)}) collective-permute-start(bf16[24,2048]{1,0:T(8,128)(2,1)S(1)} %get-tuple-element.47), channel_id=1, source_target_pairs={{0,16},{4,20},{8,24},{12,28},{16,0},{20,4},{24,8},{28,12},{1,17},{... | collective-permute-start | bytes 294920 | tf_op jit(solution)/shard_map/ppermute | solution.py:310
  12.3 20.4 %collective-permute-start.6 = (bf16[24,2048]{1,0:T(8,128)(2,1)S(1)}, bf16[24,2048]{1,0:T(8,128)(2,1)S(1)}, u32[]{:S(2)}, u32[]{:S(2)}) collective-permute-start(bf16[24,2048]{1,0:T(8,128)(2,1)S(1)} %get-tuple-element.47), channel_id=1, source_target_pairs={{0,24},{4,28},{8,0},{12,4},{16,8},{20,12},{24,16},{28,20},{1,25},{... | collective-permute-start | bytes 294920 | tf_op jit(solution)/shard_map/ppermute | solution.py:310
  19.3 15.9 %collective-permute-start.8 = (bf16[24,4096]{1,0:T(8,128)(2,1)S(1)}, bf16[24,4096]{1,0:T(8,128)(2,1)S(1)}, u32[]{:S(2)}, u32[]{:S(2)}) collective-permute-start(bf16[24,4096]{1,0:T(8,128)(2,1)S(1)} %copy-done), channel_id=1, source_target_pairs={{0,8},{4,12},{8,16},{12,20},{16,24},{20,28},{24,0},{28,4},{1,9},{5... | collective-permute-start | bytes 589832 | tf_op jit(solution)/shard_map/ppermute | solution.py:310
  21.1 18.0 %collective-permute-start.9 = (bf16[24,4096]{1,0:T(8,128)(2,1)S(1)}, bf16[24,4096]{1,0:T(8,128)(2,1)S(1)}, u32[]{:S(2)}, u32[]{:S(2)}) collective-permute-start(bf16[24,4096]{1,0:T(8,128)(2,1)S(1)} %copy-done), channel_id=1, source_target_pairs={{0,16},{4,20},{8,24},{12,28},{16,0},{20,4},{24,8},{28,12},{1,17},{... | collective-permute-start | bytes 589832 | tf_op jit(solution)/shard_map/ppermute | solution.py:310
  32.7 10.4 %collective-permute-start.10 = (bf16[24,4096]{1,0:T(8,128)(2,1)S(1)}, bf16[24,4096]{1,0:T(8,128)(2,1)S(1)}, u32[]{:S(2)}, u32[]{:S(2)}) collective-permute-start(bf16[24,4096]{1,0:T(8,128)(2,1)S(1)} %copy-done), channel_id=1, source_target_pairs={{0,24},{4,28},{8,0},{12,4},{16,8},{20,12},{24,16},{28,20},{1,25},{... | collective-permute-start | bytes 589832 | tf_op jit(solution)/shard_map/ppermute | solution.py:310
  32.7 11.0 %collective-permute-start.19 = (bf16[24,2048]{1,0:T(8,128)(2,1)S(1)}, bf16[24,2048]{1,0:T(8,128)(2,1)S(1)}, u32[]{:S(2)}, u32[]{:S(2)}) collective-permute-start(bf16[24,2048]{1,0:T(8,128)(2,1)S(1)} %get-tuple-element.63), channel_id=1, source_target_pairs={{0,3},{1,2},{2,1},{3,0},{4,7},{5,6},{6,5},{7,4},{8,11},{9,10},{10,... | collective-permute-start | bytes 294920 | tf_op jit(solution)/shard_map/ppermute | solution.py:318
  35.2 8.6 %collective-permute-start.18 = (bf16[24,2048]{1,0:T(8,128)(2,1)S(1)}, bf16[24,2048]{1,0:T(8,128)(2,1)S(1)}, u32[]{:S(2)}, u32[]{:S(2)}) collective-permute-start(bf16[24,2048]{1,0:T(8,128)(2,1)S(1)} %get-tuple-element.62), channel_id=1, source_target_pairs={{0,2},{1,3},{2,0},{3,1},{4,6},{5,7},{6,4},{7,5},{8,10},{9,11},{10,... | collective-permute-start | bytes 294920 | tf_op jit(solution)/shard_map/ppermute | solution.py:318
  39.0 4.8 %collective-permute-start.17 = (bf16[24,2048]{1,0:T(8,128)(2,1)S(1)}, bf16[24,2048]{1,0:T(8,128)(2,1)S(1)}, u32[]{:S(2)}, u32[]{:S(2)}) collective-permute-start(bf16[24,2048]{1,0:T(8,128)(2,1)S(1)} %get-tuple-element.61), channel_id=1, source_target_pairs={{0,1},{1,0},{2,3},{3,2},{4,5},{5,4},{6,7},{7,6},{8,9},{9,8},{10,11... | collective-permute-start | bytes 294920 | tf_op jit(solution)/shard_map/ppermute | solution.py:318
  43.1 6.4 %collective-permute-start.7 = (bf16[96,2048]{1,0:T(8,128)(2,1)S(1)}, bf16[96,2048]{1,0:T(8,128)(2,1)S(1)}, u32[]{:S(2)}, u32[]{:S(2)}) collective-permute-start(bf16[96,2048]{1,0:T(8,128)(2,1)S(1)} %constant_dynamic-update-slice_fusion.4.refs_0_), channel_id=1, source_target_pairs={{0,4},{4,0},{8,12},{12,8},{16,20},{20,16},{24,28},{28,24},{1,5},{5... | collective-permute-start | bytes 1179656 | tf_op jit(solution)/shard_map/ppermute | solution.py:314
  43.1 19.6 %collective-permute-start.11 = (bf16[96,4096]{1,0:T(8,128)(2,1)S(1)}, bf16[96,4096]{1,0:T(8,128)(2,1)S(1)}, u32[]{:S(2)}, u32[]{:S(2)}) collective-permute-start(bf16[96,4096]{1,0:T(8,128)(2,1)S(1)} %constant_dynamic-update-slice_fusion.8.refs_0_), channel_id=1, source_target_pairs={{0,4},{4,0},{8,12},{12,8},{16,20},{20,16},{24,28},{28,24},{1,5},{5... | collective-permute-start | bytes 2359304 | tf_op jit(solution)/shard_map/ppermute | solution.py:314
  43.7 12.7 %collective-permute-start.3 = (bf16[96,2048]{1,0:T(8,128)(2,1)S(1)}, bf16[96,2048]{1,0:T(8,128)(2,1)S(1)}, u32[]{:S(2)}, u32[]{:S(2)}) collective-permute-start(bf16[96,2048]{1,0:T(8,128)(2,1)S(1)} %constant_dynamic-update-slice_fusion.refs_0_), channel_id=1, source_target_pairs={{0,4},{4,0},{8,12},{12,8},{16,20},{20,16},{24,28},{28,24},{1,5},{5... | collective-permute-start | bytes 1179656 | tf_op jit(solution)/shard_map/ppermute | solution.py:314
  43.9 44.5 %collective-permute-start.22 = (bf16[4,24,2048]{2,1,0:T(8,128)(2,1)S(1)}, bf16[4,24,2048]{2,1,0:T(8,128)(2,1)S(1)}, u32[]{:S(2)}, u32[]{:S(2)}) collective-permute-start(bf16[4,24,2048]{2,1,0:T(8,128)(2,1)S(1)} %get-tuple-element.106), channel_id=1, source_target_pairs={{0,24},{4,28},{8,0},{12,4},{16,8},{20,12},{24,16},{28,20},{1,25},{... | collective-permute-start | bytes 1179656 | tf_op jit(solution)/shard_map/ppermute | solution.py:310
  49.5 39.0 %collective-permute-start.21 = (bf16[4,24,2048]{2,1,0:T(8,128)(2,1)S(1)}, bf16[4,24,2048]{2,1,0:T(8,128)(2,1)S(1)}, u32[]{:S(2)}, u32[]{:S(2)}) collective-permute-start(bf16[4,24,2048]{2,1,0:T(8,128)(2,1)S(1)} %get-tuple-element.106), channel_id=1, source_target_pairs={{0,16},{4,20},{8,24},{12,28},{16,0},{20,4},{24,8},{28,12},{1,17},{... | collective-permute-start | bytes 1179656 | tf_op jit(solution)/shard_map/ppermute | solution.py:310
  49.5 39.0 %collective-permute-start.20 = (bf16[4,24,2048]{2,1,0:T(8,128)(2,1)S(1)}, bf16[4,24,2048]{2,1,0:T(8,128)(2,1)S(1)}, u32[]{:S(2)}, u32[]{:S(2)}) collective-permute-start(bf16[4,24,2048]{2,1,0:T(8,128)(2,1)S(1)} %get-tuple-element.106), channel_id=1, source_target_pairs={{0,8},{4,12},{8,16},{12,20},{16,24},{20,28},{24,0},{28,4},{1,9},{5... | collective-permute-start | bytes 1179656 | tf_op jit(solution)/shard_map/ppermute | solution.py:310
  86.8 19.5 %collective-permute-start.12 = (bf16[2,96,4096]{2,1,0:T(8,128)(2,1)S(1)}, bf16[2,96,4096]{2,1,0:T(8,128)(2,1)S(1)}, u32[]{:S(2)}, u32[]{:S(2)}) collective-permute-start(bf16[2,96,4096]{2,1,0:T(8,128)(2,1)S(1)} %get-tuple-element.54), channel_id=1, source_target_pairs={{0,4},{4,0},{8,12},{12,8},{16,20},{20,16},{24,28},{28,24},{1,5},{5... | collective-permute-start | bytes 4718600 | tf_op jit(solution)/shard_map/ppermute | solution.py:314
  86.8 17.8 %collective-permute-start.31 = (bf16[192,1792]{1,0:T(8,128)(2,1)S(1)}, bf16[192,1792]{1,0:T(8,128)(2,1)S(1)}, u32[]{:S(2)}, u32[]{:S(2)}) collective-permute-start(bf16[192,1792]{1,0:T(8,128)(2,1)S(1)} %get-tuple-element.50.refs_0_), channel_id=1, source_target_pairs={{0,2},{1,3},{2,0},{3,1},{4,6},{5,7},{6,4},{7,5},{8,10},{9,11},{10,... | collective-permute-start | bytes 2064392 | tf_op jit(solution)/shard_map/ppermute | solution.py:318
  88.7 24.4 %collective-permute-start.23 = (bf16[4,4,24,2048]{3,2,0,1:T(8,128)(2,1)S(1)}, bf16[4,4,24,2048]{3,2,0,1:T(8,128)(2,1)S(1)}, u32[]{:S(2)}, u32[]{:S(2)}) collective-permute-start(bf16[4,4,24,2048]{3,2,0,1:T(8,128)(2,1)S(1)} %get-tuple-element.83), channel_id=1, source_target_pairs={{0,4},{4,0},{8,12},{12,8},{16,20},{20,16},{24,28},{28,24},{1,5},{5... | collective-permute-start | bytes 4718600 | tf_op jit(solution)/shard_map/ppermute | solution.py:314
  88.9 19.3 %collective-permute-start.30 = (bf16[192,1792]{1,0:T(8,128)(2,1)S(1)}, bf16[192,1792]{1,0:T(8,128)(2,1)S(1)}, u32[]{:S(2)}, u32[]{:S(2)}) collective-permute-start(bf16[192,1792]{1,0:T(8,128)(2,1)S(1)} %get-tuple-element.50.refs_0_), channel_id=1, source_target_pairs={{0,1},{1,0},{2,3},{3,2},{4,5},{5,4},{6,7},{7,6},{8,9},{9,8},{10,11... | collective-permute-start | bytes 2064392 | tf_op jit(solution)/shard_map/ppermute | solution.py:318
  90.4 46.3 %collective-permute-start.24 = (bf16[2,192,1792]{2,1,0:T(8,128)(2,1)S(1)}, bf16[2,192,1792]{2,1,0:T(8,128)(2,1)S(1)}, u32[]{:S(2)}, u32[]{:S(2)}) collective-permute-start(bf16[2,192,1792]{2,1,0:T(8,128)(2,1)S(1)} %turn.1.refs_1_), channel_id=1, source_target_pairs={{0,1},{1,0},{2,3},{3,2},{4,5},{5,4},{6,7},{7,6},{8,9},{9,8},{10,11... | collective-permute-start | bytes 4128776 | tf_op jit(solution)/shard_map/ppermute | solution.py:318
  104.7 37.0 %collective-permute-start.25 = (bf16[2,192,1792]{2,1,0:T(8,128)(2,1)S(1)}, bf16[2,192,1792]{2,1,0:T(8,128)(2,1)S(1)}, u32[]{:S(2)}, u32[]{:S(2)}) collective-permute-start(bf16[2,192,1792]{2,1,0:T(8,128)(2,1)S(1)} %turn.1.refs_1_), channel_id=1, source_target_pairs={{0,2},{1,3},{2,0},{3,1},{4,6},{5,7},{6,4},{7,5},{8,10},{9,11},{10,... | collective-permute-start | bytes 4128776 | tf_op jit(solution)/shard_map/ppermute | solution.py:318
  106.2 37.2 %collective-permute-start.32 = (bf16[96,1792]{1,0:T(8,128)(2,1)S(1)}, bf16[96,1792]{1,0:T(8,128)(2,1)S(1)}, u32[]{:S(2)}, u32[]{:S(2)}) collective-permute-start(bf16[96,1792]{1,0:T(8,128)(2,1)S(1)} %get-tuple-element.75), channel_id=1, source_target_pairs={{0,1},{1,0},{2,3},{3,2},{4,5},{5,4},{6,7},{7,6},{8,9},{9,8},{10,11... | collective-permute-start | bytes 1032200 | tf_op jit(solution)/shard_map/ppermute | solution.py:318
  108.2 12.3 %collective-permute-start.15 = (bf16[2,24,4096]{2,1,0:T(8,128)(2,1)S(1)}, bf16[2,24,4096]{2,1,0:T(8,128)(2,1)S(1)}, u32[]{:S(2)}, u32[]{:S(2)}) collective-permute-start(bf16[2,24,4096]{2,1,0:T(8,128)(2,1)S(1)} %get-tuple-element.59), channel_id=1, source_target_pairs={{0,8},{4,12},{24,16},{28,20},{1,9},{5,13},{25,17},{29,21},{2,10},{... | collective-permute-start | bytes 1179656 | tf_op jit(solution)/shard_map/ppermute | solution.py:358
  113.0 31.9 %collective-permute-start.33 = (bf16[96,1792]{1,0:T(8,128)(2,1)S(1)}, bf16[96,1792]{1,0:T(8,128)(2,1)S(1)}, u32[]{:S(2)}, u32[]{:S(2)}) collective-permute-start(bf16[96,1792]{1,0:T(8,128)(2,1)S(1)} %get-tuple-element.74), channel_id=1, source_target_pairs={{0,2},{1,3},{2,0},{3,1},{4,6},{5,7},{6,4},{7,5},{8,10},{9,11},{10,... | collective-permute-start | bytes 1032200 | tf_op jit(solution)/shard_map/ppermute | solution.py:318
  120.5 47.0 %collective-permute-start.13 = (bf16[2,24,4096]{2,1,0:T(8,128)(2,1)S(1)}, bf16[2,24,4096]{2,1,0:T(8,128)(2,1)S(1)}, u32[]{:S(2)}, u32[]{:S(2)}) collective-permute-start(bf16[2,24,4096]{2,1,0:T(8,128)(2,1)S(1)} %get-tuple-element.56), channel_id=1, source_target_pairs={{8,0},{12,4},{16,8},{20,12},{24,16},{28,20},{9,1},{13,5},{17,9},{2... | collective-permute-start | bytes 1179656 | tf_op jit(solution)/shard_map/ppermute | solution.py:358
  136.7 30.8 %collective-permute-start.14 = (bf16[2,24,4096]{2,1,0:T(8,128)(2,1)S(1)}, bf16[2,24,4096]{2,1,0:T(8,128)(2,1)S(1)}, u32[]{:S(2)}, u32[]{:S(2)}) collective-permute-start(bf16[2,24,4096]{2,1,0:T(8,128)(2,1)S(1)} %get-tuple-element.57), channel_id=1, source_target_pairs={{0,8},{4,12},{8,16},{12,20},{16,24},{20,28},{1,9},{5,13},{9,17},{1... | collective-permute-start | bytes 1179656 | tf_op jit(solution)/shard_map/ppermute | solution.py:358
  141.7 25.8 %collective-permute-start.16 = (bf16[2,24,4096]{2,1,0:T(8,128)(2,1)S(1)}, bf16[2,24,4096]{2,1,0:T(8,128)(2,1)S(1)}, u32[]{:S(2)}, u32[]{:S(2)}) collective-permute-start(bf16[2,24,4096]{2,1,0:T(8,128)(2,1)S(1)} %add_convert_fusion), channel_id=1, source_target_pairs={{0,16},{4,20},{8,24},{12,28},{16,0},{20,4},{24,8},{28,12},{1,17},{... | collective-permute-start | bytes 1179656 | tf_op jit(solution)/shard_map/ppermute | solution.py:310
  143.5 9.5 %collective-permute-start.26 = (bf16[96,1792]{1,0:T(8,128)(2,1)S(1)}, bf16[96,1792]{1,0:T(8,128)(2,1)S(1)}, u32[]{:S(2)}, u32[]{:S(2)}) collective-permute-start(bf16[96,1792]{1,0:T(8,128)(2,1)S(1)} %get-tuple-element.88), channel_id=1, source_target_pairs={{0,1},{1,0},{2,3},{3,2},{4,5},{5,4},{6,7},{7,6},{8,9},{9,8},{10,11... | collective-permute-start | bytes 1032200 | tf_op jit(solution)/shard_map/ppermute | solution.py:318
  145.0 9.5 %collective-permute-start.27 = (bf16[96,1792]{1,0:T(8,128)(2,1)S(1)}, bf16[96,1792]{1,0:T(8,128)(2,1)S(1)}, u32[]{:S(2)}, u32[]{:S(2)}) collective-permute-start(bf16[96,1792]{1,0:T(8,128)(2,1)S(1)} %get-tuple-element.86), channel_id=1, source_target_pairs={{0,2},{1,3},{2,0},{3,1},{4,6},{5,7},{6,4},{7,5},{8,10},{9,11},{10,... | collective-permute-start | bytes 1032200 | tf_op jit(solution)/shard_map/ppermute | solution.py:318
  152.9 8.6 %collective-permute-start.28 = (bf16[96,1792]{1,0:T(8,128)(2,1)S(1)}, bf16[96,1792]{1,0:T(8,128)(2,1)S(1)}, u32[]{:S(2)}, u32[]{:S(2)}) collective-permute-start(bf16[96,1792]{1,0:T(8,128)(2,1)S(1)} %get-tuple-element.87), channel_id=1, source_target_pairs={{0,1},{1,0},{2,3},{3,2},{4,5},{5,4},{6,7},{7,6},{8,9},{9,8},{10,11... | collective-permute-start | bytes 1032200 | tf_op jit(solution)/shard_map/ppermute | solution.py:318
  154.5 8.4 %collective-permute-start.29 = (bf16[96,1792]{1,0:T(8,128)(2,1)S(1)}, bf16[96,1792]{1,0:T(8,128)(2,1)S(1)}, u32[]{:S(2)}, u32[]{:S(2)}) collective-permute-start(bf16[96,1792]{1,0:T(8,128)(2,1)S(1)} %get-tuple-element.85), channel_id=1, source_target_pairs={{0,2},{1,3},{2,0},{3,1},{4,6},{5,7},{6,4},{7,5},{8,10},{9,11},{10,... | collective-permute-start | bytes 1032200 | tf_op jit(solution)/shard_map/ppermute | solution.py:318

commit v11 on v10

--- a/solution.py
+++ b/solution.py
@@ -291,10 +291,12 @@
     )(first, own, mate)
 
 
+def sums_dot(left, right):
+    return lax.dot_general(left, right, (((0,), (0,)), ((), ())), preferred_element_type=F32)
+
+
 def rows_dot(left, right):
-    return lax.dot_general(
-        left, right, (((0,), (0,)), ((), ())), preferred_element_type=F32
-    ).astype(BF)
+    return sums_dot(left, right).astype(BF)
 
 
 def on_device(tokens, modality, gate, up, down, out_grad):
@@ -395,7 +397,8 @@
     all_ub = relay(all_ub)
     down_grad = rows_dot(stack(all_hid), cot_all)
     gate_grad = rows_dot(tok_all, stack(all_gb))
-    up_grad = rows_dot(tok_all, stack(all_ub))
+    up_grad = sums_dot(tok_all[:-rows], stack(all_ub[:-1]))
+    up_grad = (up_grad + sums_dot(tok_all[-rows:], stack(all_ub[-1:]))).astype(BF)
     terms = after(terms, [up_grad])
 
     def total(side):

time: 169 us -> 168 us (level)
  waiting for transfers between devices: 58.1 us -> 55.2 us
    dot_general x3 -> x4, matrix products: 13.7 us -> 15.2 us  [sums_dot(): lax.dot_general(left, right, (((0,), (0,)), ((), ())), preferred_element_...]
    unnamed x31 -> x29, local copies, waits for them, and re-layouts: 3.11 us -> 3.99 us
  transfers between devices with their start and end apart: 34 -> 34, of which waited for: 12 -> 10; matrix products, arithmetic and copies ran while one was open for 9% -> 11% of each run, Pallas kernels for 22% -> 22%
where the time goes in v11:
time: 168 us; the launch traced here: 167 us
  waiting for transfers between devices  55.2 us (33%)
  starting transfers between devices  52 us (31%)
  Pallas kernels  37.3 us (22%)
  matrix products  15.2 us (9%)
  local copies, waits for them, and re-layouts  4.71 us (3%)
  other arithmetic  1.95 us (1%)
    ppermute x13, waiting for transfers between devices, across(): return lax.ppermute(value, 'seq', [(g, g ^ mask) for g in range(groups)])  33.5 us
    ppermute x13, starting transfers between devices, shift(): lax.ppermute(value, 'dp', [(z * CORES + c, (z + k) % ring * CORES + c) fo...  24.7 us
    ppermute x13, waiting for transfers between devices, shift(): lax.ppermute(value, 'dp', [(z * CORES + c, (z + k) % ring * CORES + c) fo...  16.4 us
    pallas_call x1, Pallas kernels, leave(): pl.pallas_call(lambda *refs: leave_kernel(step, *refs), in_specs=[VMEM] *...  16.4 us
    dot_general x4, matrix products, sums_dot(): lax.dot_general(left, right, (((0,), (0,)), ((), ())), preferred_element_...  15.2 us
    ppermute x13, starting transfers between devices, across(): return lax.ppermute(value, 'seq', [(g, g ^ mask) for g in range(groups)])  15 us
    pallas_call x2, Pallas kernels, enter(): pl.pallas_call(lambda *refs: enter_kernel(tile, last, *refs), in_specs=[V...  12.6 us
    ppermute x3, starting transfers between devices, along(): lax.ppermute(value, 'dp', [(a * CORES + c, b * CORES + c) for a, b in pai...  11 us
  transfers between devices with their start and end apart: 34, of which 10 were waited for; matrix products, arithmetic and copies ran while one was open for 11% of the time, Pallas kernels for 22%

profile of v11, /device:TPU:0, one launch (start us, length us, event | category | flops | bytes accessed | tf_op | source)
XLA Modules:
  0.0 167.5 jit_solution(16467245112605889730)
XLA Ops:
  0.7 0.9 copy-done
  1.6 0.9 copy-done.1
  2.5 0.7 copy-done.2
  3.2 0.3 pick.1
  3.5 3.1 %collective-permute-start = (bf16[24,2048]{1,0:T(8,128)(2,1)S(1)}, bf16[24,2048]{1,0:T(8,128)(2,1)S(1)}, u32[]{:S(2)}, u32[]{:S(2)}) collective-permute-start(bf16[24,2048]{1,0:T(8,128)(2,1)S(1)} %get-tuple-element.46), channel_id=1, source_target_pairs={{0,8},{4,12},{8,16},{12,20},{16,24},{20,28},{24,0},{28,4},{1,9},{5... | collective-permute-start | bytes 294920 | tf_op jit(solution)/shard_map/ppermute | solution.py:312
  6.6 2.6 %collective-permute-start.1 = (bf16[24,2048]{1,0:T(8,128)(2,1)S(1)}, bf16[24,2048]{1,0:T(8,128)(2,1)S(1)}, u32[]{:S(2)}, u32[]{:S(2)}) collective-permute-start(bf16[24,2048]{1,0:T(8,128)(2,1)S(1)} %get-tuple-element.46), channel_id=1, source_target_pairs={{0,16},{4,20},{8,24},{12,28},{16,0},{20,4},{24,8},{28,12},{1,17},{... | collective-permute-start | bytes 294920 | tf_op jit(solution)/shard_map/ppermute | solution.py:312
  9.2 1.3 collective-permute-start.2
  10.6 0.7 collective-permute-start.4
  11.2 0.3 collective-permute-start.5
  11.6 0.9 constant_dynamic-update-slice_fusion.11
  12.6 2.9 %collective-permute-start.6 = (bf16[24,2048]{1,0:T(8,128)(2,1)S(1)}, bf16[24,2048]{1,0:T(8,128)(2,1)S(1)}, u32[]{:S(2)}, u32[]{:S(2)}) collective-permute-start(bf16[24,2048]{1,0:T(8,128)(2,1)S(1)} %get-tuple-element.47), channel_id=1, source_target_pairs={{0,24},{4,28},{8,0},{12,4},{16,8},{20,12},{24,16},{28,20},{1,25},{... | collective-permute-start | bytes 294920 | tf_op jit(solution)/shard_map/ppermute | solution.py:312
  15.4 3.9 %collective-permute-done.1 = bf16[24,2048]{1,0:T(8,128)(2,1)S(1)} collective-permute-done((bf16[24,2048]{1,0:T(8,128)(2,1)S(1)}, bf16[24,2048]{1,0:T(8,128)(2,1)S(1)}, u32[]{:S(2)}, u32[]{:S(2)}) %collective-permute-start.1) | collective-permute-done | bytes 98336 | tf_op jit(solution)/shard_map/ppermute | solution.py:312
  19.3 1.7 %collective-permute-start.8 = (bf16[24,4096]{1,0:T(8,128)(2,1)}, bf16[24,4096]{1,0:T(8,128)(2,1)S(1)}, u32[]{:S(2)}, u32[]{:S(2)}) collective-permute-start(bf16[24,4096]{1,0:T(8,128)(2,1)} %cot_ref.1), channel_id=1, source_target_pairs={{0,8},{4,12},{8,16},{12,20},{16,24},{20,28},{24,0},{28,4},{1,9},{5... | collective-permute-start | bytes 589832 | tf_op jit(solution)/shard_map/ppermute | solution.py:312
  21.1 4.9 %collective-permute-start.9 = (bf16[24,4096]{1,0:T(8,128)(2,1)}, bf16[24,4096]{1,0:T(8,128)(2,1)S(1)}, u32[]{:S(2)}, u32[]{:S(2)}) collective-permute-start(bf16[24,4096]{1,0:T(8,128)(2,1)} %cot_ref.1), channel_id=1, source_target_pairs={{0,16},{4,20},{8,24},{12,28},{16,0},{20,4},{24,8},{28,12},{1,17},{... | collective-permute-start | bytes 589832 | tf_op jit(solution)/shard_map/ppermute | solution.py:312
  25.9 6.7 %collective-permute-done.5 = bf16[24,2048]{1,0:T(8,128)(2,1)S(1)} collective-permute-done((bf16[24,2048]{1,0:T(8,128)(2,1)S(1)}, bf16[24,2048]{1,0:T(8,128)(2,1)S(1)}, u32[]{:S(2)}, u32[]{:S(2)}) %collective-permute-start.5) | collective-permute-done | bytes 98336 | tf_op jit(solution)/shard_map/ppermute | solution.py:312
  32.7 2.5 %collective-permute-start.19 = (bf16[24,2048]{1,0:T(8,128)(2,1)S(1)}, bf16[24,2048]{1,0:T(8,128)(2,1)S(1)}, u32[]{:S(2)}, u32[]{:S(2)}) collective-permute-start(bf16[24,2048]{1,0:T(8,128)(2,1)S(1)} %get-tuple-element.63), channel_id=1, source_target_pairs={{0,3},{1,2},{2,1},{3,0},{4,7},{5,6},{6,5},{7,4},{8,11},{9,10},{10,... | collective-permute-start | bytes 294920 | tf_op jit(solution)/shard_map/ppermute | solution.py:320
  35.2 0.6 collective-permute-start.18
  35.8 3.2 %collective-permute-done.9 = bf16[24,4096]{1,0:T(8,128)(2,1)S(1)} collective-permute-done((bf16[24,4096]{1,0:T(8,128)(2,1)}, bf16[24,4096]{1,0:T(8,128)(2,1)S(1)}, u32[]{:S(2)}, u32[]{:S(2)}) %collective-permute-start.9) | collective-permute-done | bytes 196640 | tf_op jit(solution)/shard_map/ppermute | solution.py:312
  39.0 1.5 collective-permute-start.17
  40.5 2.6 %collective-permute-done.10 = bf16[24,4096]{1,0:T(8,128)(2,1)S(1)} collective-permute-done((bf16[24,4096]{1,0:T(8,128)(2,1)}, bf16[24,4096]{1,0:T(8,128)(2,1)S(1)}, u32[]{:S(2)}, u32[]{:S(2)}) %collective-permute-start.10) | collective-permute-done | bytes 196640 | tf_op jit(solution)/shard_map/ppermute | solution.py:312
  43.1 0.6 collective-permute-start.11
  43.7 0.1 collective-permute-start.3
  43.8 0.1 fusion.9
  43.9 5.6 %collective-permute-start.22 = (bf16[4,24,2048]{2,1,0:T(8,128)(2,1)S(1)}, bf16[4,24,2048]{2,1,0:T(8,128)(2,1)S(1)}, u32[]{:S(2)}, u32[]{:S(2)}) collective-permute-start(bf16[4,24,2048]{2,1,0:T(8,128)(2,1)S(1)} %get-tuple-element.106), channel_id=1, source_target_pairs={{0,24},{4,28},{8,0},{12,4},{16,8},{20,12},{24,16},{28,20},{1,25},{... | collective-permute-start | bytes 1179656 | tf_op jit(solution)/shard_map/ppermute | solution.py:312
  49.5 0.6 collective-permute-start.20
  50.1 6.3 %enter.2 = (f32[192,1792]{1,0:T(8,128)S(1)}, f32[192,1792]{1,0:T(8,128)S(1)}) custom-call(bf16[96,2048]{1,0:T(8,128)(2,1)S(1)} %constant_dynamic-update-slice_fusion.4.refs_0_, bf16[96,2048]{1,0:T(8,128)(2,1)S(1)} %collective-permute-done.7.refs_1_, bf16[4096,1792]{1,0:T(8,128)(2,1)} %refs_2_.7, bf16[4096,1792]{1,0:T(8,128)(2,1)} %refs_3_.5), custom_call_target="tpu_custom_call" | custom-call | flops 2818572288 | bytes 14680064 | tf_op jit(solution)/shard_map/enter/pallas_call | solution.py:156
  56.4 6.3 %enter.3 = (bf16[192,1792]{1,0:T(8,128)(2,1)S(1)}, f32[192,1792]{1,0:T(8,128)S(1)}, f32[192,1792]{1,0:T(8,128)S(1)}) custom-call(bf16[96,2048]{1,0:T(8,128)(2,1)S(1)} %constant_dynamic-update-slice_fusion.refs_0_, bf16[96,2048]{1,0:T(8,128)(2,1)S(1)} %collective-permute-done.3.refs_1_, bf16[4096,1792]{1,0:T(8,128)(2,1)} %refs_2_.7, ...), custom_call_target="tpu_custom_call" | custom-call | flops 2818572288 | bytes 14680064 | tf_op jit(solution)/shard_map/enter/pallas_call | solution.py:156
  62.7 1.6 collective-permute-start.31
  64.3 7.6 %turn.1.refs_1_ = bf16[2,192,1792]{2,1,0:T(8,128)(2,1)S(1)} custom-call(bf16[96,4096]{1,0:T(8,128)(2,1)S(1)} %constant_dynamic-update-slice_fusion.8.refs_0_, bf16[96,4096]{1,0:T(8,128)(2,1)S(1)} %collective-permute-done.11.refs_1_, bf16[1792,4096]{1,0:T(8,128)(2,1)} %refs_4_.1, f32[192,1792]{1,0:T(8,128)S(1)} %get-tuple-element.51.refs_3_, ...), custom_call_target="tpu_custom_call" | custom-call | flops 2818572288 | bytes 14680064 | tf_op jit(solution)/shard_map/turn/pallas_call | solution.py:200
  72.0 16.4 %leave.1 = (bf16[2,96,4096]{2,1,0:T(8,128)(2,1)S(1)}, bf16[2,96,4096]{2,1,0:T(8,128)(2,1)S(1)}) custom-call(bf16[192,1792]{1,0:T(8,128)(2,1)S(1)} %get-tuple-element.50.refs_0_, bf16[2,192,1792]{2,1,0:T(8,128)(2,1)S(1)} %turn.1.refs_1_, bf16[4096,1792]{1,0:T(8,128)(2,1)} %refs_2_.7, bf16[4096,1792]{1,0:T(8,128)(2,1)} %refs_3_.5, bf16[1792,4096]{1,0:T(8,128)(2,1)} %refs_4_.1), custom_call_target="tpu_custom_call" | custom-call | flops 8455716864 | bytes 44040192 | tf_op jit(solution)/shard_map/leave/pallas_call | solution.py:247
  88.3 0.1 collective-permute-start.12
  88.4 0.3 pad_maximum_fusion.1
  88.7 0.5 collective-permute-start.23
  89.2 1.5 collective-permute-start.30
  90.8 0.6 collective-permute-start.24
  91.4 0.5 collective-permute-start.25
  91.9 15.6 %collective-permute-done.30 = bf16[192,1792]{1,0:T(8,128)(2,1)S(1)} collective-permute-done((bf16[192,1792]{1,0:T(8,128)(2,1)S(1)}, bf16[192,1792]{1,0:T(8,128)(2,1)S(1)}, u32[]{:S(2)}, u32[]{:S(2)}) %collective-permute-start.30) | collective-permute-done | bytes 688160 | tf_op jit(solution)/shard_map/ppermute | solution.py:320
  107.6 1.5 collective-permute-start.32
  109.1 0.6 collective-permute-start.33
  109.7 0.4 fold.1
  110.1 4.8 %collective-permute-start.15 = (bf16[2,24,4096]{2,1,0:T(8,128)(2,1)S(1)}, bf16[2,24,4096]{2,1,0:T(8,128)(2,1)S(1)}, u32[]{:S(2)}, u32[]{:S(2)}) collective-permute-start(bf16[2,24,4096]{2,1,0:T(8,128)(2,1)S(1)} %get-tuple-element.59), channel_id=1, source_target_pairs={{0,8},{4,12},{24,16},{28,20},{1,9},{5,13},{25,17},{29,21},{2,10},{... | collective-permute-start | bytes 1179656 | tf_op jit(solution)/shard_map/ppermute | solution.py:360
  114.9 0.1 fusion.1
  115.0 0.1 copy.11
  115.1 0.4 pad_maximum_fusion
  115.5 0.1 copy.12
  115.7 0.2 copy.13
  115.9 5.3 %collective-permute-done.15 = bf16[2,24,4096]{2,1,0:T(8,128)(2,1)S(1)} collective-permute-done((bf16[2,24,4096]{2,1,0:T(8,128)(2,1)S(1)}, bf16[2,24,4096]{2,1,0:T(8,128)(2,1)S(1)}, u32[]{:S(2)}, u32[]{:S(2)}) %collective-permute-start.15) | collective-permute-done | bytes 393248 | tf_op jit(solution)/shard_map/ppermute | solution.py:360
  121.1 1.3 collective-permute-start.13
  122.4 0.1 add_convert_fusion.1
  122.5 14.5 %collective-permute-done.24 = bf16[2,192,1792]{2,1,0:T(8,128)(2,1)S(1)} collective-permute-done((bf16[2,192,1792]{2,1,0:T(8,128)(2,1)S(1)}, bf16[2,192,1792]{2,1,0:T(8,128)(2,1)S(1)}, u32[]{:S(2)}, u32[]{:S(2)}) %collective-permute-start.24) | collective-permute-done | bytes 1376288 | tf_op jit(solution)/shard_map/ppermute | solution.py:320
  137.0 4.9 %collective-permute-start.14 = (bf16[2,24,4096]{2,1,0:T(8,128)(2,1)S(1)}, bf16[2,24,4096]{2,1,0:T(8,128)(2,1)S(1)}, u32[]{:S(2)}, u32[]{:S(2)}) collective-permute-start(bf16[2,24,4096]{2,1,0:T(8,128)(2,1)S(1)} %get-tuple-element.57), channel_id=1, source_target_pairs={{0,8},{4,12},{8,16},{12,20},{16,24},{20,28},{1,9},{5,13},{9,17},{1... | collective-permute-start | bytes 1179656 | tf_op jit(solution)/shard_map/ppermute | solution.py:360
  142.0 0.9 collective-permute-start.16
  143.4 0.1 collective-permute-done.32
  143.5 1.5 collective-permute-start.28
  145.0 0.5 collective-permute-start.29
  145.8 4.5 %convolution_convert_fusion = bf16[1792,1024]{1,0:T(8,128)(2,1)} fusion(bf16[768,1792]{1,0:T(8,128)(2,1)S(1)} %constant_dynamic-update-slice_fusion.18, bf16[768,1024]{1,0:T(8,128)(2,1)S(1)} %bitcast.69), kind=kOutput, calls=%fused_computation.7 | convolution fusion | flops 2820407296 | bytes 7995392 | tf_op jit(solution)/shard_map/dot_general | solution.py:295
  150.3 3.1 %fusion.14 = f32[1024,1792]{1,0:T(8,128)S(1)} fusion(bf16[576,1024]{1,0:T(8,128)(2,1)S(1)} %bitcast.70, bf16[576,1792]{1,0:T(8,128)(2,1)S(1)} %bitcast_dynamic-update-slice_fusion.4), kind=kOutput, calls=%fused_computation.67 | convolution fusion | flops 2113929216 | bytes 10584064 | tf_op jit(solution)/shard_map/dot_general | solution.py:295
  153.4 1.6 collective-permute-start.27
  155.1 0.6 collective-permute-start.26
  155.7 4.5 %convolution_convert_fusion.1 = bf16[1024,1792]{1,0:T(8,128)(2,1)} fusion(bf16[768,1024]{1,0:T(8,128)(2,1)S(1)} %bitcast.68, bf16[768,1792]{1,0:T(8,128)(2,1)S(1)} %constant_dynamic-update-slice_fusion.14), kind=kOutput, calls=%fused_computation.8 | convolution fusion | flops 2820407296 | bytes 7995392 | tf_op jit(solution)/shard_map/dot_general | solution.py:295
  160.2 1.9 %collective-permute-done.27 = bf16[96,1792]{1,0:T(8,128)(2,1)S(1)} collective-permute-done((bf16[96,1792]{1,0:T(8,128)(2,1)S(1)}, bf16[96,1792]{1,0:T(8,128)(2,1)S(1)}, u32[]{:S(2)}, u32[]{:S(2)}) %collective-permute-start.27) | collective-permute-done | bytes 344096 | tf_op jit(solution)/shard_map/ppermute | solution.py:320
  162.1 1.3 collective-permute-done.26
  163.5 3.0 %add_convert_fusion = bf16[1024,1792]{1,0:T(8,128)(2,1)} fusion(f32[1024,1792]{1,0:T(8,128)S(1)} %fusion.14, bf16[192,1024]{1,0:T(8,128)(2,1)S(1)} %bitcast.67, bf16[96,1792]{1,0:T(8,128)(2,1)S(1)} %collective-permute-done.27, bf16[96,1792]{1,0:T(8,128)(2,1)S(1)} %collective-permute-done.26), kind=kOutput, calls=%fused_computation | convolution fusion | flops 709689344 | bytes 12091392 | tf_op jit(solution)/shard_map/dot_general | solution.py:295
  166.5 0.9 fusion.7
  (64 shorter events, 1.0 us)
Async XLA Ops:
  0.6 0.9 copy-start
  1.6 0.9 copy-start.1
  2.5 0.7 copy-start.2
  3.5 9.0 %collective-permute-start = (bf16[24,2048]{1,0:T(8,128)(2,1)S(1)}, bf16[24,2048]{1,0:T(8,128)(2,1)S(1)}, u32[]{:S(2)}, u32[]{:S(2)}) collective-permute-start(bf16[24,2048]{1,0:T(8,128)(2,1)S(1)} %get-tuple-element.46), channel_id=1, source_target_pairs={{0,8},{4,12},{8,16},{12,20},{16,24},{20,28},{24,0},{28,4},{1,9},{5... | collective-permute-start | bytes 294920 | tf_op jit(solution)/shard_map/ppermute | solution.py:312
  6.6 12.7 %collective-permute-start.1 = (bf16[24,2048]{1,0:T(8,128)(2,1)S(1)}, bf16[24,2048]{1,0:T(8,128)(2,1)S(1)}, u32[]{:S(2)}, u32[]{:S(2)}) collective-permute-start(bf16[24,2048]{1,0:T(8,128)(2,1)S(1)} %get-tuple-element.46), channel_id=1, source_target_pairs={{0,16},{4,20},{8,24},{12,28},{16,0},{20,4},{24,8},{28,12},{1,17},{... | collective-permute-start | bytes 294920 | tf_op jit(solution)/shard_map/ppermute | solution.py:312
  9.2 33.9 %collective-permute-start.2 = (bf16[24,2048]{1,0:T(8,128)(2,1)S(1)}, bf16[24,2048]{1,0:T(8,128)(2,1)S(1)}, u32[]{:S(2)}, u32[]{:S(2)}) collective-permute-start(bf16[24,2048]{1,0:T(8,128)(2,1)S(1)} %get-tuple-element.46), channel_id=1, source_target_pairs={{0,24},{4,28},{8,0},{12,4},{16,8},{20,12},{24,16},{28,20},{1,25},{... | collective-permute-start | bytes 294920 | tf_op jit(solution)/shard_map/ppermute | solution.py:312
  10.6 10.5 %collective-permute-start.4 = (bf16[24,2048]{1,0:T(8,128)(2,1)S(1)}, bf16[24,2048]{1,0:T(8,128)(2,1)S(1)}, u32[]{:S(2)}, u32[]{:S(2)}) collective-permute-start(bf16[24,2048]{1,0:T(8,128)(2,1)S(1)} %get-tuple-element.47), channel_id=1, source_target_pairs={{0,8},{4,12},{8,16},{12,20},{16,24},{20,28},{24,0},{28,4},{1,9},{5... | collective-permute-start | bytes 294920 | tf_op jit(solution)/shard_map/ppermute | solution.py:312
  11.2 21.4 %collective-permute-start.5 = (bf16[24,2048]{1,0:T(8,128)(2,1)S(1)}, bf16[24,2048]{1,0:T(8,128)(2,1)S(1)}, u32[]{:S(2)}, u32[]{:S(2)}) collective-permute-start(bf16[24,2048]{1,0:T(8,128)(2,1)S(1)} %get-tuple-element.47), channel_id=1, source_target_pairs={{0,16},{4,20},{8,24},{12,28},{16,0},{20,4},{24,8},{28,12},{1,17},{... | collective-permute-start | bytes 294920 | tf_op jit(solution)/shard_map/ppermute | solution.py:312
  12.6 20.1 %collective-permute-start.6 = (bf16[24,2048]{1,0:T(8,128)(2,1)S(1)}, bf16[24,2048]{1,0:T(8,128)(2,1)S(1)}, u32[]{:S(2)}, u32[]{:S(2)}) collective-permute-start(bf16[24,2048]{1,0:T(8,128)(2,1)S(1)} %get-tuple-element.47), channel_id=1, source_target_pairs={{0,24},{4,28},{8,0},{12,4},{16,8},{20,12},{24,16},{28,20},{1,25},{... | collective-permute-start | bytes 294920 | tf_op jit(solution)/shard_map/ppermute | solution.py:312
  19.3 15.9 %collective-permute-start.8 = (bf16[24,4096]{1,0:T(8,128)(2,1)}, bf16[24,4096]{1,0:T(8,128)(2,1)S(1)}, u32[]{:S(2)}, u32[]{:S(2)}) collective-permute-start(bf16[24,4096]{1,0:T(8,128)(2,1)} %cot_ref.1), channel_id=1, source_target_pairs={{0,8},{4,12},{8,16},{12,20},{16,24},{20,28},{24,0},{28,4},{1,9},{5... | collective-permute-start | bytes 589832 | tf_op jit(solution)/shard_map/ppermute | solution.py:312
  21.1 17.9 %collective-permute-start.9 = (bf16[24,4096]{1,0:T(8,128)(2,1)}, bf16[24,4096]{1,0:T(8,128)(2,1)S(1)}, u32[]{:S(2)}, u32[]{:S(2)}) collective-permute-start(bf16[24,4096]{1,0:T(8,128)(2,1)} %cot_ref.1), channel_id=1, source_target_pairs={{0,16},{4,20},{8,24},{12,28},{16,0},{20,4},{24,8},{28,12},{1,17},{... | collective-permute-start | bytes 589832 | tf_op jit(solution)/shard_map/ppermute | solution.py:312
  32.6 10.4 %collective-permute-start.10 = (bf16[24,4096]{1,0:T(8,128)(2,1)}, bf16[24,4096]{1,0:T(8,128)(2,1)S(1)}, u32[]{:S(2)}, u32[]{:S(2)}) collective-permute-start(bf16[24,4096]{1,0:T(8,128)(2,1)} %cot_ref.1), channel_id=1, source_target_pairs={{0,24},{4,28},{8,0},{12,4},{16,8},{20,12},{24,16},{28,20},{1,25},{... | collective-permute-start | bytes 589832 | tf_op jit(solution)/shard_map/ppermute | solution.py:312
  32.7 11.0 %collective-permute-start.19 = (bf16[24,2048]{1,0:T(8,128)(2,1)S(1)}, bf16[24,2048]{1,0:T(8,128)(2,1)S(1)}, u32[]{:S(2)}, u32[]{:S(2)}) collective-permute-start(bf16[24,2048]{1,0:T(8,128)(2,1)S(1)} %get-tuple-element.63), channel_id=1, source_target_pairs={{0,3},{1,2},{2,1},{3,0},{4,7},{5,6},{6,5},{7,4},{8,11},{9,10},{10,... | collective-permute-start | bytes 294920 | tf_op jit(solution)/shard_map/ppermute | solution.py:320
  35.2 8.6 %collective-permute-start.18 = (bf16[24,2048]{1,0:T(8,128)(2,1)S(1)}, bf16[24,2048]{1,0:T(8,128)(2,1)S(1)}, u32[]{:S(2)}, u32[]{:S(2)}) collective-permute-start(bf16[24,2048]{1,0:T(8,128)(2,1)S(1)} %get-tuple-element.62), channel_id=1, source_target_pairs={{0,2},{1,3},{2,0},{3,1},{4,6},{5,7},{6,4},{7,5},{8,10},{9,11},{10,... | collective-permute-start | bytes 294920 | tf_op jit(solution)/shard_map/ppermute | solution.py:320
  39.0 4.8 %collective-permute-start.17 = (bf16[24,2048]{1,0:T(8,128)(2,1)S(1)}, bf16[24,2048]{1,0:T(8,128)(2,1)S(1)}, u32[]{:S(2)}, u32[]{:S(2)}) collective-permute-start(bf16[24,2048]{1,0:T(8,128)(2,1)S(1)} %get-tuple-element.61), channel_id=1, source_target_pairs={{0,1},{1,0},{2,3},{3,2},{4,5},{5,4},{6,7},{7,6},{8,9},{9,8},{10,11... | collective-permute-start | bytes 294920 | tf_op jit(solution)/shard_map/ppermute | solution.py:320
  43.1 6.4 %collective-permute-start.7 = (bf16[96,2048]{1,0:T(8,128)(2,1)S(1)}, bf16[96,2048]{1,0:T(8,128)(2,1)S(1)}, u32[]{:S(2)}, u32[]{:S(2)}) collective-permute-start(bf16[96,2048]{1,0:T(8,128)(2,1)S(1)} %constant_dynamic-update-slice_fusion.4.refs_0_), channel_id=1, source_target_pairs={{0,4},{4,0},{8,12},{12,8},{16,20},{20,16},{24,28},{28,24},{1,5},{5... | collective-permute-start | bytes 1179656 | tf_op jit(solution)/shard_map/ppermute | solution.py:316
  43.1 21.2 %collective-permute-start.11 = (bf16[96,4096]{1,0:T(8,128)(2,1)S(1)}, bf16[96,4096]{1,0:T(8,128)(2,1)S(1)}, u32[]{:S(2)}, u32[]{:S(2)}) collective-permute-start(bf16[96,4096]{1,0:T(8,128)(2,1)S(1)} %constant_dynamic-update-slice_fusion.8.refs_0_), channel_id=1, source_target_pairs={{0,4},{4,0},{8,12},{12,8},{16,20},{20,16},{24,28},{28,24},{1,5},{5... | collective-permute-start | bytes 2359304 | tf_op jit(solution)/shard_map/ppermute | solution.py:316
  43.7 12.7 %collective-permute-start.3 = (bf16[96,2048]{1,0:T(8,128)(2,1)S(1)}, bf16[96,2048]{1,0:T(8,128)(2,1)S(1)}, u32[]{:S(2)}, u32[]{:S(2)}) collective-permute-start(bf16[96,2048]{1,0:T(8,128)(2,1)S(1)} %constant_dynamic-update-slice_fusion.refs_0_), channel_id=1, source_target_pairs={{0,4},{4,0},{8,12},{12,8},{16,20},{20,16},{24,28},{28,24},{1,5},{5... | collective-permute-start | bytes 1179656 | tf_op jit(solution)/shard_map/ppermute | solution.py:316
  43.9 44.5 %collective-permute-start.22 = (bf16[4,24,2048]{2,1,0:T(8,128)(2,1)S(1)}, bf16[4,24,2048]{2,1,0:T(8,128)(2,1)S(1)}, u32[]{:S(2)}, u32[]{:S(2)}) collective-permute-start(bf16[4,24,2048]{2,1,0:T(8,128)(2,1)S(1)} %get-tuple-element.106), channel_id=1, source_target_pairs={{0,24},{4,28},{8,0},{12,4},{16,8},{20,12},{24,16},{28,20},{1,25},{... | collective-permute-start | bytes 1179656 | tf_op jit(solution)/shard_map/ppermute | solution.py:312
  49.4 39.0 %collective-permute-start.21 = (bf16[4,24,2048]{2,1,0:T(8,128)(2,1)S(1)}, bf16[4,24,2048]{2,1,0:T(8,128)(2,1)S(1)}, u32[]{:S(2)}, u32[]{:S(2)}) collective-permute-start(bf16[4,24,2048]{2,1,0:T(8,128)(2,1)S(1)} %get-tuple-element.106), channel_id=1, source_target_pairs={{0,16},{4,20},{8,24},{12,28},{16,0},{20,4},{24,8},{28,12},{1,17},{... | collective-permute-start | bytes 1179656 | tf_op jit(solution)/shard_map/ppermute | solution.py:312
  49.5 39.0 %collective-permute-start.20 = (bf16[4,24,2048]{2,1,0:T(8,128)(2,1)S(1)}, bf16[4,24,2048]{2,1,0:T(8,128)(2,1)S(1)}, u32[]{:S(2)}, u32[]{:S(2)}) collective-permute-start(bf16[4,24,2048]{2,1,0:T(8,128)(2,1)S(1)} %get-tuple-element.106), channel_id=1, source_target_pairs={{0,8},{4,12},{8,16},{12,20},{16,24},{20,28},{24,0},{28,4},{1,9},{5... | collective-permute-start | bytes 1179656 | tf_op jit(solution)/shard_map/ppermute | solution.py:312
  62.7 28.7 %collective-permute-start.31 = (bf16[192,1792]{1,0:T(8,128)(2,1)S(1)}, bf16[192,1792]{1,0:T(8,128)(2,1)S(1)}, u32[]{:S(2)}, u32[]{:S(2)}) collective-permute-start(bf16[192,1792]{1,0:T(8,128)(2,1)S(1)} %get-tuple-element.50.refs_0_), channel_id=1, source_target_pairs={{0,2},{1,3},{2,0},{3,1},{4,6},{5,7},{6,4},{7,5},{8,10},{9,11},{10,... | collective-permute-start | bytes 2064392 | tf_op jit(solution)/shard_map/ppermute | solution.py:320
  88.3 20.8 %collective-permute-start.12 = (bf16[2,96,4096]{2,1,0:T(8,128)(2,1)S(1)}, bf16[2,96,4096]{2,1,0:T(8,128)(2,1)S(1)}, u32[]{:S(2)}, u32[]{:S(2)}) collective-permute-start(bf16[2,96,4096]{2,1,0:T(8,128)(2,1)S(1)} %get-tuple-element.54), channel_id=1, source_target_pairs={{0,4},{4,0},{8,12},{12,8},{16,20},{20,16},{24,28},{28,24},{1,5},{5... | collective-permute-start | bytes 4718600 | tf_op jit(solution)/shard_map/ppermute | solution.py:316
  88.7 21.4 %collective-permute-start.23 = (bf16[4,4,24,2048]{3,2,0,1:T(8,128)(2,1)S(1)}, bf16[4,4,24,2048]{3,2,0,1:T(8,128)(2,1)S(1)}, u32[]{:S(2)}, u32[]{:S(2)}) collective-permute-start(bf16[4,4,24,2048]{3,2,0,1:T(8,128)(2,1)S(1)} %get-tuple-element.83), channel_id=1, source_target_pairs={{0,4},{4,0},{8,12},{12,8},{16,20},{20,16},{24,28},{28,24},{1,5},{5... | collective-permute-start | bytes 4718600 | tf_op jit(solution)/shard_map/ppermute | solution.py:316
  89.2 18.3 %collective-permute-start.30 = (bf16[192,1792]{1,0:T(8,128)(2,1)S(1)}, bf16[192,1792]{1,0:T(8,128)(2,1)S(1)}, u32[]{:S(2)}, u32[]{:S(2)}) collective-permute-start(bf16[192,1792]{1,0:T(8,128)(2,1)S(1)} %get-tuple-element.50.refs_0_), channel_id=1, source_target_pairs={{0,1},{1,0},{2,3},{3,2},{4,5},{5,4},{6,7},{7,6},{8,9},{9,8},{10,11... | collective-permute-start | bytes 2064392 | tf_op jit(solution)/shard_map/ppermute | solution.py:320
  90.8 46.3 %collective-permute-start.24 = (bf16[2,192,1792]{2,1,0:T(8,128)(2,1)S(1)}, bf16[2,192,1792]{2,1,0:T(8,128)(2,1)S(1)}, u32[]{:S(2)}, u32[]{:S(2)}) collective-permute-start(bf16[2,192,1792]{2,1,0:T(8,128)(2,1)S(1)} %turn.1.refs_1_), channel_id=1, source_target_pairs={{0,1},{1,0},{2,3},{3,2},{4,5},{5,4},{6,7},{7,6},{8,9},{9,8},{10,11... | collective-permute-start | bytes 4128776 | tf_op jit(solution)/shard_map/ppermute | solution.py:320
  91.4 50.6 %collective-permute-start.25 = (bf16[2,192,1792]{2,1,0:T(8,128)(2,1)S(1)}, bf16[2,192,1792]{2,1,0:T(8,128)(2,1)S(1)}, u32[]{:S(2)}, u32[]{:S(2)}) collective-permute-start(bf16[2,192,1792]{2,1,0:T(8,128)(2,1)S(1)} %turn.1.refs_1_), channel_id=1, source_target_pairs={{0,2},{1,3},{2,0},{3,1},{4,6},{5,7},{6,4},{7,5},{8,10},{9,11},{10,... | collective-permute-start | bytes 4128776 | tf_op jit(solution)/shard_map/ppermute | solution.py:320
  107.6 36.0 %collective-permute-start.32 = (bf16[96,1792]{1,0:T(8,128)(2,1)S(1)}, bf16[96,1792]{1,0:T(8,128)(2,1)S(1)}, u32[]{:S(2)}, u32[]{:S(2)}) collective-permute-start(bf16[96,1792]{1,0:T(8,128)(2,1)S(1)} %get-tuple-element.75), channel_id=1, source_target_pairs={{0,1},{1,0},{2,3},{3,2},{4,5},{5,4},{6,7},{7,6},{8,9},{9,8},{10,11... | collective-permute-start | bytes 1032200 | tf_op jit(solution)/shard_map/ppermute | solution.py:320
  109.1 35.9 %collective-permute-start.33 = (bf16[96,1792]{1,0:T(8,128)(2,1)S(1)}, bf16[96,1792]{1,0:T(8,128)(2,1)S(1)}, u32[]{:S(2)}, u32[]{:S(2)}) collective-permute-start(bf16[96,1792]{1,0:T(8,128)(2,1)S(1)} %get-tuple-element.74), channel_id=1, source_target_pairs={{0,2},{1,3},{2,0},{3,1},{4,6},{5,7},{6,4},{7,5},{8,10},{9,11},{10,... | collective-permute-start | bytes 1032200 | tf_op jit(solution)/shard_map/ppermute | solution.py:320
  110.1 11.1 %collective-permute-start.15 = (bf16[2,24,4096]{2,1,0:T(8,128)(2,1)S(1)}, bf16[2,24,4096]{2,1,0:T(8,128)(2,1)S(1)}, u32[]{:S(2)}, u32[]{:S(2)}) collective-permute-start(bf16[2,24,4096]{2,1,0:T(8,128)(2,1)S(1)} %get-tuple-element.59), channel_id=1, source_target_pairs={{0,8},{4,12},{24,16},{28,20},{1,9},{5,13},{25,17},{29,21},{2,10},{... | collective-permute-start | bytes 1179656 | tf_op jit(solution)/shard_map/ppermute | solution.py:360
  121.1 45.4 %collective-permute-start.13 = (bf16[2,24,4096]{2,1,0:T(8,128)(2,1)S(1)}, bf16[2,24,4096]{2,1,0:T(8,128)(2,1)S(1)}, u32[]{:S(2)}, u32[]{:S(2)}) collective-permute-start(bf16[2,24,4096]{2,1,0:T(8,128)(2,1)S(1)} %get-tuple-element.56), channel_id=1, source_target_pairs={{8,0},{12,4},{16,8},{20,12},{24,16},{28,20},{9,1},{13,5},{17,9},{2... | collective-permute-start | bytes 1179656 | tf_op jit(solution)/shard_map/ppermute | solution.py:360
  137.0 29.5 %collective-permute-start.14 = (bf16[2,24,4096]{2,1,0:T(8,128)(2,1)S(1)}, bf16[2,24,4096]{2,1,0:T(8,128)(2,1)S(1)}, u32[]{:S(2)}, u32[]{:S(2)}) collective-permute-start(bf16[2,24,4096]{2,1,0:T(8,128)(2,1)S(1)} %get-tuple-element.57), channel_id=1, source_target_pairs={{0,8},{4,12},{8,16},{12,20},{16,24},{20,28},{1,9},{5,13},{9,17},{1... | collective-permute-start | bytes 1179656 | tf_op jit(solution)/shard_map/ppermute | solution.py:360
  142.0 24.5 %collective-permute-start.16 = (bf16[2,24,4096]{2,1,0:T(8,128)(2,1)S(1)}, bf16[2,24,4096]{2,1,0:T(8,128)(2,1)S(1)}, u32[]{:S(2)}, u32[]{:S(2)}) collective-permute-start(bf16[2,24,4096]{2,1,0:T(8,128)(2,1)S(1)} %add_convert_fusion.1), channel_id=1, source_target_pairs={{0,16},{4,20},{8,24},{12,28},{16,0},{20,4},{24,8},{28,12},{1,17},{... | collective-permute-start | bytes 1179656 | tf_op jit(solution)/shard_map/ppermute | solution.py:312
  143.5 9.9 %collective-permute-start.28 = (bf16[96,1792]{1,0:T(8,128)(2,1)S(1)}, bf16[96,1792]{1,0:T(8,128)(2,1)S(1)}, u32[]{:S(2)}, u32[]{:S(2)}) collective-permute-start(bf16[96,1792]{1,0:T(8,128)(2,1)S(1)} %get-tuple-element.87), channel_id=1, source_target_pairs={{0,1},{1,0},{2,3},{3,2},{4,5},{5,4},{6,7},{7,6},{8,9},{9,8},{10,11... | collective-permute-start | bytes 1032200 | tf_op jit(solution)/shard_map/ppermute | solution.py:320
  145.0 10.0 %collective-permute-start.29 = (bf16[96,1792]{1,0:T(8,128)(2,1)S(1)}, bf16[96,1792]{1,0:T(8,128)(2,1)S(1)}, u32[]{:S(2)}, u32[]{:S(2)}) collective-permute-start(bf16[96,1792]{1,0:T(8,128)(2,1)S(1)} %get-tuple-element.85), channel_id=1, source_target_pairs={{0,2},{1,3},{2,0},{3,1},{4,6},{5,7},{6,4},{7,5},{8,10},{9,11},{10,... | collective-permute-start | bytes 1032200 | tf_op jit(solution)/shard_map/ppermute | solution.py:320
  153.4 8.7 %collective-permute-start.27 = (bf16[96,1792]{1,0:T(8,128)(2,1)S(1)}, bf16[96,1792]{1,0:T(8,128)(2,1)S(1)}, u32[]{:S(2)}, u32[]{:S(2)}) collective-permute-start(bf16[96,1792]{1,0:T(8,128)(2,1)S(1)} %get-tuple-element.86), channel_id=1, source_target_pairs={{0,2},{1,3},{2,0},{3,1},{4,6},{5,7},{6,4},{7,5},{8,10},{9,11},{10,... | collective-permute-start | bytes 1032200 | tf_op jit(solution)/shard_map/ppermute | solution.py:320
  155.1 8.4 %collective-permute-start.26 = (bf16[96,1792]{1,0:T(8,128)(2,1)S(1)}, bf16[96,1792]{1,0:T(8,128)(2,1)S(1)}, u32[]{:S(2)}, u32[]{:S(2)}) collective-permute-start(bf16[96,1792]{1,0:T(8,128)(2,1)S(1)} %get-tuple-element.88), channel_id=1, source_target_pairs={{0,1},{1,0},{2,3},{3,2},{4,5},{5,4},{6,7},{7,6},{8,9},{9,8},{10,11... | collective-permute-start | bytes 1032200 | tf_op jit(solution)/shard_map/ppermute | solution.py:320

commit v12 on v11

--- a/solution.py
+++ b/solution.py
@@ -45,9 +45,8 @@
     return jnp.dot(left, right, preferred_element_type=F32)
 
 
-def pick_kernel(seat_ref, flag_ref, tokens_ref, cot_ref, left_ref, right_ref, *refs):
-    blocks, picked_ref = refs[:-1], refs[-1]
-    rows = cot_ref.shape[0]
+def pick_kernel(flag_ref, tokens_ref, picked_ref, left_ref, right_ref):
+    rows = picked_ref.shape[0]
     count = tokens_ref.shape[0]
     flags = (flag_ref[...] == 1).astype(F32)
     before = lax.broadcasted_iota(jnp.int32, (count, count), 0)
@@ -61,6 +60,22 @@
     middle = left_ref.shape[1]
     left_ref[...] = picked_ref[:, :middle]
     right_ref[...] = picked_ref[:, middle:]
+
+
+def pick(modality, tokens, rows):
+    width = tokens.shape[1]
+    half = shape((rows, width // 2))
+    return pl.pallas_call(
+        pick_kernel,
+        in_specs=[VMEM] * 2,
+        out_specs=[VMEM] * 3,
+        out_shape=[shape((rows, width)), half, half],
+        compiler_params=grant(),
+        name="pick",
+    )(modality.reshape(1, -1), tokens)
+
+
+def cut_kernel(seat_ref, picked_ref, cot_ref, *blocks):
     part = picked_ref.shape[1] // len(blocks)
     for m, block in enumerate(blocks):
         span = pl.ds(pl.multiple_of((seat_ref[0] ^ m) * part, part), part)
@@ -68,18 +83,16 @@
         block[:, part:] = cot_ref[:, span]
 
 
-def pick(seat, modality, tokens, out_grad, groups):
+def cut(seat, picked, out_grad, groups):
     rows, width = out_grad.shape
-    half, block = shape((rows, width // 2)), shape((rows, 2 * width // groups))
-    return pl.pallas_call(
-        pick_kernel,
-        in_specs=[pl.BlockSpec(memory_space=pltpu.SMEM)] + [VMEM] * 3,
-        out_specs=[VMEM] * (2 + groups),
-        out_shape=[half, half] + [block] * groups,
-        scratch_shapes=[pltpu.VMEM((rows, width), BF)],
+    return pl.pallas_call(
+        cut_kernel,
+        in_specs=[pl.BlockSpec(memory_space=pltpu.SMEM)] + [VMEM] * 2,
+        out_specs=[VMEM] * groups,
+        out_shape=[shape((rows, 2 * width // groups))] * groups,
         compiler_params=grant(),
-        name="pick",
-    )(seat, modality.reshape(1, -1), tokens, out_grad)
+        name="cut",
+    )(seat, picked, out_grad)
 
 
 def streamed(steps, depth, copies, body, first):
@@ -300,7 +313,7 @@
 
 
 def on_device(tokens, modality, gate, up, down, out_grad):
-    _, width = out_grad.shape
+    count, width = out_grad.shape
     groups = lax.axis_size("seq")
     ring = lax.axis_size("dp") // CORES
     part = width // groups
@@ -369,7 +382,8 @@
     def stack(held):
         return jnp.concatenate(sum(held, []), axis=0)
 
-    left, right, *blocks = pick(seat, modality, tokens, out_grad, groups)
+    picked, left, right = pick(modality, tokens, count)
+    blocks = cut(seat, picked, out_grad, groups)
     tok = [gathered(side) for side in (left, right)]
     tok_mate = []
     for side in tok:
@@ -389,15 +403,15 @@
 
     mate = swap(other)
     terms, last = returned(own, mate)
-    all_hid = after(all_hid, [last])
     all_both = after(all_both, [last])
     all_gb, all_ub = ([v and [v[0][side, :rows // 2], v[0][side, rows // 2:]] for v in all_both]
                       for side in range(2))
     all_gb = relay(all_gb)
     all_ub = relay(all_ub)
+    up_grad = sums_dot(tok_all[:-rows], stack(all_ub[:-1]))
+    all_hid = after(all_hid, [up_grad])
     down_grad = rows_dot(stack(all_hid), cot_all)
     gate_grad = rows_dot(tok_all, stack(all_gb))
-    up_grad = sums_dot(tok_all[:-rows], stack(all_ub[:-1]))
     up_grad = (up_grad + sums_dot(tok_all[-rows:], stack(all_ub[-1:]))).astype(BF)
     terms = after(terms, [up_grad])
 

time: 168 us -> 168 us (level)
    ppermute x13, waiting for transfers between devices: 33.5 us -> 36 us  [across(): return lax.ppermute(value, 'seq', [(g, g ^ mask) for g in range(groups)])]
  transfers between devices with their start and end apart: 34 -> 34, of which waited for: 10 -> 11; matrix products, arithmetic and copies ran while one was open for 11% -> 11% of each run, Pallas kernels for 22% -> 22%
where the time goes in v12:
time: 168 us
  waiting for transfers between devices  56.8 us (34%)
  starting transfers between devices  50.5 us (30%)
  Pallas kernels  37.3 us (22%)
  matrix products  15.3 us (9%)
  local copies, waits for them, and re-layouts  4.7 us (3%)
  other arithmetic  1.95 us (1%)
    ppermute x13, waiting for transfers between devices, across(): return lax.ppermute(value, 'seq', [(g, g ^ mask) for g in range(groups)])  36 us
    ppermute x13, starting transfers between devices, shift(): lax.ppermute(value, 'dp', [(z * CORES + c, (z + k) % ring * CORES + c) fo...  24.7 us
    pallas_call x1, Pallas kernels, leave(): pl.pallas_call(lambda *refs: leave_kernel(step, *refs), in_specs=[VMEM] *...  16.4 us
    ppermute x13, waiting for transfers between devices, shift(): lax.ppermute(value, 'dp', [(z * CORES + c, (z + k) % ring * CORES + c) fo...  15.4 us
    dot_general x4, matrix products, sums_dot(): lax.dot_general(left, right, (((0,), (0,)), ((), ())), preferred_element_...  15.3 us
    ppermute x13, starting transfers between devices, across(): return lax.ppermute(value, 'seq', [(g, g ^ mask) for g in range(groups)])  13.5 us
    pallas_call x2, Pallas kernels, enter(): pl.pallas_call(lambda *refs: enter_kernel(tile, last, *refs), in_specs=[V...  12.6 us
    ppermute x3, starting transfers between devices, along(): lax.ppermute(value, 'dp', [(a * CORES + c, b * CORES + c) for a, b in pai...  11 us
  transfers between devices with their start and end apart: 34, of which 11 were waited for; matrix products, arithmetic and copies ran while one was open for 11% of the time, Pallas kernels for 22%

profile of v12, /device:TPU:0, one launch (start us, length us, event | category | flops | bytes accessed | tf_op | source)
XLA Modules:
  0.0 167.6 jit_solution(16049060195035026688)
XLA Ops:
  0.6 0.9 copy-done.1
  1.6 0.7 copy-done.2
  2.2 0.3 pick.1
  2.6 3.1 %collective-permute-start = (bf16[24,2048]{1,0:T(8,128)(2,1)S(1)}, bf16[24,2048]{1,0:T(8,128)(2,1)S(1)}, u32[]{:S(2)}, u32[]{:S(2)}) collective-permute-start(bf16[24,2048]{1,0:T(8,128)(2,1)S(1)} %get-tuple-element.46), channel_id=1, source_target_pairs={{0,8},{4,12},{8,16},{12,20},{16,24},{20,28},{24,0},{28,4},{1,9},{5... | collective-permute-start | bytes 294920 | tf_op jit(solution)/shard_map/ppermute | solution.py:325
  5.7 2.6 %collective-permute-start.1 = (bf16[24,2048]{1,0:T(8,128)(2,1)S(1)}, bf16[24,2048]{1,0:T(8,128)(2,1)S(1)}, u32[]{:S(2)}, u32[]{:S(2)}) collective-permute-start(bf16[24,2048]{1,0:T(8,128)(2,1)S(1)} %get-tuple-element.46), channel_id=1, source_target_pairs={{0,16},{4,20},{8,24},{12,28},{16,0},{20,4},{24,8},{28,12},{1,17},{... | collective-permute-start | bytes 294920 | tf_op jit(solution)/shard_map/ppermute | solution.py:325
  8.3 1.3 collective-permute-start.2
  9.6 0.7 collective-permute-start.4
  10.3 0.3 collective-permute-start.5
  10.6 0.9 constant_dynamic-update-slice_fusion.11
  11.6 0.9 copy-done
  12.6 2.9 %collective-permute-start.6 = (bf16[24,2048]{1,0:T(8,128)(2,1)S(1)}, bf16[24,2048]{1,0:T(8,128)(2,1)S(1)}, u32[]{:S(2)}, u32[]{:S(2)}) collective-permute-start(bf16[24,2048]{1,0:T(8,128)(2,1)S(1)} %get-tuple-element.47), channel_id=1, source_target_pairs={{0,24},{4,28},{8,0},{12,4},{16,8},{20,12},{24,16},{28,20},{1,25},{... | collective-permute-start | bytes 294920 | tf_op jit(solution)/shard_map/ppermute | solution.py:325
  15.4 2.9 %collective-permute-done.1 = bf16[24,2048]{1,0:T(8,128)(2,1)S(1)} collective-permute-done((bf16[24,2048]{1,0:T(8,128)(2,1)S(1)}, bf16[24,2048]{1,0:T(8,128)(2,1)S(1)}, u32[]{:S(2)}, u32[]{:S(2)}) %collective-permute-start.1) | collective-permute-done | bytes 98336 | tf_op jit(solution)/shard_map/ppermute | solution.py:325
  18.4 1.7 %collective-permute-start.8 = (bf16[24,4096]{1,0:T(8,128)(2,1)}, bf16[24,4096]{1,0:T(8,128)(2,1)S(1)}, u32[]{:S(2)}, u32[]{:S(2)}) collective-permute-start(bf16[24,4096]{1,0:T(8,128)(2,1)} %cot_ref.1), channel_id=1, source_target_pairs={{0,8},{4,12},{8,16},{12,20},{16,24},{20,28},{24,0},{28,4},{1,9},{5... | collective-permute-start | bytes 589832 | tf_op jit(solution)/shard_map/ppermute | solution.py:325
  20.1 4.9 %collective-permute-start.9 = (bf16[24,4096]{1,0:T(8,128)(2,1)}, bf16[24,4096]{1,0:T(8,128)(2,1)S(1)}, u32[]{:S(2)}, u32[]{:S(2)}) collective-permute-start(bf16[24,4096]{1,0:T(8,128)(2,1)} %cot_ref.1), channel_id=1, source_target_pairs={{0,16},{4,20},{8,24},{12,28},{16,0},{20,4},{24,8},{28,12},{1,17},{... | collective-permute-start | bytes 589832 | tf_op jit(solution)/shard_map/ppermute | solution.py:325
  25.0 6.7 %collective-permute-done.5 = bf16[24,2048]{1,0:T(8,128)(2,1)S(1)} collective-permute-done((bf16[24,2048]{1,0:T(8,128)(2,1)S(1)}, bf16[24,2048]{1,0:T(8,128)(2,1)S(1)}, u32[]{:S(2)}, u32[]{:S(2)}) %collective-permute-start.5) | collective-permute-done | bytes 98336 | tf_op jit(solution)/shard_map/ppermute | solution.py:325
  31.7 2.5 %collective-permute-start.19 = (bf16[24,2048]{1,0:T(8,128)(2,1)S(1)}, bf16[24,2048]{1,0:T(8,128)(2,1)S(1)}, u32[]{:S(2)}, u32[]{:S(2)}) collective-permute-start(bf16[24,2048]{1,0:T(8,128)(2,1)S(1)} %get-tuple-element.65), channel_id=1, source_target_pairs={{0,3},{1,2},{2,1},{3,0},{4,7},{5,6},{6,5},{7,4},{8,11},{9,10},{10,... | collective-permute-start | bytes 294920 | tf_op jit(solution)/shard_map/ppermute | solution.py:333
  34.3 0.6 collective-permute-start.18
  34.8 3.2 %collective-permute-done.9 = bf16[24,4096]{1,0:T(8,128)(2,1)S(1)} collective-permute-done((bf16[24,4096]{1,0:T(8,128)(2,1)}, bf16[24,4096]{1,0:T(8,128)(2,1)S(1)}, u32[]{:S(2)}, u32[]{:S(2)}) %collective-permute-start.9) | collective-permute-done | bytes 196640 | tf_op jit(solution)/shard_map/ppermute | solution.py:325
  38.1 1.5 collective-permute-start.17
  39.6 2.6 %collective-permute-done.10 = bf16[24,4096]{1,0:T(8,128)(2,1)S(1)} collective-permute-done((bf16[24,4096]{1,0:T(8,128)(2,1)}, bf16[24,4096]{1,0:T(8,128)(2,1)S(1)}, u32[]{:S(2)}, u32[]{:S(2)}) %collective-permute-start.10) | collective-permute-done | bytes 196640 | tf_op jit(solution)/shard_map/ppermute | solution.py:325
  42.2 0.6 collective-permute-start.11
  42.8 0.1 collective-permute-start.3
  42.9 0.1 fusion.9
  42.9 5.6 %collective-permute-start.22 = (bf16[4,24,2048]{2,1,0:T(8,128)(2,1)S(1)}, bf16[4,24,2048]{2,1,0:T(8,128)(2,1)S(1)}, u32[]{:S(2)}, u32[]{:S(2)}) collective-permute-start(bf16[4,24,2048]{2,1,0:T(8,128)(2,1)S(1)} %get-tuple-element.108), channel_id=1, source_target_pairs={{0,24},{4,28},{8,0},{12,4},{16,8},{20,12},{24,16},{28,20},{1,25},{... | collective-permute-start | bytes 1179656 | tf_op jit(solution)/shard_map/ppermute | solution.py:325
  48.5 0.6 collective-permute-start.20
  49.1 6.3 %enter.2 = (f32[192,1792]{1,0:T(8,128)S(1)}, f32[192,1792]{1,0:T(8,128)S(1)}) custom-call(bf16[96,2048]{1,0:T(8,128)(2,1)S(1)} %constant_dynamic-update-slice_fusion.4.refs_0_, bf16[96,2048]{1,0:T(8,128)(2,1)S(1)} %collective-permute-done.7.refs_1_, bf16[4096,1792]{1,0:T(8,128)(2,1)} %refs_2_.7, bf16[4096,1792]{1,0:T(8,128)(2,1)} %refs_3_.5), custom_call_target="tpu_custom_call" | custom-call | flops 2818572288 | bytes 14680064 | tf_op jit(solution)/shard_map/enter/pallas_call | solution.py:169
  55.5 6.3 %enter.3 = (bf16[192,1792]{1,0:T(8,128)(2,1)S(1)}, f32[192,1792]{1,0:T(8,128)S(1)}, f32[192,1792]{1,0:T(8,128)S(1)}) custom-call(bf16[96,2048]{1,0:T(8,128)(2,1)S(1)} %constant_dynamic-update-slice_fusion.refs_0_, bf16[96,2048]{1,0:T(8,128)(2,1)S(1)} %collective-permute-done.3.refs_1_, bf16[4096,1792]{1,0:T(8,128)(2,1)} %refs_2_.7, ...), custom_call_target="tpu_custom_call" | custom-call | flops 2818572288 | bytes 14680064 | tf_op jit(solution)/shard_map/enter/pallas_call | solution.py:169
  61.8 1.6 collective-permute-start.31
  63.4 7.6 %turn.1.refs_1_ = bf16[2,192,1792]{2,1,0:T(8,128)(2,1)S(1)} custom-call(bf16[96,4096]{1,0:T(8,128)(2,1)S(1)} %constant_dynamic-update-slice_fusion.8.refs_0_, bf16[96,4096]{1,0:T(8,128)(2,1)S(1)} %collective-permute-done.11.refs_1_, bf16[1792,4096]{1,0:T(8,128)(2,1)} %refs_4_.1, f32[192,1792]{1,0:T(8,128)S(1)} %get-tuple-element.51.refs_3_, ...), custom_call_target="tpu_custom_call" | custom-call | flops 2818572288 | bytes 14680064 | tf_op jit(solution)/shard_map/turn/pallas_call | solution.py:213
  71.0 16.4 %leave.1 = (bf16[2,96,4096]{2,1,0:T(8,128)(2,1)S(1)}, bf16[2,96,4096]{2,1,0:T(8,128)(2,1)S(1)}) custom-call(bf16[192,1792]{1,0:T(8,128)(2,1)S(1)} %get-tuple-element.50.refs_0_, bf16[2,192,1792]{2,1,0:T(8,128)(2,1)S(1)} %turn.1.refs_1_, bf16[4096,1792]{1,0:T(8,128)(2,1)} %refs_2_.7, bf16[4096,1792]{1,0:T(8,128)(2,1)} %refs_3_.5, bf16[1792,4096]{1,0:T(8,128)(2,1)} %refs_4_.1), custom_call_target="tpu_custom_call" | custom-call | flops 8455716864 | bytes 44040192 | tf_op jit(solution)/shard_map/leave/pallas_call | solution.py:260
  87.4 0.1 collective-permute-start.12
  87.5 0.3 pad_maximum_fusion.1
  87.8 0.5 collective-permute-start.23
  88.3 1.5 collective-permute-start.30
  89.8 0.6 collective-permute-start.24
  90.4 0.5 collective-permute-start.25
  91.0 15.6 %collective-permute-done.30 = bf16[192,1792]{1,0:T(8,128)(2,1)S(1)} collective-permute-done((bf16[192,1792]{1,0:T(8,128)(2,1)S(1)}, bf16[192,1792]{1,0:T(8,128)(2,1)S(1)}, u32[]{:S(2)}, u32[]{:S(2)}) %collective-permute-start.30) | collective-permute-done | bytes 688160 | tf_op jit(solution)/shard_map/ppermute | solution.py:333
  106.6 1.5 collective-permute-start.32
  108.2 0.6 collective-permute-start.33
  108.7 0.4 fold.1
  109.1 4.8 %collective-permute-start.15 = (bf16[2,24,4096]{2,1,0:T(8,128)(2,1)S(1)}, bf16[2,24,4096]{2,1,0:T(8,128)(2,1)S(1)}, u32[]{:S(2)}, u32[]{:S(2)}) collective-permute-start(bf16[2,24,4096]{2,1,0:T(8,128)(2,1)S(1)} %get-tuple-element.59), channel_id=1, source_target_pairs={{0,8},{4,12},{24,16},{28,20},{1,9},{5,13},{25,17},{29,21},{2,10},{... | collective-permute-start | bytes 1179656 | tf_op jit(solution)/shard_map/ppermute | solution.py:373
  113.9 0.1 fusion.1
  114.0 0.1 copy.11
  114.1 0.4 pad_maximum_fusion
  114.6 0.1 copy.12
  114.7 0.2 copy.13
  114.9 5.3 %collective-permute-done.15 = bf16[2,24,4096]{2,1,0:T(8,128)(2,1)S(1)} collective-permute-done((bf16[2,24,4096]{2,1,0:T(8,128)(2,1)S(1)}, bf16[2,24,4096]{2,1,0:T(8,128)(2,1)S(1)}, u32[]{:S(2)}, u32[]{:S(2)}) %collective-permute-start.15) | collective-permute-done | bytes 393248 | tf_op jit(solution)/shard_map/ppermute | solution.py:373
  120.2 1.3 collective-permute-start.13
  121.5 0.1 add_convert_fusion.1
  121.6 14.5 %collective-permute-done.24 = bf16[2,192,1792]{2,1,0:T(8,128)(2,1)S(1)} collective-permute-done((bf16[2,192,1792]{2,1,0:T(8,128)(2,1)S(1)}, bf16[2,192,1792]{2,1,0:T(8,128)(2,1)S(1)}, u32[]{:S(2)}, u32[]{:S(2)}) %collective-permute-start.24) | collective-permute-done | bytes 1376288 | tf_op jit(solution)/shard_map/ppermute | solution.py:333
  136.1 4.9 %collective-permute-start.14 = (bf16[2,24,4096]{2,1,0:T(8,128)(2,1)S(1)}, bf16[2,24,4096]{2,1,0:T(8,128)(2,1)S(1)}, u32[]{:S(2)}, u32[]{:S(2)}) collective-permute-start(bf16[2,24,4096]{2,1,0:T(8,128)(2,1)S(1)} %get-tuple-element.57), channel_id=1, source_target_pairs={{0,8},{4,12},{8,16},{12,20},{16,24},{20,28},{1,9},{5,13},{9,17},{1... | collective-permute-start | bytes 1179656 | tf_op jit(solution)/shard_map/ppermute | solution.py:373
  141.1 0.9 collective-permute-start.16
  142.4 3.1 %fusion.14 = f32[1024,1792]{1,0:T(8,128)S(1)} fusion(bf16[576,1024]{1,0:T(8,128)(2,1)S(1)} %bitcast.70, bf16[576,1792]{1,0:T(8,128)(2,1)S(1)} %bitcast_dynamic-update-slice_fusion.4), kind=kOutput, calls=%fused_computation.67 | convolution fusion | flops 2113929216 | bytes 10584064 | tf_op jit(solution)/shard_map/dot_general | solution.py:308
  145.6 1.6 collective-permute-start.28
  147.2 0.5 collective-permute-start.29
  147.9 4.6 %convolution_convert_fusion = bf16[1792,1024]{1,0:T(8,128)(2,1)} fusion(bf16[768,1792]{1,0:T(8,128)(2,1)S(1)} %constant_dynamic-update-slice_fusion.18, bf16[768,1024]{1,0:T(8,128)(2,1)S(1)} %bitcast.69), kind=kOutput, calls=%fused_computation.7 | convolution fusion | flops 2820407296 | bytes 7995392 | tf_op jit(solution)/shard_map/dot_general | solution.py:308
  152.5 0.9 collective-permute-done.28
  153.4 0.6 collective-permute-start.27
  154.0 2.3 %collective-permute-done.29 = bf16[96,1792]{1,0:T(8,128)(2,1)S(1)} collective-permute-done((bf16[96,1792]{1,0:T(8,128)(2,1)S(1)}, bf16[96,1792]{1,0:T(8,128)(2,1)S(1)}, u32[]{:S(2)}, u32[]{:S(2)}) %collective-permute-start.29) | collective-permute-done | bytes 344096 | tf_op jit(solution)/shard_map/ppermute | solution.py:333
  156.4 4.5 %convolution_convert_fusion.1 = bf16[1024,1792]{1,0:T(8,128)(2,1)} fusion(bf16[768,1024]{1,0:T(8,128)(2,1)S(1)} %bitcast.68, bf16[768,1792]{1,0:T(8,128)(2,1)S(1)} %constant_dynamic-update-slice_fusion.14), kind=kOutput, calls=%fused_computation.8 | convolution fusion | flops 2820407296 | bytes 7995392 | tf_op jit(solution)/shard_map/dot_general | solution.py:308
  160.9 1.1 collective-permute-done.27
  162.0 1.6 collective-permute-done.26
  163.6 3.0 %add_convert_fusion = bf16[1024,1792]{1,0:T(8,128)(2,1)} fusion(f32[1024,1792]{1,0:T(8,128)S(1)} %fusion.14, bf16[192,1024]{1,0:T(8,128)(2,1)S(1)} %bitcast.67, bf16[96,1792]{1,0:T(8,128)(2,1)S(1)} %collective-permute-done.27, bf16[96,1792]{1,0:T(8,128)(2,1)S(1)} %collective-permute-done.26), kind=kOutput, calls=%fused_computation | convolution fusion | flops 709689344 | bytes 12091392 | tf_op jit(solution)/shard_map/dot_general | solution.py:308
  166.6 0.9 fusion.7
  (65 shorter events, 1.0 us)
Async XLA Ops:
  0.6 1.0 copy-start.1
  1.6 0.7 copy-start.2
  2.6 10.0 %collective-permute-start = (bf16[24,2048]{1,0:T(8,128)(2,1)S(1)}, bf16[24,2048]{1,0:T(8,128)(2,1)S(1)}, u32[]{:S(2)}, u32[]{:S(2)}) collective-permute-start(bf16[24,2048]{1,0:T(8,128)(2,1)S(1)} %get-tuple-element.46), channel_id=1, source_target_pairs={{0,8},{4,12},{8,16},{12,20},{16,24},{20,28},{24,0},{28,4},{1,9},{5... | collective-permute-start | bytes 294920 | tf_op jit(solution)/shard_map/ppermute | solution.py:325
  5.7 12.7 %collective-permute-start.1 = (bf16[24,2048]{1,0:T(8,128)(2,1)S(1)}, bf16[24,2048]{1,0:T(8,128)(2,1)S(1)}, u32[]{:S(2)}, u32[]{:S(2)}) collective-permute-start(bf16[24,2048]{1,0:T(8,128)(2,1)S(1)} %get-tuple-element.46), channel_id=1, source_target_pairs={{0,16},{4,20},{8,24},{12,28},{16,0},{20,4},{24,8},{28,12},{1,17},{... | collective-permute-start | bytes 294920 | tf_op jit(solution)/shard_map/ppermute | solution.py:325
  8.3 33.9 %collective-permute-start.2 = (bf16[24,2048]{1,0:T(8,128)(2,1)S(1)}, bf16[24,2048]{1,0:T(8,128)(2,1)S(1)}, u32[]{:S(2)}, u32[]{:S(2)}) collective-permute-start(bf16[24,2048]{1,0:T(8,128)(2,1)S(1)} %get-tuple-element.46), channel_id=1, source_target_pairs={{0,24},{4,28},{8,0},{12,4},{16,8},{20,12},{24,16},{28,20},{1,25},{... | collective-permute-start | bytes 294920 | tf_op jit(solution)/shard_map/ppermute | solution.py:325
  9.6 10.5 %collective-permute-start.4 = (bf16[24,2048]{1,0:T(8,128)(2,1)S(1)}, bf16[24,2048]{1,0:T(8,128)(2,1)S(1)}, u32[]{:S(2)}, u32[]{:S(2)}) collective-permute-start(bf16[24,2048]{1,0:T(8,128)(2,1)S(1)} %get-tuple-element.47), channel_id=1, source_target_pairs={{0,8},{4,12},{8,16},{12,20},{16,24},{20,28},{24,0},{28,4},{1,9},{5... | collective-permute-start | bytes 294920 | tf_op jit(solution)/shard_map/ppermute | solution.py:325
  10.3 21.4 %collective-permute-start.5 = (bf16[24,2048]{1,0:T(8,128)(2,1)S(1)}, bf16[24,2048]{1,0:T(8,128)(2,1)S(1)}, u32[]{:S(2)}, u32[]{:S(2)}) collective-permute-start(bf16[24,2048]{1,0:T(8,128)(2,1)S(1)} %get-tuple-element.47), channel_id=1, source_target_pairs={{0,16},{4,20},{8,24},{12,28},{16,0},{20,4},{24,8},{28,12},{1,17},{... | collective-permute-start | bytes 294920 | tf_op jit(solution)/shard_map/ppermute | solution.py:325
  11.6 0.9 copy-start
  12.6 19.2 %collective-permute-start.6 = (bf16[24,2048]{1,0:T(8,128)(2,1)S(1)}, bf16[24,2048]{1,0:T(8,128)(2,1)S(1)}, u32[]{:S(2)}, u32[]{:S(2)}) collective-permute-start(bf16[24,2048]{1,0:T(8,128)(2,1)S(1)} %get-tuple-element.47), channel_id=1, source_target_pairs={{0,24},{4,28},{8,0},{12,4},{16,8},{20,12},{24,16},{28,20},{1,25},{... | collective-permute-start | bytes 294920 | tf_op jit(solution)/shard_map/ppermute | solution.py:325
  18.4 15.9 %collective-permute-start.8 = (bf16[24,4096]{1,0:T(8,128)(2,1)}, bf16[24,4096]{1,0:T(8,128)(2,1)S(1)}, u32[]{:S(2)}, u32[]{:S(2)}) collective-permute-start(bf16[24,4096]{1,0:T(8,128)(2,1)} %cot_ref.1), channel_id=1, source_target_pairs={{0,8},{4,12},{8,16},{12,20},{16,24},{20,28},{24,0},{28,4},{1,9},{5... | collective-permute-start | bytes 589832 | tf_op jit(solution)/shard_map/ppermute | solution.py:325
  20.1 17.9 %collective-permute-start.9 = (bf16[24,4096]{1,0:T(8,128)(2,1)}, bf16[24,4096]{1,0:T(8,128)(2,1)S(1)}, u32[]{:S(2)}, u32[]{:S(2)}) collective-permute-start(bf16[24,4096]{1,0:T(8,128)(2,1)} %cot_ref.1), channel_id=1, source_target_pairs={{0,16},{4,20},{8,24},{12,28},{16,0},{20,4},{24,8},{28,12},{1,17},{... | collective-permute-start | bytes 589832 | tf_op jit(solution)/shard_map/ppermute | solution.py:325
  31.7 10.4 %collective-permute-start.10 = (bf16[24,4096]{1,0:T(8,128)(2,1)}, bf16[24,4096]{1,0:T(8,128)(2,1)S(1)}, u32[]{:S(2)}, u32[]{:S(2)}) collective-permute-start(bf16[24,4096]{1,0:T(8,128)(2,1)} %cot_ref.1), channel_id=1, source_target_pairs={{0,24},{4,28},{8,0},{12,4},{16,8},{20,12},{24,16},{28,20},{1,25},{... | collective-permute-start | bytes 589832 | tf_op jit(solution)/shard_map/ppermute | solution.py:325
  31.7 11.0 %collective-permute-start.19 = (bf16[24,2048]{1,0:T(8,128)(2,1)S(1)}, bf16[24,2048]{1,0:T(8,128)(2,1)S(1)}, u32[]{:S(2)}, u32[]{:S(2)}) collective-permute-start(bf16[24,2048]{1,0:T(8,128)(2,1)S(1)} %get-tuple-element.65), channel_id=1, source_target_pairs={{0,3},{1,2},{2,1},{3,0},{4,7},{5,6},{6,5},{7,4},{8,11},{9,10},{10,... | collective-permute-start | bytes 294920 | tf_op jit(solution)/shard_map/ppermute | solution.py:333
  34.3 8.6 %collective-permute-start.18 = (bf16[24,2048]{1,0:T(8,128)(2,1)S(1)}, bf16[24,2048]{1,0:T(8,128)(2,1)S(1)}, u32[]{:S(2)}, u32[]{:S(2)}) collective-permute-start(bf16[24,2048]{1,0:T(8,128)(2,1)S(1)} %get-tuple-element.64), channel_id=1, source_target_pairs={{0,2},{1,3},{2,0},{3,1},{4,6},{5,7},{6,4},{7,5},{8,10},{9,11},{10,... | collective-permute-start | bytes 294920 | tf_op jit(solution)/shard_map/ppermute | solution.py:333
  38.1 4.8 %collective-permute-start.17 = (bf16[24,2048]{1,0:T(8,128)(2,1)S(1)}, bf16[24,2048]{1,0:T(8,128)(2,1)S(1)}, u32[]{:S(2)}, u32[]{:S(2)}) collective-permute-start(bf16[24,2048]{1,0:T(8,128)(2,1)S(1)} %get-tuple-element.63), channel_id=1, source_target_pairs={{0,1},{1,0},{2,3},{3,2},{4,5},{5,4},{6,7},{7,6},{8,9},{9,8},{10,11... | collective-permute-start | bytes 294920 | tf_op jit(solution)/shard_map/ppermute | solution.py:333
  42.1 6.4 %collective-permute-start.7 = (bf16[96,2048]{1,0:T(8,128)(2,1)S(1)}, bf16[96,2048]{1,0:T(8,128)(2,1)S(1)}, u32[]{:S(2)}, u32[]{:S(2)}) collective-permute-start(bf16[96,2048]{1,0:T(8,128)(2,1)S(1)} %constant_dynamic-update-slice_fusion.4.refs_0_), channel_id=1, source_target_pairs={{0,4},{4,0},{8,12},{12,8},{16,20},{20,16},{24,28},{28,24},{1,5},{5... | collective-permute-start | bytes 1179656 | tf_op jit(solution)/shard_map/ppermute | solution.py:329
  42.2 21.2 %collective-permute-start.11 = (bf16[96,4096]{1,0:T(8,128)(2,1)S(1)}, bf16[96,4096]{1,0:T(8,128)(2,1)S(1)}, u32[]{:S(2)}, u32[]{:S(2)}) collective-permute-start(bf16[96,4096]{1,0:T(8,128)(2,1)S(1)} %constant_dynamic-update-slice_fusion.8.refs_0_), channel_id=1, source_target_pairs={{0,4},{4,0},{8,12},{12,8},{16,20},{20,16},{24,28},{28,24},{1,5},{5... | collective-permute-start | bytes 2359304 | tf_op jit(solution)/shard_map/ppermute | solution.py:329
  42.8 12.7 %collective-permute-start.3 = (bf16[96,2048]{1,0:T(8,128)(2,1)S(1)}, bf16[96,2048]{1,0:T(8,128)(2,1)S(1)}, u32[]{:S(2)}, u32[]{:S(2)}) collective-permute-start(bf16[96,2048]{1,0:T(8,128)(2,1)S(1)} %constant_dynamic-update-slice_fusion.refs_0_), channel_id=1, source_target_pairs={{0,4},{4,0},{8,12},{12,8},{16,20},{20,16},{24,28},{28,24},{1,5},{5... | collective-permute-start | bytes 1179656 | tf_op jit(solution)/shard_map/ppermute | solution.py:329
  42.9 44.5 %collective-permute-start.22 = (bf16[4,24,2048]{2,1,0:T(8,128)(2,1)S(1)}, bf16[4,24,2048]{2,1,0:T(8,128)(2,1)S(1)}, u32[]{:S(2)}, u32[]{:S(2)}) collective-permute-start(bf16[4,24,2048]{2,1,0:T(8,128)(2,1)S(1)} %get-tuple-element.108), channel_id=1, source_target_pairs={{0,24},{4,28},{8,0},{12,4},{16,8},{20,12},{24,16},{28,20},{1,25},{... | collective-permute-start | bytes 1179656 | tf_op jit(solution)/shard_map/ppermute | solution.py:325
  48.5 39.0 %collective-permute-start.21 = (bf16[4,24,2048]{2,1,0:T(8,128)(2,1)S(1)}, bf16[4,24,2048]{2,1,0:T(8,128)(2,1)S(1)}, u32[]{:S(2)}, u32[]{:S(2)}) collective-permute-start(bf16[4,24,2048]{2,1,0:T(8,128)(2,1)S(1)} %get-tuple-element.108), channel_id=1, source_target_pairs={{0,16},{4,20},{8,24},{12,28},{16,0},{20,4},{24,8},{28,12},{1,17},{... | collective-permute-start | bytes 1179656 | tf_op jit(solution)/shard_map/ppermute | solution.py:325
  48.5 39.0 %collective-permute-start.20 = (bf16[4,24,2048]{2,1,0:T(8,128)(2,1)S(1)}, bf16[4,24,2048]{2,1,0:T(8,128)(2,1)S(1)}, u32[]{:S(2)}, u32[]{:S(2)}) collective-permute-start(bf16[4,24,2048]{2,1,0:T(8,128)(2,1)S(1)} %get-tuple-element.108), channel_id=1, source_target_pairs={{0,8},{4,12},{8,16},{12,20},{16,24},{20,28},{24,0},{28,4},{1,9},{5... | collective-permute-start | bytes 1179656 | tf_op jit(solution)/shard_map/ppermute | solution.py:325
  61.8 28.7 %collective-permute-start.31 = (bf16[192,1792]{1,0:T(8,128)(2,1)S(1)}, bf16[192,1792]{1,0:T(8,128)(2,1)S(1)}, u32[]{:S(2)}, u32[]{:S(2)}) collective-permute-start(bf16[192,1792]{1,0:T(8,128)(2,1)S(1)} %get-tuple-element.50.refs_0_), channel_id=1, source_target_pairs={{0,2},{1,3},{2,0},{3,1},{4,6},{5,7},{6,4},{7,5},{8,10},{9,11},{10,... | collective-permute-start | bytes 2064392 | tf_op jit(solution)/shard_map/ppermute | solution.py:333
  87.4 20.8 %collective-permute-start.12 = (bf16[2,96,4096]{2,1,0:T(8,128)(2,1)S(1)}, bf16[2,96,4096]{2,1,0:T(8,128)(2,1)S(1)}, u32[]{:S(2)}, u32[]{:S(2)}) collective-permute-start(bf16[2,96,4096]{2,1,0:T(8,128)(2,1)S(1)} %get-tuple-element.54), channel_id=1, source_target_pairs={{0,4},{4,0},{8,12},{12,8},{16,20},{20,16},{24,28},{28,24},{1,5},{5... | collective-permute-start | bytes 4718600 | tf_op jit(solution)/shard_map/ppermute | solution.py:329
  87.8 21.4 %collective-permute-start.23 = (bf16[4,4,24,2048]{3,2,0,1:T(8,128)(2,1)S(1)}, bf16[4,4,24,2048]{3,2,0,1:T(8,128)(2,1)S(1)}, u32[]{:S(2)}, u32[]{:S(2)}) collective-permute-start(bf16[4,4,24,2048]{3,2,0,1:T(8,128)(2,1)S(1)} %get-tuple-element.85), channel_id=1, source_target_pairs={{0,4},{4,0},{8,12},{12,8},{16,20},{20,16},{24,28},{28,24},{1,5},{5... | collective-permute-start | bytes 4718600 | tf_op jit(solution)/shard_map/ppermute | solution.py:329
  88.3 18.3 %collective-permute-start.30 = (bf16[192,1792]{1,0:T(8,128)(2,1)S(1)}, bf16[192,1792]{1,0:T(8,128)(2,1)S(1)}, u32[]{:S(2)}, u32[]{:S(2)}) collective-permute-start(bf16[192,1792]{1,0:T(8,128)(2,1)S(1)} %get-tuple-element.50.refs_0_), channel_id=1, source_target_pairs={{0,1},{1,0},{2,3},{3,2},{4,5},{5,4},{6,7},{7,6},{8,9},{9,8},{10,11... | collective-permute-start | bytes 2064392 | tf_op jit(solution)/shard_map/ppermute | solution.py:333
  89.8 46.3 %collective-permute-start.24 = (bf16[2,192,1792]{2,1,0:T(8,128)(2,1)S(1)}, bf16[2,192,1792]{2,1,0:T(8,128)(2,1)S(1)}, u32[]{:S(2)}, u32[]{:S(2)}) collective-permute-start(bf16[2,192,1792]{2,1,0:T(8,128)(2,1)S(1)} %turn.1.refs_1_), channel_id=1, source_target_pairs={{0,1},{1,0},{2,3},{3,2},{4,5},{5,4},{6,7},{7,6},{8,9},{9,8},{10,11... | collective-permute-start | bytes 4128776 | tf_op jit(solution)/shard_map/ppermute | solution.py:333
  90.4 50.6 %collective-permute-start.25 = (bf16[2,192,1792]{2,1,0:T(8,128)(2,1)S(1)}, bf16[2,192,1792]{2,1,0:T(8,128)(2,1)S(1)}, u32[]{:S(2)}, u32[]{:S(2)}) collective-permute-start(bf16[2,192,1792]{2,1,0:T(8,128)(2,1)S(1)} %turn.1.refs_1_), channel_id=1, source_target_pairs={{0,2},{1,3},{2,0},{3,1},{4,6},{5,7},{6,4},{7,5},{8,10},{9,11},{10,... | collective-permute-start | bytes 4128776 | tf_op jit(solution)/shard_map/ppermute | solution.py:333
  106.6 39.0 %collective-permute-start.32 = (bf16[96,1792]{1,0:T(8,128)(2,1)S(1)}, bf16[96,1792]{1,0:T(8,128)(2,1)S(1)}, u32[]{:S(2)}, u32[]{:S(2)}) collective-permute-start(bf16[96,1792]{1,0:T(8,128)(2,1)S(1)} %get-tuple-element.77), channel_id=1, source_target_pairs={{0,1},{1,0},{2,3},{3,2},{4,5},{5,4},{6,7},{7,6},{8,9},{9,8},{10,11... | collective-permute-start | bytes 1032200 | tf_op jit(solution)/shard_map/ppermute | solution.py:333
  108.2 39.0 %collective-permute-start.33 = (bf16[96,1792]{1,0:T(8,128)(2,1)S(1)}, bf16[96,1792]{1,0:T(8,128)(2,1)S(1)}, u32[]{:S(2)}, u32[]{:S(2)}) collective-permute-start(bf16[96,1792]{1,0:T(8,128)(2,1)S(1)} %get-tuple-element.76), channel_id=1, source_target_pairs={{0,2},{1,3},{2,0},{3,1},{4,6},{5,7},{6,4},{7,5},{8,10},{9,11},{10,... | collective-permute-start | bytes 1032200 | tf_op jit(solution)/shard_map/ppermute | solution.py:333
  109.1 11.1 %collective-permute-start.15 = (bf16[2,24,4096]{2,1,0:T(8,128)(2,1)S(1)}, bf16[2,24,4096]{2,1,0:T(8,128)(2,1)S(1)}, u32[]{:S(2)}, u32[]{:S(2)}) collective-permute-start(bf16[2,24,4096]{2,1,0:T(8,128)(2,1)S(1)} %get-tuple-element.59), channel_id=1, source_target_pairs={{0,8},{4,12},{24,16},{28,20},{1,9},{5,13},{25,17},{29,21},{2,10},{... | collective-permute-start | bytes 1179656 | tf_op jit(solution)/shard_map/ppermute | solution.py:373
  120.2 46.4 %collective-permute-start.13 = (bf16[2,24,4096]{2,1,0:T(8,128)(2,1)S(1)}, bf16[2,24,4096]{2,1,0:T(8,128)(2,1)S(1)}, u32[]{:S(2)}, u32[]{:S(2)}) collective-permute-start(bf16[2,24,4096]{2,1,0:T(8,128)(2,1)S(1)} %get-tuple-element.56), channel_id=1, source_target_pairs={{8,0},{12,4},{16,8},{20,12},{24,16},{28,20},{9,1},{13,5},{17,9},{2... | collective-permute-start | bytes 1179656 | tf_op jit(solution)/shard_map/ppermute | solution.py:373
  136.1 30.5 %collective-permute-start.14 = (bf16[2,24,4096]{2,1,0:T(8,128)(2,1)S(1)}, bf16[2,24,4096]{2,1,0:T(8,128)(2,1)S(1)}, u32[]{:S(2)}, u32[]{:S(2)}) collective-permute-start(bf16[2,24,4096]{2,1,0:T(8,128)(2,1)S(1)} %get-tuple-element.57), channel_id=1, source_target_pairs={{0,8},{4,12},{8,16},{12,20},{16,24},{20,28},{1,9},{5,13},{9,17},{1... | collective-permute-start | bytes 1179656 | tf_op jit(solution)/shard_map/ppermute | solution.py:373
  141.1 25.5 %collective-permute-start.16 = (bf16[2,24,4096]{2,1,0:T(8,128)(2,1)S(1)}, bf16[2,24,4096]{2,1,0:T(8,128)(2,1)S(1)}, u32[]{:S(2)}, u32[]{:S(2)}) collective-permute-start(bf16[2,24,4096]{2,1,0:T(8,128)(2,1)S(1)} %add_convert_fusion.1), channel_id=1, source_target_pairs={{0,16},{4,20},{8,24},{12,28},{16,0},{20,4},{24,8},{28,12},{1,17},{... | collective-permute-start | bytes 1179656 | tf_op jit(solution)/shard_map/ppermute | solution.py:325
  145.6 7.8 %collective-permute-start.28 = (bf16[96,1792]{1,0:T(8,128)(2,1)S(1)}, bf16[96,1792]{1,0:T(8,128)(2,1)S(1)}, u32[]{:S(2)}, u32[]{:S(2)}) collective-permute-start(bf16[96,1792]{1,0:T(8,128)(2,1)S(1)} %get-tuple-element.89), channel_id=1, source_target_pairs={{0,1},{1,0},{2,3},{3,2},{4,5},{5,4},{6,7},{7,6},{8,9},{9,8},{10,11... | collective-permute-start | bytes 1032200 | tf_op jit(solution)/shard_map/ppermute | solution.py:333
  147.2 9.2 %collective-permute-start.29 = (bf16[96,1792]{1,0:T(8,128)(2,1)S(1)}, bf16[96,1792]{1,0:T(8,128)(2,1)S(1)}, u32[]{:S(2)}, u32[]{:S(2)}) collective-permute-start(bf16[96,1792]{1,0:T(8,128)(2,1)S(1)} %get-tuple-element.87), channel_id=1, source_target_pairs={{0,2},{1,3},{2,0},{3,1},{4,6},{5,7},{6,4},{7,5},{8,10},{9,11},{10,... | collective-permute-start | bytes 1032200 | tf_op jit(solution)/shard_map/ppermute | solution.py:333
  153.4 8.6 %collective-permute-start.27 = (bf16[96,1792]{1,0:T(8,128)(2,1)S(1)}, bf16[96,1792]{1,0:T(8,128)(2,1)S(1)}, u32[]{:S(2)}, u32[]{:S(2)}) collective-permute-start(bf16[96,1792]{1,0:T(8,128)(2,1)S(1)} %get-tuple-element.88), channel_id=1, source_target_pairs={{0,2},{1,3},{2,0},{3,1},{4,6},{5,7},{6,4},{7,5},{8,10},{9,11},{10,... | collective-permute-start | bytes 1032200 | tf_op jit(solution)/shard_map/ppermute | solution.py:333
  156.3 7.2 %collective-permute-start.26 = (bf16[96,1792]{1,0:T(8,128)(2,1)S(1)}, bf16[96,1792]{1,0:T(8,128)(2,1)S(1)}, u32[]{:S(2)}, u32[]{:S(2)}) collective-permute-start(bf16[96,1792]{1,0:T(8,128)(2,1)S(1)} %get-tuple-element.90), channel_id=1, source_target_pairs={{0,1},{1,0},{2,3},{3,2},{4,5},{5,4},{6,7},{7,6},{8,9},{9,8},{10,11... | collective-permute-start | bytes 1032200 | tf_op jit(solution)/shard_map/ppermute | solution.py:333
